TPU v7x, 128 devices: a whole 4x4x4 slice. The times are simulated.
128 devices in a mesh: dp: 4 (over y_lo, core), seq: 32 (over x, y_hi, z).
Axes of the slice: x: 4, y: 4 (y_hi: 2, y_lo: 2; y = y_hi * 2 + y_lo), z: 4, core: 2. Of those that a mesh axis runs over, the one named last changes fastest.
Arguments:
- tokens: bfloat16 [4, 16384, 2048], P('dp', 'seq'), may hold values from -5 to 5, as said below
- gain_first: float32 [2048], replicated, may hold values from 0.25 to 1.75
- inputs_first: bfloat16 [2048, 3072], P(('dp', 'seq')), may hold values from -1 to 1, as said below
- output_first: bfloat16 [1024, 2048], P(('dp', 'seq')), may hold values from -0.5 to 0.5
- gain_second: float32 [2048], replicated, may hold values from 0.25 to 1.75
- inputs_second: bfloat16 [2048, 3072], P(('dp', 'seq')), may hold values from -1 to 1, as said below
- output_second: bfloat16 [1024, 2048], P(('dp', 'seq')), may hold values from -0.5 to 0.5
- starts: int32 [4, 32], P('dp'), may hold values from 0 to 32256, as said below
- band_edges: int32 [2], replicated, may hold values from 4 to 62, as said below
Outputs:
- layer_out: bfloat16 [4, 16384, 2048], P('dp', 'seq')
Inputs may be any that keep to these rules, and one draw needn't show every extreme that they name: `tokens`: entries are real-valued and lie within -5 to 5. `inputs_first`: entries lie within -6 / sqrt(2048) to 6 / sqrt(2048). `inputs_second`: entries lie within -6 / sqrt(2048) to 6 / sqrt(2048). `starts`: along a sequence each start exceeds the one before by 512 to 1024; the first is at most 512. band_edges[0] < band_edges[1], with at least 4 between them; band_edges[1] is 62.
All inputs are finite; a program needn't handle non-finite values.
Results may differ from a plain program's by a relative error of at most 0.025.
Values may be sent and summed in bfloat16 or wider, within the bound.
No kernel may reach another device: no remote copies, remote signals or barrier semaphores. Data moves between devices by JAX's collectives and lax.ppermute only.
A program may use at most 128 MiB of HBM per device.

v0:
```python
import math

import jax
import jax.numpy as jnp
from jax import lax
from jax.sharding import PartitionSpec as P

HEADS = 8
HEAD = 128
C = 512
SCALE = 8


def normed(values, gain):
    as_float = values.astype(jnp.float32)
    inv_rms = lax.rsqrt(jnp.mean(as_float * as_float, axis=-1, keepdims=True) + 1e-05)
    return (as_float * inv_rms * gain).astype(jnp.bfloat16)


def frequencies(band_edges, half_size):
    dim_index = jnp.arange(half_size, dtype=jnp.float32)
    base_freq = jnp.power(10000.0, -dim_index / half_size)
    lower_edge = band_edges[0].astype(jnp.float32)
    upper_edge = band_edges[1].astype(jnp.float32)
    ramp_share = jnp.clip((dim_index - lower_edge) / (upper_edge - lower_edge), 0.0, 1.0)
    return base_freq * (1.0 - ramp_share) + base_freq * ramp_share / SCALE


def rotary(projected, positions, frequency):
    half_size = frequency.shape[0]
    angles = positions.astype(jnp.float32)[..., None] * frequency
    mscale = 0.1 * math.log(SCALE) + 1.0
    cosine = (jnp.cos(angles) * mscale)[..., None, :]
    sine_part = (jnp.sin(angles) * mscale)[..., None, :]
    first_half = projected[..., :half_size]
    second_half = projected[..., half_size:]
    return jnp.concatenate(
        [
            first_half * cosine - second_half * sine_part,
            second_half * cosine + first_half * sine_part,
        ],
        axis=-1,
    ).astype(jnp.bfloat16)


def softmax_rows(scores):
    row_max = jnp.max(scores, axis=-1, keepdims=True)
    weights = jnp.exp(scores - row_max)
    return (weights / jnp.sum(weights, axis=-1, keepdims=True)).astype(jnp.bfloat16)


def attend_block(triple):
    queries, key_rows, values = triple
    length = queries.shape[0]
    scores = jnp.einsum(
        "qd,kd->qk", queries, key_rows, preferred_element_type=jnp.float32
    ) / math.sqrt(queries.shape[-1])
    causal = jnp.arange(length)[None, :] <= jnp.arange(length)[:, None]
    scores = jnp.where(causal, scores, -1e30)
    probability = softmax_rows(scores)
    return jnp.dot(probability, values, preferred_element_type=jnp.float32).astype(jnp.bfloat16)


def row_attention(queries, key_rows, values):
    grid_rows, row_len, head_count, head_size = queries.shape

    def flatten_heads(tensor):
        return tensor.transpose(0, 2, 1, 3).reshape(grid_rows * head_count, row_len, head_size)

    result = lax.map(
        attend_block, (flatten_heads(queries), flatten_heads(key_rows), flatten_heads(values))
    )
    return result.reshape(grid_rows, head_count, row_len, head_size).transpose(0, 2, 1, 3)


def column_attention(queries, key_rows, values):
    length = queries.shape[0]
    scores = jnp.einsum(
        "rchd,schd->chrs", queries, key_rows, preferred_element_type=jnp.float32
    ) / math.sqrt(queries.shape[-1])
    causal = jnp.arange(length)[None, :] <= jnp.arange(length)[:, None]
    scores = jnp.where(causal[None, None], scores, -1e30)
    probability = softmax_rows(scores)
    return jnp.einsum(
        "chrs,schd->rchd", probability, values, preferred_element_type=jnp.float32
    ).astype(jnp.bfloat16)


def columns_then_back(triple):
    attended = column_attention(triple[0], triple[1], triple[2])
    return lax.all_to_all(attended, "seq", split_axis=0, concat_axis=1, tiled=True)


def accumulate(hidden, block_rows):
    return jnp.dot(hidden, block_rows, preferred_element_type=jnp.float32)


def shards(
    tokens,
    gain_first,
    inputs_first,
    output_first,
    gain_second,
    inputs_second,
    output_second,
    starts,
    band_edges,
):
    residual = tokens[0]
    tok_count, model_width = residual.shape
    rows_dev = tok_count // C
    attn_width = HEADS * HEAD
    frequency = frequencies(band_edges, HEAD // 2)
    block_starts = starts[0]
    own_start = lax.dynamic_index_in_dim(block_starts, lax.axis_index("seq"), 0, keepdims=False)
    position_grid = (own_start + jnp.arange(tok_count, dtype=jnp.int32)).reshape(rows_dev, C)
    hidden = normed(residual, gain_first)
    group_rows = lax.all_gather(inputs_first, "seq", axis=0, tiled=True)
    projected = accumulate(hidden, lax.all_gather(group_rows, "dp", axis=0, tiled=True))
    projected = projected.reshape(rows_dev, C, 3, HEADS, HEAD)
    queries = rotary(projected[:, :, 0], position_grid, frequency)
    key_rows = rotary(projected[:, :, 1], position_grid, frequency)
    values = projected[:, :, 2].astype(jnp.bfloat16)
    attended = row_attention(queries, key_rows, values).reshape(tok_count, attn_width)
    group_rows = lax.all_gather(output_first, "seq", axis=0, tiled=True)
    branch = accumulate(attended, lax.all_gather(group_rows, "dp", axis=0, tiled=True))
    middle = (residual.astype(jnp.float32) + branch).astype(jnp.bfloat16)
    hidden = normed(middle, gain_second)
    second_rows = lax.all_gather(inputs_second, "seq", axis=0, tiled=True)
    projected = accumulate(hidden, lax.all_gather(second_rows, "dp", axis=0, tiled=True)).reshape(
        rows_dev, C, 3, HEADS, HEAD
    )
    queries = rotary(projected[:, :, 0], position_grid, frequency)
    key_rows = rotary(projected[:, :, 1], position_grid, frequency)
    values = projected[:, :, 2].astype(jnp.bfloat16)
    attended = columns_then_back(
        (
            lax.all_to_all(queries, "seq", split_axis=1, concat_axis=0, tiled=True),
            lax.all_to_all(key_rows, "seq", split_axis=1, concat_axis=0, tiled=True),
            lax.all_to_all(values, "seq", split_axis=1, concat_axis=0, tiled=True),
        )
    )
    attended = attended.reshape(tok_count, attn_width)
    group_rows = lax.all_gather(output_second, "seq", axis=0, tiled=True)
    branch = accumulate(attended, lax.all_gather(group_rows, "dp", axis=0, tiled=True))
    return (middle.astype(jnp.float32) + branch).astype(jnp.bfloat16)[None]


def solution(mesh):
    return jax.shard_map(
        shards,
        mesh=mesh,
        in_specs=(
            P("dp", "seq", None),
            P(),
            P(("dp", "seq"), None),
            P(("dp", "seq"), None),
            P(),
            P(("dp", "seq"), None),
            P(("dp", "seq"), None),
            P("dp", None),
            P(),
        ),
        out_specs=P("dp", "seq", None),
        check_vma=False,
    )
```

profile of v0, /device:TPU:0, one launch (start us, length us, event | category | flops | bytes accessed | tf_op | source)
XLA Modules:
  0.0 710.8 jit_solution(3117279610338200591)
XLA Ops:
  6.5 0.7 all-gather.9.cloned.1.call-update
  7.3 0.7 all-gather.13.cloned.1.call-update
  8.1 0.7 all-gather.17.cloned.1.call-update
  9.4 78.6 %all-gather.9.cloned.1.call-done = bf16[512,3072]{1,0:T(8,128)(2,1)} async-done(((bf16[16,3072]{1,0:T(8,128)(2,1)}), bf16[512,3072]{1,0:T(8,128)(2,1)}) %all-gather.9.cloned.1.call-update) | async-done | bytes 3145744 | tf_op jit(solution)/shard_map/all_gather | solution.py:118
  88.0 66.6 %all-gather.13.cloned.1.call-done = bf16[256,2048]{1,0:T(8,128)(2,1)} async-done(((bf16[8,2048]{1,0:T(8,128)(2,1)}), bf16[256,2048]{1,0:T(8,128)(2,1)}) %all-gather.13.cloned.1.call-update) | async-done | bytes 1048592 | tf_op jit(solution)/shard_map/all_gather | solution.py:125
  154.7 74.8 %all-gather.17.cloned.1.call-done = bf16[512,3072]{1,0:T(8,128)(2,1)} async-done(((bf16[16,3072]{1,0:T(8,128)(2,1)}), bf16[512,3072]{1,0:T(8,128)(2,1)}) %all-gather.17.cloned.1.call-update) | async-done | bytes 3145744 | tf_op jit(solution)/shard_map/all_gather | solution.py:129
  229.6 0.7 fusion.62
  231.7 0.7 constant_dynamic-slice_fusion
  232.3 0.7 add_convert_fusion.4
  233.6 0.5 fusion.45
  234.1 62.0 %all-gather.21.cloned.1.call-done = bf16[256,2048]{1,0:T(8,128)(2,1)} async-done(((bf16[8,2048]{1,0:T(8,128)(2,1)}), bf16[256,2048]{1,0:T(8,128)(2,1)}) %all-gather.21.cloned.1.call-update) | async-done | bytes 1048592 | tf_op jit(solution)/shard_map/all_gather | solution.py:144
  296.1 112.7 %all-gather.11.cloned.1.call-done = bf16[2048,3072]{1,0:T(8,128)(2,1)} async-done(((bf16[512,3072]{1,0:T(8,128)(2,1)}), bf16[2048,3072]{1,0:T(8,128)(2,1)}) %all-gather.11.cloned.1.call-update) | async-done | bytes 12582928 | tf_op jit(solution)/shard_map/all_gather | solution.py:119
  408.8 16.9 %copy.33 = bf16[3072,2048]{1,0:T(8,128)(2,1)} copy(bf16[3072,2048]{0,1:T(8,128)(2,1)} %bitcast.97) | data formatting | bytes 25165824 | tf_op jit(solution)/shard_map/dot_general | solution.py:95
  425.7 9.6 %convolution_bitcast_fusion = f32[1,512,3,8,128]{1,4,3,2,0:T(8,128)S(1)} fusion(bf16[3,8,128,2048]{3,2,1,0:T(8,128)(2,1)} %bitcast.98, bf16[1,512,2048]{2,1,0:T(8,128)(2,1)S(1)} %copy-done.3, f32[2048]{0:T(1024)S(1)} %copy-done.5, f32[512]{0:T(512)S(1)} %add_rsqrt_fusion.1), kind=kOutput, calls=%fused_computation.34 | convolution fusion | flops 6446645248 | bytes 20981760 | tf_op jit(solution)/shard_map/dot_general | solution.py:95
  435.8 1.1 fusion.33
  436.9 0.7 subtract_convert_fusion.2
  437.7 1.5 maximum_bitcast_fusion
  439.1 28.9 %while.10 = (s32[]{:T(128)}, bf16[8,512,128]{1,2,0:T(8,128)(2,1)}, bf16[8,512,128]{1,2,0:T(8,128)(2,1)}, bf16[8,512,128]{1,2,0:T(8,128)(2,1)}, bf16[8,512,128]{1,2,0:T(8,128)(2,1)}, /*index=5*/s32[]{:T(128)}) while((s32[]{:T(128)}, bf16[8,512,128]{1,2,0:T(8,128)(2,1)}, bf16[8,512,128]{1,2,0:T(8,128)(2,1)}, bf16[8,512,128]{1,2,0:T(8,128)(2,1)}, ...), condition=%wide.region_4.5_spmd, body=%wide.region_1.4_spmd.sunk | while | flops 136641536 | bytes 4206661 | solution.py:70
  439.1 1.3 fusion.78
  440.7 1.3 fusion.80
  442.1 0.7 constant_dynamic-update-slice_fusion.2
  442.8 1.3 fusion.78
  444.3 1.3 fusion.80
  445.7 0.7 constant_dynamic-update-slice_fusion.2
  446.4 1.3 fusion.78
  447.9 1.3 fusion.80
  449.3 0.7 constant_dynamic-update-slice_fusion.2
  450.0 1.3 fusion.78
  451.5 1.3 fusion.80
  452.9 0.7 constant_dynamic-update-slice_fusion.2
  453.6 1.3 fusion.78
  455.1 1.3 fusion.80
  456.5 0.7 constant_dynamic-update-slice_fusion.2
  457.2 1.3 fusion.78
  458.7 1.3 fusion.80
  460.1 0.7 constant_dynamic-update-slice_fusion.2
  460.8 1.3 fusion.78
  462.3 1.3 fusion.80
  463.7 0.7 constant_dynamic-update-slice_fusion.2
  464.4 1.3 fusion.78
  465.9 1.3 fusion.80
  467.3 0.7 constant_dynamic-update-slice_fusion.2
  468.0 6.6 fusion.18
  474.6 102.0 %all-gather.19.cloned.1.call-done = bf16[2048,3072]{1,0:T(8,128)(2,1)} async-done(((bf16[512,3072]{1,0:T(8,128)(2,1)}), bf16[2048,3072]{1,0:T(8,128)(2,1)}) %all-gather.19.cloned.1.call-update) | async-done | bytes 12582928 | tf_op jit(solution)/shard_map/all_gather | solution.py:130
  576.6 10.4 %fusion.23 = f32[512,3072]{0,1:T(8,128)S(1)} fusion(bf16[2048,3072]{1,0:T(8,128)(2,1)} %all-gather.19.cloned.1.call-done, bf16[512,2048]{1,0:T(8,128)(2,1)} %get-tuple-element.81, f32[2048]{0:T(1024)S(1)} %copy-done.6, f32[512]{0:T(512)S(1)} %add_rsqrt_fusion), kind=kOutput, calls=%fused_computation.35 | convolution fusion | flops 6446645248 | bytes 20981760 | tf_op jit(solution)/shard_map/dot_general | solution.py:95
  587.0 0.6 slice_bitcast_fusion.1
  587.7 2.0 copy-done.2
  589.7 0.7 subtract_convert_fusion.1
  590.5 1.5 copy.40
  592.0 9.8 %all-to-all-start.1 = ((bf16[1,512,8,128]{3,2,0,1:T(8,128)(2,1)}), bf16[1,512,8,128]{3,2,0,1:T(8,128)(2,1)S(1)}, u32[]{:S(2)}, u32[]{:S(2)}) async-start(bf16[1,512,8,128]{3,2,0,1:T(8,128)(2,1)} %copy.40), calls=%async_computation.1 | async-start | bytes 2097152 | tf_op jit(solution)/shard_map/all_to_all | solution.py:138
  601.9 1.5 copy.41
  603.4 19.6 %all-to-all-done.1 = bf16[1,512,8,128]{3,2,0,1:T(8,128)(2,1)S(1)} async-done(((bf16[1,512,8,128]{3,2,0,1:T(8,128)(2,1)}), bf16[1,512,8,128]{3,2,0,1:T(8,128)(2,1)S(1)}, u32[]{:S(2)}, u32[]{:S(2)}) %all-to-all-start.1) | async-done | bytes 1048608 | tf_op jit(solution)/shard_map/all_to_all | solution.py:138
  623.0 5.4 all-to-all-start.2
  628.3 1.7 fusion.34
  630.1 1.5 copy.39
  631.5 17.8 %all-to-all-done.2 = bf16[1,512,8,128]{3,2,0,1:T(8,128)(2,1)S(1)} async-done(((bf16[1,512,8,128]{3,2,0,1:T(8,128)(2,1)}), bf16[1,512,8,128]{3,2,0,1:T(8,128)(2,1)S(1)}, u32[]{:S(2)}, u32[]{:S(2)}) %all-to-all-start.2) | async-done | bytes 1048608 | tf_op jit(solution)/shard_map/all_to_all | solution.py:139
  649.3 4.7 all-to-all-start
  654.0 3.3 fusion.63
  657.3 14.7 %all-to-all-done = bf16[1,512,8,128]{3,2,0,1:T(8,128)(2,1)S(1)} async-done(((bf16[1,512,8,128]{3,2,0,1:T(8,128)(2,1)}), bf16[1,512,8,128]{3,2,0,1:T(8,128)(2,1)S(1)}, u32[]{:S(2)}, u32[]{:S(2)}) %all-to-all-start) | async-done | bytes 1048608 | tf_op jit(solution)/shard_map/all_to_all | solution.py:140
  672.0 2.6 fusion.32
  674.6 1.4 copy.46
  676.0 4.6 all-to-all-start.3
  680.6 17.5 %all-to-all-done.3 = bf16[32,16,8,128]{3,2,1,0:T(8,128)(2,1)S(1)} async-done(((bf16[32,16,8,128]{3,2,1,0:T(8,128)(2,1)}), bf16[32,16,8,128]{3,2,1,0:T(8,128)(2,1)S(1)}, u32[]{:S(2)}, u32[]{:S(2)}) %all-to-all-start.3) | async-done | bytes 1048608 | tf_op jit(solution)/shard_map/all_to_all | solution.py:91
  698.1 5.9 fusion.22
  (55 shorter events, 4.6 us)
Async XLA Ops:
  6.5 225.1 %copy-start = (s32[1,32]{1,0:T(1,128)S(1)}, s32[1,32]{1,0:T(1,128)}, u32[]{:S(2)}) copy-start(s32[1,32]{1,0:T(1,128)} %param.18) | copy-start | bytes 388
  6.5 81.4 %all-gather.9.cloned.1.call-start = ((), (), s32[]{:S(2)}) async-start(), calls=%async_computation.4 | async-start | bytes 3244032 | tf_op jit(solution)/shard_map/all_gather | solution.py:118
  7.3 147.4 %all-gather.13.cloned.1.call-start = ((), (), s32[]{:S(2)}) async-start(), calls=%async_computation.6 | async-start | bytes 1081344 | tf_op jit(solution)/shard_map/all_gather | solution.py:125
  8.0 221.5 %all-gather.17.cloned.1.call-start = ((), (), s32[]{:S(2)}) async-start(), calls=%async_computation.8 | async-start | bytes 3244032 | tf_op jit(solution)/shard_map/all_gather | solution.py:129
  8.7 287.3 %all-gather.21.cloned.1.call-start = ((), (), s32[]{:S(2)}) async-start(), calls=%async_computation.10 | async-start | bytes 1081344 | tf_op jit(solution)/shard_map/all_gather | solution.py:144
  9.3 399.5 %all-gather.11.cloned.1.call-start = ((), (), s32[]{:S(2)}) async-start(), calls=%async_computation.5 | async-start | bytes 15728640 | tf_op jit(solution)/shard_map/all_gather | solution.py:119
  88.0 380.0 %all-gather.15.cloned.1.call-start = ((), (), s32[]{:S(2)}) async-start(), calls=%async_computation.7 | async-start | bytes 5242880 | tf_op jit(solution)/shard_map/all_gather | solution.py:126
  154.6 75.0 %copy-start.4 = (s32[2]{0:T(128)S(1)}, s32[2]{0:T(128)}, u32[]{:S(2)}) copy-start(s32[2]{0:T(128)} %param.19) | copy-start | bytes 28
  154.6 78.4 %copy-start.3 = (bf16[1,512,2048]{2,1,0:T(8,128)(2,1)S(1)}, bf16[1,512,2048]{2,1,0:T(8,128)(2,1)}, u32[]{:S(2)}) copy-start(bf16[1,512,2048]{2,1,0:T(8,128)(2,1)} %param.11) | copy-start | bytes 6291460
  154.7 422.0 %all-gather.19.cloned.1.call-start = ((), (), s32[]{:S(2)}) async-start(), calls=%async_computation.9 | async-start | bytes 15728640 | tf_op jit(solution)/shard_map/all_gather | solution.py:130
  229.6 451.0 %all-gather.23.cloned.1.call-start = ((), (), s32[]{:S(2)}) async-start(), calls=%async_computation.11 | async-start | bytes 5242880 | tf_op jit(solution)/shard_map/all_gather | solution.py:145
  408.8 16.9 %copy-start.5 = (f32[2048]{0:T(1024)S(1)}, f32[2048]{0:T(1024)}, u32[]{:S(2)}) copy-start(f32[2048]{0:T(1024)} %param.12) | copy-start | bytes 24580
  468.0 108.6 %copy-start.6 = (f32[2048]{0:T(1024)S(1)}, f32[2048]{0:T(1024)}, u32[]{:S(2)}) copy-start(f32[2048]{0:T(1024)} %param.15) | copy-start | bytes 24580
  587.0 2.7 copy-start.2
  592.0 31.0 %all-to-all-start.1 = ((bf16[1,512,8,128]{3,2,0,1:T(8,128)(2,1)}), bf16[1,512,8,128]{3,2,0,1:T(8,128)(2,1)S(1)}, u32[]{:S(2)}, u32[]{:S(2)}) async-start(bf16[1,512,8,128]{3,2,0,1:T(8,128)(2,1)} %copy.40), calls=%async_computation.1 | async-start | bytes 2097152 | tf_op jit(solution)/shard_map/all_to_all | solution.py:138
  623.0 26.3 %all-to-all-start.2 = ((bf16[1,512,8,128]{3,2,0,1:T(8,128)(2,1)}), bf16[1,512,8,128]{3,2,0,1:T(8,128)(2,1)S(1)}, u32[]{:S(2)}, u32[]{:S(2)}) async-start(bf16[1,512,8,128]{3,2,0,1:T(8,128)(2,1)} %copy.41), calls=%async_computation.2 | async-start | bytes 2097152 | tf_op jit(solution)/shard_map/all_to_all | solution.py:139
  649.3 22.7 %all-to-all-start = ((bf16[1,512,8,128]{3,2,0,1:T(8,128)(2,1)}), bf16[1,512,8,128]{3,2,0,1:T(8,128)(2,1)S(1)}, u32[]{:S(2)}, u32[]{:S(2)}) async-start(bf16[1,512,8,128]{3,2,0,1:T(8,128)(2,1)} %copy.39), calls=%async_computation | async-start | bytes 2097152 | tf_op jit(solution)/shard_map/all_to_all | solution.py:140
  674.6 23.5 %copy-start.7 = (bf16[512,2048]{1,0:T(8,128)(2,1)S(1)}, bf16[512,2048]{1,0:T(8,128)(2,1)}, u32[]{:S(2)}) copy-start(bf16[512,2048]{1,0:T(8,128)(2,1)} %get-tuple-element.81) | copy-start | bytes 6291460
  676.0 22.1 %all-to-all-start.3 = ((bf16[32,16,8,128]{3,2,1,0:T(8,128)(2,1)}), bf16[32,16,8,128]{3,2,1,0:T(8,128)(2,1)S(1)}, u32[]{:S(2)}, u32[]{:S(2)}) async-start(bf16[32,16,8,128]{3,2,1,0:T(8,128)(2,1)} %copy.46), calls=%async_computation.3 | async-start | bytes 2097152 | tf_op jit(solution)/shard_map/all_to_all | solution.py:91
  698.1 5.9 copy-start.1
Sparse Core Ops, SparseCore 0:
  10.4 77.4 all-gather.8
  90.9 63.6 all-gather.12
  157.7 71.8 all-gather.16
  232.4 63.6 all-gather.20
  297.6 111.1 all-gather.10
  410.4 48.7 all-gather.14
  460.8 115.8 all-gather.18
  578.3 71.1 all-gather.22
where the time goes:
time: 712 us; the launch traced here: 711 us
  waiting for transfers between devices  569 us (80%)
  matrix products  59.2 us (8%)
  local copies, waits for them, and re-layouts  36.2 us (5%)
  starting transfers between devices  24.8 us (3%)
  between operations  15 us (2%)
    all_gather x3, waiting for transfers between devices, shards(): lax.all_gather(group_rows, 'dp', axis=0, tiled=True)  113 us
    all_gather x1, waiting for transfers between devices, shards(): lax.all_gather(second_rows, 'dp', axis=0, tiled=True)  102 us
    all_gather x1, waiting for transfers between devices, shards(): group_rows = lax.all_gather(inputs_first, 'seq', axis=0, tiled=True)  78.6 us
    all_gather x1, waiting for transfers between devices, shards(): second_rows = lax.all_gather(inputs_second, 'seq', axis=0, tiled=True)  74.8 us
    all_gather x1, waiting for transfers between devices, shards(): group_rows = lax.all_gather(output_first, 'seq', axis=0, tiled=True)  66.6 us
    all_gather x1, waiting for transfers between devices, shards(): group_rows = lax.all_gather(output_second, 'seq', axis=0, tiled=True)  62 us
    dot_general x4, matrix products, accumulate(): return jnp.dot(hidden, block_rows, preferred_element_type=jnp.float32)  32.4 us
    all_to_all x1, waiting for transfers between devices, shards(): lax.all_to_all(queries, 'seq', split_axis=1, concat_axis=0, tiled=True)  19.6 us
  transfers between devices with their start and end apart: 12, of which 10 were waited for; matrix products, arithmetic and copies ran while one was open for 13% of the time, Pallas kernels for 0%

commit v1 on v0

v1 whole, which is shorter than its diff:
```python
import math

import jax
import jax.numpy as jnp
from jax import lax
from jax.experimental import pallas as pl
from jax.experimental.pallas import tpu as pltpu
from jax.sharding import Mesh, PartitionSpec as P

HEADS = 8
HEAD = 128
C = 512
SCALE = 8
D = 2048
WIDTH = HEADS * HEAD
N_SEQ = 32
COLS = C // N_SEQ
PAIR = 2 * HEAD
STEPS = WIDTH // PAIR
ALL_CHIPS = ("ylo", "seq")
LOG2E = 1.4426950408889634
MIB = 1 << 20


def frequencies(band_edges, half_size):
    dim_index = jnp.arange(half_size, dtype=jnp.float32)
    base_freq = jnp.power(10000.0, -dim_index / half_size)
    lower_edge = band_edges[0].astype(jnp.float32)
    upper_edge = band_edges[1].astype(jnp.float32)
    ramp_share = jnp.clip((dim_index - lower_edge) / (upper_edge - lower_edge), 0.0, 1.0)
    return base_freq * (1.0 - ramp_share) + base_freq * ramp_share / SCALE


def rotary_tables(positions, frequency):
    angles = positions.astype(jnp.float32)[:, None] * frequency
    mscale = 0.1 * math.log(SCALE) + 1.0
    cosine = jnp.cos(angles) * mscale
    sine = jnp.sin(angles) * mscale
    return jnp.concatenate([cosine, cosine], -1), jnp.concatenate([-sine, sine], -1)


def dot(a, b):
    return jnp.dot(a, b, preferred_element_type=jnp.float32)


def dot_t(a, b):
    return lax.dot_general(a, b, (((1,), (1,)), ((), ())), preferred_element_type=jnp.float32)


def slot_of(block, core):
    other = jnp.where(lax.rem(block, 2) == core, 0, 2)
    return other + block // 2


def rotate(heads, cos, sin):
    return heads * cos + pltpu.roll(heads, HEAD // 2, 1) * sin


def softmax_times(scores, keep, values):
    scores = jnp.where(keep, scores, -1e30)
    top = jnp.max(scores, axis=-1, keepdims=True)
    weights = jnp.exp2((scores - top) * (LOG2E / math.sqrt(HEAD)))
    total = jnp.sum(weights, axis=-1, keepdims=True)
    return dot(weights.astype(jnp.bfloat16), values) / total


def project(hid_ref, own_ref, other_ref):
    half = own_ref.shape[0]
    return dot(hid_ref[:, :half], own_ref[...]) + dot(hid_ref[:, half:], other_ref[...])


def row_kernel(core_ref, x_ref, gain_ref, cos_ref, sin_ref, qo, ko, vo, qs, ks, vs, out_ref, hid_ref):
    core = core_ref[0]

    @pl.when(pl.program_id(0) == 0)
    def _():
        def chunk(i, _):
            rows = pl.ds(pl.multiple_of(i * 32, 32), 32)
            x = x_ref[rows, :].astype(jnp.float32)
            inv = lax.rsqrt(jnp.mean(x * x, axis=-1, keepdims=True) + 1e-05)
            hidden = (x * inv * gain_ref[...]).astype(jnp.bfloat16)
            width = D // 4
            for block in range(4):
                lanes = pl.ds(pl.multiple_of(slot_of(block, core) * width, width), width)
                hid_ref[rows, lanes] = hidden[:, block * width : (block + 1) * width]
            return 0

        lax.fori_loop(0, C // 32, chunk, 0)

    q2 = project(hid_ref, qo, qs)
    k2 = project(hid_ref, ko, ks)
    v2 = project(hid_ref, vo, vs).astype(jnp.bfloat16)
    for h in range(2):
        lanes = slice(h * HEAD, (h + 1) * HEAD)
        q = rotate(q2[:, lanes], cos_ref[...], sin_ref[...]).astype(jnp.bfloat16)
        k = rotate(k2[:, lanes], cos_ref[...], sin_ref[...]).astype(jnp.bfloat16)
        v = v2[:, lanes]
        size = 256
        for b in range(C // size):
            end = (b + 1) * size
            scores = dot_t(q[b * size : end], k[:end])
            row = lax.broadcasted_iota(jnp.int32, scores.shape, 0) + b * size
            keep = lax.broadcasted_iota(jnp.int32, scores.shape, 1) <= row
            out_ref[b * size : end, lanes] = softmax_times(scores, keep, v[:end]).astype(jnp.bfloat16)


def column_kernel(core_ref, x_ref, cos_ref, sin_ref, qo, ko, vo, qs, ks, vs, out_ref, hid_ref):
    core = core_ref[0]

    def selection(transposed):
        a = lax.broadcasted_iota(jnp.int32, (C, C), 1 if transposed else 0)
        b = lax.broadcasted_iota(jnp.int32, (C, C), 0 if transposed else 1)
        same = (a // N_SEQ == lax.rem(b, COLS)) & (lax.rem(a, N_SEQ) == b // COLS)
        return jnp.where(same, 1.0, 0.0).astype(jnp.bfloat16)

    @pl.when(pl.program_id(0) == 0)
    def _():
        pick = selection(False)
        width = D // 4
        for block in range(4):
            lanes = pl.ds(pl.multiple_of(slot_of(block, core) * width, width), width)
            moved = dot(pick, x_ref[:, block * width : (block + 1) * width])
            hid_ref[:, lanes] = moved.astype(jnp.bfloat16)

    q2 = project(hid_ref, qo, qs)
    k2 = project(hid_ref, ko, ks)
    v2 = project(hid_ref, vo, vs).astype(jnp.bfloat16)
    size = 128
    row = lax.broadcasted_iota(jnp.int32, (size, size), 0)
    col = lax.broadcasted_iota(jnp.int32, (size, size), 1)
    keep = (row // N_SEQ == col // N_SEQ) & (col <= row)
    heads = []
    for h in range(2):
        lanes = slice(h * HEAD, (h + 1) * HEAD)
        q = rotate(q2[:, lanes], cos_ref[...], sin_ref[...]).astype(jnp.bfloat16)
        k = rotate(k2[:, lanes], cos_ref[...], sin_ref[...]).astype(jnp.bfloat16)
        v = v2[:, lanes]
        blocks = []
        for b in range(C // size):
            rows = slice(b * size, (b + 1) * size)
            blocks.append(softmax_times(dot_t(q[rows], k[rows]), keep, v[rows]).astype(jnp.bfloat16))
        heads.append(jnp.concatenate(blocks, 0))
    attended = jnp.concatenate(heads, 1)
    out_ref[...] = dot(selection(True), attended).astype(jnp.bfloat16)


def attend(kernel, core, x, gain, tables, own, other):
    half = own.shape[0]

    def weight(part):
        return pl.BlockSpec((half, PAIR), lambda i: (0, part * STEPS + i))

    whole = lambda shape: pl.BlockSpec(shape, lambda i: (0, 0), pipeline_mode=pl.Buffered(1))
    specs = [pl.BlockSpec(memory_space=pltpu.SMEM), whole((C, D))]
    args = [core, x]
    if gain is not None:
        specs.append(whole((1, D)))
        args.append(gain)
    specs += [whole((C, HEAD)), whole((C, HEAD))] + [weight(p) for p in range(3)] * 2
    args += [*tables, own, own, own, other, other, other]
    return pl.pallas_call(
        kernel,
        grid=(STEPS,),
        out_shape=jax.ShapeDtypeStruct((C, WIDTH), jnp.bfloat16),
        in_specs=specs,
        out_specs=pl.BlockSpec((C, PAIR), lambda i: (0, i)),
        scratch_shapes=[pltpu.VMEM((C, D), jnp.bfloat16)],
        compiler_params=pltpu.CompilerParams(
            dimension_semantics=("arbitrary",), vmem_limit_bytes=40 * MIB
        ),
        cost_estimate=pl.CostEstimate(
            flops=2 * C * D * 3 * WIDTH + 4 * C * C * WIDTH,
            bytes_accessed=2 * (C * D + 3 * D * WIDTH + C * WIDTH),
            transcendentals=C * C * HEADS,
        ),
    )(*args)


def branch_sum(core, att_ref, own_ref, other_ref, resid_ref):
    width = WIDTH // 4
    total = resid_ref[...].astype(jnp.float32)
    for slot in range(4):
        block = jnp.where(slot < 2, core, 1 - core) + 2 * (slot % 2)
        lanes = pl.ds(pl.multiple_of(block * width, width), width)
        ref = own_ref if slot < 2 else other_ref
        rows = slice((slot % 2) * width, (slot % 2 + 1) * width)
        total = total + dot(att_ref[:, lanes], ref[rows, :])
    return total


def middle_kernel(core_ref, att_ref, own_ref, other_ref, resid_ref, gain_ref, mid_ref, hid_ref):
    middle = branch_sum(core_ref[0], att_ref, own_ref, other_ref, resid_ref).astype(jnp.bfloat16)
    mid_ref[...] = middle
    x = middle.astype(jnp.float32)
    inv = lax.rsqrt(jnp.mean(x * x, axis=-1, keepdims=True) + 1e-05)
    hid_ref[...] = (x * inv * gain_ref[...]).astype(jnp.bfloat16)


def final_kernel(core_ref, att_ref, own_ref, other_ref, resid_ref, out_ref):
    out_ref[...] = branch_sum(core_ref[0], att_ref, own_ref, other_ref, resid_ref).astype(jnp.bfloat16)


def output_layer(kernel, core, attended, own, other, resid, gain):
    size = 128
    block = lambda width: pl.BlockSpec((size, width), lambda i: (i, 0))
    whole = lambda shape: pl.BlockSpec(shape, lambda i: (0, 0), pipeline_mode=pl.Buffered(1))
    specs = [
        pl.BlockSpec(memory_space=pltpu.SMEM),
        block(WIDTH),
        whole(own.shape),
        whole(other.shape),
        block(D),
    ]
    args = [core, attended, own, other, resid]
    outs = 1
    if gain is not None:
        specs.append(whole((1, D)))
        args.append(gain)
        outs = 2
    shape = jax.ShapeDtypeStruct((C, D), jnp.bfloat16)
    return pl.pallas_call(
        kernel,
        grid=(C // size,),
        out_shape=[shape] * outs,
        in_specs=specs,
        out_specs=[block(D)] * outs,
        compiler_params=pltpu.CompilerParams(
            dimension_semantics=("arbitrary",), vmem_limit_bytes=40 * MIB
        ),
        cost_estimate=pl.CostEstimate(
            flops=2 * C * D * WIDTH,
            bytes_accessed=2 * ((1 + outs) * C * D + D * WIDTH + C * WIDTH),
            transcendentals=0,
        ),
    )(*args)


def shards(tokens, gain_first, inputs_first, output_first, gain_second, inputs_second, output_second, starts, band_edges):
    residual = tokens[0]
    core = lax.axis_index("core")
    core_scalar = core.astype(jnp.int32).reshape(1)
    seq = lax.axis_index("seq")

    def gather(weight):
        own = lax.all_gather(weight, ALL_CHIPS, axis=0, tiled=True)
        return own, lax.ppermute(own, "core", [(0, 1), (1, 0)])

    in_first = gather(inputs_first)
    out_first = gather(output_first)
    in_second = gather(inputs_second)
    out_second = gather(output_second)

    frequency = frequencies(band_edges, HEAD // 2)
    block_starts = starts[0]
    own_start = lax.dynamic_index_in_dim(block_starts, seq, 0, keepdims=False)
    row_tables = rotary_tables(own_start + jnp.arange(C, dtype=jnp.int32), frequency)
    columns = seq.astype(jnp.int32) * COLS + jnp.arange(COLS, dtype=jnp.int32)
    column_positions = (columns[:, None] + block_starts[None, :]).reshape(C)
    column_tables = rotary_tables(column_positions, frequency)

    attended = attend(row_kernel, core_scalar, residual, gain_first.reshape(1, D), row_tables, *in_first)
    middle, hidden = output_layer(
        middle_kernel, core_scalar, attended, *out_first, residual, gain_second.reshape(1, D)
    )
    hidden = lax.all_to_all(hidden, "seq", split_axis=0, concat_axis=0, tiled=True)
    attended = attend(column_kernel, core_scalar, hidden, None, column_tables, *in_second)
    attended = lax.all_to_all(attended, "seq", split_axis=0, concat_axis=0, tiled=True)
    (out,) = output_layer(final_kernel, core_scalar, attended, *out_second, middle, None)
    return out[None]


def solution(mesh):
    split = Mesh(mesh.devices.reshape(2, 2, N_SEQ), ("ylo", "core", "seq"))
    dp = ("ylo", "core")
    every = ("ylo", "core", "seq")
    return jax.shard_map(
        shards,
        mesh=split,
        in_specs=(
            P(dp, "seq", None),
            P(),
            P(every, None),
            P(every, None),
            P(),
            P(every, None),
            P(every, None),
            P(dp, None),
            P(),
        ),
        out_specs=P(dp, "seq", None),
        check_vma=False,
    )
```

time: 712 us -> 1430 us (2.01)
  waiting for transfers between devices: 569 us -> 1340 us
  matrix products: 59.2 us -> 0 us
  Pallas kernels: 0 us -> 49.9 us
  local copies, waits for them, and re-layouts: 36.2 us -> 14.1 us
  starting transfers between devices: 24.8 us -> 8.08 us
    all_gather x8 -> x4, waiting for transfers between devices: 497 us -> 1320 us  [gather(): own = lax.all_gather(weight, ALL_CHIPS, axis=0, tiled=True)]
    dot_general x21 -> x0, matrix products: 56 us -> none  [the longest x4 32.4 us: accumulate(): return jnp.dot(hidden, block_rows, preferred_element_type=jnp.float32)]
    all_to_all x4 -> x2, waiting for transfers between devices: 69.6 us -> 18.2 us  [the longest x1 18.2 us: shards(): lax.all_to_all(attended, 'seq', split_axis=0, concat_axis=0, tiled=True)]
    pallas_call x0 -> x4, Pallas kernels: none -> 49.9 us  [the longest x2 39.1 us: attend(): pl.pallas_call(kernel, grid=(STEPS,), out_shape=jax.ShapeDtypeStruct((C,...]
    dot_general x1 -> x0, local copies, waits for them, and re-layouts: 16.9 us -> none  [accumulate(): return jnp.dot(hidden, block_rows, preferred_element_type=jnp.float32)]
    all_to_all x4 -> x2, starting transfers between devices: 24.5 us -> 7.95 us  [the longest x1 4.01 us: shards(): lax.all_to_all(hidden, 'seq', split_axis=0, concat_axis=0, tiled=True)]
  transfers between devices with their start and end apart: 12 -> 10, of which waited for: 10 -> 5; matrix products, arithmetic and copies ran while one was open for 13% -> 0% of each run, Pallas kernels for 0% -> 3%
where the time goes in v1:
time: 1430 us
  waiting for transfers between devices  1340 us (94%)
  Pallas kernels  49.9 us (3%)
  between operations  14.6 us (1%)
    all_gather x4, waiting for transfers between devices, gather(): own = lax.all_gather(weight, ALL_CHIPS, axis=0, tiled=True)  1320 us
    pallas_call x2, Pallas kernels, attend(): pl.pallas_call(kernel, grid=(STEPS,), out_shape=jax.ShapeDtypeStruct((C,...  39.1 us
  transfers between devices with their start and end apart: 10, of which 5 were waited for; matrix products, arithmetic and copies ran while one was open for 0% of the time, Pallas kernels for 3%

profile of v1, /device:TPU:0, one launch (start us, length us, event | category | flops | bytes accessed | tf_op | source)
XLA Modules:
  0.0 1426.0 jit_solution(3920988727346579037)
XLA Ops:
  6.5 0.0 copy-start.2
  6.5 0.0 copy-start.7
  6.5 0.0 all-gather.5.cloned.1.call-start
  6.5 0.7 all-gather.5.cloned.1.call-update
  7.3 0.0 all-gather.9.cloned.1.call-start
  7.3 0.7 all-gather.9.cloned.1.call-update
  8.0 0.0 all-gather.7.cloned.1.call-start
  8.1 341.7 %all-gather.5.cloned.1.call-done.qo.ko.vo = bf16[1024,3072]{1,0:T(8,128)(2,1)} async-done(((bf16[16,3072]{1,0:T(8,128)(2,1)}), bf16[1024,3072]{1,0:T(8,128)(2,1)}) %all-gather.5.cloned.1.call-update) | async-done | bytes 6291472 | tf_op jit(solution)/shard_map/all_gather | solution.py:245
  349.7 0.0 collective-permute-start
  349.7 0.0 all-gather.7.cloned.1.call-update
  349.8 0.0 all-gather.11.cloned.1.call-start
  349.8 339.9 %all-gather.9.cloned.1.call-done.qo.ko.vo = bf16[1024,3072]{1,0:T(8,128)(2,1)} async-done(((bf16[16,3072]{1,0:T(8,128)(2,1)}), bf16[1024,3072]{1,0:T(8,128)(2,1)}) %all-gather.9.cloned.1.call-update) | async-done | bytes 6291472 | tf_op jit(solution)/shard_map/all_gather | solution.py:245
  689.7 0.0 collective-permute-start.2
  689.7 0.0 all-gather.11.cloned.1.call-update
  689.7 332.2 %all-gather.7.cloned.1.call-done.own_ref = bf16[512,2048]{1,0:T(8,128)(2,1)} async-done(((bf16[8,2048]{1,0:T(8,128)(2,1)}), bf16[512,2048]{1,0:T(8,128)(2,1)}) %all-gather.7.cloned.1.call-update) | async-done | bytes 2097168 | tf_op jit(solution)/shard_map/all_gather | solution.py:245
  1021.9 0.0 collective-permute-start.1
  1021.9 1.3 fusion.6
  1024.5 1.3 constant_dynamic-slice_fusion
  1025.8 0.7 add_convert_fusion
  1026.6 0.1 convert_element_type.35
  1026.7 0.6 add_convert_fusion.1
  1027.3 1.9 fusion.4
  1029.2 0.2 pad_maximum_fusion
  1029.4 0.0 collective-permute-done.qs.ks.vs
  1029.5 0.0 copy-done.2
  1029.5 0.0 copy-done.7
  1029.5 0.0 copy-start
  1029.5 2.8 copy-done
  1032.3 0.0 copy-start.8
  1032.3 0.0 copy-start.9
  1032.3 18.2 %shard_map.91.att_ref = bf16[512,1024]{1,0:T(8,128)(2,1)S(1)} custom-call(s32[1]{0:T(128)} %bitcast.core_ref, bf16[512,2048]{1,0:T(8,128)(2,1)S(1)} %bitcast.15, f32[1,2048]{1,0:T(1,128)S(1)} %bitcast.18, f32[512,128]{1,0:T(8,128)S(1)} %get-tuple-element.20.cos_ref, f32[512,128]{1,0:T(8,128)S(1)} %get-tuple-element.21.sin_ref, ...), custom_call_target="tpu_custom_call" | custom-call | flops 7516192768 | bytes 15728640 | tf_op jit(solution)/shard_map/pallas_call | solution.py:161
  1050.5 0.0 collective-permute-done.1.other_ref
  1050.5 0.0 copy-done.8
  1050.5 0.0 copy-done.9
  1050.5 5.4 shard_map.92
  1055.9 0.0 copy-start.4
  1055.9 1.3 copy-done.4
  1057.2 0.0 copy-start.6
  1057.2 1.3 copy-done.6
  1058.5 4.0 all-to-all-start
  1062.6 302.2 %all-gather.11.cloned.1.call-done.own_ref = bf16[512,2048]{1,0:T(8,128)(2,1)} async-done(((bf16[8,2048]{1,0:T(8,128)(2,1)}), bf16[512,2048]{1,0:T(8,128)(2,1)}) %all-gather.11.cloned.1.call-update) | async-done | bytes 2097168 | tf_op jit(solution)/shard_map/all_gather | solution.py:245
  1364.8 0.0 collective-permute-start.3
  1364.8 0.2 pad_maximum_fusion.2
  1365.0 0.0 collective-permute-done.2.qs.ks.vs
  1365.0 0.0 all-to-all-done
  1365.0 0.0 copy-start.1
  1365.0 2.8 copy-done.1
  1367.8 20.9 %shard_map.93 = bf16[512,1024]{1,0:T(8,128)(2,1)} custom-call(s32[1]{0:T(128)} %bitcast.core_ref, bf16[512,2048]{1,0:T(8,128)(2,1)S(1)} %bitcast.13, f32[512,128]{1,0:T(8,128)S(1)} %get-tuple-element.22.cos_ref, f32[512,128]{1,0:T(8,128)S(1)} %get-tuple-element.23.sin_ref, bf16[1024,3072]{1,0:T(8,128)(2,1)S(1)} %copy-done.1, ...), custom_call_target="tpu_custom_call" | custom-call | flops 7516192768 | bytes 15728640 | tf_op jit(solution)/shard_map/pallas_call | solution.py:161
  1388.7 3.9 all-to-all-start.1
  1392.6 0.0 collective-permute-done.3.other_ref
  1392.6 18.2 %all-to-all-done.1 = bf16[32,16,1024]{2,1,0:T(8,128)(2,1)S(1)} async-done(((bf16[32,16,1024]{2,1,0:T(8,128)(2,1)}), bf16[32,16,1024]{2,1,0:T(8,128)(2,1)S(1)}, u32[]{:S(2)}, u32[]{:S(2)}) %all-to-all-start.1) | async-done | bytes 1048608 | tf_op jit(solution)/shard_map/all_to_all | solution.py:267
  1410.9 0.0 copy-start.3
  1410.9 1.6 copy-done.3
  1412.5 0.0 copy-start.5
  1412.5 1.6 copy-done.5
  1414.1 5.4 shard_map.94
  (2 shorter events, 0.0 us)
Async XLA Ops:
  6.5 1022.9 %copy-start.2 = (bf16[1,512,2048]{2,1,0:T(8,128)(2,1)S(1)}, bf16[1,512,2048]{2,1,0:T(8,128)(2,1)}, u32[]{:S(2)}) copy-start(bf16[1,512,2048]{2,1,0:T(8,128)(2,1)} %param.9) | copy-start | bytes 6291460
  6.5 1022.9 %copy-start.7 = (f32[2048]{0:T(1024)S(1)}, f32[2048]{0:T(1024)}, u32[]{:S(2)}) copy-start(f32[2048]{0:T(1024)} %param.10) | copy-start | bytes 24580
  6.5 343.2 %all-gather.5.cloned.1.call-start = ((), (), s32[]{:S(2)}) async-start(), calls=%async_computation.2 | async-start | bytes 6389760 | tf_op jit(solution)/shard_map/all_gather | solution.py:245
  7.3 682.4 %all-gather.9.cloned.1.call-start = ((), (), s32[]{:S(2)}) async-start(), calls=%async_computation.4 | async-start | bytes 6389760 | tf_op jit(solution)/shard_map/all_gather | solution.py:245
  8.0 1013.9 %all-gather.7.cloned.1.call-start = ((), (), s32[]{:S(2)}) async-start(), calls=%async_computation.3 | async-start | bytes 2129920 | tf_op jit(solution)/shard_map/all_gather | solution.py:245
  349.7 679.7 %collective-permute-start = (bf16[1024,3072]{1,0:T(8,128)(2,1)}, bf16[1024,3072]{1,0:T(8,128)(2,1)}, u32[]{:S(2)}, u32[]{:S(2)}) collective-permute-start(bf16[1024,3072]{1,0:T(8,128)(2,1)} %all-gather.5.cloned.1.call-done.qo.ko.vo), channel_id=1, source_target_pairs={{0,32},{32,0},{1,33},{33,1},{2,34},{34,2},{3,35},{35,3},{4,36},{36... | collective-permute-start | bytes 18874376 | tf_op jit(solution)/shard_map/ppermute | solution.py:246
  349.8 1015.0 %all-gather.11.cloned.1.call-start = ((), (), s32[]{:S(2)}) async-start(), calls=%async_computation.5 | async-start | bytes 2129920 | tf_op jit(solution)/shard_map/all_gather | solution.py:245
  689.7 675.3 %collective-permute-start.2 = (bf16[1024,3072]{1,0:T(8,128)(2,1)}, bf16[1024,3072]{1,0:T(8,128)(2,1)}, u32[]{:S(2)}, u32[]{:S(2)}) collective-permute-start(bf16[1024,3072]{1,0:T(8,128)(2,1)} %all-gather.9.cloned.1.call-done.qo.ko.vo), channel_id=1, source_target_pairs={{0,32},{32,0},{1,33},{33,1},{2,34},{34,2},{3,35},{35,3},{4,36},{36... | collective-permute-start | bytes 18874376 | tf_op jit(solution)/shard_map/ppermute | solution.py:246
  1021.9 28.6 %collective-permute-start.1 = (bf16[512,2048]{1,0:T(8,128)(2,1)}, bf16[512,2048]{1,0:T(8,128)(2,1)}, u32[]{:S(2)}, u32[]{:S(2)}) collective-permute-start(bf16[512,2048]{1,0:T(8,128)(2,1)} %all-gather.7.cloned.1.call-done.own_ref), channel_id=1, source_target_pairs={{0,32},{32,0},{1,33},{33,1},{2,34},{34,2},{3,35},{35,3},{4,36},{36... | collective-permute-start | bytes 6291464 | tf_op jit(solution)/shard_map/ppermute | solution.py:246
  1029.5 2.8 copy-start
  1032.3 18.2 %copy-start.8 = (bf16[512,2048]{1,0:T(8,128)(2,1)S(1)}, bf16[512,2048]{1,0:T(8,128)(2,1)}, u32[]{:S(2)}) copy-start(bf16[512,2048]{1,0:T(8,128)(2,1)} %all-gather.7.cloned.1.call-done.own_ref) | copy-start | bytes 6291460
  1032.3 18.3 %copy-start.9 = (f32[2048]{0:T(1024)S(1)}, f32[2048]{0:T(1024)}, u32[]{:S(2)}) copy-start(f32[2048]{0:T(1024)} %param.13) | copy-start | bytes 24580
  1055.9 1.3 copy-start.4
  1057.2 1.3 copy-start.6
  1058.5 306.4 %all-to-all-start = ((bf16[32,16,2048]{2,1,0:T(8,128)(2,1)}), bf16[32,16,2048]{2,1,0:T(8,128)(2,1)S(1)}, u32[]{:S(2)}, u32[]{:S(2)}) async-start(bf16[32,16,2048]{2,1,0:T(8,128)(2,1)} %bitcast.17), calls=%async_computation | async-start | bytes 4194304 | tf_op jit(solution)/shard_map/all_to_all | solution.py:265
  1364.8 27.9 %collective-permute-start.3 = (bf16[512,2048]{1,0:T(8,128)(2,1)}, bf16[512,2048]{1,0:T(8,128)(2,1)}, u32[]{:S(2)}, u32[]{:S(2)}) collective-permute-start(bf16[512,2048]{1,0:T(8,128)(2,1)} %all-gather.11.cloned.1.call-done.own_ref), channel_id=1, source_target_pairs={{0,32},{32,0},{1,33},{33,1},{2,34},{34,2},{3,35},{35,3},{4,36},{36... | collective-permute-start | bytes 6291464 | tf_op jit(solution)/shard_map/ppermute | solution.py:246
  1365.0 2.8 copy-start.1
  1388.7 22.2 %all-to-all-start.1 = ((bf16[32,16,1024]{2,1,0:T(8,128)(2,1)}), bf16[32,16,1024]{2,1,0:T(8,128)(2,1)S(1)}, u32[]{:S(2)}, u32[]{:S(2)}) async-start(bf16[32,16,1024]{2,1,0:T(8,128)(2,1)} %bitcast.10), calls=%async_computation.1 | async-start | bytes 2097152 | tf_op jit(solution)/shard_map/all_to_all | solution.py:267
  1410.9 1.6 copy-start.3
  1412.5 1.6 copy-start.5
Sparse Core Ops, SparseCore 0:
  9.0 340.6 all-gather.4
  351.4 338.2 all-gather.8
  691.3 330.5 all-gather.6
  1023.4 341.3 all-gather.10

commit v2 on v1

--- a/solution.py
+++ b/solution.py
@@ -17,7 +17,11 @@
 COLS = C // N_SEQ
 PAIR = 2 * HEAD
 STEPS = WIDTH // PAIR
-ALL_CHIPS = ("ylo", "seq")
+SEQ = ("x", "yhi", "z")
+QKV_PART = 3 * WIDTH // 2
+PART = 2 * WIDTH
+RELATIVE = ((0, 0, PART), (3, 0, PART), (1, 0, PART), (2, 0, PART // 2), (2, PART // 2, PART))
+STACKED = (0, 3, 1, 2)
 LOG2E = 1.4426950408889634
 MIB = 1 << 20
 
@@ -69,39 +73,167 @@
     return dot(hid_ref[:, :half], own_ref[...]) + dot(hid_ref[:, half:], other_ref[...])
 
 
-def row_kernel(core_ref, x_ref, gain_ref, cos_ref, sin_ref, qo, ko, vo, qs, ks, vs, out_ref, hid_ref):
+def norm_kernel(core_ref, x_ref, gain_ref, hid_ref):
     core = core_ref[0]
 
-    @pl.when(pl.program_id(0) == 0)
-    def _():
-        def chunk(i, _):
-            rows = pl.ds(pl.multiple_of(i * 32, 32), 32)
-            x = x_ref[rows, :].astype(jnp.float32)
-            inv = lax.rsqrt(jnp.mean(x * x, axis=-1, keepdims=True) + 1e-05)
-            hidden = (x * inv * gain_ref[...]).astype(jnp.bfloat16)
-            width = D // 4
-            for block in range(4):
-                lanes = pl.ds(pl.multiple_of(slot_of(block, core) * width, width), width)
-                hid_ref[rows, lanes] = hidden[:, block * width : (block + 1) * width]
-            return 0
-
-        lax.fori_loop(0, C // 32, chunk, 0)
-
-    q2 = project(hid_ref, qo, qs)
-    k2 = project(hid_ref, ko, ks)
-    v2 = project(hid_ref, vo, vs).astype(jnp.bfloat16)
-    for h in range(2):
-        lanes = slice(h * HEAD, (h + 1) * HEAD)
-        q = rotate(q2[:, lanes], cos_ref[...], sin_ref[...]).astype(jnp.bfloat16)
-        k = rotate(k2[:, lanes], cos_ref[...], sin_ref[...]).astype(jnp.bfloat16)
-        v = v2[:, lanes]
-        size = 256
-        for b in range(C // size):
-            end = (b + 1) * size
-            scores = dot_t(q[b * size : end], k[:end])
-            row = lax.broadcasted_iota(jnp.int32, scores.shape, 0) + b * size
-            keep = lax.broadcasted_iota(jnp.int32, scores.shape, 1) <= row
-            out_ref[b * size : end, lanes] = softmax_times(scores, keep, v[:end]).astype(jnp.bfloat16)
+    def chunk(i, _):
+        rows = pl.ds(pl.multiple_of(i * 32, 32), 32)
+        x = x_ref[rows, :].astype(jnp.float32)
+        inv = lax.rsqrt(jnp.mean(x * x, axis=-1, keepdims=True) + 1e-05)
+        hidden = (x * inv * gain_ref[...]).astype(jnp.bfloat16)
+        width = D // 4
+        for block in range(4):
+            lanes = pl.ds(pl.multiple_of(slot_of(block, core) * width, width), width)
+            hid_ref[rows, lanes] = hidden[:, block * width : (block + 1) * width]
+        return 0
+
+    lax.fori_loop(0, C // 32, chunk, 0)
+
+
+def normed_slots(core, x, gain):
+    vmem = pl.BlockSpec(memory_space=pltpu.VMEM)
+    return pl.pallas_call(
+        norm_kernel,
+        out_shape=jax.ShapeDtypeStruct((C, D), jnp.bfloat16),
+        in_specs=[pl.BlockSpec(memory_space=pltpu.SMEM), vmem, vmem],
+        out_specs=vmem,
+        compiler_params=pltpu.CompilerParams(vmem_limit_bytes=16 * MIB),
+        cost_estimate=pl.CostEstimate(flops=4 * C * D, bytes_accessed=4 * C * D, transcendentals=C),
+    )(core, x, gain)
+
+
+def row_kernel(place_ref, x_ref, hid_ref, gain_ref, cos_ref, sin_ref, *refs):
+    pieces = refs[: 4 * len(RELATIVE)]
+    mid_ref, next_ref, w_ref, o_ref, att_ref, sems = refs[4 * len(RELATIVE) :]
+    core, my_x, my_y = place_ref[0], place_ref[1], place_ref[2]
+
+    def block_of(part, stacked, ring):
+        x, y = (stacked, ring) if part == 0 else (ring, stacked)
+        x = lax.rem(my_x + x, 4)
+        y = lax.rem(my_y + y, 4)
+        return lax.rem(y, 2) * 8 + x * 2 + y // 2
+
+    def copies(slot, part, outputs):
+        first = (slot * 2 + part) * len(RELATIVE)
+        for index, (ring, low, high) in enumerate(RELATIVE):
+            src = pieces[first + index]
+            if outputs:
+                if high < PART:
+                    continue
+                lanes, target = pl.ds(QKV_PART - low, PART - QKV_PART), None
+            else:
+                end = min(high, QKV_PART)
+                lanes, target = pl.ds(0, end - low), pl.ds(low, end - low)
+            for k, stacked in enumerate(STACKED):
+                block = block_of(part, stacked, ring)
+                if outputs:
+                    width = PART - QKV_PART
+                    dst = o_ref.at[slot, block, :, :, pl.ds(part * width, width)]
+                else:
+                    dst = w_ref.at[slot, part, block, :, :, target]
+                sem = sems.at[4 + slot if outputs else slot * 2 + part]
+                pltpu.make_async_copy(src.at[k, :, :, lanes], dst, sem).start()
+
+    for part in range(2):
+        for slot in range(2):
+            copies(slot, part, False)
+    for part in range(2):
+        for slot in range(2):
+            copies(slot, part, True)
+
+    def arrived(ref, sem):
+        pltpu.make_async_copy(ref, ref, sem).wait()
+
+    half = D // 2
+
+    def step(g, _):
+        part = g // 2
+        for p in range(2):
+
+            @pl.when(g == 2 * p)
+            def _():
+                for slot in range(2):
+                    arrived(w_ref.at[slot, p], sems.at[slot * 2 + p])
+
+        base = lax.rem(g, 2) * (3 * PAIR)
+
+        def weight(slot, kind):
+            lanes = pl.ds(pl.multiple_of(base + kind * PAIR, PAIR), PAIR)
+            return w_ref[slot, part, :, :, :, lanes].reshape(half, PAIR)
+
+        def projected(kind):
+            return dot(hid_ref[:, :half], weight(0, kind)) + dot(hid_ref[:, half:], weight(1, kind))
+
+        q2 = projected(0)
+        k2 = projected(1)
+        v2 = projected(2).astype(jnp.bfloat16)
+        for h in range(2):
+            lanes = slice(h * HEAD, (h + 1) * HEAD)
+            q = rotate(q2[:, lanes], cos_ref[...], sin_ref[...]).astype(jnp.bfloat16)
+            k = rotate(k2[:, lanes], cos_ref[...], sin_ref[...]).astype(jnp.bfloat16)
+            v = v2[:, lanes]
+            size = 256
+            for b in range(C // size):
+                end = (b + 1) * size
+                scores = dot_t(q[b * size : end], k[:end])
+                row = lax.broadcasted_iota(jnp.int32, scores.shape, 0) + b * size
+                keep = lax.broadcasted_iota(jnp.int32, scores.shape, 1) <= row
+                att_ref[g, b * size : end, lanes] = softmax_times(scores, keep, v[:end]).astype(jnp.bfloat16)
+        return 0
+
+    lax.fori_loop(0, STEPS, step, 0)
+    for slot in range(2):
+        arrived(o_ref.at[slot], sems.at[4 + slot])
+
+    def finish(i, _):
+        rows = pl.ds(pl.multiple_of(i * 128, 128), 128)
+        halves = []
+        squares = jnp.zeros((128, 1), jnp.float32)
+        for h in range(2):
+            lanes = slice(h * half, (h + 1) * half)
+            total = x_ref[rows, lanes].astype(jnp.float32)
+            for slot in range(2):
+                for j in range(2):
+                    block = (core if slot == 0 else 1 - core) + 2 * j
+                    weight = o_ref[slot, j * 8 : (j + 1) * 8, h].reshape(PAIR, half)
+                    total = total + dot(att_ref[block, rows, :], weight)
+            middle = total.astype(jnp.bfloat16)
+            mid_ref[rows, lanes] = middle
+            middle = middle.astype(jnp.float32)
+            squares = squares + jnp.sum(middle * middle, axis=-1, keepdims=True)
+            halves.append(middle)
+        inv = lax.rsqrt(squares / D + 1e-05)
+        for h in range(2):
+            lanes = slice(h * half, (h + 1) * half)
+            next_ref[rows, lanes] = (halves[h] * inv * gain_ref[:, lanes]).astype(jnp.bfloat16)
+        return 0
+
+    lax.fori_loop(0, C // 128, finish, 0)
+
+
+def row_layer(place, x, hidden, gain, tables, pieces):
+    vmem = pl.BlockSpec(memory_space=pltpu.VMEM)
+    shape = jax.ShapeDtypeStruct((C, D), jnp.bfloat16)
+    return pl.pallas_call(
+        row_kernel,
+        out_shape=[shape, shape],
+        in_specs=[pl.BlockSpec(memory_space=pltpu.SMEM)]
+        + [vmem] * 5
+        + [pl.BlockSpec(memory_space=pl.ANY)] * len(pieces),
+        out_specs=[vmem, vmem],
+        scratch_shapes=[
+            pltpu.VMEM((2, 2, 16, 2, 32, QKV_PART), jnp.bfloat16),
+            pltpu.VMEM((2, 16, 2, 32, D // 2), jnp.bfloat16),
+            pltpu.VMEM((STEPS, C, PAIR), jnp.bfloat16),
+            pltpu.SemaphoreType.DMA((6,)),
+        ],
+        compiler_params=pltpu.CompilerParams(vmem_limit_bytes=48 * MIB),
+        cost_estimate=pl.CostEstimate(
+            flops=2 * C * D * 4 * WIDTH + 4 * C * C * WIDTH,
+            bytes_accessed=2 * (4 * C * D + 4 * D * WIDTH),
+            transcendentals=C * C * HEADS,
+        ),
+    )(place, x, hidden, gain, *tables, *pieces)
 
 
 def column_kernel(core_ref, x_ref, cos_ref, sin_ref, qo, ko, vo, qs, ks, vs, out_ref, hid_ref):
@@ -144,7 +276,7 @@
     out_ref[...] = dot(selection(True), attended).astype(jnp.bfloat16)
 
 
-def attend(kernel, core, x, gain, tables, own, other):
+def attend(kernel, core, x, tables, own, other):
     half = own.shape[0]
 
     def weight(part):
@@ -153,9 +285,6 @@
     whole = lambda shape: pl.BlockSpec(shape, lambda i: (0, 0), pipeline_mode=pl.Buffered(1))
     specs = [pl.BlockSpec(memory_space=pltpu.SMEM), whole((C, D))]
     args = [core, x]
-    if gain is not None:
-        specs.append(whole((1, D)))
-        args.append(gain)
     specs += [whole((C, HEAD)), whole((C, HEAD))] + [weight(p) for p in range(3)] * 2
     args += [*tables, own, own, own, other, other, other]
     return pl.pallas_call(
@@ -188,67 +317,104 @@
     return total
 
 
-def middle_kernel(core_ref, att_ref, own_ref, other_ref, resid_ref, gain_ref, mid_ref, hid_ref):
-    middle = branch_sum(core_ref[0], att_ref, own_ref, other_ref, resid_ref).astype(jnp.bfloat16)
-    mid_ref[...] = middle
-    x = middle.astype(jnp.float32)
-    inv = lax.rsqrt(jnp.mean(x * x, axis=-1, keepdims=True) + 1e-05)
-    hid_ref[...] = (x * inv * gain_ref[...]).astype(jnp.bfloat16)
-
-
 def final_kernel(core_ref, att_ref, own_ref, other_ref, resid_ref, out_ref):
     out_ref[...] = branch_sum(core_ref[0], att_ref, own_ref, other_ref, resid_ref).astype(jnp.bfloat16)
 
 
-def output_layer(kernel, core, attended, own, other, resid, gain):
+def output_layer(core, attended, own, other, resid):
     size = 128
     block = lambda width: pl.BlockSpec((size, width), lambda i: (i, 0))
     whole = lambda shape: pl.BlockSpec(shape, lambda i: (0, 0), pipeline_mode=pl.Buffered(1))
-    specs = [
-        pl.BlockSpec(memory_space=pltpu.SMEM),
-        block(WIDTH),
-        whole(own.shape),
-        whole(other.shape),
-        block(D),
-    ]
-    args = [core, attended, own, other, resid]
-    outs = 1
-    if gain is not None:
-        specs.append(whole((1, D)))
-        args.append(gain)
-        outs = 2
-    shape = jax.ShapeDtypeStruct((C, D), jnp.bfloat16)
     return pl.pallas_call(
-        kernel,
+        final_kernel,
         grid=(C // size,),
-        out_shape=[shape] * outs,
-        in_specs=specs,
-        out_specs=[block(D)] * outs,
+        out_shape=jax.ShapeDtypeStruct((C, D), jnp.bfloat16),
+        in_specs=[
+            pl.BlockSpec(memory_space=pltpu.SMEM),
+            block(WIDTH),
+            whole(own.shape),
+            whole(other.shape),
+            block(D),
+        ],
+        out_specs=block(D),
         compiler_params=pltpu.CompilerParams(
             dimension_semantics=("arbitrary",), vmem_limit_bytes=40 * MIB
         ),
         cost_estimate=pl.CostEstimate(
             flops=2 * C * D * WIDTH,
-            bytes_accessed=2 * ((1 + outs) * C * D + D * WIDTH + C * WIDTH),
+            bytes_accessed=2 * (2 * C * D + D * WIDTH + C * WIDTH),
             transcendentals=0,
         ),
-    )(*args)
+    )(core, attended, own, other, resid)
+
+
+def shift(value, axis, by):
+    if axis == "y":
+        where = lambda y: (y % 2) * 2 + y // 2
+        return lax.ppermute(value, ("ylo", "yhi"), [(where(y), where((y + by) % 4)) for y in range(4)])
+    return lax.ppermute(value, axis, [(i, (i + by) % 4) for i in range(4)])
+
+
+def ring(value, axis):
+    half = value.shape[-1] // 2
+    left = shift(value, axis, 1)
+    right = shift(value, axis, -1)
+    return [value, left, right, shift(left[..., :half], axis, 1), shift(right[..., half:], axis, -1)]
+
+
+def stack(pieces):
+    own, left, right, low, high = pieces
+    return jnp.stack([own, left, right, jnp.concatenate([low, high], -1)])
+
+
+def swap(value):
+    return lax.ppermute(value, "core", [(0, 1), (1, 0)])
+
+
+def fold_output(output):
+    return jnp.concatenate([output[:, : D // 2], output[:, D // 2 :]], 0)
+
+
+def row_weights(inputs, output):
+    by_step = inputs.reshape(-1, 3, STEPS, PAIR).transpose(0, 2, 1, 3).reshape(-1, 3 * WIDTH)
+    shard = jnp.concatenate([by_step, fold_output(output)], 1)
+    line = lax.all_gather(shard, "z", axis=0)
+    qkv = line[:, :, : 3 * WIDTH].reshape(2, 32, 3 * WIDTH)
+    out = line[:, :, 3 * WIDTH :].reshape(4, 2, 8, WIDTH).transpose(1, 0, 2, 3).reshape(2, 32, WIDTH)
+    parts = []
+    for p in range(2):
+        lanes = slice(p * QKV_PART, (p + 1) * QKV_PART)
+        rest = slice(p * WIDTH // 2, (p + 1) * WIDTH // 2)
+        parts.append(jnp.concatenate([qkv[:, :, lanes], out[:, :, rest]], -1))
+    stacks = [stack(ring(parts[0], "x")), stack(ring(parts[1], "y"))]
+    stacks = lax.optimization_barrier(stacks)
+    own = [ring(stacks[0], "y"), ring(stacks[1], "x")]
+    return own, stacks
+
+
+def column_weights(inputs, output):
+    shard = jnp.concatenate([inputs, fold_output(output)], 1)
+    line = lax.all_gather(shard, ("ylo", "yhi"), axis=0)
+    plane = lax.all_gather(line, ("x", "z"), axis=0)
+    plane = plane.reshape(4, 4, 2, 2, 16, 4 * WIDTH).transpose(2, 0, 3, 1, 4, 5)
+    qkv = plane[..., : 3 * WIDTH].reshape(D // 2, 3 * WIDTH)
+    out = plane[..., 3 * WIDTH :].reshape(64, 2, 8, WIDTH).transpose(0, 2, 1, 3).reshape(WIDTH // 2, D)
+    return (qkv, swap(qkv)), (out, swap(out))
 
 
 def shards(tokens, gain_first, inputs_first, output_first, gain_second, inputs_second, output_second, starts, band_edges):
     residual = tokens[0]
-    core = lax.axis_index("core")
-    core_scalar = core.astype(jnp.int32).reshape(1)
-    seq = lax.axis_index("seq")
-
-    def gather(weight):
-        own = lax.all_gather(weight, ALL_CHIPS, axis=0, tiled=True)
-        return own, lax.ppermute(own, "core", [(0, 1), (1, 0)])
-
-    in_first = gather(inputs_first)
-    out_first = gather(output_first)
-    in_second = gather(inputs_second)
-    out_second = gather(output_second)
+    core = lax.axis_index("core").astype(jnp.int32)
+    core_scalar = core.reshape(1)
+    seq = lax.axis_index(SEQ)
+    my_y = lax.axis_index("yhi") * 2 + lax.axis_index("ylo")
+    place = jnp.stack([core, lax.axis_index("x").astype(jnp.int32), my_y.astype(jnp.int32)])
+
+    own, stacks = row_weights(inputs_first, output_first)
+    inputs_second, output_second, stacks = lax.optimization_barrier((inputs_second, output_second, stacks))
+    in_second, out_second = column_weights(inputs_second, output_second)
+    pieces = [piece for part in own for piece in part]
+    pieces = pieces + [swap(piece) for piece in pieces]
 
     frequency = frequencies(band_edges, HEAD // 2)
     block_starts = starts[0]
@@ -258,26 +424,23 @@
     column_positions = (columns[:, None] + block_starts[None, :]).reshape(C)
     column_tables = rotary_tables(column_positions, frequency)
 
-    attended = attend(row_kernel, core_scalar, residual, gain_first.reshape(1, D), row_tables, *in_first)
-    middle, hidden = output_layer(
-        middle_kernel, core_scalar, attended, *out_first, residual, gain_second.reshape(1, D)
-    )
-    hidden = lax.all_to_all(hidden, "seq", split_axis=0, concat_axis=0, tiled=True)
-    attended = attend(column_kernel, core_scalar, hidden, None, column_tables, *in_second)
-    attended = lax.all_to_all(attended, "seq", split_axis=0, concat_axis=0, tiled=True)
-    (out,) = output_layer(final_kernel, core_scalar, attended, *out_second, middle, None)
-    return out[None]
+    hidden = normed_slots(core_scalar, residual, gain_first.reshape(1, D))
+    middle, hidden = row_layer(place, residual, hidden, gain_second.reshape(1, D), row_tables, pieces)
+    hidden = lax.all_to_all(hidden, SEQ, split_axis=0, concat_axis=0, tiled=True)
+    attended = attend(column_kernel, core_scalar, hidden, column_tables, *in_second)
+    attended = lax.all_to_all(attended, SEQ, split_axis=0, concat_axis=0, tiled=True)
+    return output_layer(core_scalar, attended, *out_second, middle)[None]
 
 
 def solution(mesh):
-    split = Mesh(mesh.devices.reshape(2, 2, N_SEQ), ("ylo", "core", "seq"))
+    split = Mesh(mesh.devices.reshape(2, 2, 4, 2, 4), ("ylo", "core") + SEQ)
     dp = ("ylo", "core")
-    every = ("ylo", "core", "seq")
+    every = dp + SEQ
     return jax.shard_map(
         shards,
         mesh=split,
         in_specs=(
-            P(dp, "seq", None),
+            P(dp, SEQ, None),
             P(),
             P(every, None),
             P(every, None),
@@ -287,6 +450,6 @@
             P(dp, None),
             P(),
         ),
-        out_specs=P(dp, "seq", None),
+        out_specs=P(dp, SEQ, None),
         check_vma=False,
     )

time: 1430 us -> 329 us (0.23)
  waiting for transfers between devices: 1340 us -> 162 us
  starting transfers between devices: 8.08 us -> 42.5 us
  blocking collectives: 0 us -> 29.6 us
    all_gather x4 -> x1, waiting for transfers between devices: 1320 us -> 69.5 us  [column_weights(): plane = lax.all_gather(line, ('x', 'z'), axis=0)]
    ppermute x4 -> x28, waiting for transfers between devices: 0.01 us -> 47.9 us  [the longest x8 35.6 us: shift(): return lax.ppermute(value, axis, [(i, (i + by) % 4) for i in range(4)])]
    all_gather x0 -> x2, blocking collectives: none -> 29.6 us  [the longest x1 15.5 us: column_weights(): line = lax.all_gather(shard, ('ylo', 'yhi'), axis=0)]
    ppermute x4 -> x28, starting transfers between devices: 0.01 us -> 28.8 us  [the longest x8 13.2 us: shift(): return lax.ppermute(value, axis, [(i, (i + by) % 4) for i in range(4)])]
    all_to_all x2, waiting for transfers between devices: 18.2 us -> 44.6 us  [the longest x1 26.8 us: shards(): lax.all_to_all(hidden, SEQ, split_axis=0, concat_axis=0, tiled=True)]
    pallas_call x2 -> x3, Pallas kernels: 10.8 us -> 32.1 us  [the longest x1 24.6 us: row_layer(): pl.pallas_call(row_kernel, out_shape=[shape, shape], in_specs=[pl.BlockSp...]
    pallas_call x2 -> x1, Pallas kernels: 39.1 us -> 21.4 us  [attend(): pl.pallas_call(kernel, grid=(STEPS,), out_shape=jax.ShapeDtypeStruct((C,...]
  transfers between devices with their start and end apart: 10 -> 31, of which waited for: 5 -> 9; matrix products, arithmetic and copies ran while one was open for 0% -> 5% of each run, Pallas kernels for 3% -> 15%
where the time goes in v2:
time: 329 us; the launch traced here: 328 us
  waiting for transfers between devices  162 us (49%)
  Pallas kernels  53.5 us (16%)
  starting transfers between devices  42.5 us (13%)
  blocking collectives  29.6 us (9%)
  local copies, waits for them, and re-layouts  20.1 us (6%)
  between operations  15.1 us (5%)
  other arithmetic  5.31 us (2%)
    all_gather x1, waiting for transfers between devices, column_weights(): plane = lax.all_gather(line, ('x', 'z'), axis=0)  69.5 us
    ppermute x8, waiting for transfers between devices, shift(): return lax.ppermute(value, axis, [(i, (i + by) % 4) for i in range(4)])  35.6 us
    all_to_all x1, waiting for transfers between devices, shards(): lax.all_to_all(hidden, SEQ, split_axis=0, concat_axis=0, tiled=True)  26.8 us
    pallas_call x1, Pallas kernels, row_layer(): pl.pallas_call(row_kernel, out_shape=[shape, shape], in_specs=[pl.BlockSp...  24.6 us
    pallas_call x1, Pallas kernels, attend(): pl.pallas_call(kernel, grid=(STEPS,), out_shape=jax.ShapeDtypeStruct((C,...  21.4 us
    all_to_all x1, waiting for transfers between devices, shards(): lax.all_to_all(attended, SEQ, split_axis=0, concat_axis=0, tiled=True)  17.9 us
    all_gather x1, blocking collectives, column_weights(): line = lax.all_gather(shard, ('ylo', 'yhi'), axis=0)  15.5 us
    all_gather x1, blocking collectives, row_weights(): line = lax.all_gather(shard, 'z', axis=0)  14.1 us
  transfers between devices with their start and end apart: 31, of which 9 were waited for; matrix products, arithmetic and copies ran while one was open for 5% of the time, Pallas kernels for 15%

profile of v2, /device:TPU:0, one launch (start us, length us, event | category | flops | bytes accessed | tf_op | source)
XLA Modules:
  0.0 328.1 jit_solution(7270103345594349373)
XLA Ops:
  6.5 0.7 fusion.11
  7.3 0.9 reshape.86
  8.3 0.1 reshape.87
  8.4 14.1 %all-gather = bf16[64,4096]{1,0:T(8,128)(2,1)S(1)} all-gather(bf16[16,4096]{1,0:T(8,128)(2,1)S(1)} %maximum_maximum_fusion), channel_id=2, replica_groups=mesh['ylo'=2,'core'=2,'x'=4,'yhi'=2,'z'=4] {'z'}, dimensions={0}, use_global_device_ids=true | all-gather | bytes 655360 | tf_op jit(solution)/shard_map/all_gather | solution.py:381
  22.6 2.8 collective-permute-start.1
  25.5 3.1 collective-permute-start.5
  28.6 1.0 collective-permute-done.1
  29.6 3.8 %collective-permute-start.3 = (bf16[2,32,1024]{2,1,0:T(8,128)(2,1)S(1)}, bf16[2,32,1024]{2,1,0:T(8,128)(2,1)S(1)}, u32[]{:S(2)}, u32[]{:S(2)}) collective-permute-start(bf16[2,32,1024]{2,1,0:T(8,128)(2,1)S(1)} %slice.93), channel_id=1, source_target_pairs={{0,24},{8,0},{16,8},{24,16},{1,25},{9,1},{17,9},{25,17},{2,26},{10... | collective-permute-start | bytes 393224 | tf_op jit(solution)/shard_map/ppermute | solution.py:355
  33.5 3.1 collective-permute-start.7
  36.7 2.9 collective-permute-done.2
  39.7 0.1 pad_maximum_fusion.refs_0_
  39.8 3.0 collective-permute-done.6
  42.9 1.1 pad_maximum_fusion.1.refs_5_
  44.0 15.5 %all-gather.1 = bf16[64,4096]{1,0:T(8,128)(2,1)} all-gather(bf16[16,4096]{1,0:T(8,128)(2,1)S(1)} %maximum_maximum_fusion.1), channel_id=3, replica_groups=mesh['ylo'=2,'core'=2,'x'=4,'yhi'=2,'z'=4] {'ylo','yhi'}, dimensions={0}, use_global_device_ids=true | all-gather | bytes 655360 | tf_op jit(solution)/shard_map/all_gather | solution.py:397
  59.5 0.2 collective-permute-start.8
  59.7 3.1 collective-permute-start.9
  62.9 69.5 %all-gather.5.cloned.1.call-done = bf16[64,16,4096]{2,1,0:T(8,128)(2,1)} async-done(((bf16[4,16,4096]{2,1,0:T(8,128)(2,1)}), bf16[64,16,4096]{2,1,0:T(8,128)(2,1)}) %all-gather.5.cloned.1.call-update) | async-done | bytes 8388624 | tf_op jit(solution)/shard_map/all_gather | solution.py:398
  132.4 3.2 slice.102
  135.6 3.1 copy.19
  138.8 0.1 collective-permute-start.26
  138.9 1.5 collective-permute-start.12
  140.4 1.8 collective-permute-start.13
  142.2 0.5 collective-permute-start.21
  142.7 1.1 slice.98
  143.8 1.1 slice.99
  144.9 20.8 %collective-permute-done.12.refs_6_ = bf16[4,2,32,2048]{3,2,1,0:T(8,128)(2,1)S(1)} collective-permute-done((bf16[4,2,32,2048]{3,2,1,0:T(8,128)(2,1)S(1)}, bf16[4,2,32,2048]{3,2,1,0:T(8,128)(2,1)S(1)}, u32[]{:S(2)}, u32[]{:S(2)}) %collective-permute-start.12) | collective-permute-done | bytes 1048608 | tf_op jit(solution)/shard_map/ppermute | solution.py:355
  165.7 1.5 collective-permute-start.10
  167.2 1.8 collective-permute-start.11
  169.0 0.5 collective-permute-start.18
  169.4 1.0 slice.100
  170.4 0.9 slice.101
  171.3 9.2 %collective-permute-done.10.refs_3_ = bf16[4,2,32,1024]{3,2,1,0:T(8,128)(2,1)} collective-permute-done((bf16[4,2,32,1024]{3,2,1,0:T(8,128)(2,1)S(1)}, bf16[4,2,32,1024]{3,2,1,0:T(8,128)(2,1)}, u32[]{:S(2)}, u32[]{:S(2)}) %collective-permute-start.10) | collective-permute-done | bytes 524320 | tf_op jit(solution)/shard_map/ppermute | solution.py:354
  180.5 0.3 collective-permute-start.14
  180.7 3.0 collective-permute-start.15
  183.7 10.8 %collective-permute-done.14.refs_8_ = bf16[4,2,32,1024]{3,2,1,0:T(8,128)(2,1)} collective-permute-done((bf16[4,2,32,1024]{3,2,1,0:T(8,128)(2,1)}, bf16[4,2,32,1024]{3,2,1,0:T(8,128)(2,1)}, u32[]{:S(2)}, u32[]{:S(2)}) %collective-permute-start.14) | collective-permute-done | bytes 524320 | tf_op jit(solution)/shard_map/ppermute | solution.py:355
  194.6 0.5 collective-permute-start.20
  195.1 0.6 fusion.12
  196.9 0.1 collective-permute-start.22
  197.0 0.5 collective-permute-start.23
  197.6 0.1 collective-permute-start.24
  197.7 0.4 collective-permute-start.25
  198.1 0.1 pad_add_fusion.place_ref
  198.2 0.1 convert_element_type.35
  198.3 0.6 constant_dynamic-slice_fusion
  198.9 2.1 shard_map.91.hid_ref
  201.0 1.3 copy-done.3
  202.3 0.6 add_convert_fusion.1
  202.9 2.8 fusion.4
  205.7 0.2 pad_maximum_fusion.2
  205.9 24.6 %shard_map.92 = (bf16[512,2048]{1,0:T(8,128)(2,1)}, bf16[512,2048]{1,0:T(8,128)(2,1)}) custom-call(s32[3]{0:T(128)S(1)} %pad_add_fusion.place_ref, bf16[512,2048]{1,0:T(8,128)(2,1)} %bitcast.53, bf16[512,2048]{1,0:T(8,128)(2,1)} %copy-done.3, f32[1,2048]{1,0:T(1,128)S(1)} %bitcast.56, f32[512,128]{1,0:T(8,128)S(1)} %get-tuple-element.40.cos_ref, ...), custom_call_target="tpu_custom_call" | custom-call | flops 9663676416 | bytes 25165824 | tf_op jit(solution)/shard_map/pallas_call | solution.py:217
  230.6 8.1 %all-to-all-start = ((bf16[32,16,2048]{2,1,0:T(8,128)(2,1)}), bf16[32,16,2048]{2,1,0:T(8,128)(2,1)}, u32[]{:S(2)}, u32[]{:S(2)}) async-start(bf16[32,16,2048]{2,1,0:T(8,128)(2,1)} %bitcast.62), calls=%async_computation | async-start | bytes 4194304 | tf_op jit(solution)/shard_map/all_to_all | solution.py:429
  238.7 1.8 slice.103
  240.4 0.2 copy.20
  240.6 0.1 collective-permute-start.27
  240.7 0.7 copy-done.7
  241.4 0.1 copy-done.8
  241.5 0.2 pad_maximum_fusion.6
  241.7 26.8 %all-to-all-done = bf16[32,16,2048]{2,1,0:T(8,128)(2,1)} async-done(((bf16[32,16,2048]{2,1,0:T(8,128)(2,1)}), bf16[32,16,2048]{2,1,0:T(8,128)(2,1)}, u32[]{:S(2)}, u32[]{:S(2)}) %all-to-all-start) | async-done | bytes 2097184 | tf_op jit(solution)/shard_map/all_to_all | solution.py:429
  268.4 21.4 %shard_map.93 = bf16[512,1024]{1,0:T(8,128)(2,1)S(1)} custom-call(s32[1]{0:T(128)} %bitcast.core_ref, bf16[512,2048]{1,0:T(8,128)(2,1)} %bitcast.24.x_ref, f32[512,128]{1,0:T(8,128)S(1)} %get-tuple-element.42.cos_ref, f32[512,128]{1,0:T(8,128)S(1)} %get-tuple-element.43.sin_ref, bf16[1024,3072]{1,0:T(8,128)(2,1)} %bitcast.29.qo.ko.vo, ...), custom_call_target="tpu_custom_call" | custom-call | flops 7516192768 | bytes 15728640 | tf_op jit(solution)/shard_map/pallas_call | solution.py:290
  289.9 1.0 copy-done
  290.8 5.6 %all-to-all-start.1 = ((bf16[32,16,1024]{2,1,0:T(8,128)(2,1)}), bf16[32,16,1024]{2,1,0:T(8,128)(2,1)S(1)}, u32[]{:S(2)}, u32[]{:S(2)}) async-start(bf16[32,16,1024]{2,1,0:T(8,128)(2,1)} %bitcast.52), calls=%async_computation.1 | async-start | bytes 2097152 | tf_op jit(solution)/shard_map/all_to_all | solution.py:431
  296.4 17.9 %all-to-all-done.1 = bf16[32,16,1024]{2,1,0:T(8,128)(2,1)S(1)} async-done(((bf16[32,16,1024]{2,1,0:T(8,128)(2,1)}), bf16[32,16,1024]{2,1,0:T(8,128)(2,1)S(1)}, u32[]{:S(2)}, u32[]{:S(2)}) %all-to-all-start.1) | async-done | bytes 1048608 | tf_op jit(solution)/shard_map/all_to_all | solution.py:431
  314.3 1.6 copy-done.1
  315.9 5.4 %shard_map.94 = bf16[512,2048]{1,0:T(8,128)(2,1)} custom-call(s32[1]{0:T(128)} %bitcast.core_ref, bf16[512,1024]{1,0:T(8,128)(2,1)S(1)} %bitcast.51, bf16[512,2048]{1,0:T(8,128)(2,1)S(1)} %bitcast.50, bf16[512,2048]{1,0:T(8,128)(2,1)} %collective-permute-done.27.other_ref, bf16[512,2048]{1,0:T(8,128)(2,1)S(1)} %copy-done.1), custom_call_target="tpu_custom_call" | custom-call | flops 2147483648 | bytes 9437184 | tf_op jit(solution)/shard_map/pallas_call | solution.py:328
  (79 shorter events, 0.7 us)
Async XLA Ops:
  6.5 125.9 %all-gather.5.cloned.1.call-start = ((), (), s32[]{:S(2)}) async-start(), calls=%async_computation.2 | async-start | bytes 8912896 | tf_op jit(solution)/shard_map/all_gather | solution.py:398
  22.6 7.0 %collective-permute-start.1 = (bf16[2,32,2048]{2,1,0:T(8,128)(2,1)S(1)}, bf16[2,32,2048]{2,1,0:T(8,128)(2,1)S(1)}, u32[]{:S(2)}, u32[]{:S(2)}) collective-permute-start(bf16[2,32,2048]{2,1,0:T(8,128)(2,1)S(1)} %get-tuple-element.22), channel_id=1, source_target_pairs={{0,24},{8,0},{16,8},{24,16},{1,25},{9,1},{17,9},{25,17},{2,26},{10... | collective-permute-start | bytes 786440 | tf_op jit(solution)/shard_map/ppermute | solution.py:355
  25.5 7.9 %collective-permute-start = (bf16[2,32,2048]{2,1,0:T(8,128)(2,1)S(1)}, bf16[2,32,2048]{2,1,0:T(8,128)(2,1)S(1)}, u32[]{:S(2)}, u32[]{:S(2)}) collective-permute-start(bf16[2,32,2048]{2,1,0:T(8,128)(2,1)S(1)} %get-tuple-element.22), channel_id=1, source_target_pairs={{0,8},{8,16},{16,24},{24,0},{1,9},{9,17},{17,25},{25,1},{2,10},{10... | collective-permute-start | bytes 786440 | tf_op jit(solution)/shard_map/ppermute | solution.py:355
  25.5 8.0 %collective-permute-start.5 = (bf16[2,32,2048]{2,1,0:T(8,128)(2,1)S(1)}, bf16[2,32,2048]{2,1,0:T(8,128)(2,1)S(1)}, u32[]{:S(2)}, u32[]{:S(2)}) collective-permute-start(bf16[2,32,2048]{2,1,0:T(8,128)(2,1)S(1)} %get-tuple-element.20), channel_id=1, source_target_pairs={{0,68},{64,0},{4,64},{68,4},{1,69},{65,1},{5,65},{69,5},{2,70},{66... | collective-permute-start | bytes 786440 | tf_op jit(solution)/shard_map/ppermute | solution.py:354
  28.6 8.0 %collective-permute-start.4 = (bf16[2,32,2048]{2,1,0:T(8,128)(2,1)S(1)}, bf16[2,32,2048]{2,1,0:T(8,128)(2,1)S(1)}, u32[]{:S(2)}, u32[]{:S(2)}) collective-permute-start(bf16[2,32,2048]{2,1,0:T(8,128)(2,1)S(1)} %get-tuple-element.20), channel_id=1, source_target_pairs={{0,64},{64,4},{4,68},{68,0},{1,65},{65,5},{5,69},{69,1},{2,66},{66... | collective-permute-start | bytes 786440 | tf_op jit(solution)/shard_map/ppermute | solution.py:354
  29.6 7.1 %collective-permute-start.3 = (bf16[2,32,1024]{2,1,0:T(8,128)(2,1)S(1)}, bf16[2,32,1024]{2,1,0:T(8,128)(2,1)S(1)}, u32[]{:S(2)}, u32[]{:S(2)}) collective-permute-start(bf16[2,32,1024]{2,1,0:T(8,128)(2,1)S(1)} %slice.93), channel_id=1, source_target_pairs={{0,24},{8,0},{16,8},{24,16},{1,25},{9,1},{17,9},{25,17},{2,26},{10... | collective-permute-start | bytes 393224 | tf_op jit(solution)/shard_map/ppermute | solution.py:355
  33.4 6.2 %collective-permute-start.2 = (bf16[2,32,1024]{2,1,0:T(8,128)(2,1)S(1)}, bf16[2,32,1024]{2,1,0:T(8,128)(2,1)S(1)}, u32[]{:S(2)}, u32[]{:S(2)}) collective-permute-start(bf16[2,32,1024]{2,1,0:T(8,128)(2,1)S(1)} %slice.92), channel_id=1, source_target_pairs={{0,8},{8,16},{16,24},{24,0},{1,9},{9,17},{17,25},{25,1},{2,10},{10... | collective-permute-start | bytes 393224 | tf_op jit(solution)/shard_map/ppermute | solution.py:355
  33.5 6.3 %collective-permute-start.7 = (bf16[2,32,1024]{2,1,0:T(8,128)(2,1)S(1)}, bf16[2,32,1024]{2,1,0:T(8,128)(2,1)S(1)}, u32[]{:S(2)}, u32[]{:S(2)}) collective-permute-start(bf16[2,32,1024]{2,1,0:T(8,128)(2,1)S(1)} %slice.97), channel_id=1, source_target_pairs={{0,68},{64,0},{4,64},{68,4},{1,69},{65,1},{5,65},{69,5},{2,70},{66... | collective-permute-start | bytes 393224 | tf_op jit(solution)/shard_map/ppermute | solution.py:354
  36.6 6.2 %collective-permute-start.6 = (bf16[2,32,1024]{2,1,0:T(8,128)(2,1)S(1)}, bf16[2,32,1024]{2,1,0:T(8,128)(2,1)S(1)}, u32[]{:S(2)}, u32[]{:S(2)}) collective-permute-start(bf16[2,32,1024]{2,1,0:T(8,128)(2,1)S(1)} %slice.96), channel_id=1, source_target_pairs={{0,64},{64,4},{4,68},{68,0},{1,65},{65,5},{5,69},{69,1},{2,66},{66... | collective-permute-start | bytes 393224 | tf_op jit(solution)/shard_map/ppermute | solution.py:354
  39.7 4.3 %copy-start.12 = (bf16[8,2048]{1,0:T(8,128)(2,1)S(1)}, bf16[8,2048]{1,0:T(8,128)(2,1)}, u32[]{:S(2)}) copy-start(bf16[8,2048]{1,0:T(8,128)(2,1)} %param.15) | copy-start | bytes 98308
  39.7 4.3 %copy-start.11 = (bf16[16,3072]{1,0:T(8,128)(2,1)S(1)}, bf16[16,3072]{1,0:T(8,128)(2,1)}, u32[]{:S(2)}) copy-start(bf16[16,3072]{1,0:T(8,128)(2,1)} %param.14) | copy-start | bytes 294916
  59.5 82.7 %collective-permute-start.8 = (bf16[4,2,32,2048]{3,2,1,0:T(8,128)(2,1)S(1)}, bf16[4,2,32,2048]{3,2,1,0:T(8,128)(2,1)}, u32[]{:S(2)}, u32[]{:S(2)}) collective-permute-start(bf16[4,2,32,2048]{3,2,1,0:T(8,128)(2,1)S(1)} %pad_maximum_fusion.refs_0_), channel_id=1, source_target_pairs={{0,64},{64,4},{4,68},{68,0},{1,65},{65,5},{5,69},{69,1},{2,66},{66... | collective-permute-start | bytes 3145736 | tf_op jit(solution)/shard_map/ppermute | solution.py:354
  59.7 82.5 %collective-permute-start.9 = (bf16[4,2,32,2048]{3,2,1,0:T(8,128)(2,1)S(1)}, bf16[4,2,32,2048]{3,2,1,0:T(8,128)(2,1)}, u32[]{:S(2)}, u32[]{:S(2)}) collective-permute-start(bf16[4,2,32,2048]{3,2,1,0:T(8,128)(2,1)S(1)} %pad_maximum_fusion.refs_0_), channel_id=1, source_target_pairs={{0,68},{64,0},{4,64},{68,4},{1,69},{65,1},{5,65},{69,5},{2,70},{66... | collective-permute-start | bytes 3145736 | tf_op jit(solution)/shard_map/ppermute | solution.py:354
  135.6 3.3 copy-start.6
  138.8 56.3 %copy-start.13 = (s32[2]{0:T(128)S(1)}, s32[2]{0:T(128)}, u32[]{:S(2)}) copy-start(s32[2]{0:T(128)} %param.17) | copy-start | bytes 28
  138.8 58.7 %copy-start.14 = (s32[1,32]{1,0:T(1,128)S(1)}, s32[1,32]{1,0:T(1,128)}, u32[]{:S(2)}) copy-start(s32[1,32]{1,0:T(1,128)} %param.16) | copy-start | bytes 388
  138.8 60.1 %copy-start.2 = (bf16[1,512,2048]{2,1,0:T(8,128)(2,1)S(1)}, bf16[1,512,2048]{2,1,0:T(8,128)(2,1)}, u32[]{:S(2)}) copy-start(bf16[1,512,2048]{2,1,0:T(8,128)(2,1)} %param.9) | copy-start | bytes 6291460
  138.8 60.1 %copy-start.4 = (f32[2048]{0:T(1024)S(1)}, f32[2048]{0:T(1024)}, u32[]{:S(2)}) copy-start(f32[2048]{0:T(1024)} %param.10) | copy-start | bytes 24580
  138.8 129.6 %collective-permute-start.26 = (bf16[1024,3072]{1,0:T(8,128)(2,1)}, bf16[1024,3072]{1,0:T(8,128)(2,1)}, u32[]{:S(2)}, u32[]{:S(2)}) collective-permute-start(bf16[1024,3072]{1,0:T(8,128)(2,1)} %bitcast.29.qo.ko.vo), channel_id=1, source_target_pairs={{0,32},{32,0},{1,33},{33,1},{2,34},{34,2},{3,35},{35,3},{4,36},{36... | collective-permute-start | bytes 18874376 | tf_op jit(solution)/shard_map/ppermute | solution.py:371
  138.9 26.8 %collective-permute-start.12 = (bf16[4,2,32,2048]{3,2,1,0:T(8,128)(2,1)S(1)}, bf16[4,2,32,2048]{3,2,1,0:T(8,128)(2,1)S(1)}, u32[]{:S(2)}, u32[]{:S(2)}) collective-permute-start(bf16[4,2,32,2048]{3,2,1,0:T(8,128)(2,1)S(1)} %copy-done.6), channel_id=1, source_target_pairs={{0,8},{8,16},{16,24},{24,0},{1,9},{9,17},{17,25},{25,1},{2,10},{10... | collective-permute-start | bytes 3145736 | tf_op jit(solution)/shard_map/ppermute | solution.py:355
  140.4 26.7 %collective-permute-start.13 = (bf16[4,2,32,2048]{3,2,1,0:T(8,128)(2,1)S(1)}, bf16[4,2,32,2048]{3,2,1,0:T(8,128)(2,1)S(1)}, u32[]{:S(2)}, u32[]{:S(2)}) collective-permute-start(bf16[4,2,32,2048]{3,2,1,0:T(8,128)(2,1)S(1)} %copy-done.6), channel_id=1, source_target_pairs={{0,24},{8,0},{16,8},{24,16},{1,25},{9,1},{17,9},{25,17},{2,26},{10... | collective-permute-start | bytes 3145736 | tf_op jit(solution)/shard_map/ppermute | solution.py:355
  142.2 26.7 %collective-permute-start.16 = (bf16[4,2,32,2048]{3,2,1,0:T(8,128)(2,1)S(1)}, bf16[4,2,32,2048]{3,2,1,0:T(8,128)(2,1)S(1)}, u32[]{:S(2)}, u32[]{:S(2)}) collective-permute-start(bf16[4,2,32,2048]{3,2,1,0:T(8,128)(2,1)S(1)} %pad_maximum_fusion.refs_0_), channel_id=1, source_target_pairs={{0,32},{32,0},{1,33},{33,1},{2,34},{34,2},{3,35},{35,3},{4,36},{36... | collective-permute-start | bytes 3145736 | tf_op jit(solution)/shard_map/ppermute | solution.py:371
  142.2 26.7 %collective-permute-start.21 = (bf16[4,2,32,2048]{3,2,1,0:T(8,128)(2,1)S(1)}, bf16[4,2,32,2048]{3,2,1,0:T(8,128)(2,1)S(1)}, u32[]{:S(2)}, u32[]{:S(2)}) collective-permute-start(bf16[4,2,32,2048]{3,2,1,0:T(8,128)(2,1)S(1)} %copy-done.6), channel_id=1, source_target_pairs={{0,32},{32,0},{1,33},{33,1},{2,34},{34,2},{3,35},{35,3},{4,36},{36... | collective-permute-start | bytes 3145736 | tf_op jit(solution)/shard_map/ppermute | solution.py:371
  165.7 15.1 %copy-start.9 = (bf16[4,2,32,2048]{3,2,1,0:T(8,128)(2,1)}, bf16[4,2,32,2048]{3,2,1,0:T(8,128)(2,1)S(1)}, u32[]{:S(2)}) copy-start(bf16[4,2,32,2048]{3,2,1,0:T(8,128)(2,1)S(1)} %collective-permute-done.12.refs_6_) | copy-start | bytes 3145732
  165.7 14.8 %collective-permute-start.10 = (bf16[4,2,32,1024]{3,2,1,0:T(8,128)(2,1)S(1)}, bf16[4,2,32,1024]{3,2,1,0:T(8,128)(2,1)}, u32[]{:S(2)}, u32[]{:S(2)}) collective-permute-start(bf16[4,2,32,1024]{3,2,1,0:T(8,128)(2,1)S(1)} %slice.98), channel_id=1, source_target_pairs={{0,64},{64,4},{4,68},{68,0},{1,65},{65,5},{5,69},{69,1},{2,66},{66... | collective-permute-start | bytes 1572872 | tf_op jit(solution)/shard_map/ppermute | solution.py:354
  167.2 16.5 %copy-start.10 = (bf16[4,2,32,2048]{3,2,1,0:T(8,128)(2,1)}, bf16[4,2,32,2048]{3,2,1,0:T(8,128)(2,1)S(1)}, u32[]{:S(2)}) copy-start(bf16[4,2,32,2048]{3,2,1,0:T(8,128)(2,1)S(1)} %collective-permute-done.13.refs_7_) | copy-start | bytes 3145732
  167.2 13.6 %collective-permute-start.11 = (bf16[4,2,32,1024]{3,2,1,0:T(8,128)(2,1)S(1)}, bf16[4,2,32,1024]{3,2,1,0:T(8,128)(2,1)}, u32[]{:S(2)}, u32[]{:S(2)}) collective-permute-start(bf16[4,2,32,1024]{3,2,1,0:T(8,128)(2,1)S(1)} %slice.99), channel_id=1, source_target_pairs={{0,68},{64,0},{4,64},{68,4},{1,69},{65,1},{5,65},{69,5},{2,70},{66... | collective-permute-start | bytes 1572872 | tf_op jit(solution)/shard_map/ppermute | solution.py:354
  168.9 14.8 %copy-start.15 = (bf16[4,2,32,2048]{3,2,1,0:T(8,128)(2,1)}, bf16[4,2,32,2048]{3,2,1,0:T(8,128)(2,1)S(1)}, u32[]{:S(2)}) copy-start(bf16[4,2,32,2048]{3,2,1,0:T(8,128)(2,1)S(1)} %collective-permute-done.16.refs_10_) | copy-start | bytes 3145732
  168.9 27.9 %collective-permute-start.17 = (bf16[4,2,32,2048]{3,2,1,0:T(8,128)(2,1)}, bf16[4,2,32,2048]{3,2,1,0:T(8,128)(2,1)}, u32[]{:S(2)}, u32[]{:S(2)}) collective-permute-start(bf16[4,2,32,2048]{3,2,1,0:T(8,128)(2,1)} %collective-permute-done.8.refs_1_), channel_id=1, source_target_pairs={{0,32},{32,0},{1,33},{33,1},{2,34},{34,2},{3,35},{35,3},{4,36},{36... | collective-permute-start | bytes 3145736 | tf_op jit(solution)/shard_map/ppermute | solution.py:371
  168.9 14.8 %copy-start.16 = (bf16[4,2,32,2048]{3,2,1,0:T(8,128)(2,1)}, bf16[4,2,32,2048]{3,2,1,0:T(8,128)(2,1)S(1)}, u32[]{:S(2)}) copy-start(bf16[4,2,32,2048]{3,2,1,0:T(8,128)(2,1)S(1)} %collective-permute-done.21.refs_15_) | copy-start | bytes 3145732
  169.0 28.0 %collective-permute-start.18 = (bf16[4,2,32,2048]{3,2,1,0:T(8,128)(2,1)}, bf16[4,2,32,2048]{3,2,1,0:T(8,128)(2,1)}, u32[]{:S(2)}, u32[]{:S(2)}) collective-permute-start(bf16[4,2,32,2048]{3,2,1,0:T(8,128)(2,1)} %collective-permute-done.9.refs_2_), channel_id=1, source_target_pairs={{0,32},{32,0},{1,33},{33,1},{2,34},{34,2},{3,35},{35,3},{4,36},{36... | collective-permute-start | bytes 3145736 | tf_op jit(solution)/shard_map/ppermute | solution.py:371
  180.5 14.1 %collective-permute-start.14 = (bf16[4,2,32,1024]{3,2,1,0:T(8,128)(2,1)}, bf16[4,2,32,1024]{3,2,1,0:T(8,128)(2,1)}, u32[]{:S(2)}, u32[]{:S(2)}) collective-permute-start(bf16[4,2,32,1024]{3,2,1,0:T(8,128)(2,1)} %slice.100), channel_id=1, source_target_pairs={{0,8},{8,16},{16,24},{24,0},{1,9},{9,17},{17,25},{25,1},{2,10},{10... | collective-permute-start | bytes 1572872 | tf_op jit(solution)/shard_map/ppermute | solution.py:355
  180.7 13.8 %collective-permute-start.15 = (bf16[4,2,32,1024]{3,2,1,0:T(8,128)(2,1)}, bf16[4,2,32,1024]{3,2,1,0:T(8,128)(2,1)}, u32[]{:S(2)}, u32[]{:S(2)}) collective-permute-start(bf16[4,2,32,1024]{3,2,1,0:T(8,128)(2,1)} %slice.101), channel_id=1, source_target_pairs={{0,24},{8,0},{16,8},{24,16},{1,25},{9,1},{17,9},{25,17},{2,26},{10... | collective-permute-start | bytes 1572872 | tf_op jit(solution)/shard_map/ppermute | solution.py:355
  194.6 3.0 collective-permute-start.19
  194.6 3.1 collective-permute-start.20
  196.9 9.0 %collective-permute-start.22 = (bf16[4,2,32,2048]{3,2,1,0:T(8,128)(2,1)}, bf16[4,2,32,2048]{3,2,1,0:T(8,128)(2,1)}, u32[]{:S(2)}, u32[]{:S(2)}) collective-permute-start(bf16[4,2,32,2048]{3,2,1,0:T(8,128)(2,1)} %copy-done.9), channel_id=1, source_target_pairs={{0,32},{32,0},{1,33},{33,1},{2,34},{34,2},{3,35},{35,3},{4,36},{36... | collective-permute-start | bytes 3145736 | tf_op jit(solution)/shard_map/ppermute | solution.py:371
  197.0 8.9 %collective-permute-start.23 = (bf16[4,2,32,2048]{3,2,1,0:T(8,128)(2,1)}, bf16[4,2,32,2048]{3,2,1,0:T(8,128)(2,1)}, u32[]{:S(2)}, u32[]{:S(2)}) collective-permute-start(bf16[4,2,32,2048]{3,2,1,0:T(8,128)(2,1)} %copy-done.10), channel_id=1, source_target_pairs={{0,32},{32,0},{1,33},{33,1},{2,34},{34,2},{3,35},{35,3},{4,36},{36... | collective-permute-start | bytes 3145736 | tf_op jit(solution)/shard_map/ppermute | solution.py:371
  197.6 8.3 %collective-permute-start.24 = (bf16[4,2,32,1024]{3,2,1,0:T(8,128)(2,1)}, bf16[4,2,32,1024]{3,2,1,0:T(8,128)(2,1)}, u32[]{:S(2)}, u32[]{:S(2)}) collective-permute-start(bf16[4,2,32,1024]{3,2,1,0:T(8,128)(2,1)} %collective-permute-done.14.refs_8_), channel_id=1, source_target_pairs={{0,32},{32,0},{1,33},{33,1},{2,34},{34,2},{3,35},{35,3},{4,36},{36... | collective-permute-start | bytes 1572872 | tf_op jit(solution)/shard_map/ppermute | solution.py:371
  197.7 8.2 %collective-permute-start.25 = (bf16[4,2,32,1024]{3,2,1,0:T(8,128)(2,1)}, bf16[4,2,32,1024]{3,2,1,0:T(8,128)(2,1)}, u32[]{:S(2)}, u32[]{:S(2)}) collective-permute-start(bf16[4,2,32,1024]{3,2,1,0:T(8,128)(2,1)} %collective-permute-done.15.refs_9_), channel_id=1, source_target_pairs={{0,32},{32,0},{1,33},{33,1},{2,34},{34,2},{3,35},{35,3},{4,36},{36... | collective-permute-start | bytes 1572872 | tf_op jit(solution)/shard_map/ppermute | solution.py:371
  201.0 1.3 copy-start.3
  202.3 3.6 %copy-start.5 = (f32[2048]{0:T(1024)S(1)}, f32[2048]{0:T(1024)}, u32[]{:S(2)}) copy-start(f32[2048]{0:T(1024)} %param.13) | copy-start | bytes 24580
  230.6 37.9 %all-to-all-start = ((bf16[32,16,2048]{2,1,0:T(8,128)(2,1)}), bf16[32,16,2048]{2,1,0:T(8,128)(2,1)}, u32[]{:S(2)}, u32[]{:S(2)}) async-start(bf16[32,16,2048]{2,1,0:T(8,128)(2,1)} %bitcast.62), calls=%async_computation | async-start | bytes 4194304 | tf_op jit(solution)/shard_map/all_to_all | solution.py:429
  240.4 1.0 copy-start.7
  240.4 1.0 copy-start.8
  240.6 55.8 %collective-permute-start.27 = (bf16[512,2048]{1,0:T(8,128)(2,1)S(1)}, bf16[512,2048]{1,0:T(8,128)(2,1)}, u32[]{:S(2)}, u32[]{:S(2)}) collective-permute-start(bf16[512,2048]{1,0:T(8,128)(2,1)S(1)} %bitcast.49), channel_id=1, source_target_pairs={{0,32},{32,0},{1,33},{33,1},{2,34},{34,2},{3,35},{35,3},{4,36},{36... | collective-permute-start | bytes 6291464 | tf_op jit(solution)/shard_map/ppermute | solution.py:371
  289.9 1.0 copy-start
  290.8 23.5 %all-to-all-start.1 = ((bf16[32,16,1024]{2,1,0:T(8,128)(2,1)}), bf16[32,16,1024]{2,1,0:T(8,128)(2,1)S(1)}, u32[]{:S(2)}, u32[]{:S(2)}) async-start(bf16[32,16,1024]{2,1,0:T(8,128)(2,1)} %bitcast.52), calls=%async_computation.1 | async-start | bytes 2097152 | tf_op jit(solution)/shard_map/all_to_all | solution.py:431
  314.3 1.6 copy-start.1
Sparse Core Ops, SparseCore 0:
  59.7 72.6 all-gather.4

commit v3 on v2

--- a/solution.py
+++ b/solution.py
@@ -66,11 +66,6 @@
     weights = jnp.exp2((scores - top) * (LOG2E / math.sqrt(HEAD)))
     total = jnp.sum(weights, axis=-1, keepdims=True)
     return dot(weights.astype(jnp.bfloat16), values) / total
-
-
-def project(hid_ref, own_ref, other_ref):
-    half = own_ref.shape[0]
-    return dot(hid_ref[:, :half], own_ref[...]) + dot(hid_ref[:, half:], other_ref[...])
 
 
 def norm_kernel(core_ref, x_ref, gain_ref, hid_ref):
@@ -236,8 +231,19 @@
     )(place, x, hidden, gain, *tables, *pieces)
 
 
-def column_kernel(core_ref, x_ref, cos_ref, sin_ref, qo, ko, vo, qs, ks, vs, out_ref, hid_ref):
+def column_kernel(core_ref, x_ref, cos_ref, sin_ref, own_plane, other_plane, out_ref, w_ref, hid_ref, sems):
     core = core_ref[0]
+    half = D // 2
+    triple = 3 * PAIR
+
+    for g in range(STEPS):
+        lanes = pl.ds(g * triple, triple)
+        for slot, plane in enumerate((own_plane, other_plane)):
+            for ylo in range(2):
+                for yhi in range(2):
+                    src = plane.at[:, :, ylo, yhi, :, lanes]
+                    dst = w_ref.at[g, slot, ylo, :, yhi]
+                    pltpu.make_async_copy(src, dst, sems.at[g]).start()
 
     def selection(transposed):
         a = lax.broadcasted_iota(jnp.int32, (C, C), 1 if transposed else 0)
@@ -245,64 +251,70 @@
         same = (a // N_SEQ == lax.rem(b, COLS)) & (lax.rem(a, N_SEQ) == b // COLS)
         return jnp.where(same, 1.0, 0.0).astype(jnp.bfloat16)
 
-    @pl.when(pl.program_id(0) == 0)
-    def _():
-        pick = selection(False)
-        width = D // 4
-        for block in range(4):
-            lanes = pl.ds(pl.multiple_of(slot_of(block, core) * width, width), width)
-            moved = dot(pick, x_ref[:, block * width : (block + 1) * width])
-            hid_ref[:, lanes] = moved.astype(jnp.bfloat16)
-
-    q2 = project(hid_ref, qo, qs)
-    k2 = project(hid_ref, ko, ks)
-    v2 = project(hid_ref, vo, vs).astype(jnp.bfloat16)
+    pick = selection(False)
+    width = D // 4
+    for block in range(4):
+        lanes = pl.ds(pl.multiple_of(slot_of(block, core) * width, width), width)
+        moved = dot(pick, x_ref[:, block * width : (block + 1) * width])
+        hid_ref[:, lanes] = moved.astype(jnp.bfloat16)
+
+    back = selection(True)
     size = 128
     row = lax.broadcasted_iota(jnp.int32, (size, size), 0)
     col = lax.broadcasted_iota(jnp.int32, (size, size), 1)
     keep = (row // N_SEQ == col // N_SEQ) & (col <= row)
-    heads = []
-    for h in range(2):
-        lanes = slice(h * HEAD, (h + 1) * HEAD)
-        q = rotate(q2[:, lanes], cos_ref[...], sin_ref[...]).astype(jnp.bfloat16)
-        k = rotate(k2[:, lanes], cos_ref[...], sin_ref[...]).astype(jnp.bfloat16)
-        v = v2[:, lanes]
-        blocks = []
-        for b in range(C // size):
-            rows = slice(b * size, (b + 1) * size)
-            blocks.append(softmax_times(dot_t(q[rows], k[rows]), keep, v[rows]).astype(jnp.bfloat16))
-        heads.append(jnp.concatenate(blocks, 0))
-    attended = jnp.concatenate(heads, 1)
-    out_ref[...] = dot(selection(True), attended).astype(jnp.bfloat16)
-
-
-def attend(kernel, core, x, tables, own, other):
-    half = own.shape[0]
-
-    def weight(part):
-        return pl.BlockSpec((half, PAIR), lambda i: (0, part * STEPS + i))
-
-    whole = lambda shape: pl.BlockSpec(shape, lambda i: (0, 0), pipeline_mode=pl.Buffered(1))
-    specs = [pl.BlockSpec(memory_space=pltpu.SMEM), whole((C, D))]
-    args = [core, x]
-    specs += [whole((C, HEAD)), whole((C, HEAD))] + [weight(p) for p in range(3)] * 2
-    args += [*tables, own, own, own, other, other, other]
+
+    def step(g, _):
+        pltpu.make_async_copy(w_ref.at[g], w_ref.at[g], sems.at[g]).wait()
+
+        def weight(slot, kind):
+            lanes = slice(kind * PAIR, (kind + 1) * PAIR)
+            return w_ref[g, slot, :, :, :, :, :, lanes].reshape(half, PAIR)
+
+        def projected(kind):
+            return dot(hid_ref[:, :half], weight(0, kind)) + dot(hid_ref[:, half:], weight(1, kind))
+
+        q2 = projected(0)
+        k2 = projected(1)
+        v2 = projected(2).astype(jnp.bfloat16)
+        heads = []
+        for h in range(2):
+            lanes = slice(h * HEAD, (h + 1) * HEAD)
+            q = rotate(q2[:, lanes], cos_ref[...], sin_ref[...]).astype(jnp.bfloat16)
+            k = rotate(k2[:, lanes], cos_ref[...], sin_ref[...]).astype(jnp.bfloat16)
+            v = v2[:, lanes]
+            blocks = []
+            for b in range(C // size):
+                rows = slice(b * size, (b + 1) * size)
+                blocks.append(softmax_times(dot_t(q[rows], k[rows]), keep, v[rows]).astype(jnp.bfloat16))
+            heads.append(jnp.concatenate(blocks, 0))
+        attended = jnp.concatenate(heads, 1)
+        lanes = pl.ds(pl.multiple_of(g * PAIR, PAIR), PAIR)
+        out_ref[:, lanes] = dot(back, attended).astype(jnp.bfloat16)
+        return 0
+
+    lax.fori_loop(0, STEPS, step, 0)
+
+
+def column_layer(core, x, tables, planes):
+    vmem = pl.BlockSpec(memory_space=pltpu.VMEM)
     return pl.pallas_call(
-        kernel,
-        grid=(STEPS,),
+        column_kernel,
         out_shape=jax.ShapeDtypeStruct((C, WIDTH), jnp.bfloat16),
-        in_specs=specs,
-        out_specs=pl.BlockSpec((C, PAIR), lambda i: (0, i)),
-        scratch_shapes=[pltpu.VMEM((C, D), jnp.bfloat16)],
-        compiler_params=pltpu.CompilerParams(
-            dimension_semantics=("arbitrary",), vmem_limit_bytes=40 * MIB
-        ),
+        in_specs=[pl.BlockSpec(memory_space=pltpu.SMEM)] + [vmem] * 3 + [pl.BlockSpec(memory_space=pl.ANY)] * 2,
+        out_specs=vmem,
+        scratch_shapes=[
+            pltpu.VMEM((STEPS, 2, 2, 4, 2, 4, 16, 3 * PAIR), jnp.bfloat16),
+            pltpu.VMEM((C, D), jnp.bfloat16),
+            pltpu.SemaphoreType.DMA((STEPS,)),
+        ],
+        compiler_params=pltpu.CompilerParams(vmem_limit_bytes=40 * MIB),
         cost_estimate=pl.CostEstimate(
             flops=2 * C * D * 3 * WIDTH + 4 * C * C * WIDTH,
             bytes_accessed=2 * (C * D + 3 * D * WIDTH + C * WIDTH),
             transcendentals=C * C * HEADS,
         ),
-    )(*args)
+    )(core, x, *tables, *planes)
 
 
 def branch_sum(core, att_ref, own_ref, other_ref, resid_ref):
@@ -375,31 +387,38 @@
     return jnp.concatenate([output[:, : D // 2], output[:, D // 2 :]], 0)
 
 
-def row_weights(inputs, output):
-    by_step = inputs.reshape(-1, 3, STEPS, PAIR).transpose(0, 2, 1, 3).reshape(-1, 3 * WIDTH)
-    shard = jnp.concatenate([by_step, fold_output(output)], 1)
-    line = lax.all_gather(shard, "z", axis=0)
-    qkv = line[:, :, : 3 * WIDTH].reshape(2, 32, 3 * WIDTH)
-    out = line[:, :, 3 * WIDTH :].reshape(4, 2, 8, WIDTH).transpose(1, 0, 2, 3).reshape(2, 32, WIDTH)
+def by_step(inputs):
+    return inputs.reshape(-1, 3, STEPS, PAIR).transpose(0, 2, 1, 3).reshape(-1, 3 * WIDTH)
+
+
+def row_weights(inputs, output, line):
+    shard = jnp.concatenate([by_step(inputs), fold_output(output)], 1)
+    rows = lax.all_gather(shard, "z", axis=0)
+    qkv = rows[:, :, : 3 * WIDTH].reshape(2, 32, 3 * WIDTH)
+    out = rows[:, :, 3 * WIDTH :].reshape(4, 2, 8, WIDTH).transpose(1, 0, 2, 3).reshape(2, 32, WIDTH)
     parts = []
     for p in range(2):
         lanes = slice(p * QKV_PART, (p + 1) * QKV_PART)
         rest = slice(p * WIDTH // 2, (p + 1) * WIDTH // 2)
         parts.append(jnp.concatenate([qkv[:, :, lanes], out[:, :, rest]], -1))
     stacks = [stack(ring(parts[0], "x")), stack(ring(parts[1], "y"))]
-    stacks = lax.optimization_barrier(stacks)
+    stacks, line = lax.optimization_barrier((stacks, line))
     own = [ring(stacks[0], "y"), ring(stacks[1], "x")]
-    return own, stacks
-
-
-def column_weights(inputs, output):
-    shard = jnp.concatenate([inputs, fold_output(output)], 1)
-    line = lax.all_gather(shard, ("ylo", "yhi"), axis=0)
-    plane = lax.all_gather(line, ("x", "z"), axis=0)
-    plane = plane.reshape(4, 4, 2, 2, 16, 4 * WIDTH).transpose(2, 0, 3, 1, 4, 5)
-    qkv = plane[..., : 3 * WIDTH].reshape(D // 2, 3 * WIDTH)
-    out = plane[..., 3 * WIDTH :].reshape(64, 2, 8, WIDTH).transpose(0, 2, 1, 3).reshape(WIDTH // 2, D)
-    return (qkv, swap(qkv)), (out, swap(out))
+    return own, line
+
+
+def column_line(inputs, output):
+    shard = jnp.concatenate([by_step(inputs), fold_output(output)], 1)
+    return lax.all_gather(jnp.concatenate([shard, shard], 1), ("ylo", "yhi"), axis=0)
+
+
+def column_plane(line):
+    return lax.all_gather(line[:, :, : 4 * WIDTH], ("x", "z"), axis=0).reshape(4, 4, 2, 2, 16, 4 * WIDTH)
+
+
+def column_output(plane):
+    out = plane[..., 3 * WIDTH :].transpose(2, 0, 3, 1, 4, 5)
+    return out.reshape(64, 2, 8, WIDTH).transpose(0, 2, 1, 3).reshape(WIDTH // 2, D)
 
 
 def shards(tokens, gain_first, inputs_first, output_first, gain_second, inputs_second, output_second, starts, band_edges):
@@ -410,9 +429,9 @@
     my_y = lax.axis_index("yhi") * 2 + lax.axis_index("ylo")
     place = jnp.stack([core, lax.axis_index("x").astype(jnp.int32), my_y.astype(jnp.int32)])
 
-    own, stacks = row_weights(inputs_first, output_first)
-    inputs_second, output_second, stacks = lax.optimization_barrier((inputs_second, output_second, stacks))
-    in_second, out_second = column_weights(inputs_second, output_second)
+    line = column_line(inputs_second, output_second)
+    own, line = row_weights(inputs_first, output_first, line)
+    plane = column_plane(line)
     pieces = [piece for part in own for piece in part]
     pieces = pieces + [swap(piece) for piece in pieces]
 
@@ -426,10 +445,12 @@
 
     hidden = normed_slots(core_scalar, residual, gain_first.reshape(1, D))
     middle, hidden = row_layer(place, residual, hidden, gain_second.reshape(1, D), row_tables, pieces)
+    plane, hidden = lax.optimization_barrier((plane, hidden))
+    planes = (plane, swap(plane))
     hidden = lax.all_to_all(hidden, SEQ, split_axis=0, concat_axis=0, tiled=True)
-    attended = attend(column_kernel, core_scalar, hidden, column_tables, *in_second)
+    attended = column_layer(core_scalar, hidden, column_tables, planes)
     attended = lax.all_to_all(attended, SEQ, split_axis=0, concat_axis=0, tiled=True)
-    return output_layer(core_scalar, attended, *out_second, middle)[None]
+    return output_layer(core_scalar, attended, *[column_output(p) for p in planes], middle)[None]
 
 
 def solution(mesh):

time: 329 us -> 253 us (0.77)
  waiting for transfers between devices: 162 us -> 104 us
  blocking collectives: 29.6 us -> 14.1 us
  Pallas kernels: 53.5 us -> 50.2 us
    all_gather x1 -> x2, waiting for transfers between devices: 69.5 us -> 0.04 us  [the longest x1 0.02 us: column_line(): lax.all_gather(jnp.concatenate([shard, shard], 1), ('ylo', 'yhi'), axis=0)]
    ppermute x8, waiting for transfers between devices: 12.2 us -> 33.6 us  [shift(): lax.ppermute(value, ('ylo', 'yhi'), [(where(y), where((y + by) % 4)) for...]
    all_gather x2 -> x1, blocking collectives: 29.6 us -> 14.1 us  [row_weights(): rows = lax.all_gather(shard, 'z', axis=0)]
    ppermute x8, waiting for transfers between devices: 35.6 us -> 29 us  [shift(): return lax.ppermute(value, axis, [(i, (i + by) % 4) for i in range(4)])]
    slice x5 -> x2, local copies, waits for them, and re-layouts: 8.34 us -> 1.95 us  [the longest x1 1.92 us: column_plane(): line[:, :, :4 * WIDTH]]
    all_to_all x1, waiting for transfers between devices: 17.9 us -> 12.5 us  [shards(): lax.all_to_all(attended, SEQ, split_axis=0, concat_axis=0, tiled=True)]
    transpose x0 -> x4, local copies, waits for them, and re-layouts: none -> 5.19 us  [column_output(): out = plane[..., 3 * WIDTH:].transpose(2, 0, 3, 1, 4, 5)]
    unnamed x34 -> x32, local copies, waits for them, and re-layouts: 4.66 us -> 8.84 us
  transfers between devices with their start and end apart: 31 -> 31, of which waited for: 9 -> 9; matrix products, arithmetic and copies ran while one was open for 5% -> 6% of each run, Pallas kernels for 15% -> 11%
where the time goes in v3:
time: 253 us
  waiting for transfers between devices  104 us (41%)
  Pallas kernels  50.2 us (20%)
  starting transfers between devices  40.1 us (16%)
  local copies, waits for them, and re-layouts  22.9 us (9%)
  between operations  15.2 us (6%)
  blocking collectives  14.1 us (6%)
  other arithmetic  6.02 us (2%)
    ppermute x8, waiting for transfers between devices, shift(): lax.ppermute(value, ('ylo', 'yhi'), [(where(y), where((y + by) % 4)) for...  33.6 us
    all_to_all x1, waiting for transfers between devices, shards(): lax.all_to_all(hidden, SEQ, split_axis=0, concat_axis=0, tiled=True)  29.1 us
    ppermute x8, waiting for transfers between devices, shift(): return lax.ppermute(value, axis, [(i, (i + by) % 4) for i in range(4)])  29 us
    pallas_call x1, Pallas kernels, row_layer(): pl.pallas_call(row_kernel, out_shape=[shape, shape], in_specs=[pl.BlockSp...  24.6 us
    pallas_call x1, Pallas kernels, column_layer(): pl.pallas_call(column_kernel, out_shape=jax.ShapeDtypeStruct((C, WIDTH),...  19.8 us
    all_gather x1, blocking collectives, row_weights(): rows = lax.all_gather(shard, 'z', axis=0)  14.1 us
    ppermute x8, starting transfers between devices, shift(): return lax.ppermute(value, axis, [(i, (i + by) % 4) for i in range(4)])  13.2 us
    all_to_all x1, waiting for transfers between devices, shards(): lax.all_to_all(attended, SEQ, split_axis=0, concat_axis=0, tiled=True)  12.5 us
  transfers between devices with their start and end apart: 31, of which 9 were waited for; matrix products, arithmetic and copies ran while one was open for 6% of the time, Pallas kernels for 11%

profile of v3, /device:TPU:0, one launch (start us, length us, event | category | flops | bytes accessed | tf_op | source)
XLA Modules:
  0.0 252.6 jit_solution(7858975739524120407)
XLA Ops:
  6.5 0.7 fusion.10
  7.3 0.9 reshape.98
  8.3 0.1 reshape.99
  8.4 0.7 maximum_maximum_fusion
  9.2 0.7 fusion.11
  9.9 0.9 reshape.93
  10.9 0.1 reshape.94
  11.1 14.1 %all-gather = bf16[64,4096]{1,0:T(8,128)(2,1)S(1)} all-gather(bf16[16,4096]{1,0:T(8,128)(2,1)S(1)} %maximum_maximum_fusion.1), channel_id=2, replica_groups=mesh['ylo'=2,'core'=2,'x'=4,'yhi'=2,'z'=4] {'z'}, dimensions={0}, use_global_device_ids=true | all-gather | bytes 655360 | tf_op jit(solution)/shard_map/all_gather | solution.py:396
  25.3 1.6 collective-permute-start.4
  26.9 1.7 collective-permute-start.5
  28.7 1.6 collective-permute-start
  30.2 1.7 collective-permute-start.1
  32.0 14.4 %collective-permute-done.4 = bf16[2,32,2048]{2,1,0:T(8,128)(2,1)S(1)} collective-permute-done((bf16[2,32,2048]{2,1,0:T(8,128)(2,1)S(1)}, bf16[2,32,2048]{2,1,0:T(8,128)(2,1)S(1)}, u32[]{:S(2)}, u32[]{:S(2)}) %collective-permute-start.4) | collective-permute-done | bytes 262176 | tf_op jit(solution)/shard_map/ppermute | solution.py:366
  46.5 3.3 %collective-permute-start.7 = (bf16[2,32,1024]{2,1,0:T(8,128)(2,1)S(1)}, bf16[2,32,1024]{2,1,0:T(8,128)(2,1)S(1)}, u32[]{:S(2)}, u32[]{:S(2)}) collective-permute-start(bf16[2,32,1024]{2,1,0:T(8,128)(2,1)S(1)} %slice.101), channel_id=1, source_target_pairs={{0,68},{64,0},{4,64},{68,4},{1,69},{65,1},{5,65},{69,5},{2,70},{66... | collective-permute-start | bytes 393224 | tf_op jit(solution)/shard_map/ppermute | solution.py:366
  49.8 1.5 collective-permute-start.2
  51.4 1.8 collective-permute-start.3
  53.2 2.8 %collective-permute-done.2 = bf16[2,32,1024]{2,1,0:T(8,128)(2,1)S(1)} collective-permute-done((bf16[2,32,1024]{2,1,0:T(8,128)(2,1)S(1)}, bf16[2,32,1024]{2,1,0:T(8,128)(2,1)S(1)}, u32[]{:S(2)}, u32[]{:S(2)}) %collective-permute-start.2) | collective-permute-done | bytes 131104 | tf_op jit(solution)/shard_map/ppermute | solution.py:367
  56.0 0.4 collective-permute-done.3
  56.4 1.1 pad_maximum_fusion.1.refs_5_
  57.5 0.1 pad_maximum_fusion.refs_0_
  57.7 1.9 slice.83
  59.8 3.2 %collective-permute-start.9 = (bf16[4,2,32,2048]{3,2,1,0:T(8,128)(2,1)S(1)}, bf16[4,2,32,2048]{3,2,1,0:T(8,128)(2,1)S(1)}, u32[]{:S(2)}, u32[]{:S(2)}) collective-permute-start(bf16[4,2,32,2048]{3,2,1,0:T(8,128)(2,1)S(1)} %pad_maximum_fusion.refs_0_), channel_id=1, source_target_pairs={{0,68},{64,0},{4,64},{68,4},{1,69},{65,1},{5,65},{69,5},{2,70},{66... | collective-permute-start | bytes 3145736 | tf_op jit(solution)/shard_map/ppermute | solution.py:366
  63.0 1.5 collective-permute-start.12
  64.5 1.8 collective-permute-start.13
  66.2 16.3 %collective-permute-done.8.refs_1_ = bf16[4,2,32,2048]{3,2,1,0:T(8,128)(2,1)S(1)} collective-permute-done((bf16[4,2,32,2048]{3,2,1,0:T(8,128)(2,1)S(1)}, bf16[4,2,32,2048]{3,2,1,0:T(8,128)(2,1)S(1)}, u32[]{:S(2)}, u32[]{:S(2)}) %collective-permute-start.8) | collective-permute-done | bytes 1048608 | tf_op jit(solution)/shard_map/ppermute | solution.py:366
  82.6 0.9 copy-done.9
  83.5 11.0 %collective-permute-done.12.refs_6_ = bf16[4,2,32,2048]{3,2,1,0:T(8,128)(2,1)S(1)} collective-permute-done((bf16[4,2,32,2048]{3,2,1,0:T(8,128)(2,1)}, bf16[4,2,32,2048]{3,2,1,0:T(8,128)(2,1)S(1)}, u32[]{:S(2)}, u32[]{:S(2)}) %collective-permute-start.12) | collective-permute-done | bytes 1048608 | tf_op jit(solution)/shard_map/ppermute | solution.py:367
  94.5 1.5 collective-permute-start.11
  96.0 0.8 slice.104
  96.8 1.2 collective-permute-start.14
  98.0 0.9 slice.105
  98.8 2.1 collective-permute-start.15
  100.9 2.9 %collective-permute-done.11.refs_4_ = bf16[4,2,32,1024]{3,2,1,0:T(8,128)(2,1)} collective-permute-done((bf16[4,2,32,1024]{3,2,1,0:T(8,128)(2,1)S(1)}, bf16[4,2,32,1024]{3,2,1,0:T(8,128)(2,1)}, u32[]{:S(2)}, u32[]{:S(2)}) %collective-permute-start.11) | collective-permute-done | bytes 524320 | tf_op jit(solution)/shard_map/ppermute | solution.py:366
  103.8 14.8 %collective-permute-done.14.refs_8_ = bf16[4,2,32,1024]{3,2,1,0:T(8,128)(2,1)} collective-permute-done((bf16[4,2,32,1024]{3,2,1,0:T(8,128)(2,1)}, bf16[4,2,32,1024]{3,2,1,0:T(8,128)(2,1)}, u32[]{:S(2)}, u32[]{:S(2)}) %collective-permute-start.14) | collective-permute-done | bytes 524320 | tf_op jit(solution)/shard_map/ppermute | solution.py:367
  118.6 0.6 fusion.12
  120.6 0.6 collective-permute-start.17
  121.2 0.1 collective-permute-start.18
  121.3 0.4 collective-permute-start.22
  121.7 0.1 collective-permute-start.23
  122.0 0.6 collective-permute-start.25
  122.6 0.1 pad_add_fusion.place_ref
  122.6 0.6 constant_dynamic-slice_fusion
  123.2 0.1 convert_element_type.35
  123.3 2.1 shard_map.91.hid_ref
  125.4 1.3 copy-done.3
  126.8 0.6 add_convert_fusion.1
  127.4 2.8 %fusion.4 = (f32[512,64]{1,0:T(8,128)S(1)}, f32[512,64]{1,0:T(8,128)}, f32[512,64]{1,0:T(8,128)}, f32[512,64]{1,0:T(8,128)S(1)}, f32[512,64]{1,0:T(8,128)S(1)}, /*index=5*/f32[512,64]{1,0:T(8,128)S(1)}) fusion(f32[64]{0:T(128)S(1)} %multiply_add_fusion, f32[512]{0:T(512)S(1)} %convert_element_type.35, f32[512]{0:T(512)S(1)} %add_convert_fusion.1), kind=kLoop, calls=%fused_computation.26 | loop fusion | flops 262144 | bytes 790784 | tf_op jit(solution)/shard_map/neg | solution.py:43
  130.1 0.2 pad_maximum_fusion.4
  130.4 24.6 %shard_map.92 = (bf16[512,2048]{1,0:T(8,128)(2,1)}, bf16[512,2048]{1,0:T(8,128)(2,1)}) custom-call(s32[3]{0:T(128)S(1)} %pad_add_fusion.place_ref, bf16[512,2048]{1,0:T(8,128)(2,1)} %bitcast.61, bf16[512,2048]{1,0:T(8,128)(2,1)} %copy-done.3, f32[1,2048]{1,0:T(1,128)S(1)} %bitcast.68, f32[512,128]{1,0:T(8,128)S(1)} %get-tuple-element.42.cos_ref, ...), custom_call_target="tpu_custom_call" | custom-call | flops 9663676416 | bytes 25165824 | tf_op jit(solution)/shard_map/pallas_call | solution.py:212
  155.0 0.2 collective-permute-start.26
  155.2 6.5 %all-to-all-start = ((bf16[32,16,2048]{2,1,0:T(8,128)(2,1)}), bf16[32,16,2048]{2,1,0:T(8,128)(2,1)S(1)}, u32[]{:S(2)}, u32[]{:S(2)}) async-start(bf16[32,16,2048]{2,1,0:T(8,128)(2,1)} %bitcast.71), calls=%async_computation | async-start | bytes 4194304 | tf_op jit(solution)/shard_map/all_to_all | solution.py:450
  161.8 0.2 pad_maximum_fusion.6
  162.0 29.1 %all-to-all-done = bf16[32,16,2048]{2,1,0:T(8,128)(2,1)S(1)} async-done(((bf16[32,16,2048]{2,1,0:T(8,128)(2,1)}), bf16[32,16,2048]{2,1,0:T(8,128)(2,1)S(1)}, u32[]{:S(2)}, u32[]{:S(2)}) %all-to-all-start) | async-done | bytes 2097184 | tf_op jit(solution)/shard_map/all_to_all | solution.py:450
  191.1 3.4 %copy-done.4 = bf16[64,16,4096]{2,1,0:T(8,128)(2,1)S(1)} copy-done((bf16[64,16,4096]{2,1,0:T(8,128)(2,1)S(1)}, bf16[64,16,4096]{2,1,0:T(8,128)(2,1)}, u32[]{:S(2)}) %copy-start.4) | copy-done | bytes 8388632
  194.4 19.8 %shard_map.93 = bf16[512,1024]{1,0:T(8,128)(2,1)} custom-call(s32[1]{0:T(128)} %bitcast.core_ref, bf16[512,2048]{1,0:T(8,128)(2,1)S(1)} %bitcast.63, f32[512,128]{1,0:T(8,128)S(1)} %get-tuple-element.44.cos_ref, f32[512,128]{1,0:T(8,128)S(1)} %get-tuple-element.45.sin_ref, bf16[4,4,2,2,16,4096]{5,4,3,2,1,0:T(8,128)(2,1)S(1)} %bitcast.66, ...), custom_call_target="tpu_custom_call" | custom-call | flops 7516192768 | bytes 15728640 | tf_op jit(solution)/shard_map/pallas_call | solution.py:301
  214.2 7.0 %all-to-all-start.1 = ((bf16[32,16,1024]{2,1,0:T(8,128)(2,1)}), bf16[32,16,1024]{2,1,0:T(8,128)(2,1)S(1)}, u32[]{:S(2)}, u32[]{:S(2)}) async-start(bf16[32,16,1024]{2,1,0:T(8,128)(2,1)} %bitcast.29), calls=%async_computation.1 | async-start | bytes 2097152 | tf_op jit(solution)/shard_map/all_to_all | solution.py:452
  221.2 1.8 slice_bitcast_fusion.1
  223.0 0.2 copy.18
  223.1 1.8 slice_bitcast_fusion
  224.9 1.5 copy.19
  226.4 12.5 %all-to-all-done.1 = bf16[32,16,1024]{2,1,0:T(8,128)(2,1)S(1)} async-done(((bf16[32,16,1024]{2,1,0:T(8,128)(2,1)}), bf16[32,16,1024]{2,1,0:T(8,128)(2,1)S(1)}, u32[]{:S(2)}, u32[]{:S(2)}) %all-to-all-start.1) | async-done | bytes 1048608 | tf_op jit(solution)/shard_map/all_to_all | solution.py:452
  238.9 1.6 copy-done
  240.4 1.6 copy-done.1
  242.0 3.8 %shard_map.94 = bf16[512,2048]{1,0:T(8,128)(2,1)} custom-call(s32[1]{0:T(128)} %bitcast.core_ref, bf16[512,1024]{1,0:T(8,128)(2,1)S(1)} %bitcast.60, bf16[512,2048]{1,0:T(8,128)(2,1)S(1)} %bitcast.58, bf16[512,2048]{1,0:T(8,128)(2,1)S(1)} %bitcast.59, bf16[512,2048]{1,0:T(8,128)(2,1)S(1)} %copy-done.1), custom_call_target="tpu_custom_call" | custom-call | flops 2147483648 | bytes 9437184 | tf_op jit(solution)/shard_map/pallas_call | solution.py:340
  (81 shorter events, 0.9 us)
Async XLA Ops:
  6.5 51.2 %all-gather.6.cloned.1.call-start = ((), (), s32[]{:S(2)}) async-start(), calls=%async_computation.2 | async-start | bytes 1310720 | tf_op jit(solution)/shard_map/all_gather | solution.py:412
  9.1 145.9 %all-gather.8.cloned.1.call-start = ((), (), s32[]{:S(2)}) async-start(), calls=%async_computation.3 | async-start | bytes 8912896 | tf_op jit(solution)/shard_map/all_gather | solution.py:416
  25.3 21.1 %collective-permute-start.4 = (bf16[2,32,2048]{2,1,0:T(8,128)(2,1)S(1)}, bf16[2,32,2048]{2,1,0:T(8,128)(2,1)S(1)}, u32[]{:S(2)}, u32[]{:S(2)}) collective-permute-start(bf16[2,32,2048]{2,1,0:T(8,128)(2,1)S(1)} %get-tuple-element.22), channel_id=1, source_target_pairs={{0,64},{64,4},{4,68},{68,0},{1,65},{65,5},{5,69},{69,1},{2,66},{66... | collective-permute-start | bytes 786440 | tf_op jit(solution)/shard_map/ppermute | solution.py:366
  26.9 19.5 %collective-permute-start.5 = (bf16[2,32,2048]{2,1,0:T(8,128)(2,1)S(1)}, bf16[2,32,2048]{2,1,0:T(8,128)(2,1)S(1)}, u32[]{:S(2)}, u32[]{:S(2)}) collective-permute-start(bf16[2,32,2048]{2,1,0:T(8,128)(2,1)S(1)} %get-tuple-element.22), channel_id=1, source_target_pairs={{0,68},{64,0},{4,64},{68,4},{1,69},{65,1},{5,65},{69,5},{2,70},{66... | collective-permute-start | bytes 786440 | tf_op jit(solution)/shard_map/ppermute | solution.py:366
  28.7 21.1 %collective-permute-start = (bf16[2,32,2048]{2,1,0:T(8,128)(2,1)S(1)}, bf16[2,32,2048]{2,1,0:T(8,128)(2,1)S(1)}, u32[]{:S(2)}, u32[]{:S(2)}) collective-permute-start(bf16[2,32,2048]{2,1,0:T(8,128)(2,1)S(1)} %get-tuple-element.24), channel_id=1, source_target_pairs={{0,8},{8,16},{16,24},{24,0},{1,9},{9,17},{17,25},{25,1},{2,10},{10... | collective-permute-start | bytes 786440 | tf_op jit(solution)/shard_map/ppermute | solution.py:367
  30.2 21.1 %collective-permute-start.1 = (bf16[2,32,2048]{2,1,0:T(8,128)(2,1)S(1)}, bf16[2,32,2048]{2,1,0:T(8,128)(2,1)S(1)}, u32[]{:S(2)}, u32[]{:S(2)}) collective-permute-start(bf16[2,32,2048]{2,1,0:T(8,128)(2,1)S(1)} %get-tuple-element.24), channel_id=1, source_target_pairs={{0,24},{8,0},{16,8},{24,16},{1,25},{9,1},{17,9},{25,17},{2,26},{10... | collective-permute-start | bytes 786440 | tf_op jit(solution)/shard_map/ppermute | solution.py:367
  46.4 6.8 %collective-permute-start.6 = (bf16[2,32,1024]{2,1,0:T(8,128)(2,1)S(1)}, bf16[2,32,1024]{2,1,0:T(8,128)(2,1)S(1)}, u32[]{:S(2)}, u32[]{:S(2)}) collective-permute-start(bf16[2,32,1024]{2,1,0:T(8,128)(2,1)S(1)} %slice.100), channel_id=1, source_target_pairs={{0,64},{64,4},{4,68},{68,0},{1,65},{65,5},{5,69},{69,1},{2,66},{66... | collective-permute-start | bytes 393224 | tf_op jit(solution)/shard_map/ppermute | solution.py:366
  46.5 6.7 %collective-permute-start.7 = (bf16[2,32,1024]{2,1,0:T(8,128)(2,1)S(1)}, bf16[2,32,1024]{2,1,0:T(8,128)(2,1)S(1)}, u32[]{:S(2)}, u32[]{:S(2)}) collective-permute-start(bf16[2,32,1024]{2,1,0:T(8,128)(2,1)S(1)} %slice.101), channel_id=1, source_target_pairs={{0,68},{64,0},{4,64},{68,4},{1,69},{65,1},{5,65},{69,5},{2,70},{66... | collective-permute-start | bytes 393224 | tf_op jit(solution)/shard_map/ppermute | solution.py:366
  49.8 6.2 %collective-permute-start.2 = (bf16[2,32,1024]{2,1,0:T(8,128)(2,1)S(1)}, bf16[2,32,1024]{2,1,0:T(8,128)(2,1)S(1)}, u32[]{:S(2)}, u32[]{:S(2)}) collective-permute-start(bf16[2,32,1024]{2,1,0:T(8,128)(2,1)S(1)} %slice.96), channel_id=1, source_target_pairs={{0,8},{8,16},{16,24},{24,0},{1,9},{9,17},{17,25},{25,1},{2,10},{10... | collective-permute-start | bytes 393224 | tf_op jit(solution)/shard_map/ppermute | solution.py:367
  51.4 5.0 %collective-permute-start.3 = (bf16[2,32,1024]{2,1,0:T(8,128)(2,1)S(1)}, bf16[2,32,1024]{2,1,0:T(8,128)(2,1)S(1)}, u32[]{:S(2)}, u32[]{:S(2)}) collective-permute-start(bf16[2,32,1024]{2,1,0:T(8,128)(2,1)S(1)} %slice.97), channel_id=1, source_target_pairs={{0,24},{8,0},{16,8},{24,16},{1,25},{9,1},{17,9},{25,17},{2,26},{10... | collective-permute-start | bytes 393224 | tf_op jit(solution)/shard_map/ppermute | solution.py:367
  59.6 59.0 %copy-start.13 = (s32[2]{0:T(128)S(1)}, s32[2]{0:T(128)}, u32[]{:S(2)}) copy-start(s32[2]{0:T(128)} %param.17) | copy-start | bytes 28
  59.7 62.2 %copy-start.14 = (s32[1,32]{1,0:T(1,128)S(1)}, s32[1,32]{1,0:T(1,128)}, u32[]{:S(2)}) copy-start(s32[1,32]{1,0:T(1,128)} %param.16) | copy-start | bytes 388
  59.7 63.6 %copy-start.2 = (bf16[1,512,2048]{2,1,0:T(8,128)(2,1)S(1)}, bf16[1,512,2048]{2,1,0:T(8,128)(2,1)}, u32[]{:S(2)}) copy-start(bf16[1,512,2048]{2,1,0:T(8,128)(2,1)} %param.9) | copy-start | bytes 6291460
  59.7 63.6 %copy-start.5 = (f32[2048]{0:T(1024)S(1)}, f32[2048]{0:T(1024)}, u32[]{:S(2)}) copy-start(f32[2048]{0:T(1024)} %param.10) | copy-start | bytes 24580
  59.7 22.8 %collective-permute-start.8 = (bf16[4,2,32,2048]{3,2,1,0:T(8,128)(2,1)S(1)}, bf16[4,2,32,2048]{3,2,1,0:T(8,128)(2,1)S(1)}, u32[]{:S(2)}, u32[]{:S(2)}) collective-permute-start(bf16[4,2,32,2048]{3,2,1,0:T(8,128)(2,1)S(1)} %pad_maximum_fusion.refs_0_), channel_id=1, source_target_pairs={{0,64},{64,4},{4,68},{68,0},{1,65},{65,5},{5,69},{69,1},{2,66},{66... | collective-permute-start | bytes 3145736 | tf_op jit(solution)/shard_map/ppermute | solution.py:366
  59.8 22.8 %collective-permute-start.9 = (bf16[4,2,32,2048]{3,2,1,0:T(8,128)(2,1)S(1)}, bf16[4,2,32,2048]{3,2,1,0:T(8,128)(2,1)S(1)}, u32[]{:S(2)}, u32[]{:S(2)}) collective-permute-start(bf16[4,2,32,2048]{3,2,1,0:T(8,128)(2,1)S(1)} %pad_maximum_fusion.refs_0_), channel_id=1, source_target_pairs={{0,68},{64,0},{4,64},{68,4},{1,69},{65,1},{5,65},{69,5},{2,70},{66... | collective-permute-start | bytes 3145736 | tf_op jit(solution)/shard_map/ppermute | solution.py:366
  63.0 31.5 %collective-permute-start.12 = (bf16[4,2,32,2048]{3,2,1,0:T(8,128)(2,1)}, bf16[4,2,32,2048]{3,2,1,0:T(8,128)(2,1)S(1)}, u32[]{:S(2)}, u32[]{:S(2)}) collective-permute-start(bf16[4,2,32,2048]{3,2,1,0:T(8,128)(2,1)} %pad_maximum_fusion.1.refs_5_), channel_id=1, source_target_pairs={{0,8},{8,16},{16,24},{24,0},{1,9},{9,17},{17,25},{25,1},{2,10},{10... | collective-permute-start | bytes 3145736 | tf_op jit(solution)/shard_map/ppermute | solution.py:367
  64.5 32.3 %collective-permute-start.13 = (bf16[4,2,32,2048]{3,2,1,0:T(8,128)(2,1)}, bf16[4,2,32,2048]{3,2,1,0:T(8,128)(2,1)S(1)}, u32[]{:S(2)}, u32[]{:S(2)}) collective-permute-start(bf16[4,2,32,2048]{3,2,1,0:T(8,128)(2,1)} %pad_maximum_fusion.1.refs_5_), channel_id=1, source_target_pairs={{0,24},{8,0},{16,8},{24,16},{1,25},{9,1},{17,9},{25,17},{2,26},{10... | collective-permute-start | bytes 3145736 | tf_op jit(solution)/shard_map/ppermute | solution.py:367
  66.2 32.6 %collective-permute-start.16 = (bf16[4,2,32,2048]{3,2,1,0:T(8,128)(2,1)S(1)}, bf16[4,2,32,2048]{3,2,1,0:T(8,128)(2,1)S(1)}, u32[]{:S(2)}, u32[]{:S(2)}) collective-permute-start(bf16[4,2,32,2048]{3,2,1,0:T(8,128)(2,1)S(1)} %pad_maximum_fusion.refs_0_), channel_id=1, source_target_pairs={{0,32},{32,0},{1,33},{33,1},{2,34},{34,2},{3,35},{35,3},{4,36},{36... | collective-permute-start | bytes 3145736 | tf_op jit(solution)/shard_map/ppermute | solution.py:383
  82.5 1.0 copy-start.9
  82.5 38.1 %collective-permute-start.21 = (bf16[4,2,32,2048]{3,2,1,0:T(8,128)(2,1)}, bf16[4,2,32,2048]{3,2,1,0:T(8,128)(2,1)}, u32[]{:S(2)}, u32[]{:S(2)}) collective-permute-start(bf16[4,2,32,2048]{3,2,1,0:T(8,128)(2,1)} %pad_maximum_fusion.1.refs_5_), channel_id=1, source_target_pairs={{0,32},{32,0},{1,33},{33,1},{2,34},{34,2},{3,35},{35,3},{4,36},{36... | collective-permute-start | bytes 3145736 | tf_op jit(solution)/shard_map/ppermute | solution.py:383
  83.5 20.3 %copy-start.10 = (bf16[4,2,32,2048]{3,2,1,0:T(8,128)(2,1)}, bf16[4,2,32,2048]{3,2,1,0:T(8,128)(2,1)S(1)}, u32[]{:S(2)}) copy-start(bf16[4,2,32,2048]{3,2,1,0:T(8,128)(2,1)S(1)} %collective-permute-done.9.refs_2_) | copy-start | bytes 3145732
  83.5 17.4 %collective-permute-start.10 = (bf16[4,2,32,1024]{3,2,1,0:T(8,128)(2,1)S(1)}, bf16[4,2,32,1024]{3,2,1,0:T(8,128)(2,1)}, u32[]{:S(2)}, u32[]{:S(2)}) collective-permute-start(bf16[4,2,32,1024]{3,2,1,0:T(8,128)(2,1)S(1)} %slice.102), channel_id=1, source_target_pairs={{0,64},{64,4},{4,68},{68,0},{1,65},{65,5},{5,69},{69,1},{2,66},{66... | collective-permute-start | bytes 1572872 | tf_op jit(solution)/shard_map/ppermute | solution.py:366
  94.5 9.3 %copy-start.11 = (bf16[4,2,32,2048]{3,2,1,0:T(8,128)(2,1)}, bf16[4,2,32,2048]{3,2,1,0:T(8,128)(2,1)S(1)}, u32[]{:S(2)}) copy-start(bf16[4,2,32,2048]{3,2,1,0:T(8,128)(2,1)S(1)} %collective-permute-done.12.refs_6_) | copy-start | bytes 3145732
  94.5 9.3 %collective-permute-start.11 = (bf16[4,2,32,1024]{3,2,1,0:T(8,128)(2,1)S(1)}, bf16[4,2,32,1024]{3,2,1,0:T(8,128)(2,1)}, u32[]{:S(2)}, u32[]{:S(2)}) collective-permute-start(bf16[4,2,32,1024]{3,2,1,0:T(8,128)(2,1)S(1)} %slice.103), channel_id=1, source_target_pairs={{0,68},{64,0},{4,64},{68,4},{1,69},{65,1},{5,65},{69,5},{2,70},{66... | collective-permute-start | bytes 1572872 | tf_op jit(solution)/shard_map/ppermute | solution.py:366
  96.8 7.0 %copy-start.12 = (bf16[4,2,32,2048]{3,2,1,0:T(8,128)(2,1)}, bf16[4,2,32,2048]{3,2,1,0:T(8,128)(2,1)S(1)}, u32[]{:S(2)}) copy-start(bf16[4,2,32,2048]{3,2,1,0:T(8,128)(2,1)S(1)} %collective-permute-done.13.refs_7_) | copy-start | bytes 3145732
  96.8 21.8 %collective-permute-start.14 = (bf16[4,2,32,1024]{3,2,1,0:T(8,128)(2,1)}, bf16[4,2,32,1024]{3,2,1,0:T(8,128)(2,1)}, u32[]{:S(2)}, u32[]{:S(2)}) collective-permute-start(bf16[4,2,32,1024]{3,2,1,0:T(8,128)(2,1)} %slice.104), channel_id=1, source_target_pairs={{0,8},{8,16},{16,24},{24,0},{1,9},{9,17},{17,25},{25,1},{2,10},{10... | collective-permute-start | bytes 1572872 | tf_op jit(solution)/shard_map/ppermute | solution.py:367
  98.8 5.0 %copy-start.15 = (bf16[4,2,32,2048]{3,2,1,0:T(8,128)(2,1)}, bf16[4,2,32,2048]{3,2,1,0:T(8,128)(2,1)S(1)}, u32[]{:S(2)}) copy-start(bf16[4,2,32,2048]{3,2,1,0:T(8,128)(2,1)S(1)} %collective-permute-done.16.refs_10_) | copy-start | bytes 3145732
  98.8 22.4 %collective-permute-start.15 = (bf16[4,2,32,1024]{3,2,1,0:T(8,128)(2,1)}, bf16[4,2,32,1024]{3,2,1,0:T(8,128)(2,1)}, u32[]{:S(2)}, u32[]{:S(2)}) collective-permute-start(bf16[4,2,32,1024]{3,2,1,0:T(8,128)(2,1)} %slice.105), channel_id=1, source_target_pairs={{0,24},{8,0},{16,8},{24,16},{1,25},{9,1},{17,9},{25,17},{2,26},{10... | collective-permute-start | bytes 1572872 | tf_op jit(solution)/shard_map/ppermute | solution.py:367
  100.9 20.4 %collective-permute-start.19 = (bf16[4,2,32,1024]{3,2,1,0:T(8,128)(2,1)}, bf16[4,2,32,1024]{3,2,1,0:T(8,128)(2,1)}, u32[]{:S(2)}, u32[]{:S(2)}) collective-permute-start(bf16[4,2,32,1024]{3,2,1,0:T(8,128)(2,1)} %collective-permute-done.10.refs_3_), channel_id=1, source_target_pairs={{0,32},{32,0},{1,33},{33,1},{2,34},{34,2},{3,35},{35,3},{4,36},{36... | collective-permute-start | bytes 1572872 | tf_op jit(solution)/shard_map/ppermute | solution.py:383
  103.8 18.0 %collective-permute-start.20 = (bf16[4,2,32,1024]{3,2,1,0:T(8,128)(2,1)}, bf16[4,2,32,1024]{3,2,1,0:T(8,128)(2,1)}, u32[]{:S(2)}, u32[]{:S(2)}) collective-permute-start(bf16[4,2,32,1024]{3,2,1,0:T(8,128)(2,1)} %collective-permute-done.11.refs_4_), channel_id=1, source_target_pairs={{0,32},{32,0},{1,33},{33,1},{2,34},{34,2},{3,35},{35,3},{4,36},{36... | collective-permute-start | bytes 1572872 | tf_op jit(solution)/shard_map/ppermute | solution.py:383
  118.6 3.3 %collective-permute-start.24 = (bf16[4,2,32,1024]{3,2,1,0:T(8,128)(2,1)}, bf16[4,2,32,1024]{3,2,1,0:T(8,128)(2,1)}, u32[]{:S(2)}, u32[]{:S(2)}) collective-permute-start(bf16[4,2,32,1024]{3,2,1,0:T(8,128)(2,1)} %collective-permute-done.14.refs_8_), channel_id=1, source_target_pairs={{0,32},{32,0},{1,33},{33,1},{2,34},{34,2},{3,35},{35,3},{4,36},{36... | collective-permute-start | bytes 1572872 | tf_op jit(solution)/shard_map/ppermute | solution.py:383
  120.6 9.7 %collective-permute-start.17 = (bf16[4,2,32,2048]{3,2,1,0:T(8,128)(2,1)}, bf16[4,2,32,2048]{3,2,1,0:T(8,128)(2,1)}, u32[]{:S(2)}, u32[]{:S(2)}) collective-permute-start(bf16[4,2,32,2048]{3,2,1,0:T(8,128)(2,1)} %copy-done.9), channel_id=1, source_target_pairs={{0,32},{32,0},{1,33},{33,1},{2,34},{34,2},{3,35},{35,3},{4,36},{36... | collective-permute-start | bytes 3145736 | tf_op jit(solution)/shard_map/ppermute | solution.py:383
  121.2 9.1 %collective-permute-start.18 = (bf16[4,2,32,2048]{3,2,1,0:T(8,128)(2,1)}, bf16[4,2,32,2048]{3,2,1,0:T(8,128)(2,1)}, u32[]{:S(2)}, u32[]{:S(2)}) collective-permute-start(bf16[4,2,32,2048]{3,2,1,0:T(8,128)(2,1)} %copy-done.10), channel_id=1, source_target_pairs={{0,32},{32,0},{1,33},{33,1},{2,34},{34,2},{3,35},{35,3},{4,36},{36... | collective-permute-start | bytes 3145736 | tf_op jit(solution)/shard_map/ppermute | solution.py:383
  121.3 9.0 %collective-permute-start.22 = (bf16[4,2,32,2048]{3,2,1,0:T(8,128)(2,1)}, bf16[4,2,32,2048]{3,2,1,0:T(8,128)(2,1)}, u32[]{:S(2)}, u32[]{:S(2)}) collective-permute-start(bf16[4,2,32,2048]{3,2,1,0:T(8,128)(2,1)} %copy-done.11), channel_id=1, source_target_pairs={{0,32},{32,0},{1,33},{33,1},{2,34},{34,2},{3,35},{35,3},{4,36},{36... | collective-permute-start | bytes 3145736 | tf_op jit(solution)/shard_map/ppermute | solution.py:383
  121.7 8.6 %collective-permute-start.23 = (bf16[4,2,32,2048]{3,2,1,0:T(8,128)(2,1)}, bf16[4,2,32,2048]{3,2,1,0:T(8,128)(2,1)}, u32[]{:S(2)}, u32[]{:S(2)}) collective-permute-start(bf16[4,2,32,2048]{3,2,1,0:T(8,128)(2,1)} %copy-done.12), channel_id=1, source_target_pairs={{0,32},{32,0},{1,33},{33,1},{2,34},{34,2},{3,35},{35,3},{4,36},{36... | collective-permute-start | bytes 3145736 | tf_op jit(solution)/shard_map/ppermute | solution.py:383
  122.0 8.4 %collective-permute-start.25 = (bf16[4,2,32,1024]{3,2,1,0:T(8,128)(2,1)}, bf16[4,2,32,1024]{3,2,1,0:T(8,128)(2,1)}, u32[]{:S(2)}, u32[]{:S(2)}) collective-permute-start(bf16[4,2,32,1024]{3,2,1,0:T(8,128)(2,1)} %collective-permute-done.15.refs_9_), channel_id=1, source_target_pairs={{0,32},{32,0},{1,33},{33,1},{2,34},{34,2},{3,35},{35,3},{4,36},{36... | collective-permute-start | bytes 1572872 | tf_op jit(solution)/shard_map/ppermute | solution.py:383
  125.4 1.3 copy-start.3
  126.8 3.6 %copy-start.6 = (f32[2048]{0:T(1024)S(1)}, f32[2048]{0:T(1024)}, u32[]{:S(2)}) copy-start(f32[2048]{0:T(1024)} %param.13) | copy-start | bytes 24580
  155.0 36.0 %collective-permute-start.26 = (bf16[4,4,2,2,16,4096]{5,4,3,2,1,0:T(8,128)(2,1)}, bf16[4,4,2,2,16,4096]{5,4,3,2,1,0:T(8,128)(2,1)}, u32[]{:S(2)}, u32[]{:S(2)}) collective-permute-start(bf16[4,4,2,2,16,4096]{5,4,3,2,1,0:T(8,128)(2,1)} %bitcast.64), channel_id=1, source_target_pairs={{0,32},{32,0},{1,33},{33,1},{2,34},{34,2},{3,35},{35,3},{4,36},{36... | collective-permute-start | bytes 25165832 | tf_op jit(solution)/shard_map/ppermute | solution.py:383
  155.2 6.5 %copy-start.7 = (f32[512,64]{1,0:T(8,128)S(1)}, f32[512,64]{1,0:T(8,128)}, u32[]{:S(2)}) copy-start(f32[512,64]{1,0:T(8,128)} %get-tuple-element.32) | copy-start | bytes 393220
  155.2 6.6 %copy-start.8 = (f32[512,64]{1,0:T(8,128)S(1)}, f32[512,64]{1,0:T(8,128)}, u32[]{:S(2)}) copy-start(f32[512,64]{1,0:T(8,128)} %get-tuple-element.33) | copy-start | bytes 393220
  155.2 35.8 %all-to-all-start = ((bf16[32,16,2048]{2,1,0:T(8,128)(2,1)}), bf16[32,16,2048]{2,1,0:T(8,128)(2,1)S(1)}, u32[]{:S(2)}, u32[]{:S(2)}) async-start(bf16[32,16,2048]{2,1,0:T(8,128)(2,1)} %bitcast.71), calls=%async_computation | async-start | bytes 4194304 | tf_op jit(solution)/shard_map/all_to_all | solution.py:450
  191.1 3.4 %copy-start.4 = (bf16[64,16,4096]{2,1,0:T(8,128)(2,1)S(1)}, bf16[64,16,4096]{2,1,0:T(8,128)(2,1)}, u32[]{:S(2)}) copy-start(bf16[64,16,4096]{2,1,0:T(8,128)(2,1)} %all-gather.8.cloned.1.call-done) | copy-start | bytes 25165828
  214.2 24.7 %all-to-all-start.1 = ((bf16[32,16,1024]{2,1,0:T(8,128)(2,1)}), bf16[32,16,1024]{2,1,0:T(8,128)(2,1)S(1)}, u32[]{:S(2)}, u32[]{:S(2)}) async-start(bf16[32,16,1024]{2,1,0:T(8,128)(2,1)} %bitcast.29), calls=%async_computation.1 | async-start | bytes 2097152 | tf_op jit(solution)/shard_map/all_to_all | solution.py:452
  238.9 1.6 copy-start
  240.4 1.6 copy-start.1
Sparse Core Ops, SparseCore 0:
  9.3 38.7 all-gather.5
  59.8 80.0 all-gather.7

commit v4 on v3

--- a/solution.py
+++ b/solution.py
@@ -87,6 +87,7 @@
 
 def normed_slots(core, x, gain):
     vmem = pl.BlockSpec(memory_space=pltpu.VMEM)
+    hbm = pl.BlockSpec(memory_space=pltpu.HBM)
     return pl.pallas_call(
         norm_kernel,
         out_shape=jax.ShapeDtypeStruct((C, D), jnp.bfloat16),
@@ -97,10 +98,8 @@
     )(core, x, gain)
 
 
-def row_kernel(place_ref, x_ref, hid_ref, gain_ref, cos_ref, sin_ref, *refs):
-    pieces = refs[: 4 * len(RELATIVE)]
-    mid_ref, next_ref, w_ref, o_ref, att_ref, sems = refs[4 * len(RELATIVE) :]
-    core, my_x, my_y = place_ref[0], place_ref[1], place_ref[2]
+def start_copies(place_ref, pieces, sems, w_ref=None, o_ref=None):
+    my_x, my_y = place_ref[1], place_ref[2]
 
     def block_of(part, stacked, ring):
         x, y = (stacked, ring) if part == 0 else (ring, stacked)
@@ -108,7 +107,7 @@
         y = lax.rem(my_y + y, 4)
         return lax.rem(y, 2) * 8 + x * 2 + y // 2
 
-    def copies(slot, part, outputs):
+    def move(slot, part, outputs):
         first = (slot * 2 + part) * len(RELATIVE)
         for index, (ring, low, high) in enumerate(RELATIVE):
             src = pieces[first + index]
@@ -129,32 +128,54 @@
                 sem = sems.at[4 + slot if outputs else slot * 2 + part]
                 pltpu.make_async_copy(src.at[k, :, :, lanes], dst, sem).start()
 
-    for part in range(2):
-        for slot in range(2):
-            copies(slot, part, False)
-    for part in range(2):
-        for slot in range(2):
-            copies(slot, part, True)
-
-    def arrived(ref, sem):
-        pltpu.make_async_copy(ref, ref, sem).wait()
-
+    for outputs, ref in ((False, w_ref), (True, o_ref)):
+        if ref is not None:
+            for part in range(2):
+                for slot in range(2):
+                    move(slot, part, outputs)
+
+
+def arrived(ref, sem):
+    pltpu.make_async_copy(ref, ref, sem).wait()
+
+
+def step_weights(w_ref, sems, g):
+    part = g // 2
+    for p in range(2):
+
+        @pl.when(g == 2 * p)
+        def _():
+            for slot in range(2):
+                arrived(w_ref.at[slot, p], sems.at[slot * 2 + p])
+
+    base = lax.rem(g, 2) * (3 * PAIR)
+
+    def weight(slot, kind):
+        lanes = pl.ds(pl.multiple_of(base + kind * PAIR, PAIR), PAIR)
+        return w_ref[slot, part, :, :, :, lanes].reshape(D // 2, PAIR)
+
+    return weight
+
+
+def output_sum(core, att_ref, rows, o_ref, h, total):
+    for slot in range(2):
+        for j in range(2):
+            block = (core if slot == 0 else 1 - core) + 2 * j
+            lanes = pl.ds(pl.multiple_of(block * PAIR, PAIR), PAIR)
+            weight = o_ref[slot, j * 8 : (j + 1) * 8, h].reshape(PAIR, D // 2)
+            total = total + dot(att_ref[rows, lanes], weight)
+    return total
+
+
+def row_kernel(place_ref, x_ref, hid_ref, gain_ref, cos_ref, sin_ref, *refs):
+    pieces = refs[: 4 * len(RELATIVE)]
+    mid_ref, next_ref, w_ref, o_ref, att_ref, sems = refs[4 * len(RELATIVE) :]
+    core = place_ref[0]
+    start_copies(place_ref, pieces, sems, w_ref, o_ref)
     half = D // 2
 
     def step(g, _):
-        part = g // 2
-        for p in range(2):
-
-            @pl.when(g == 2 * p)
-            def _():
-                for slot in range(2):
-                    arrived(w_ref.at[slot, p], sems.at[slot * 2 + p])
-
-        base = lax.rem(g, 2) * (3 * PAIR)
-
-        def weight(slot, kind):
-            lanes = pl.ds(pl.multiple_of(base + kind * PAIR, PAIR), PAIR)
-            return w_ref[slot, part, :, :, :, lanes].reshape(half, PAIR)
+        weight = step_weights(w_ref, sems, g)
 
         def projected(kind):
             return dot(hid_ref[:, :half], weight(0, kind)) + dot(hid_ref[:, half:], weight(1, kind))
@@ -173,7 +194,8 @@
                 scores = dot_t(q[b * size : end], k[:end])
                 row = lax.broadcasted_iota(jnp.int32, scores.shape, 0) + b * size
                 keep = lax.broadcasted_iota(jnp.int32, scores.shape, 1) <= row
-                att_ref[g, b * size : end, lanes] = softmax_times(scores, keep, v[:end]).astype(jnp.bfloat16)
+                target = pl.ds(pl.multiple_of(g * PAIR + h * HEAD, HEAD), HEAD)
+                att_ref[b * size : end, target] = softmax_times(scores, keep, v[:end]).astype(jnp.bfloat16)
         return 0
 
     lax.fori_loop(0, STEPS, step, 0)
@@ -186,12 +208,7 @@
         squares = jnp.zeros((128, 1), jnp.float32)
         for h in range(2):
             lanes = slice(h * half, (h + 1) * half)
-            total = x_ref[rows, lanes].astype(jnp.float32)
-            for slot in range(2):
-                for j in range(2):
-                    block = (core if slot == 0 else 1 - core) + 2 * j
-                    weight = o_ref[slot, j * 8 : (j + 1) * 8, h].reshape(PAIR, half)
-                    total = total + dot(att_ref[block, rows, :], weight)
+            total = output_sum(core, att_ref, rows, o_ref, h, x_ref[rows, lanes].astype(jnp.float32))
             middle = total.astype(jnp.bfloat16)
             mid_ref[rows, lanes] = middle
             middle = middle.astype(jnp.float32)
@@ -208,18 +225,19 @@
 
 def row_layer(place, x, hidden, gain, tables, pieces):
     vmem = pl.BlockSpec(memory_space=pltpu.VMEM)
+    hbm = pl.BlockSpec(memory_space=pltpu.HBM)
     shape = jax.ShapeDtypeStruct((C, D), jnp.bfloat16)
     return pl.pallas_call(
         row_kernel,
         out_shape=[shape, shape],
         in_specs=[pl.BlockSpec(memory_space=pltpu.SMEM)]
         + [vmem] * 5
-        + [pl.BlockSpec(memory_space=pl.ANY)] * len(pieces),
+        + [hbm] * len(pieces),
         out_specs=[vmem, vmem],
         scratch_shapes=[
             pltpu.VMEM((2, 2, 16, 2, 32, QKV_PART), jnp.bfloat16),
             pltpu.VMEM((2, 16, 2, 32, D // 2), jnp.bfloat16),
-            pltpu.VMEM((STEPS, C, PAIR), jnp.bfloat16),
+            pltpu.VMEM((C, WIDTH), jnp.bfloat16),
             pltpu.SemaphoreType.DMA((6,)),
         ],
         compiler_params=pltpu.CompilerParams(vmem_limit_bytes=48 * MIB),
@@ -231,19 +249,12 @@
     )(place, x, hidden, gain, *tables, *pieces)
 
 
-def column_kernel(core_ref, x_ref, cos_ref, sin_ref, own_plane, other_plane, out_ref, w_ref, hid_ref, sems):
-    core = core_ref[0]
+def column_kernel(place_ref, x_ref, cos_ref, sin_ref, *refs):
+    pieces = refs[: 4 * len(RELATIVE)]
+    out_ref, w_ref, hid_ref, sems = refs[4 * len(RELATIVE) :]
+    core = place_ref[0]
     half = D // 2
-    triple = 3 * PAIR
-
-    for g in range(STEPS):
-        lanes = pl.ds(g * triple, triple)
-        for slot, plane in enumerate((own_plane, other_plane)):
-            for ylo in range(2):
-                for yhi in range(2):
-                    src = plane.at[:, :, ylo, yhi, :, lanes]
-                    dst = w_ref.at[g, slot, ylo, :, yhi]
-                    pltpu.make_async_copy(src, dst, sems.at[g]).start()
+    start_copies(place_ref, pieces, sems, w_ref)
 
     def selection(transposed):
         a = lax.broadcasted_iota(jnp.int32, (C, C), 1 if transposed else 0)
@@ -265,11 +276,7 @@
     keep = (row // N_SEQ == col // N_SEQ) & (col <= row)
 
     def step(g, _):
-        pltpu.make_async_copy(w_ref.at[g], w_ref.at[g], sems.at[g]).wait()
-
-        def weight(slot, kind):
-            lanes = slice(kind * PAIR, (kind + 1) * PAIR)
-            return w_ref[g, slot, :, :, :, :, :, lanes].reshape(half, PAIR)
+        weight = step_weights(w_ref, sems, g)
 
         def projected(kind):
             return dot(hid_ref[:, :half], weight(0, kind)) + dot(hid_ref[:, half:], weight(1, kind))
@@ -296,17 +303,18 @@
     lax.fori_loop(0, STEPS, step, 0)
 
 
-def column_layer(core, x, tables, planes):
+def column_layer(place, x, tables, pieces):
     vmem = pl.BlockSpec(memory_space=pltpu.VMEM)
+    hbm = pl.BlockSpec(memory_space=pltpu.HBM)
     return pl.pallas_call(
         column_kernel,
         out_shape=jax.ShapeDtypeStruct((C, WIDTH), jnp.bfloat16),
-        in_specs=[pl.BlockSpec(memory_space=pltpu.SMEM)] + [vmem] * 3 + [pl.BlockSpec(memory_space=pl.ANY)] * 2,
+        in_specs=[pl.BlockSpec(memory_space=pltpu.SMEM)] + [vmem] * 3 + [hbm] * len(pieces),
         out_specs=vmem,
         scratch_shapes=[
-            pltpu.VMEM((STEPS, 2, 2, 4, 2, 4, 16, 3 * PAIR), jnp.bfloat16),
+            pltpu.VMEM((2, 2, 16, 2, 32, QKV_PART), jnp.bfloat16),
             pltpu.VMEM((C, D), jnp.bfloat16),
-            pltpu.SemaphoreType.DMA((STEPS,)),
+            pltpu.SemaphoreType.DMA((4,)),
         ],
         compiler_params=pltpu.CompilerParams(vmem_limit_bytes=40 * MIB),
         cost_estimate=pl.CostEstimate(
@@ -314,50 +322,50 @@
             bytes_accessed=2 * (C * D + 3 * D * WIDTH + C * WIDTH),
             transcendentals=C * C * HEADS,
         ),
-    )(core, x, *tables, *planes)
-
-
-def branch_sum(core, att_ref, own_ref, other_ref, resid_ref):
-    width = WIDTH // 4
-    total = resid_ref[...].astype(jnp.float32)
-    for slot in range(4):
-        block = jnp.where(slot < 2, core, 1 - core) + 2 * (slot % 2)
-        lanes = pl.ds(pl.multiple_of(block * width, width), width)
-        ref = own_ref if slot < 2 else other_ref
-        rows = slice((slot % 2) * width, (slot % 2 + 1) * width)
-        total = total + dot(att_ref[:, lanes], ref[rows, :])
-    return total
-
-
-def final_kernel(core_ref, att_ref, own_ref, other_ref, resid_ref, out_ref):
-    out_ref[...] = branch_sum(core_ref[0], att_ref, own_ref, other_ref, resid_ref).astype(jnp.bfloat16)
-
-
-def output_layer(core, attended, own, other, resid):
+    )(place, x, *tables, *pieces)
+
+
+def final_kernel(place_ref, att_ref, x_ref, *refs):
+    pieces = refs[: 4 * len(RELATIVE)]
+    out_ref, o_ref, sems = refs[4 * len(RELATIVE) :]
+    core = place_ref[0]
+    half = D // 2
+
+    @pl.when(pl.program_id(0) == 0)
+    def _():
+        start_copies(place_ref, pieces, sems, o_ref=o_ref)
+        for slot in range(2):
+            arrived(o_ref.at[slot], sems.at[4 + slot])
+
+    for h in range(2):
+        lanes = slice(h * half, (h + 1) * half)
+        total = x_ref[:, lanes].astype(jnp.float32)
+        out_ref[:, lanes] = output_sum(core, att_ref, slice(None), o_ref, h, total).astype(jnp.bfloat16)
+
+
+def final_layer(place, attended, x, pieces):
     size = 128
     block = lambda width: pl.BlockSpec((size, width), lambda i: (i, 0))
-    whole = lambda shape: pl.BlockSpec(shape, lambda i: (0, 0), pipeline_mode=pl.Buffered(1))
+    hbm = pl.BlockSpec(memory_space=pltpu.HBM)
     return pl.pallas_call(
         final_kernel,
         grid=(C // size,),
         out_shape=jax.ShapeDtypeStruct((C, D), jnp.bfloat16),
-        in_specs=[
-            pl.BlockSpec(memory_space=pltpu.SMEM),
-            block(WIDTH),
-            whole(own.shape),
-            whole(other.shape),
-            block(D),
+        in_specs=[pl.BlockSpec(memory_space=pltpu.SMEM), block(WIDTH), block(D)] + [hbm] * len(pieces),
+        out_specs=block(D),
+        scratch_shapes=[
+            pltpu.VMEM((2, 16, 2, 32, D // 2), jnp.bfloat16),
+            pltpu.SemaphoreType.DMA((6,)),
         ],
-        out_specs=block(D),
         compiler_params=pltpu.CompilerParams(
-            dimension_semantics=("arbitrary",), vmem_limit_bytes=40 * MIB
+            dimension_semantics=("arbitrary",), vmem_limit_bytes=24 * MIB
         ),
         cost_estimate=pl.CostEstimate(
             flops=2 * C * D * WIDTH,
             bytes_accessed=2 * (2 * C * D + D * WIDTH + C * WIDTH),
             transcendentals=0,
         ),
-    )(core, attended, own, other, resid)
+    )(place, attended, x, *pieces)
 
 
 def shift(value, axis, by):
@@ -367,11 +375,14 @@
     return lax.ppermute(value, axis, [(i, (i + by) % 4) for i in range(4)])
 
 
-def ring(value, axis):
-    half = value.shape[-1] // 2
-    left = shift(value, axis, 1)
-    right = shift(value, axis, -1)
-    return [value, left, right, shift(left[..., :half], axis, 1), shift(right[..., half:], axis, -1)]
+def first_hops(value, axis):
+    return [value, shift(value, axis, 1), shift(value, axis, -1)]
+
+
+def forwards(hops, axis):
+    own, left, right = hops
+    half = own.shape[-1] // 2
+    return hops + [shift(left[..., :half], axis, 1), shift(right[..., half:], axis, -1)]
 
 
 def stack(pieces):
@@ -391,7 +402,7 @@
     return inputs.reshape(-1, 3, STEPS, PAIR).transpose(0, 2, 1, 3).reshape(-1, 3 * WIDTH)
 
 
-def row_weights(inputs, output, line):
+def lines(inputs, output):
     shard = jnp.concatenate([by_step(inputs), fold_output(output)], 1)
     rows = lax.all_gather(shard, "z", axis=0)
     qkv = rows[:, :, : 3 * WIDTH].reshape(2, 32, 3 * WIDTH)
@@ -401,24 +412,26 @@
         lanes = slice(p * QKV_PART, (p + 1) * QKV_PART)
         rest = slice(p * WIDTH // 2, (p + 1) * WIDTH // 2)
         parts.append(jnp.concatenate([qkv[:, :, lanes], out[:, :, rest]], -1))
-    stacks = [stack(ring(parts[0], "x")), stack(ring(parts[1], "y"))]
-    stacks, line = lax.optimization_barrier((stacks, line))
-    own = [ring(stacks[0], "y"), ring(stacks[1], "x")]
-    return own, line
-
-
-def column_line(inputs, output):
-    shard = jnp.concatenate([by_step(inputs), fold_output(output)], 1)
-    return lax.all_gather(jnp.concatenate([shard, shard], 1), ("ylo", "yhi"), axis=0)
-
-
-def column_plane(line):
-    return lax.all_gather(line[:, :, : 4 * WIDTH], ("x", "z"), axis=0).reshape(4, 4, 2, 2, 16, 4 * WIDTH)
-
-
-def column_output(plane):
-    out = plane[..., 3 * WIDTH :].transpose(2, 0, 3, 1, 4, 5)
-    return out.reshape(64, 2, 8, WIDTH).transpose(0, 2, 1, 3).reshape(WIDTH // 2, D)
+    return parts
+
+
+def inner_rings(parts):
+    hops = [first_hops(part, axis) for part, axis in zip(parts, "xy")]
+    return [stack(forwards(hop, axis)) for hop, axis in zip(hops, "xy")]
+
+
+def outer_hops(stacks):
+    return [first_hops(part, axis) for part, axis in zip(stacks, "yx")]
+
+
+def outer_forwards(hops):
+    return [forwards(hop, axis) for hop, axis in zip(hops, "yx")]
+
+
+def both_cores(parts, swapped):
+    own = [piece for part in parts for piece in part]
+    other = [swapped[index] if index in swapped else swap(piece) for index, piece in enumerate(own)]
+    return own + other
 
 
 def shards(tokens, gain_first, inputs_first, output_first, gain_second, inputs_second, output_second, starts, band_edges):
@@ -429,12 +442,6 @@
     my_y = lax.axis_index("yhi") * 2 + lax.axis_index("ylo")
     place = jnp.stack([core, lax.axis_index("x").astype(jnp.int32), my_y.astype(jnp.int32)])
 
-    line = column_line(inputs_second, output_second)
-    own, line = row_weights(inputs_first, output_first, line)
-    plane = column_plane(line)
-    pieces = [piece for part in own for piece in part]
-    pieces = pieces + [swap(piece) for piece in pieces]
-
     frequency = frequencies(band_edges, HEAD // 2)
     block_starts = starts[0]
     own_start = lax.dynamic_index_in_dim(block_starts, seq, 0, keepdims=False)
@@ -444,13 +451,25 @@
     column_tables = rotary_tables(column_positions, frequency)
 
     hidden = normed_slots(core_scalar, residual, gain_first.reshape(1, D))
+
+    first = inner_rings(lines(inputs_first, output_first))
+    first, hidden, row_tables, column_tables = lax.optimization_barrier((first, hidden, row_tables, column_tables))
+    first_hop = outer_hops(first)
+    swapped = {0: swap(first[0]), 5: swap(first[1])}
+    inputs_second, output_second, swapped = lax.optimization_barrier((inputs_second, output_second, swapped))
+    second = lines(inputs_second, output_second)
+    pieces = both_cores(outer_forwards(first_hop), swapped)
+    second = inner_rings(second)
+    second, place = lax.optimization_barrier((second, place))
+    second_hop = outer_hops(second)
+
     middle, hidden = row_layer(place, residual, hidden, gain_second.reshape(1, D), row_tables, pieces)
-    plane, hidden = lax.optimization_barrier((plane, hidden))
-    planes = (plane, swap(plane))
+    second_hop, hidden = lax.optimization_barrier((second_hop, hidden))
+    pieces = both_cores(outer_forwards(second_hop), {})
     hidden = lax.all_to_all(hidden, SEQ, split_axis=0, concat_axis=0, tiled=True)
-    attended = column_layer(core_scalar, hidden, column_tables, planes)
+    attended = column_layer(place, hidden, column_tables, pieces)
     attended = lax.all_to_all(attended, SEQ, split_axis=0, concat_axis=0, tiled=True)
-    return output_layer(core_scalar, attended, *[column_output(p) for p in planes], middle)[None]
+    return final_layer(place, attended, middle, pieces)[None]
 
 
 def solution(mesh):

time: 253 us -> 274 us (1.083)
  waiting for transfers between devices: 104 us -> 51.6 us
  blocking collectives: 14.1 us -> 60.7 us
  starting transfers between devices: 40.1 us -> 56.1 us
  local copies, waits for them, and re-layouts: 22.9 us -> 35.9 us
  between operations: 15.2 us -> 2.29 us
  other arithmetic: 6.02 us -> 12 us
  Pallas kernels: 50.2 us -> 54.2 us
    all_to_all x0 -> x1, blocking collectives: none -> 33.4 us  [shards(): lax.all_to_all(attended, SEQ, split_axis=0, concat_axis=0, tiled=True)]
    ppermute x8 -> x16, waiting for transfers between devices: 29 us -> 12 us  [shift(): return lax.ppermute(value, axis, [(i, (i + by) % 4) for i in range(4)])]
    all_to_all x1, waiting for transfers between devices: 29.1 us -> 14.5 us  [shards(): lax.all_to_all(hidden, SEQ, split_axis=0, concat_axis=0, tiled=True)]
    all_gather x1 -> x2, blocking collectives: 14.1 us -> 27.3 us  [lines(): rows = lax.all_gather(shard, 'z', axis=0)]
    all_to_all x1 -> x0, waiting for transfers between devices: 12.5 us -> none  [shards(): lax.all_to_all(attended, SEQ, split_axis=0, concat_axis=0, tiled=True)]
    ppermute x8 -> x16, waiting for transfers between devices: 33.6 us -> 21.7 us  [shift(): lax.ppermute(value, ('ylo', 'yhi'), [(where(y), where((y + by) % 4)) for...]
    slice x12 -> x22, local copies, waits for them, and re-layouts: 3.81 us -> 14.1 us  [the longest x8 7.36 us: forwards(): right[..., half:]]
    unnamed x32 -> x114, local copies, waits for them, and re-layouts: 8.84 us -> 18.3 us
  transfers between devices with their start and end apart: 31 -> 53, of which waited for: 9 -> 12; matrix products, arithmetic and copies ran while one was open for 6% -> 9% of each run, Pallas kernels for 11% -> 10%
where the time goes in v4:
time: 274 us; the launch traced here: 273 us
  blocking collectives  60.7 us (22%)
  starting transfers between devices  56.1 us (20%)
  Pallas kernels  54.2 us (20%)
  waiting for transfers between devices  51.6 us (19%)
  local copies, waits for them, and re-layouts  35.9 us (13%)
  other arithmetic  12 us (4%)
    all_to_all x1, blocking collectives, shards(): lax.all_to_all(attended, SEQ, split_axis=0, concat_axis=0, tiled=True)  33.4 us
    all_gather x2, blocking collectives, lines(): rows = lax.all_gather(shard, 'z', axis=0)  27.3 us
    pallas_call x1, Pallas kernels, row_layer(): pl.pallas_call(row_kernel, out_shape=[shape, shape], in_specs=[pl.BlockSp...  24.3 us
    ppermute x16, waiting for transfers between devices, shift(): lax.ppermute(value, ('ylo', 'yhi'), [(where(y), where((y + by) % 4)) for...  21.7 us
    pallas_call x1, Pallas kernels, column_layer(): pl.pallas_call(column_kernel, out_shape=jax.ShapeDtypeStruct((C, WIDTH),...  21.5 us
    ppermute x16, starting transfers between devices, shift(): lax.ppermute(value, ('ylo', 'yhi'), [(where(y), where((y + by) % 4)) for...  20.6 us
    ppermute x16, starting transfers between devices, shift(): return lax.ppermute(value, axis, [(i, (i + by) % 4) for i in range(4)])  20.4 us
    unnamed x114, local copies, waits for them, and re-layouts  18.3 us
  transfers between devices with their start and end apart: 53, of which 12 were waited for; matrix products, arithmetic and copies ran while one was open for 9% of the time, Pallas kernels for 10%

profile of v4, /device:TPU:0, one launch (start us, length us, event | category | flops | bytes accessed | tf_op | source)
XLA Modules:
  0.0 272.8 jit_solution(13278066391538148733)
XLA Ops:
  0.7 0.9 reshape.86
  1.9 14.1 %all-gather = bf16[64,4096]{1,0:T(8,128)(2,1)S(1)} all-gather(bf16[16,4096]{1,0:T(8,128)(2,1)S(1)} %maximum_maximum_fusion), channel_id=2, replica_groups=mesh['ylo'=2,'core'=2,'x'=4,'yhi'=2,'z'=4] {'z'}, dimensions={0}, use_global_device_ids=true | all-gather | bytes 655360 | tf_op jit(solution)/shard_map/all_gather | solution.py:407
  16.9 1.6 collective-permute-start.4
  18.5 1.7 collective-permute-start.5
  20.9 1.5 collective-permute-start
  22.4 1.7 collective-permute-start.1
  27.5 1.9 fusion.4
  29.5 0.9 slice.144
  30.9 1.6 slice.145
  32.4 2.9 %collective-permute-start.7 = (bf16[2,32,1024]{2,1,0:T(8,128)(2,1)}, bf16[2,32,1024]{2,1,0:T(8,128)(2,1)}, u32[]{:S(2)}, u32[]{:S(2)}) collective-permute-start(bf16[2,32,1024]{2,1,0:T(8,128)(2,1)} %slice.145), channel_id=1, source_target_pairs={{0,68},{64,0},{4,64},{68,4},{1,69},{65,1},{5,65},{69,5},{2,70},{66... | collective-permute-start | bytes 393224 | tf_op jit(solution)/shard_map/ppermute | solution.py:374
  36.2 2.1 shard_map.91.hid_ref
  38.3 1.0 pad_maximum_fusion.6
  39.3 0.9 slice.140
  41.5 3.0 %collective-permute-start.3 = (bf16[2,32,1024]{2,1,0:T(8,128)(2,1)S(1)}, bf16[2,32,1024]{2,1,0:T(8,128)(2,1)S(1)}, u32[]{:S(2)}, u32[]{:S(2)}) collective-permute-start(bf16[2,32,1024]{2,1,0:T(8,128)(2,1)S(1)} %slice.141), channel_id=1, source_target_pairs={{0,24},{8,0},{16,8},{24,16},{1,25},{9,1},{17,9},{25,17},{2,26},{10... | collective-permute-start | bytes 393224 | tf_op jit(solution)/shard_map/ppermute | solution.py:375
  44.5 1.0 maximum_bitcast_fusion.1
  45.5 1.2 pad_maximum_fusion.1.refs_5_
  47.1 1.2 pad_maximum_fusion.refs_0_
  49.5 1.4 collective-permute-start.22
  50.9 3.6 %collective-permute-start.27 = (bf16[4,2,32,2048]{3,2,1,0:T(8,128)(2,1)S(1)}, bf16[4,2,32,2048]{3,2,1,0:T(8,128)(2,1)}, u32[]{:S(2)}, u32[]{:S(2)}) collective-permute-start(bf16[4,2,32,2048]{3,2,1,0:T(8,128)(2,1)S(1)} %pad_maximum_fusion.1.refs_5_), channel_id=1, source_target_pairs={{0,24},{8,0},{16,8},{24,16},{1,25},{9,1},{17,9},{25,17},{2,26},{10... | collective-permute-start | bytes 3145736 | tf_op jit(solution)/shard_map/ppermute | solution.py:375
  54.5 1.0 copy-done.53
  55.8 13.2 %all-gather.1 = bf16[64,4096]{1,0:T(8,128)(2,1)S(1)} all-gather(bf16[16,4096]{1,0:T(8,128)(2,1)S(1)} %maximum_maximum_fusion.1), channel_id=3, replica_groups=mesh['ylo'=2,'core'=2,'x'=4,'yhi'=2,'z'=4] {'z'}, dimensions={0}, use_global_device_ids=true | all-gather | bytes 655360 | tf_op jit(solution)/shard_map/all_gather | solution.py:407
  69.3 4.9 %collective-permute-done.23.refs_2_ = bf16[4,2,32,2048]{3,2,1,0:T(8,128)(2,1)} collective-permute-done((bf16[4,2,32,2048]{3,2,1,0:T(8,128)(2,1)S(1)}, bf16[4,2,32,2048]{3,2,1,0:T(8,128)(2,1)}, u32[]{:S(2)}, u32[]{:S(2)}) %collective-permute-start.23) | collective-permute-done | bytes 1048608 | tf_op jit(solution)/shard_map/ppermute | solution.py:374
  74.2 1.8 collective-permute-start.15
  76.9 0.9 collective-permute-start.10
  77.8 3.4 %collective-permute-done.14 = bf16[2,32,2048]{2,1,0:T(8,128)(2,1)S(1)} collective-permute-done((bf16[2,32,2048]{2,1,0:T(8,128)(2,1)S(1)}, bf16[2,32,2048]{2,1,0:T(8,128)(2,1)S(1)}, u32[]{:S(2)}, u32[]{:S(2)}) %collective-permute-start.14) | collective-permute-done | bytes 262176 | tf_op jit(solution)/shard_map/ppermute | solution.py:374
  81.2 3.6 %collective-permute-start.11 = (bf16[2,32,2048]{2,1,0:T(8,128)(2,1)S(1)}, bf16[2,32,2048]{2,1,0:T(8,128)(2,1)S(1)}, u32[]{:S(2)}, u32[]{:S(2)}) collective-permute-start(bf16[2,32,2048]{2,1,0:T(8,128)(2,1)S(1)} %get-tuple-element.58), channel_id=1, source_target_pairs={{0,24},{8,0},{16,8},{24,16},{1,25},{9,1},{17,9},{25,17},{2,26},{10... | collective-permute-start | bytes 786440 | tf_op jit(solution)/shard_map/ppermute | solution.py:375
  84.8 1.1 slice.157
  86.0 2.1 collective-permute-start.16
  88.1 1.2 collective-permute-start.17
  89.3 1.1 slice.156
  92.3 9.0 %collective-permute-done.17 = bf16[2,32,1024]{2,1,0:T(8,128)(2,1)S(1)} collective-permute-done((bf16[2,32,1024]{2,1,0:T(8,128)(2,1)S(1)}, bf16[2,32,1024]{2,1,0:T(8,128)(2,1)S(1)}, u32[]{:S(2)}, u32[]{:S(2)}) %collective-permute-start.17) | collective-permute-done | bytes 131104 | tf_op jit(solution)/shard_map/ppermute | solution.py:374
  101.5 1.9 slice.159
  103.4 1.9 slice.158
  105.3 1.3 collective-permute-done.13
  108.0 9.5 %collective-permute-done.29.refs_9_ = bf16[4,2,32,1024]{3,2,1,0:T(8,128)(2,1)} collective-permute-done((bf16[4,2,32,1024]{3,2,1,0:T(8,128)(2,1)}, bf16[4,2,32,1024]{3,2,1,0:T(8,128)(2,1)}, u32[]{:S(2)}, u32[]{:S(2)}) %collective-permute-start.29) | collective-permute-done | bytes 524320 | tf_op jit(solution)/shard_map/ppermute | solution.py:375
  119.1 0.9 maximum_bitcast_fusion.3
  120.6 1.0 maximum_bitcast_fusion.2
  122.1 2.4 collective-permute-start.19
  124.4 1.5 collective-permute-start.21
  126.6 1.0 copy-done.56
  127.6 24.3 %shard_map.92 = (bf16[512,2048]{1,0:T(8,128)(2,1)}, bf16[512,2048]{1,0:T(8,128)(2,1)}) custom-call(s32[3]{0:T(128)S(1)} %pad_add_fusion.place_ref, bf16[512,2048]{1,0:T(8,128)(2,1)} %bitcast.64, bf16[512,2048]{1,0:T(8,128)(2,1)} %copy-done.8, f32[1,2048]{1,0:T(1,128)S(1)} %bitcast.68, f32[512,128]{1,0:T(8,128)S(1)} %copy-done.28, f32[512,128]{1,0:T(8,128)S(1)} %copy-done.29, ...), custom_call_target="tpu_custom_call" | custom-call | flops 9663676416 | bytes 25165824 | tf_op jit(solution)/shard_map/pallas_call | solution.py:230
  152.0 0.9 slice.134
  152.9 1.0 slice.135
  154.0 2.6 collective-permute-start.41
  157.4 3.2 %collective-permute-start.39 = (bf16[4,2,32,1024]{3,2,1,0:T(8,128)(2,1)}, bf16[4,2,32,1024]{3,2,1,0:T(8,128)(2,1)}, u32[]{:S(2)}, u32[]{:S(2)}) collective-permute-start(bf16[4,2,32,1024]{3,2,1,0:T(8,128)(2,1)} %slice.133), channel_id=1, source_target_pairs={{0,68},{64,0},{4,64},{68,4},{1,69},{65,1},{5,65},{69,5},{2,70},{66... | collective-permute-start | bytes 1572872 | tf_op jit(solution)/shard_map/ppermute | solution.py:374
  161.9 10.2 %all-to-all-start = ((bf16[32,16,2048]{2,1,0:T(8,128)(2,1)}), bf16[32,16,2048]{2,1,0:T(8,128)(2,1)}, u32[]{:S(2)}, u32[]{:S(2)}) async-start(bf16[32,16,2048]{2,1,0:T(8,128)(2,1)} %bitcast.73), calls=%async_computation | async-start | bytes 4194304 | tf_op jit(solution)/shard_map/all_to_all | solution.py:469
  173.0 2.8 %collective-permute-done.38.refs_3_ = bf16[4,2,32,1024]{3,2,1,0:T(8,128)(2,1)} collective-permute-done((bf16[4,2,32,1024]{3,2,1,0:T(8,128)(2,1)}, bf16[4,2,32,1024]{3,2,1,0:T(8,128)(2,1)}, u32[]{:S(2)}, u32[]{:S(2)}) %collective-permute-start.38) | collective-permute-done | bytes 524320 | tf_op jit(solution)/shard_map/ppermute | solution.py:374
  180.5 3.4 %collective-permute-done.47.refs_15_ = bf16[4,2,32,2048]{3,2,1,0:T(8,128)(2,1)S(1)} collective-permute-done((bf16[4,2,32,2048]{3,2,1,0:T(8,128)(2,1)S(1)}, bf16[4,2,32,2048]{3,2,1,0:T(8,128)(2,1)S(1)}, u32[]{:S(2)}, u32[]{:S(2)}) %collective-permute-start.47) | collective-permute-done | bytes 1048608 | tf_op jit(solution)/shard_map/ppermute | solution.py:394
  183.9 1.0 copy-done.9
  184.9 1.0 copy-done.11
  185.9 1.0 copy-done.15
  186.8 14.5 %all-to-all-done = bf16[32,16,2048]{2,1,0:T(8,128)(2,1)} async-done(((bf16[32,16,2048]{2,1,0:T(8,128)(2,1)}), bf16[32,16,2048]{2,1,0:T(8,128)(2,1)}, u32[]{:S(2)}, u32[]{:S(2)}) %all-to-all-start) | async-done | bytes 2097184 | tf_op jit(solution)/shard_map/all_to_all | solution.py:469
  201.4 1.2 copy-done.1
  202.6 1.2 copy-done.3
  203.8 1.2 copy-done.5
  205.0 1.2 copy-done.10
  206.3 1.0 copy-done.20
  207.3 1.0 copy-done.22
  208.3 1.0 copy-done.24
  209.4 1.0 copy-done.26
  210.4 0.9 copy-done.27
  211.4 21.5 %shard_map.93 = bf16[512,1024]{1,0:T(8,128)(2,1)S(1)} custom-call(s32[3]{0:T(128)S(1)} %pad_add_fusion.place_ref, bf16[512,2048]{1,0:T(8,128)(2,1)} %bitcast.39.x_ref, f32[512,128]{1,0:T(8,128)S(1)} %get-tuple-element.42.cos_ref, f32[512,128]{1,0:T(8,128)S(1)} %copy-done.27, bf16[4,2,32,2048]{3,2,1,0:T(8,128)(2,1)S(1)} %pad_maximum_fusion.2.refs_0_, ...), custom_call_target="tpu_custom_call" | custom-call | flops 7516192768 | bytes 15728640 | tf_op jit(solution)/shard_map/pallas_call | solution.py:309
  232.9 33.4 %all_to_all.22 = bf16[32,16,1024]{2,1,0:T(8,128)(2,1)S(1)} all-to-all(bf16[32,16,1024]{2,1,0:T(8,128)(2,1)S(1)} %bitcast.66), channel_id=1, replica_groups=mesh['ylo'=2,'core'=2,'x'=4,'yhi'=2,'z'=4] {'x','yhi','z'}, dimensions={0} | all-to-all | bytes 2097152 | tf_op jit(solution)/shard_map/all_to_all | solution.py:471
  266.3 6.2 %shard_map.94 = bf16[512,2048]{1,0:T(8,128)(2,1)} custom-call(s32[3]{0:T(128)S(1)} %pad_add_fusion.place_ref, bf16[512,1024]{1,0:T(8,128)(2,1)S(1)} %bitcast.63, bf16[512,2048]{1,0:T(8,128)(2,1)S(1)} %copy-done.6, bf16[4,2,32,2048]{3,2,1,0:T(8,128)(2,1)S(1)} %pad_maximum_fusion.2.refs_0_, bf16[4,2,32,2048]{3,2,1,0:T(8,128)(2,1)S(1)} %copy-done.1, ...), custom_call_target="tpu_custom_call" | custom-call | flops 2147483648 | bytes 9437184 | tf_op jit(solution)/shard_map/pallas_call | solution.py:350
  (220 shorter events, 24.7 us)
Async XLA Ops:
  1.9 22.3 %copy-start.51 = (s32[2]{0:T(128)S(1)}, s32[2]{0:T(128)}, u32[]{:S(2)}) copy-start(s32[2]{0:T(128)} %param.17) | copy-start | bytes 28
  1.9 24.1 %copy-start.52 = (s32[1,32]{1,0:T(1,128)S(1)}, s32[1,32]{1,0:T(1,128)}, u32[]{:S(2)}) copy-start(s32[1,32]{1,0:T(1,128)} %param.16) | copy-start | bytes 388
  16.9 12.6 %collective-permute-start.4 = (bf16[2,32,2048]{2,1,0:T(8,128)(2,1)}, bf16[2,32,2048]{2,1,0:T(8,128)(2,1)}, u32[]{:S(2)}, u32[]{:S(2)}) collective-permute-start(bf16[2,32,2048]{2,1,0:T(8,128)(2,1)} %get-tuple-element.60), channel_id=1, source_target_pairs={{0,64},{64,4},{4,68},{68,0},{1,65},{65,5},{5,69},{69,1},{2,66},{66... | collective-permute-start | bytes 786440 | tf_op jit(solution)/shard_map/ppermute | solution.py:374
  18.5 12.3 %collective-permute-start.5 = (bf16[2,32,2048]{2,1,0:T(8,128)(2,1)}, bf16[2,32,2048]{2,1,0:T(8,128)(2,1)}, u32[]{:S(2)}, u32[]{:S(2)}) collective-permute-start(bf16[2,32,2048]{2,1,0:T(8,128)(2,1)} %get-tuple-element.60), channel_id=1, source_target_pairs={{0,68},{64,0},{4,64},{68,4},{1,69},{65,1},{5,65},{69,5},{2,70},{66... | collective-permute-start | bytes 786440 | tf_op jit(solution)/shard_map/ppermute | solution.py:374
  20.2 16.0 %copy-start.30 = (f32[2048]{0:T(1024)S(1)}, f32[2048]{0:T(1024)}, u32[]{:S(2)}) copy-start(f32[2048]{0:T(1024)} %param.10) | copy-start | bytes 24580
  20.9 18.4 %collective-permute-start = (bf16[2,32,2048]{2,1,0:T(8,128)(2,1)}, bf16[2,32,2048]{2,1,0:T(8,128)(2,1)}, u32[]{:S(2)}, u32[]{:S(2)}) collective-permute-start(bf16[2,32,2048]{2,1,0:T(8,128)(2,1)} %get-tuple-element.62), channel_id=1, source_target_pairs={{0,8},{8,16},{16,24},{24,0},{1,9},{9,17},{17,25},{25,1},{2,10},{10... | collective-permute-start | bytes 786440 | tf_op jit(solution)/shard_map/ppermute | solution.py:375
  22.4 18.2 %collective-permute-start.1 = (bf16[2,32,2048]{2,1,0:T(8,128)(2,1)}, bf16[2,32,2048]{2,1,0:T(8,128)(2,1)}, u32[]{:S(2)}, u32[]{:S(2)}) collective-permute-start(bf16[2,32,2048]{2,1,0:T(8,128)(2,1)} %get-tuple-element.62), channel_id=1, source_target_pairs={{0,24},{8,0},{16,8},{24,16},{1,25},{9,1},{17,9},{25,17},{2,26},{10... | collective-permute-start | bytes 786440 | tf_op jit(solution)/shard_map/ppermute | solution.py:375
  30.4 14.1 %collective-permute-start.6 = (bf16[2,32,1024]{2,1,0:T(8,128)(2,1)S(1)}, bf16[2,32,1024]{2,1,0:T(8,128)(2,1)}, u32[]{:S(2)}, u32[]{:S(2)}) collective-permute-start(bf16[2,32,1024]{2,1,0:T(8,128)(2,1)S(1)} %slice.144), channel_id=1, source_target_pairs={{0,64},{64,4},{4,68},{68,0},{1,65},{65,5},{5,69},{69,1},{2,66},{66... | collective-permute-start | bytes 393224 | tf_op jit(solution)/shard_map/ppermute | solution.py:374
  32.4 12.1 %collective-permute-start.7 = (bf16[2,32,1024]{2,1,0:T(8,128)(2,1)}, bf16[2,32,1024]{2,1,0:T(8,128)(2,1)}, u32[]{:S(2)}, u32[]{:S(2)}) collective-permute-start(bf16[2,32,1024]{2,1,0:T(8,128)(2,1)} %slice.145), channel_id=1, source_target_pairs={{0,68},{64,0},{4,64},{68,4},{1,69},{65,1},{5,65},{69,5},{2,70},{66... | collective-permute-start | bytes 393224 | tf_op jit(solution)/shard_map/ppermute | solution.py:374
  40.2 6.5 %collective-permute-start.2 = (bf16[2,32,1024]{2,1,0:T(8,128)(2,1)S(1)}, bf16[2,32,1024]{2,1,0:T(8,128)(2,1)S(1)}, u32[]{:S(2)}, u32[]{:S(2)}) collective-permute-start(bf16[2,32,1024]{2,1,0:T(8,128)(2,1)S(1)} %slice.140), channel_id=1, source_target_pairs={{0,8},{8,16},{16,24},{24,0},{1,9},{9,17},{17,25},{25,1},{2,10},{10... | collective-permute-start | bytes 393224 | tf_op jit(solution)/shard_map/ppermute | solution.py:375
  41.5 5.5 %collective-permute-start.3 = (bf16[2,32,1024]{2,1,0:T(8,128)(2,1)S(1)}, bf16[2,32,1024]{2,1,0:T(8,128)(2,1)S(1)}, u32[]{:S(2)}, u32[]{:S(2)}) collective-permute-start(bf16[2,32,1024]{2,1,0:T(8,128)(2,1)S(1)} %slice.141), channel_id=1, source_target_pairs={{0,24},{8,0},{16,8},{24,16},{1,25},{9,1},{17,9},{25,17},{2,26},{10... | collective-permute-start | bytes 393224 | tf_op jit(solution)/shard_map/ppermute | solution.py:375
  46.8 22.2 %copy-start.40 = (bf16[4,2,32,2048]{3,2,1,0:T(8,128)(2,1)}, bf16[4,2,32,2048]{3,2,1,0:T(8,128)(2,1)S(1)}, u32[]{:S(2)}) copy-start(bf16[4,2,32,2048]{3,2,1,0:T(8,128)(2,1)S(1)} %pad_maximum_fusion.1.refs_5_) | copy-start | bytes 3145732
  48.3 20.9 %copy-start.17 = (bf16[4,2,32,2048]{3,2,1,0:T(8,128)(2,1)}, bf16[4,2,32,2048]{3,2,1,0:T(8,128)(2,1)S(1)}, u32[]{:S(2)}) copy-start(bf16[4,2,32,2048]{3,2,1,0:T(8,128)(2,1)S(1)} %pad_maximum_fusion.refs_0_) | copy-start | bytes 3145732
  48.3 6.2 %collective-permute-start.8 = (bf16[4,2,32,2048]{3,2,1,0:T(8,128)(2,1)S(1)}, bf16[4,2,32,2048]{3,2,1,0:T(8,128)(2,1)S(1)}, u32[]{:S(2)}, u32[]{:S(2)}) collective-permute-start(bf16[4,2,32,2048]{3,2,1,0:T(8,128)(2,1)S(1)} %pad_maximum_fusion.refs_0_), channel_id=1, source_target_pairs={{0,32},{32,0},{1,33},{33,1},{2,34},{34,2},{3,35},{35,3},{4,36},{36... | collective-permute-start | bytes 3145736 | tf_op jit(solution)/shard_map/ppermute | solution.py:394
  48.4 7.1 %collective-permute-start.9 = (bf16[4,2,32,2048]{3,2,1,0:T(8,128)(2,1)S(1)}, bf16[4,2,32,2048]{3,2,1,0:T(8,128)(2,1)}, u32[]{:S(2)}, u32[]{:S(2)}) collective-permute-start(bf16[4,2,32,2048]{3,2,1,0:T(8,128)(2,1)S(1)} %pad_maximum_fusion.1.refs_5_), channel_id=1, source_target_pairs={{0,32},{32,0},{1,33},{33,1},{2,34},{34,2},{3,35},{35,3},{4,36},{36... | collective-permute-start | bytes 3145736 | tf_op jit(solution)/shard_map/ppermute | solution.py:394
  48.9 25.3 %collective-permute-start.23 = (bf16[4,2,32,2048]{3,2,1,0:T(8,128)(2,1)S(1)}, bf16[4,2,32,2048]{3,2,1,0:T(8,128)(2,1)}, u32[]{:S(2)}, u32[]{:S(2)}) collective-permute-start(bf16[4,2,32,2048]{3,2,1,0:T(8,128)(2,1)S(1)} %pad_maximum_fusion.refs_0_), channel_id=1, source_target_pairs={{0,68},{64,0},{4,64},{68,4},{1,69},{65,1},{5,65},{69,5},{2,70},{66... | collective-permute-start | bytes 3145736 | tf_op jit(solution)/shard_map/ppermute | solution.py:374
  49.5 27.4 %collective-permute-start.22 = (bf16[4,2,32,2048]{3,2,1,0:T(8,128)(2,1)S(1)}, bf16[4,2,32,2048]{3,2,1,0:T(8,128)(2,1)}, u32[]{:S(2)}, u32[]{:S(2)}) collective-permute-start(bf16[4,2,32,2048]{3,2,1,0:T(8,128)(2,1)S(1)} %pad_maximum_fusion.refs_0_), channel_id=1, source_target_pairs={{0,64},{64,4},{4,68},{68,0},{1,65},{65,5},{5,69},{69,1},{2,66},{66... | collective-permute-start | bytes 3145736 | tf_op jit(solution)/shard_map/ppermute | solution.py:374
  50.9 35.1 %collective-permute-start.27 = (bf16[4,2,32,2048]{3,2,1,0:T(8,128)(2,1)S(1)}, bf16[4,2,32,2048]{3,2,1,0:T(8,128)(2,1)}, u32[]{:S(2)}, u32[]{:S(2)}) collective-permute-start(bf16[4,2,32,2048]{3,2,1,0:T(8,128)(2,1)S(1)} %pad_maximum_fusion.1.refs_5_), channel_id=1, source_target_pairs={{0,24},{8,0},{16,8},{24,16},{1,25},{9,1},{17,9},{25,17},{2,26},{10... | collective-permute-start | bytes 3145736 | tf_op jit(solution)/shard_map/ppermute | solution.py:375
  54.5 33.6 %collective-permute-start.26 = (bf16[4,2,32,2048]{3,2,1,0:T(8,128)(2,1)S(1)}, bf16[4,2,32,2048]{3,2,1,0:T(8,128)(2,1)}, u32[]{:S(2)}, u32[]{:S(2)}) collective-permute-start(bf16[4,2,32,2048]{3,2,1,0:T(8,128)(2,1)S(1)} %pad_maximum_fusion.1.refs_5_), channel_id=1, source_target_pairs={{0,8},{8,16},{16,24},{24,0},{1,9},{9,17},{17,25},{25,1},{2,10},{10... | collective-permute-start | bytes 3145736 | tf_op jit(solution)/shard_map/ppermute | solution.py:375
  69.2 12.0 %collective-permute-start.14 = (bf16[2,32,2048]{2,1,0:T(8,128)(2,1)S(1)}, bf16[2,32,2048]{2,1,0:T(8,128)(2,1)S(1)}, u32[]{:S(2)}, u32[]{:S(2)}) collective-permute-start(bf16[2,32,2048]{2,1,0:T(8,128)(2,1)S(1)} %get-tuple-element.56), channel_id=1, source_target_pairs={{0,64},{64,4},{4,68},{68,0},{1,65},{65,5},{5,69},{69,1},{2,66},{66... | collective-permute-start | bytes 786440 | tf_op jit(solution)/shard_map/ppermute | solution.py:374
  74.2 11.7 %collective-permute-start.15 = (bf16[2,32,2048]{2,1,0:T(8,128)(2,1)S(1)}, bf16[2,32,2048]{2,1,0:T(8,128)(2,1)S(1)}, u32[]{:S(2)}, u32[]{:S(2)}) collective-permute-start(bf16[2,32,2048]{2,1,0:T(8,128)(2,1)S(1)} %get-tuple-element.56), channel_id=1, source_target_pairs={{0,68},{64,0},{4,64},{68,4},{1,69},{65,1},{5,65},{69,5},{2,70},{66... | collective-permute-start | bytes 786440 | tf_op jit(solution)/shard_map/ppermute | solution.py:374
  76.9 13.6 %collective-permute-start.10 = (bf16[2,32,2048]{2,1,0:T(8,128)(2,1)S(1)}, bf16[2,32,2048]{2,1,0:T(8,128)(2,1)S(1)}, u32[]{:S(2)}, u32[]{:S(2)}) collective-permute-start(bf16[2,32,2048]{2,1,0:T(8,128)(2,1)S(1)} %get-tuple-element.58), channel_id=1, source_target_pairs={{0,8},{8,16},{16,24},{24,0},{1,9},{9,17},{17,25},{25,1},{2,10},{10... | collective-permute-start | bytes 786440 | tf_op jit(solution)/shard_map/ppermute | solution.py:375
  81.2 9.3 %collective-permute-start.11 = (bf16[2,32,2048]{2,1,0:T(8,128)(2,1)S(1)}, bf16[2,32,2048]{2,1,0:T(8,128)(2,1)S(1)}, u32[]{:S(2)}, u32[]{:S(2)}) collective-permute-start(bf16[2,32,2048]{2,1,0:T(8,128)(2,1)S(1)} %get-tuple-element.58), channel_id=1, source_target_pairs={{0,24},{8,0},{16,8},{24,16},{1,25},{9,1},{17,9},{25,17},{2,26},{10... | collective-permute-start | bytes 786440 | tf_op jit(solution)/shard_map/ppermute | solution.py:375
  85.9 21.4 %collective-permute-start.25 = (bf16[4,2,32,1024]{3,2,1,0:T(8,128)(2,1)S(1)}, bf16[4,2,32,1024]{3,2,1,0:T(8,128)(2,1)S(1)}, u32[]{:S(2)}, u32[]{:S(2)}) collective-permute-start(bf16[4,2,32,1024]{3,2,1,0:T(8,128)(2,1)S(1)} %slice.157), channel_id=1, source_target_pairs={{0,68},{64,0},{4,64},{68,4},{1,69},{65,1},{5,65},{69,5},{2,70},{66... | collective-permute-start | bytes 1572872 | tf_op jit(solution)/shard_map/ppermute | solution.py:374
  86.0 6.2 %collective-permute-start.16 = (bf16[2,32,1024]{2,1,0:T(8,128)(2,1)S(1)}, bf16[2,32,1024]{2,1,0:T(8,128)(2,1)S(1)}, u32[]{:S(2)}, u32[]{:S(2)}) collective-permute-start(bf16[2,32,1024]{2,1,0:T(8,128)(2,1)S(1)} %slice.154), channel_id=1, source_target_pairs={{0,64},{64,4},{4,68},{68,0},{1,65},{65,5},{5,69},{69,1},{2,66},{66... | collective-permute-start | bytes 393224 | tf_op jit(solution)/shard_map/ppermute | solution.py:374
  88.1 13.2 %collective-permute-start.17 = (bf16[2,32,1024]{2,1,0:T(8,128)(2,1)S(1)}, bf16[2,32,1024]{2,1,0:T(8,128)(2,1)S(1)}, u32[]{:S(2)}, u32[]{:S(2)}) collective-permute-start(bf16[2,32,1024]{2,1,0:T(8,128)(2,1)S(1)} %slice.155), channel_id=1, source_target_pairs={{0,68},{64,0},{4,64},{68,4},{1,69},{65,1},{5,65},{69,5},{2,70},{66... | collective-permute-start | bytes 393224 | tf_op jit(solution)/shard_map/ppermute | solution.py:374
  90.4 17.0 %copy-start.42 = (bf16[2,32,2048]{2,1,0:T(8,128)(2,1)}, bf16[2,32,2048]{2,1,0:T(8,128)(2,1)S(1)}, u32[]{:S(2)}) copy-start(bf16[2,32,2048]{2,1,0:T(8,128)(2,1)S(1)} %collective-permute-done.10) | copy-start | bytes 786436
  90.4 29.6 %collective-permute-start.31 = (bf16[4,2,32,2048]{3,2,1,0:T(8,128)(2,1)}, bf16[4,2,32,2048]{3,2,1,0:T(8,128)(2,1)}, u32[]{:S(2)}, u32[]{:S(2)}) collective-permute-start(bf16[4,2,32,2048]{3,2,1,0:T(8,128)(2,1)} %collective-permute-done.23.refs_2_), channel_id=1, source_target_pairs={{0,32},{32,0},{1,33},{33,1},{2,34},{34,2},{3,35},{35,3},{4,36},{36... | collective-permute-start | bytes 3145736 | tf_op jit(solution)/shard_map/ppermute | solution.py:394
  90.5 16.9 %copy-start.44 = (bf16[2,32,2048]{2,1,0:T(8,128)(2,1)}, bf16[2,32,2048]{2,1,0:T(8,128)(2,1)S(1)}, u32[]{:S(2)}) copy-start(bf16[2,32,2048]{2,1,0:T(8,128)(2,1)S(1)} %collective-permute-done.11) | copy-start | bytes 786436
  90.6 16.9 %collective-permute-start.24 = (bf16[4,2,32,1024]{3,2,1,0:T(8,128)(2,1)S(1)}, bf16[4,2,32,1024]{3,2,1,0:T(8,128)(2,1)S(1)}, u32[]{:S(2)}, u32[]{:S(2)}) collective-permute-start(bf16[4,2,32,1024]{3,2,1,0:T(8,128)(2,1)S(1)} %slice.156), channel_id=1, source_target_pairs={{0,64},{64,4},{4,68},{68,0},{1,65},{65,5},{5,69},{69,1},{2,66},{66... | collective-permute-start | bytes 1572872 | tf_op jit(solution)/shard_map/ppermute | solution.py:374
  92.3 13.0 %collective-permute-start.12 = (bf16[2,32,1024]{2,1,0:T(8,128)(2,1)S(1)}, bf16[2,32,1024]{2,1,0:T(8,128)(2,1)S(1)}, u32[]{:S(2)}, u32[]{:S(2)}) collective-permute-start(bf16[2,32,1024]{2,1,0:T(8,128)(2,1)S(1)} %slice.150), channel_id=1, source_target_pairs={{0,8},{8,16},{16,24},{24,0},{1,9},{9,17},{17,25},{25,1},{2,10},{10... | collective-permute-start | bytes 393224 | tf_op jit(solution)/shard_map/ppermute | solution.py:375
  101.2 5.4 %collective-permute-start.13 = (bf16[2,32,1024]{2,1,0:T(8,128)(2,1)S(1)}, bf16[2,32,1024]{2,1,0:T(8,128)(2,1)S(1)}, u32[]{:S(2)}, u32[]{:S(2)}) collective-permute-start(bf16[2,32,1024]{2,1,0:T(8,128)(2,1)S(1)} %slice.151), channel_id=1, source_target_pairs={{0,24},{8,0},{16,8},{24,16},{1,25},{9,1},{17,9},{25,17},{2,26},{10... | collective-permute-start | bytes 393224 | tf_op jit(solution)/shard_map/ppermute | solution.py:375
  105.3 12.3 %collective-permute-start.29 = (bf16[4,2,32,1024]{3,2,1,0:T(8,128)(2,1)}, bf16[4,2,32,1024]{3,2,1,0:T(8,128)(2,1)}, u32[]{:S(2)}, u32[]{:S(2)}) collective-permute-start(bf16[4,2,32,1024]{3,2,1,0:T(8,128)(2,1)} %slice.159), channel_id=1, source_target_pairs={{0,24},{8,0},{16,8},{24,16},{1,25},{9,1},{17,9},{25,17},{2,26},{10... | collective-permute-start | bytes 1572872 | tf_op jit(solution)/shard_map/ppermute | solution.py:375
  106.6 11.9 %collective-permute-start.28 = (bf16[4,2,32,1024]{3,2,1,0:T(8,128)(2,1)}, bf16[4,2,32,1024]{3,2,1,0:T(8,128)(2,1)}, u32[]{:S(2)}, u32[]{:S(2)}) collective-permute-start(bf16[4,2,32,1024]{3,2,1,0:T(8,128)(2,1)} %slice.158), channel_id=1, source_target_pairs={{0,8},{8,16},{16,24},{24,0},{1,9},{9,17},{17,25},{25,1},{2,10},{10... | collective-permute-start | bytes 1572872 | tf_op jit(solution)/shard_map/ppermute | solution.py:375
  107.3 11.2 %collective-permute-start.33 = (bf16[4,2,32,1024]{3,2,1,0:T(8,128)(2,1)S(1)}, bf16[4,2,32,1024]{3,2,1,0:T(8,128)(2,1)S(1)}, u32[]{:S(2)}, u32[]{:S(2)}) collective-permute-start(bf16[4,2,32,1024]{3,2,1,0:T(8,128)(2,1)S(1)} %collective-permute-done.25.refs_4_), channel_id=1, source_target_pairs={{0,32},{32,0},{1,33},{33,1},{2,34},{34,2},{3,35},{35,3},{4,36},{36... | collective-permute-start | bytes 1572872 | tf_op jit(solution)/shard_map/ppermute | solution.py:394
  107.5 12.8 %collective-permute-start.32 = (bf16[4,2,32,1024]{3,2,1,0:T(8,128)(2,1)S(1)}, bf16[4,2,32,1024]{3,2,1,0:T(8,128)(2,1)S(1)}, u32[]{:S(2)}, u32[]{:S(2)}) collective-permute-start(bf16[4,2,32,1024]{3,2,1,0:T(8,128)(2,1)S(1)} %collective-permute-done.24.refs_3_), channel_id=1, source_target_pairs={{0,32},{32,0},{1,33},{33,1},{2,34},{34,2},{3,35},{35,3},{4,36},{36... | collective-permute-start | bytes 1572872 | tf_op jit(solution)/shard_map/ppermute | solution.py:394
  117.6 4.5 %collective-permute-start.30 = (bf16[4,2,32,2048]{3,2,1,0:T(8,128)(2,1)}, bf16[4,2,32,2048]{3,2,1,0:T(8,128)(2,1)S(1)}, u32[]{:S(2)}, u32[]{:S(2)}) collective-permute-start(bf16[4,2,32,2048]{3,2,1,0:T(8,128)(2,1)} %collective-permute-done.22.refs_1_), channel_id=1, source_target_pairs={{0,32},{32,0},{1,33},{33,1},{2,34},{34,2},{3,35},{35,3},{4,36},{36... | collective-permute-start | bytes 3145736 | tf_op jit(solution)/shard_map/ppermute | solution.py:394
  118.5 6.0 %collective-permute-start.35 = (bf16[4,2,32,2048]{3,2,1,0:T(8,128)(2,1)}, bf16[4,2,32,2048]{3,2,1,0:T(8,128)(2,1)S(1)}, u32[]{:S(2)}, u32[]{:S(2)}) collective-permute-start(bf16[4,2,32,2048]{3,2,1,0:T(8,128)(2,1)} %collective-permute-done.27.refs_7_), channel_id=1, source_target_pairs={{0,32},{32,0},{1,33},{33,1},{2,34},{34,2},{3,35},{35,3},{4,36},{36... | collective-permute-start | bytes 3145736 | tf_op jit(solution)/shard_map/ppermute | solution.py:394
  118.6 8.0 %collective-permute-start.34 = (bf16[4,2,32,2048]{3,2,1,0:T(8,128)(2,1)}, bf16[4,2,32,2048]{3,2,1,0:T(8,128)(2,1)S(1)}, u32[]{:S(2)}, u32[]{:S(2)}) collective-permute-start(bf16[4,2,32,2048]{3,2,1,0:T(8,128)(2,1)} %collective-permute-done.26.refs_6_), channel_id=1, source_target_pairs={{0,32},{32,0},{1,33},{33,1},{2,34},{34,2},{3,35},{35,3},{4,36},{36... | collective-permute-start | bytes 3145736 | tf_op jit(solution)/shard_map/ppermute | solution.py:394
  120.0 4.4 %collective-permute-start.37 = (bf16[4,2,32,1024]{3,2,1,0:T(8,128)(2,1)}, bf16[4,2,32,1024]{3,2,1,0:T(8,128)(2,1)S(1)}, u32[]{:S(2)}, u32[]{:S(2)}) collective-permute-start(bf16[4,2,32,1024]{3,2,1,0:T(8,128)(2,1)} %collective-permute-done.29.refs_9_), channel_id=1, source_target_pairs={{0,32},{32,0},{1,33},{33,1},{2,34},{34,2},{3,35},{35,3},{4,36},{36... | collective-permute-start | bytes 1572872 | tf_op jit(solution)/shard_map/ppermute | solution.py:394
  120.3 5.6 %collective-permute-start.36 = (bf16[4,2,32,1024]{3,2,1,0:T(8,128)(2,1)}, bf16[4,2,32,1024]{3,2,1,0:T(8,128)(2,1)S(1)}, u32[]{:S(2)}, u32[]{:S(2)}) collective-permute-start(bf16[4,2,32,1024]{3,2,1,0:T(8,128)(2,1)} %collective-permute-done.28.refs_8_), channel_id=1, source_target_pairs={{0,32},{32,0},{1,33},{33,1},{2,34},{34,2},{3,35},{35,3},{4,36},{36... | collective-permute-start | bytes 1572872 | tf_op jit(solution)/shard_map/ppermute | solution.py:394
  122.1 29.9 %collective-permute-start.19 = (bf16[4,2,32,2048]{3,2,1,0:T(8,128)(2,1)S(1)}, bf16[4,2,32,2048]{3,2,1,0:T(8,128)(2,1)S(1)}, u32[]{:S(2)}, u32[]{:S(2)}) collective-permute-start(bf16[4,2,32,2048]{3,2,1,0:T(8,128)(2,1)S(1)} %pad_maximum_fusion.2.refs_0_), channel_id=1, source_target_pairs={{0,68},{64,0},{4,64},{68,4},{1,69},{65,1},{5,65},{69,5},{2,70},{66... | collective-permute-start | bytes 3145736 | tf_op jit(solution)/shard_map/ppermute | solution.py:374
  124.4 27.5 %collective-permute-start.18 = (bf16[4,2,32,2048]{3,2,1,0:T(8,128)(2,1)S(1)}, bf16[4,2,32,2048]{3,2,1,0:T(8,128)(2,1)S(1)}, u32[]{:S(2)}, u32[]{:S(2)}) collective-permute-start(bf16[4,2,32,2048]{3,2,1,0:T(8,128)(2,1)S(1)} %pad_maximum_fusion.2.refs_0_), channel_id=1, source_target_pairs={{0,64},{64,4},{4,68},{68,0},{1,65},{65,5},{5,69},{69,1},{2,66},{66... | collective-permute-start | bytes 3145736 | tf_op jit(solution)/shard_map/ppermute | solution.py:374
  124.4 27.5 %collective-permute-start.21 = (bf16[4,2,32,2048]{3,2,1,0:T(8,128)(2,1)S(1)}, bf16[4,2,32,2048]{3,2,1,0:T(8,128)(2,1)S(1)}, u32[]{:S(2)}, u32[]{:S(2)}) collective-permute-start(bf16[4,2,32,2048]{3,2,1,0:T(8,128)(2,1)S(1)} %pad_maximum_fusion.3.refs_5_), channel_id=1, source_target_pairs={{0,24},{8,0},{16,8},{24,16},{1,25},{9,1},{17,9},{25,17},{2,26},{10... | collective-permute-start | bytes 3145736 | tf_op jit(solution)/shard_map/ppermute | solution.py:375
  125.9 26.1 %collective-permute-start.20 = (bf16[4,2,32,2048]{3,2,1,0:T(8,128)(2,1)S(1)}, bf16[4,2,32,2048]{3,2,1,0:T(8,128)(2,1)S(1)}, u32[]{:S(2)}, u32[]{:S(2)}) collective-permute-start(bf16[4,2,32,2048]{3,2,1,0:T(8,128)(2,1)S(1)} %pad_maximum_fusion.3.refs_5_), channel_id=1, source_target_pairs={{0,8},{8,16},{16,24},{24,0},{1,9},{9,17},{17,25},{25,1},{2,10},{10... | collective-permute-start | bytes 3145736 | tf_op jit(solution)/shard_map/ppermute | solution.py:375
  154.0 18.1 %collective-permute-start.41 = (bf16[4,2,32,1024]{3,2,1,0:T(8,128)(2,1)}, bf16[4,2,32,1024]{3,2,1,0:T(8,128)(2,1)}, u32[]{:S(2)}, u32[]{:S(2)}) collective-permute-start(bf16[4,2,32,1024]{3,2,1,0:T(8,128)(2,1)} %slice.135), channel_id=1, source_target_pairs={{0,24},{8,0},{16,8},{24,16},{1,25},{9,1},{17,9},{25,17},{2,26},{10... | collective-permute-start | bytes 1572872 | tf_op jit(solution)/shard_map/ppermute | solution.py:375
  156.6 15.9 %collective-permute-start.40 = (bf16[4,2,32,1024]{3,2,1,0:T(8,128)(2,1)}, bf16[4,2,32,1024]{3,2,1,0:T(8,128)(2,1)}, u32[]{:S(2)}, u32[]{:S(2)}) collective-permute-start(bf16[4,2,32,1024]{3,2,1,0:T(8,128)(2,1)} %slice.134), channel_id=1, source_target_pairs={{0,8},{8,16},{16,24},{24,0},{1,9},{9,17},{17,25},{25,1},{2,10},{10... | collective-permute-start | bytes 1572872 | tf_op jit(solution)/shard_map/ppermute | solution.py:375
  157.4 15.3 %collective-permute-start.39 = (bf16[4,2,32,1024]{3,2,1,0:T(8,128)(2,1)}, bf16[4,2,32,1024]{3,2,1,0:T(8,128)(2,1)}, u32[]{:S(2)}, u32[]{:S(2)}) collective-permute-start(bf16[4,2,32,1024]{3,2,1,0:T(8,128)(2,1)} %slice.133), channel_id=1, source_target_pairs={{0,68},{64,0},{4,64},{68,4},{1,69},{65,1},{5,65},{69,5},{2,70},{66... | collective-permute-start | bytes 1572872 | tf_op jit(solution)/shard_map/ppermute | solution.py:374
  161.5 14.2 %collective-permute-start.38 = (bf16[4,2,32,1024]{3,2,1,0:T(8,128)(2,1)}, bf16[4,2,32,1024]{3,2,1,0:T(8,128)(2,1)}, u32[]{:S(2)}, u32[]{:S(2)}) collective-permute-start(bf16[4,2,32,1024]{3,2,1,0:T(8,128)(2,1)} %slice.132), channel_id=1, source_target_pairs={{0,64},{64,4},{4,68},{68,0},{1,65},{65,5},{5,69},{69,1},{2,66},{66... | collective-permute-start | bytes 1572872 | tf_op jit(solution)/shard_map/ppermute | solution.py:374
  161.8 18.2 %collective-permute-start.42 = (bf16[4,2,32,2048]{3,2,1,0:T(8,128)(2,1)S(1)}, bf16[4,2,32,2048]{3,2,1,0:T(8,128)(2,1)}, u32[]{:S(2)}, u32[]{:S(2)}) collective-permute-start(bf16[4,2,32,2048]{3,2,1,0:T(8,128)(2,1)S(1)} %pad_maximum_fusion.2.refs_0_), channel_id=1, source_target_pairs={{0,32},{32,0},{1,33},{33,1},{2,34},{34,2},{3,35},{35,3},{4,36},{36... | collective-permute-start | bytes 3145736 | tf_op jit(solution)/shard_map/ppermute | solution.py:394
  161.9 39.5 %all-to-all-start = ((bf16[32,16,2048]{2,1,0:T(8,128)(2,1)}), bf16[32,16,2048]{2,1,0:T(8,128)(2,1)}, u32[]{:S(2)}, u32[]{:S(2)}) async-start(bf16[32,16,2048]{2,1,0:T(8,128)(2,1)} %bitcast.73), calls=%async_computation | async-start | bytes 4194304 | tf_op jit(solution)/shard_map/all_to_all | solution.py:469
  172.1 3.6 %collective-permute-start.51 = (bf16[4,2,32,1024]{3,2,1,0:T(8,128)(2,1)}, bf16[4,2,32,1024]{3,2,1,0:T(8,128)(2,1)S(1)}, u32[]{:S(2)}, u32[]{:S(2)}) collective-permute-start(bf16[4,2,32,1024]{3,2,1,0:T(8,128)(2,1)} %collective-permute-done.41.refs_9_), channel_id=1, source_target_pairs={{0,32},{32,0},{1,33},{33,1},{2,34},{34,2},{3,35},{35,3},{4,36},{36... | collective-permute-start | bytes 1572872 | tf_op jit(solution)/shard_map/ppermute | solution.py:394
  172.4 4.6 %collective-permute-start.50 = (bf16[4,2,32,1024]{3,2,1,0:T(8,128)(2,1)}, bf16[4,2,32,1024]{3,2,1,0:T(8,128)(2,1)S(1)}, u32[]{:S(2)}, u32[]{:S(2)}) collective-permute-start(bf16[4,2,32,1024]{3,2,1,0:T(8,128)(2,1)} %collective-permute-done.40.refs_8_), channel_id=1, source_target_pairs={{0,32},{32,0},{1,33},{33,1},{2,34},{34,2},{3,35},{35,3},{4,36},{36... | collective-permute-start | bytes 1572872 | tf_op jit(solution)/shard_map/ppermute | solution.py:394
  172.7 5.1 %collective-permute-start.46 = (bf16[4,2,32,1024]{3,2,1,0:T(8,128)(2,1)}, bf16[4,2,32,1024]{3,2,1,0:T(8,128)(2,1)S(1)}, u32[]{:S(2)}, u32[]{:S(2)}) collective-permute-start(bf16[4,2,32,1024]{3,2,1,0:T(8,128)(2,1)} %collective-permute-done.39.refs_4_), channel_id=1, source_target_pairs={{0,32},{32,0},{1,33},{33,1},{2,34},{34,2},{3,35},{35,3},{4,36},{36... | collective-permute-start | bytes 1572872 | tf_op jit(solution)/shard_map/ppermute | solution.py:394
  175.7 3.4 %collective-permute-start.45 = (bf16[4,2,32,1024]{3,2,1,0:T(8,128)(2,1)}, bf16[4,2,32,1024]{3,2,1,0:T(8,128)(2,1)S(1)}, u32[]{:S(2)}, u32[]{:S(2)}) collective-permute-start(bf16[4,2,32,1024]{3,2,1,0:T(8,128)(2,1)} %collective-permute-done.38.refs_3_), channel_id=1, source_target_pairs={{0,32},{32,0},{1,33},{33,1},{2,34},{34,2},{3,35},{35,3},{4,36},{36... | collective-permute-start | bytes 1572872 | tf_op jit(solution)/shard_map/ppermute | solution.py:394
  176.6 7.3 %collective-permute-start.43 = (bf16[4,2,32,2048]{3,2,1,0:T(8,128)(2,1)}, bf16[4,2,32,2048]{3,2,1,0:T(8,128)(2,1)S(1)}, u32[]{:S(2)}, u32[]{:S(2)}) collective-permute-start(bf16[4,2,32,2048]{3,2,1,0:T(8,128)(2,1)} %copy-done), channel_id=1, source_target_pairs={{0,32},{32,0},{1,33},{33,1},{2,34},{34,2},{3,35},{35,3},{4,36},{36... | collective-permute-start | bytes 3145736 | tf_op jit(solution)/shard_map/ppermute | solution.py:394
  177.9 7.0 %collective-permute-start.44 = (bf16[4,2,32,2048]{3,2,1,0:T(8,128)(2,1)S(1)}, bf16[4,2,32,2048]{3,2,1,0:T(8,128)(2,1)S(1)}, u32[]{:S(2)}, u32[]{:S(2)}) collective-permute-start(bf16[4,2,32,2048]{3,2,1,0:T(8,128)(2,1)S(1)} %collective-permute-done.19.refs_2_), channel_id=1, source_target_pairs={{0,32},{32,0},{1,33},{33,1},{2,34},{34,2},{3,35},{35,3},{4,36},{36... | collective-permute-start | bytes 3145736 | tf_op jit(solution)/shard_map/ppermute | solution.py:394
  178.7 5.2 %collective-permute-start.47 = (bf16[4,2,32,2048]{3,2,1,0:T(8,128)(2,1)S(1)}, bf16[4,2,32,2048]{3,2,1,0:T(8,128)(2,1)S(1)}, u32[]{:S(2)}, u32[]{:S(2)}) collective-permute-start(bf16[4,2,32,2048]{3,2,1,0:T(8,128)(2,1)S(1)} %pad_maximum_fusion.3.refs_5_), channel_id=1, source_target_pairs={{0,32},{32,0},{1,33},{33,1},{2,34},{34,2},{3,35},{35,3},{4,36},{36... | collective-permute-start | bytes 3145736 | tf_op jit(solution)/shard_map/ppermute | solution.py:394
  180.0 5.9 %collective-permute-start.48 = (bf16[4,2,32,2048]{3,2,1,0:T(8,128)(2,1)}, bf16[4,2,32,2048]{3,2,1,0:T(8,128)(2,1)S(1)}, u32[]{:S(2)}, u32[]{:S(2)}) collective-permute-start(bf16[4,2,32,2048]{3,2,1,0:T(8,128)(2,1)} %copy-done.4), channel_id=1, source_target_pairs={{0,32},{32,0},{1,33},{33,1},{2,34},{34,2},{3,35},{35,3},{4,36},{36... | collective-permute-start | bytes 3145736 | tf_op jit(solution)/shard_map/ppermute | solution.py:394
  180.0 6.9 %collective-permute-start.49 = (bf16[4,2,32,2048]{3,2,1,0:T(8,128)(2,1)}, bf16[4,2,32,2048]{3,2,1,0:T(8,128)(2,1)}, u32[]{:S(2)}, u32[]{:S(2)}) collective-permute-start(bf16[4,2,32,2048]{3,2,1,0:T(8,128)(2,1)} %copy-done.2), channel_id=1, source_target_pairs={{0,32},{32,0},{1,33},{33,1},{2,34},{34,2},{3,35},{35,3},{4,36},{36... | collective-permute-start | bytes 3145736 | tf_op jit(solution)/shard_map/ppermute | solution.py:394
  211.4 55.0 %copy-start.12 = (bf16[4,2,32,2048]{3,2,1,0:T(8,128)(2,1)S(1)}, bf16[4,2,32,2048]{3,2,1,0:T(8,128)(2,1)}, u32[]{:S(2)}) copy-start(bf16[4,2,32,2048]{3,2,1,0:T(8,128)(2,1)} %copy-done.11) | copy-start | bytes 3145732
  211.4 55.0 %copy-start.14 = (bf16[4,2,32,2048]{3,2,1,0:T(8,128)(2,1)S(1)}, bf16[4,2,32,2048]{3,2,1,0:T(8,128)(2,1)}, u32[]{:S(2)}) copy-start(bf16[4,2,32,2048]{3,2,1,0:T(8,128)(2,1)} %copy-done.13) | copy-start | bytes 3145732
  211.4 55.0 %copy-start.16 = (bf16[4,2,32,2048]{3,2,1,0:T(8,128)(2,1)S(1)}, bf16[4,2,32,2048]{3,2,1,0:T(8,128)(2,1)}, u32[]{:S(2)}) copy-start(bf16[4,2,32,2048]{3,2,1,0:T(8,128)(2,1)} %copy-done.15) | copy-start | bytes 3145732
  232.9 33.4 %copy-start.6 = (bf16[512,2048]{1,0:T(8,128)(2,1)S(1)}, bf16[512,2048]{1,0:T(8,128)(2,1)}, u32[]{:S(2)}) copy-start(bf16[512,2048]{1,0:T(8,128)(2,1)} %get-tuple-element.50.x_ref) | copy-start | bytes 6291460
  (46 other events, 223.7 us)

commit v5 on v4

--- a/solution.py
+++ b/solution.py
@@ -249,12 +249,19 @@
     )(place, x, hidden, gain, *tables, *pieces)
 
 
-def column_kernel(place_ref, x_ref, cos_ref, sin_ref, *refs):
-    pieces = refs[: 4 * len(RELATIVE)]
-    out_ref, w_ref, hid_ref, sems = refs[4 * len(RELATIVE) :]
-    core = place_ref[0]
+def column_kernel(core_ref, x_ref, cos_ref, sin_ref, own_plane, other_plane, out_ref, w_ref, hid_ref, sems):
+    core = core_ref[0]
     half = D // 2
-    start_copies(place_ref, pieces, sems, w_ref)
+    triple = 3 * PAIR
+
+    for g in range(STEPS):
+        lanes = pl.ds(g * triple, triple)
+        for slot, plane in enumerate((own_plane, other_plane)):
+            for ylo in range(2):
+                for yhi in range(2):
+                    src = plane.at[:, :, ylo, yhi, :, lanes]
+                    dst = w_ref.at[g, slot, ylo, :, yhi]
+                    pltpu.make_async_copy(src, dst, sems.at[g]).start()
 
     def selection(transposed):
         a = lax.broadcasted_iota(jnp.int32, (C, C), 1 if transposed else 0)
@@ -276,7 +283,11 @@
     keep = (row // N_SEQ == col // N_SEQ) & (col <= row)
 
     def step(g, _):
-        weight = step_weights(w_ref, sems, g)
+        pltpu.make_async_copy(w_ref.at[g], w_ref.at[g], sems.at[g]).wait()
+
+        def weight(slot, kind):
+            lanes = slice(kind * PAIR, (kind + 1) * PAIR)
+            return w_ref[g, slot, :, :, :, :, :, lanes].reshape(half, PAIR)
 
         def projected(kind):
             return dot(hid_ref[:, :half], weight(0, kind)) + dot(hid_ref[:, half:], weight(1, kind))
@@ -303,69 +314,69 @@
     lax.fori_loop(0, STEPS, step, 0)
 
 
-def column_layer(place, x, tables, pieces):
+def column_layer(core, x, tables, planes):
     vmem = pl.BlockSpec(memory_space=pltpu.VMEM)
     hbm = pl.BlockSpec(memory_space=pltpu.HBM)
     return pl.pallas_call(
         column_kernel,
         out_shape=jax.ShapeDtypeStruct((C, WIDTH), jnp.bfloat16),
-        in_specs=[pl.BlockSpec(memory_space=pltpu.SMEM)] + [vmem] * 3 + [hbm] * len(pieces),
+        in_specs=[pl.BlockSpec(memory_space=pltpu.SMEM)] + [vmem] * 3 + [hbm] * 2,
         out_specs=vmem,
         scratch_shapes=[
-            pltpu.VMEM((2, 2, 16, 2, 32, QKV_PART), jnp.bfloat16),
+            pltpu.VMEM((STEPS, 2, 2, 4, 2, 4, 16, 3 * PAIR), jnp.bfloat16),
             pltpu.VMEM((C, D), jnp.bfloat16),
-            pltpu.SemaphoreType.DMA((4,)),
+            pltpu.SemaphoreType.DMA((STEPS,)),
         ],
-        compiler_params=pltpu.CompilerParams(vmem_limit_bytes=40 * MIB),
+        compiler_params=pltpu.CompilerParams(vmem_limit_bytes=56 * MIB),
         cost_estimate=pl.CostEstimate(
             flops=2 * C * D * 3 * WIDTH + 4 * C * C * WIDTH,
             bytes_accessed=2 * (C * D + 3 * D * WIDTH + C * WIDTH),
             transcendentals=C * C * HEADS,
         ),
-    )(place, x, *tables, *pieces)
-
-
-def final_kernel(place_ref, att_ref, x_ref, *refs):
-    pieces = refs[: 4 * len(RELATIVE)]
-    out_ref, o_ref, sems = refs[4 * len(RELATIVE) :]
-    core = place_ref[0]
-    half = D // 2
-
-    @pl.when(pl.program_id(0) == 0)
-    def _():
-        start_copies(place_ref, pieces, sems, o_ref=o_ref)
-        for slot in range(2):
-            arrived(o_ref.at[slot], sems.at[4 + slot])
-
-    for h in range(2):
-        lanes = slice(h * half, (h + 1) * half)
-        total = x_ref[:, lanes].astype(jnp.float32)
-        out_ref[:, lanes] = output_sum(core, att_ref, slice(None), o_ref, h, total).astype(jnp.bfloat16)
-
-
-def final_layer(place, attended, x, pieces):
+    )(core, x, *tables, *planes)
+
+
+def branch_sum(core, att_ref, own_ref, other_ref, resid_ref):
+    width = WIDTH // 4
+    total = resid_ref[...].astype(jnp.float32)
+    for slot in range(4):
+        block = jnp.where(slot < 2, core, 1 - core) + 2 * (slot % 2)
+        lanes = pl.ds(pl.multiple_of(block * width, width), width)
+        ref = own_ref if slot < 2 else other_ref
+        rows = slice((slot % 2) * width, (slot % 2 + 1) * width)
+        total = total + dot(att_ref[:, lanes], ref[rows, :])
+    return total
+
+
+def final_kernel(core_ref, att_ref, own_ref, other_ref, resid_ref, out_ref):
+    out_ref[...] = branch_sum(core_ref[0], att_ref, own_ref, other_ref, resid_ref).astype(jnp.bfloat16)
+
+
+def output_layer(core, attended, own, other, resid):
     size = 128
     block = lambda width: pl.BlockSpec((size, width), lambda i: (i, 0))
-    hbm = pl.BlockSpec(memory_space=pltpu.HBM)
+    whole = lambda shape: pl.BlockSpec(shape, lambda i: (0, 0), pipeline_mode=pl.Buffered(1))
     return pl.pallas_call(
         final_kernel,
         grid=(C // size,),
         out_shape=jax.ShapeDtypeStruct((C, D), jnp.bfloat16),
-        in_specs=[pl.BlockSpec(memory_space=pltpu.SMEM), block(WIDTH), block(D)] + [hbm] * len(pieces),
+        in_specs=[
+            pl.BlockSpec(memory_space=pltpu.SMEM),
+            block(WIDTH),
+            whole(own.shape),
+            whole(other.shape),
+            block(D),
+        ],
         out_specs=block(D),
-        scratch_shapes=[
-            pltpu.VMEM((2, 16, 2, 32, D // 2), jnp.bfloat16),
-            pltpu.SemaphoreType.DMA((6,)),
-        ],
         compiler_params=pltpu.CompilerParams(
-            dimension_semantics=("arbitrary",), vmem_limit_bytes=24 * MIB
+            dimension_semantics=("arbitrary",), vmem_limit_bytes=54 * MIB
         ),
         cost_estimate=pl.CostEstimate(
             flops=2 * C * D * WIDTH,
             bytes_accessed=2 * (2 * C * D + D * WIDTH + C * WIDTH),
             transcendentals=0,
         ),
-    )(place, attended, x, *pieces)
+    )(core, attended, own, other, resid)
 
 
 def shift(value, axis, by):
@@ -428,10 +439,23 @@
     return [forwards(hop, axis) for hop, axis in zip(hops, "yx")]
 
 
-def both_cores(parts, swapped):
+def both_cores(parts):
     own = [piece for part in parts for piece in part]
-    other = [swapped[index] if index in swapped else swap(piece) for index, piece in enumerate(own)]
-    return own + other
+    return own + [swap(piece) for piece in own]
+
+
+def column_line(inputs, output):
+    shard = jnp.concatenate([by_step(inputs), fold_output(output)], 1)
+    return lax.all_gather(shard, ("ylo", "yhi"), axis=0)
+
+
+def column_plane(line):
+    return lax.all_gather(line, ("x", "z"), axis=0).reshape(4, 4, 2, 2, 16, 4 * WIDTH)
+
+
+def column_output(plane):
+    out = plane[..., 3 * WIDTH :].transpose(2, 0, 3, 1, 4, 5)
+    return out.reshape(64, 2, 8, WIDTH).transpose(0, 2, 1, 3).reshape(WIDTH // 2, D)
 
 
 def shards(tokens, gain_first, inputs_first, output_first, gain_second, inputs_second, output_second, starts, band_edges):
@@ -452,24 +476,21 @@
 
     hidden = normed_slots(core_scalar, residual, gain_first.reshape(1, D))
 
+    line = column_line(inputs_second, output_second)
     first = inner_rings(lines(inputs_first, output_first))
     first, hidden, row_tables, column_tables = lax.optimization_barrier((first, hidden, row_tables, column_tables))
     first_hop = outer_hops(first)
-    swapped = {0: swap(first[0]), 5: swap(first[1])}
-    inputs_second, output_second, swapped = lax.optimization_barrier((inputs_second, output_second, swapped))
-    second = lines(inputs_second, output_second)
-    pieces = both_cores(outer_forwards(first_hop), swapped)
-    second = inner_rings(second)
-    second, place = lax.optimization_barrier((second, place))
-    second_hop = outer_hops(second)
+    line, _ = lax.optimization_barrier((line, first_hop))
+    plane = column_plane(line)
+    pieces = both_cores(outer_forwards(first_hop))
 
     middle, hidden = row_layer(place, residual, hidden, gain_second.reshape(1, D), row_tables, pieces)
-    second_hop, hidden = lax.optimization_barrier((second_hop, hidden))
-    pieces = both_cores(outer_forwards(second_hop), {})
+    plane, hidden = lax.optimization_barrier((plane, hidden))
+    planes = (plane, swap(plane))
     hidden = lax.all_to_all(hidden, SEQ, split_axis=0, concat_axis=0, tiled=True)
-    attended = column_layer(place, hidden, column_tables, pieces)
+    attended = column_layer(core_scalar, hidden, column_tables, planes)
     attended = lax.all_to_all(attended, SEQ, split_axis=0, concat_axis=0, tiled=True)
-    return final_layer(place, attended, middle, pieces)[None]
+    return output_layer(core_scalar, attended, *[column_output(p) for p in planes], middle)[None]
 
 
 def solution(mesh):

time: 274 us -> 262 us (0.956)
  starting transfers between devices: 56.1 us -> 34.5 us
  blocking collectives: 60.7 us -> 80.8 us
  between operations: 2.29 us -> 15.1 us
  local copies, waits for them, and re-layouts: 35.9 us -> 23.8 us
  waiting for transfers between devices: 51.6 us -> 43.1 us
  other arithmetic: 12 us -> 8.98 us
    all_gather x0 -> x1, blocking collectives: none -> 29.2 us  [column_line(): return lax.all_gather(shard, ('ylo', 'yhi'), axis=0)]
    ppermute x16 -> x8, waiting for transfers between devices: 21.7 us -> 5.84 us  [shift(): lax.ppermute(value, ('ylo', 'yhi'), [(where(y), where((y + by) % 4)) for...]
    all_gather x2 -> x1, blocking collectives: 27.3 us -> 14.1 us  [lines(): rows = lax.all_gather(shard, 'z', axis=0)]
    unnamed x114 -> x46, local copies, waits for them, and re-layouts: 18.3 us -> 6.68 us
    all_gather x0 -> x1, waiting for transfers between devices: none -> 9.39 us  [column_plane(): lax.all_gather(line, ('x', 'z'), axis=0).reshape(4, 4, 2, 2, 16, 4 * WIDTH)]
    ppermute x16 -> x8, starting transfers between devices: 20.6 us -> 13.2 us  [shift(): lax.ppermute(value, ('ylo', 'yhi'), [(where(y), where((y + by) % 4)) for...]
    ppermute x16 -> x8, starting transfers between devices: 20.4 us -> 13.6 us  [shift(): return lax.ppermute(value, axis, [(i, (i + by) % 4) for i in range(4)])]
    transpose x0 -> x4, local copies, waits for them, and re-layouts: none -> 6.57 us  [column_output(): out = plane[..., 3 * WIDTH:].transpose(2, 0, 3, 1, 4, 5)]
  transfers between devices with their start and end apart: 53 -> 29, of which waited for: 12 -> 8; matrix products, arithmetic and copies ran while one was open for 9% -> 8% of each run, Pallas kernels for 10% -> 10%
where the time goes in v5:
time: 262 us; the launch traced here: 261 us
  blocking collectives  80.8 us (31%)
  Pallas kernels  54.7 us (21%)
  waiting for transfers between devices  43.1 us (16%)
  starting transfers between devices  34.5 us (13%)
  local copies, waits for them, and re-layouts  23.8 us (9%)
  between operations  15.1 us (6%)
  other arithmetic  8.98 us (3%)
    all_to_all x1, blocking collectives, shards(): lax.all_to_all(hidden, SEQ, split_axis=0, concat_axis=0, tiled=True)  37.5 us
    all_gather x1, blocking collectives, column_line(): return lax.all_gather(shard, ('ylo', 'yhi'), axis=0)  29.2 us
    pallas_call x1, Pallas kernels, row_layer(): pl.pallas_call(row_kernel, out_shape=[shape, shape], in_specs=[pl.BlockSp...  24.4 us
    pallas_call x1, Pallas kernels, column_layer(): pl.pallas_call(column_kernel, out_shape=jax.ShapeDtypeStruct((C, WIDTH),...  21.3 us
    all_gather x1, blocking collectives, lines(): rows = lax.all_gather(shard, 'z', axis=0)  14.1 us
    ppermute x8, starting transfers between devices, shift(): return lax.ppermute(value, axis, [(i, (i + by) % 4) for i in range(4)])  13.6 us
    ppermute x8, starting transfers between devices, shift(): lax.ppermute(value, ('ylo', 'yhi'), [(where(y), where((y + by) % 4)) for...  13.2 us
    ppermute x8, waiting for transfers between devices, shift(): return lax.ppermute(value, axis, [(i, (i + by) % 4) for i in range(4)])  12.9 us
  transfers between devices with their start and end apart: 29, of which 8 were waited for; matrix products, arithmetic and copies ran while one was open for 8% of the time, Pallas kernels for 10%

profile of v5, /device:TPU:0, one launch (start us, length us, event | category | flops | bytes accessed | tf_op | source)
XLA Modules:
  0.0 260.9 jit_solution(4884843780239689543)
XLA Ops:
  6.5 0.7 fusion.10
  7.3 0.9 reshape.95
  8.4 14.1 %all-gather.1 = bf16[64,4096]{1,0:T(8,128)(2,1)S(1)} all-gather(bf16[16,4096]{1,0:T(8,128)(2,1)S(1)} %maximum_maximum_fusion.1), channel_id=3, replica_groups=mesh['ylo'=2,'core'=2,'x'=4,'yhi'=2,'z'=4] {'z'}, dimensions={0}, use_global_device_ids=true | all-gather | bytes 655360 | tf_op jit(solution)/shard_map/all_gather | solution.py:418
  22.6 0.8 fusion.6
  23.5 1.6 collective-permute-start.4
  25.0 1.7 collective-permute-start.5
  26.7 0.9 fusion.7
  27.6 1.5 collective-permute-start
  29.0 1.7 collective-permute-start.1
  30.8 0.7 constant_dynamic-slice_fusion
  31.5 0.7 add_convert_fusion.1
  32.3 0.6 fusion.12
  34.2 1.9 fusion.4
  36.2 0.4 collective-permute-start.6
  36.6 0.7 slice.97
  37.3 2.9 %collective-permute-start.7 = (bf16[2,32,1024]{2,1,0:T(8,128)(2,1)}, bf16[2,32,1024]{2,1,0:T(8,128)(2,1)}, u32[]{:S(2)}, u32[]{:S(2)}) collective-permute-start(bf16[2,32,1024]{2,1,0:T(8,128)(2,1)} %slice.97), channel_id=1, source_target_pairs={{0,68},{64,0},{4,64},{68,4},{1,69},{65,1},{5,65},{69,5},{2,70},{66... | collective-permute-start | bytes 393224 | tf_op jit(solution)/shard_map/ppermute | solution.py:385
  40.4 2.1 shard_map.91.hid_ref
  42.6 1.0 pad_maximum_fusion.6
  43.6 1.1 slice.92
  44.6 0.3 collective-permute-start.2
  45.0 0.9 slice.93
  45.9 3.0 %collective-permute-start.3 = (bf16[2,32,1024]{2,1,0:T(8,128)(2,1)S(1)}, bf16[2,32,1024]{2,1,0:T(8,128)(2,1)S(1)}, u32[]{:S(2)}, u32[]{:S(2)}) collective-permute-start(bf16[2,32,1024]{2,1,0:T(8,128)(2,1)S(1)} %slice.93), channel_id=1, source_target_pairs={{0,24},{8,0},{16,8},{24,16},{1,25},{9,1},{17,9},{25,17},{2,26},{10... | collective-permute-start | bytes 393224 | tf_op jit(solution)/shard_map/ppermute | solution.py:386
  48.9 1.0 maximum_bitcast_fusion.1
  49.9 1.1 pad_maximum_fusion.1.refs_5_
  51.1 0.4 collective-permute-done.3
  51.5 1.2 pad_maximum_fusion.refs_0_
  52.7 3.2 %collective-permute-start.9 = (bf16[4,2,32,2048]{3,2,1,0:T(8,128)(2,1)S(1)}, bf16[4,2,32,2048]{3,2,1,0:T(8,128)(2,1)}, u32[]{:S(2)}, u32[]{:S(2)}) collective-permute-start(bf16[4,2,32,2048]{3,2,1,0:T(8,128)(2,1)S(1)} %pad_maximum_fusion.refs_0_), channel_id=1, source_target_pairs={{0,68},{64,0},{4,64},{68,4},{1,69},{65,1},{5,65},{69,5},{2,70},{66... | collective-permute-start | bytes 3145736 | tf_op jit(solution)/shard_map/ppermute | solution.py:385
  55.9 1.0 collective-permute-start.10
  56.9 2.7 %collective-permute-start.11 = (bf16[4,2,32,2048]{3,2,1,0:T(8,128)(2,1)}, bf16[4,2,32,2048]{3,2,1,0:T(8,128)(2,1)}, u32[]{:S(2)}, u32[]{:S(2)}) collective-permute-start(bf16[4,2,32,2048]{3,2,1,0:T(8,128)(2,1)} %pad_maximum_fusion.1.refs_5_), channel_id=1, source_target_pairs={{0,24},{8,0},{16,8},{24,16},{1,25},{9,1},{17,9},{25,17},{2,26},{10... | collective-permute-start | bytes 3145736 | tf_op jit(solution)/shard_map/ppermute | solution.py:386
  59.9 29.2 %all-gather = bf16[64,4096]{1,0:T(8,128)(2,1)} all-gather(bf16[16,4096]{1,0:T(8,128)(2,1)S(1)} %maximum_maximum_fusion), channel_id=2, replica_groups=mesh['ylo'=2,'core'=2,'x'=4,'yhi'=2,'z'=4] {'ylo','yhi'}, dimensions={0}, use_global_device_ids=true | all-gather | bytes 655360 | tf_op jit(solution)/shard_map/all_gather | solution.py:449
  89.2 0.5 collective-permute-start.21
  89.7 1.1 slice.98
  90.8 0.4 collective-permute-start.12
  91.2 1.1 slice.99
  92.3 3.0 %collective-permute-start.13 = (bf16[4,2,32,1024]{3,2,1,0:T(8,128)(2,1)S(1)}, bf16[4,2,32,1024]{3,2,1,0:T(8,128)(2,1)S(1)}, u32[]{:S(2)}, u32[]{:S(2)}) collective-permute-start(bf16[4,2,32,1024]{3,2,1,0:T(8,128)(2,1)S(1)} %slice.99), channel_id=1, source_target_pairs={{0,68},{64,0},{4,64},{68,4},{1,69},{65,1},{5,65},{69,5},{2,70},{66... | collective-permute-start | bytes 1572872 | tf_op jit(solution)/shard_map/ppermute | solution.py:385
  95.3 1.1 slice.100
  96.4 0.5 collective-permute-start.14
  96.9 1.1 slice.101
  98.1 2.8 %collective-permute-start.15 = (bf16[4,2,32,1024]{3,2,1,0:T(8,128)(2,1)S(1)}, bf16[4,2,32,1024]{3,2,1,0:T(8,128)(2,1)}, u32[]{:S(2)}, u32[]{:S(2)}) collective-permute-start(bf16[4,2,32,1024]{3,2,1,0:T(8,128)(2,1)S(1)} %slice.101), channel_id=1, source_target_pairs={{0,24},{8,0},{16,8},{24,16},{1,25},{9,1},{17,9},{25,17},{2,26},{10... | collective-permute-start | bytes 1572872 | tf_op jit(solution)/shard_map/ppermute | solution.py:386
  100.9 5.3 %collective-permute-done.12.refs_3_ = bf16[4,2,32,1024]{3,2,1,0:T(8,128)(2,1)S(1)} collective-permute-done((bf16[4,2,32,1024]{3,2,1,0:T(8,128)(2,1)S(1)}, bf16[4,2,32,1024]{3,2,1,0:T(8,128)(2,1)S(1)}, u32[]{:S(2)}, u32[]{:S(2)}) %collective-permute-start.12) | collective-permute-done | bytes 524320 | tf_op jit(solution)/shard_map/ppermute | solution.py:385
  106.2 0.5 collective-permute-done.13.refs_4_
  106.7 0.5 collective-permute-start.17
  107.3 12.4 %collective-permute-done.14.refs_8_ = bf16[4,2,32,1024]{3,2,1,0:T(8,128)(2,1)S(1)} collective-permute-done((bf16[4,2,32,1024]{3,2,1,0:T(8,128)(2,1)S(1)}, bf16[4,2,32,1024]{3,2,1,0:T(8,128)(2,1)S(1)}, u32[]{:S(2)}, u32[]{:S(2)}) %collective-permute-start.14) | collective-permute-done | bytes 524320 | tf_op jit(solution)/shard_map/ppermute | solution.py:386
  119.7 0.4 collective-permute-start.18
  120.2 0.8 copy-done.3
  121.1 0.8 copy-done.5
  121.9 0.4 collective-permute-start.23
  122.3 0.8 copy-done.7
  123.3 3.9 %collective-permute-done.25.refs_19_ = bf16[4,2,32,1024]{3,2,1,0:T(8,128)(2,1)} collective-permute-done((bf16[4,2,32,1024]{3,2,1,0:T(8,128)(2,1)}, bf16[4,2,32,1024]{3,2,1,0:T(8,128)(2,1)}, u32[]{:S(2)}, u32[]{:S(2)}) %collective-permute-start.25) | collective-permute-done | bytes 524320 | tf_op jit(solution)/shard_map/ppermute | solution.py:405
  127.2 1.1 copy-done.4
  128.3 1.0 copy-done.6
  129.4 1.0 copy-done.8
  130.4 24.4 %shard_map.92 = (bf16[512,2048]{1,0:T(8,128)(2,1)}, bf16[512,2048]{1,0:T(8,128)(2,1)}) custom-call(s32[3]{0:T(128)S(1)} %pad_add_fusion.place_ref, bf16[512,2048]{1,0:T(8,128)(2,1)} %bitcast.58, bf16[512,2048]{1,0:T(8,128)(2,1)} %copy-done.1, f32[1,2048]{1,0:T(1,128)S(1)} %bitcast.61, f32[512,128]{1,0:T(8,128)S(1)} %get-tuple-element.21.cos_ref, ...), custom_call_target="tpu_custom_call" | custom-call | flops 9663676416 | bytes 25165824 | tf_op jit(solution)/shard_map/pallas_call | solution.py:230
  154.8 9.4 %all-gather.5.cloned.1.call-done = bf16[64,16,4096]{2,1,0:T(8,128)(2,1)} async-done(((bf16[4,16,4096]{2,1,0:T(8,128)(2,1)}), bf16[64,16,4096]{2,1,0:T(8,128)(2,1)}) %all-gather.5.cloned.1.call-update) | async-done | bytes 8388624 | tf_op jit(solution)/shard_map/all_gather | solution.py:453
  164.2 37.5 %all_to_all.22 = bf16[32,16,2048]{2,1,0:T(8,128)(2,1)} all-to-all(bf16[32,16,2048]{2,1,0:T(8,128)(2,1)} %bitcast.68), channel_id=1, replica_groups=mesh['ylo'=2,'core'=2,'x'=4,'yhi'=2,'z'=4] {'x','yhi','z'}, dimensions={0} | all-to-all | bytes 4194304 | tf_op jit(solution)/shard_map/all_to_all | solution.py:490
  201.7 21.3 %shard_map.93 = bf16[512,1024]{1,0:T(8,128)(2,1)} custom-call(s32[1]{0:T(128)} %bitcast.core_ref, bf16[512,2048]{1,0:T(8,128)(2,1)} %bitcast.69, f32[512,128]{1,0:T(8,128)} %get-tuple-element.25.cos_ref, f32[512,128]{1,0:T(8,128)} %get-tuple-element.26.sin_ref, bf16[4,4,2,2,16,4096]{5,4,3,2,1,0:T(8,128)(2,1)} %bitcast.77, ...), custom_call_target="tpu_custom_call" | custom-call | flops 7516192768 | bytes 15728640 | tf_op jit(solution)/shard_map/pallas_call | solution.py:320
  223.0 5.5 %all-to-all-start.1 = ((bf16[32,16,1024]{2,1,0:T(8,128)(2,1)}), bf16[32,16,1024]{2,1,0:T(8,128)(2,1)S(1)}, u32[]{:S(2)}, u32[]{:S(2)}) async-start(bf16[32,16,1024]{2,1,0:T(8,128)(2,1)} %bitcast.71), calls=%async_computation.1 | async-start | bytes 2097152 | tf_op jit(solution)/shard_map/all_to_all | solution.py:492
  228.5 1.8 slice_bitcast_fusion.1
  230.3 1.5 copy.18
  231.8 1.8 slice_bitcast_fusion
  233.6 1.5 copy.19
  235.1 11.1 %all-to-all-done.1 = bf16[32,16,1024]{2,1,0:T(8,128)(2,1)S(1)} async-done(((bf16[32,16,1024]{2,1,0:T(8,128)(2,1)}), bf16[32,16,1024]{2,1,0:T(8,128)(2,1)S(1)}, u32[]{:S(2)}, u32[]{:S(2)}) %all-to-all-start.1) | async-done | bytes 1048608 | tf_op jit(solution)/shard_map/all_to_all | solution.py:492
  246.2 1.0 copy-done.10
  247.2 6.9 %shard_map.94 = bf16[512,2048]{1,0:T(8,128)(2,1)} custom-call(s32[1]{0:T(128)} %bitcast.core_ref, bf16[512,1024]{1,0:T(8,128)(2,1)} %bitcast.64, bf16[512,2048]{1,0:T(8,128)(2,1)} %bitcast.62, bf16[512,2048]{1,0:T(8,128)(2,1)} %bitcast.63, bf16[512,2048]{1,0:T(8,128)(2,1)} %get-tuple-element.28.resid_ref), custom_call_target="tpu_custom_call" | custom-call | flops 2147483648 | bytes 9437184 | tf_op jit(solution)/shard_map/pallas_call | solution.py:359
  (91 shorter events, 1.5 us)
Async XLA Ops:
  6.5 157.7 %all-gather.5.cloned.1.call-start = ((), (), s32[]{:S(2)}) async-start(), calls=%async_computation.2 | async-start | bytes 8912896 | tf_op jit(solution)/shard_map/all_gather | solution.py:453
  8.4 22.4 %copy-start.20 = (s32[1,32]{1,0:T(1,128)S(1)}, s32[1,32]{1,0:T(1,128)}, u32[]{:S(2)}) copy-start(s32[1,32]{1,0:T(1,128)} %param.16) | copy-start | bytes 388
  8.4 23.9 %copy-start.19 = (s32[2]{0:T(128)S(1)}, s32[2]{0:T(128)}, u32[]{:S(2)}) copy-start(s32[2]{0:T(128)} %param.17) | copy-start | bytes 28
  23.5 12.7 %collective-permute-start.4 = (bf16[2,32,2048]{2,1,0:T(8,128)(2,1)}, bf16[2,32,2048]{2,1,0:T(8,128)(2,1)S(1)}, u32[]{:S(2)}, u32[]{:S(2)}) collective-permute-start(bf16[2,32,2048]{2,1,0:T(8,128)(2,1)} %get-tuple-element.32), channel_id=1, source_target_pairs={{0,64},{64,4},{4,68},{68,0},{1,65},{65,5},{5,69},{69,1},{2,66},{66... | collective-permute-start | bytes 786440 | tf_op jit(solution)/shard_map/ppermute | solution.py:385
  25.0 11.6 %collective-permute-start.5 = (bf16[2,32,2048]{2,1,0:T(8,128)(2,1)}, bf16[2,32,2048]{2,1,0:T(8,128)(2,1)S(1)}, u32[]{:S(2)}, u32[]{:S(2)}) collective-permute-start(bf16[2,32,2048]{2,1,0:T(8,128)(2,1)} %get-tuple-element.32), channel_id=1, source_target_pairs={{0,68},{64,0},{4,64},{68,4},{1,69},{65,1},{5,65},{69,5},{2,70},{66... | collective-permute-start | bytes 786440 | tf_op jit(solution)/shard_map/ppermute | solution.py:385
  26.7 13.7 %copy-start = (bf16[1,512,2048]{2,1,0:T(8,128)(2,1)S(1)}, bf16[1,512,2048]{2,1,0:T(8,128)(2,1)}, u32[]{:S(2)}) copy-start(bf16[1,512,2048]{2,1,0:T(8,128)(2,1)} %param.9) | copy-start | bytes 6291460
  26.7 13.7 %copy-start.2 = (f32[2048]{0:T(1024)S(1)}, f32[2048]{0:T(1024)}, u32[]{:S(2)}) copy-start(f32[2048]{0:T(1024)} %param.10) | copy-start | bytes 24580
  27.6 16.0 %collective-permute-start = (bf16[2,32,2048]{2,1,0:T(8,128)(2,1)}, bf16[2,32,2048]{2,1,0:T(8,128)(2,1)}, u32[]{:S(2)}, u32[]{:S(2)}) collective-permute-start(bf16[2,32,2048]{2,1,0:T(8,128)(2,1)} %get-tuple-element.34), channel_id=1, source_target_pairs={{0,8},{8,16},{16,24},{24,0},{1,9},{9,17},{17,25},{25,1},{2,10},{10... | collective-permute-start | bytes 786440 | tf_op jit(solution)/shard_map/ppermute | solution.py:386
  29.0 15.9 %collective-permute-start.1 = (bf16[2,32,2048]{2,1,0:T(8,128)(2,1)}, bf16[2,32,2048]{2,1,0:T(8,128)(2,1)}, u32[]{:S(2)}, u32[]{:S(2)}) collective-permute-start(bf16[2,32,2048]{2,1,0:T(8,128)(2,1)} %get-tuple-element.34), channel_id=1, source_target_pairs={{0,24},{8,0},{16,8},{24,16},{1,25},{9,1},{17,9},{25,17},{2,26},{10... | collective-permute-start | bytes 786440 | tf_op jit(solution)/shard_map/ppermute | solution.py:386
  36.1 4.0 %copy-start.13 = (bf16[2,32,2048]{2,1,0:T(8,128)(2,1)}, bf16[2,32,2048]{2,1,0:T(8,128)(2,1)S(1)}, u32[]{:S(2)}) copy-start(bf16[2,32,2048]{2,1,0:T(8,128)(2,1)S(1)} %collective-permute-done.4) | copy-start | bytes 786436
  36.2 12.8 %collective-permute-start.6 = (bf16[2,32,1024]{2,1,0:T(8,128)(2,1)S(1)}, bf16[2,32,1024]{2,1,0:T(8,128)(2,1)}, u32[]{:S(2)}, u32[]{:S(2)}) collective-permute-start(bf16[2,32,1024]{2,1,0:T(8,128)(2,1)S(1)} %slice.96), channel_id=1, source_target_pairs={{0,64},{64,4},{4,68},{68,0},{1,65},{65,5},{5,69},{69,1},{2,66},{66... | collective-permute-start | bytes 393224 | tf_op jit(solution)/shard_map/ppermute | solution.py:385
  36.6 3.6 %copy-start.15 = (bf16[2,32,2048]{2,1,0:T(8,128)(2,1)}, bf16[2,32,2048]{2,1,0:T(8,128)(2,1)S(1)}, u32[]{:S(2)}) copy-start(bf16[2,32,2048]{2,1,0:T(8,128)(2,1)S(1)} %collective-permute-done.5) | copy-start | bytes 786436
  37.3 11.6 %collective-permute-start.7 = (bf16[2,32,1024]{2,1,0:T(8,128)(2,1)}, bf16[2,32,1024]{2,1,0:T(8,128)(2,1)}, u32[]{:S(2)}, u32[]{:S(2)}) collective-permute-start(bf16[2,32,1024]{2,1,0:T(8,128)(2,1)} %slice.97), channel_id=1, source_target_pairs={{0,68},{64,0},{4,64},{68,4},{1,69},{65,1},{5,65},{69,5},{2,70},{66... | collective-permute-start | bytes 393224 | tf_op jit(solution)/shard_map/ppermute | solution.py:385
  42.5 8.5 %copy-start.1 = (bf16[512,2048]{1,0:T(8,128)(2,1)}, bf16[512,2048]{1,0:T(8,128)(2,1)S(1)}, u32[]{:S(2)}) copy-start(bf16[512,2048]{1,0:T(8,128)(2,1)S(1)} %shard_map.91.hid_ref) | copy-start | bytes 6291460
  42.5 7.4 %copy-start.12 = (bf16[1,2,32,2048]{3,2,1,0:T(8,128)(2,1)S(1)}, bf16[1,2,32,2048]{3,2,1,0:T(8,128)(2,1)}, u32[]{:S(2)}) copy-start(bf16[1,2,32,2048]{3,2,1,0:T(8,128)(2,1)} %get-tuple-element.31) | copy-start | bytes 786436
  42.5 7.4 %copy-start.14 = (bf16[2,32,2048]{2,1,0:T(8,128)(2,1)S(1)}, bf16[2,32,2048]{2,1,0:T(8,128)(2,1)}, u32[]{:S(2)}) copy-start(bf16[2,32,2048]{2,1,0:T(8,128)(2,1)} %copy-done.13) | copy-start | bytes 786436
  42.5 7.4 %copy-start.16 = (bf16[2,32,2048]{2,1,0:T(8,128)(2,1)S(1)}, bf16[2,32,2048]{2,1,0:T(8,128)(2,1)}, u32[]{:S(2)}) copy-start(bf16[2,32,2048]{2,1,0:T(8,128)(2,1)} %copy-done.15) | copy-start | bytes 786436
  43.6 7.9 %copy-start.11 = (bf16[1,2,32,2048]{3,2,1,0:T(8,128)(2,1)S(1)}, bf16[1,2,32,2048]{3,2,1,0:T(8,128)(2,1)}, u32[]{:S(2)}) copy-start(bf16[1,2,32,2048]{3,2,1,0:T(8,128)(2,1)} %get-tuple-element.33) | copy-start | bytes 786436
  44.6 6.4 %collective-permute-start.2 = (bf16[2,32,1024]{2,1,0:T(8,128)(2,1)S(1)}, bf16[2,32,1024]{2,1,0:T(8,128)(2,1)S(1)}, u32[]{:S(2)}, u32[]{:S(2)}) collective-permute-start(bf16[2,32,1024]{2,1,0:T(8,128)(2,1)S(1)} %slice.92), channel_id=1, source_target_pairs={{0,8},{8,16},{16,24},{24,0},{1,9},{9,17},{17,25},{25,1},{2,10},{10... | collective-permute-start | bytes 393224 | tf_op jit(solution)/shard_map/ppermute | solution.py:386
  45.9 5.5 %collective-permute-start.3 = (bf16[2,32,1024]{2,1,0:T(8,128)(2,1)S(1)}, bf16[2,32,1024]{2,1,0:T(8,128)(2,1)S(1)}, u32[]{:S(2)}, u32[]{:S(2)}) collective-permute-start(bf16[2,32,1024]{2,1,0:T(8,128)(2,1)S(1)} %slice.93), channel_id=1, source_target_pairs={{0,24},{8,0},{16,8},{24,16},{1,25},{9,1},{17,9},{25,17},{2,26},{10... | collective-permute-start | bytes 393224 | tf_op jit(solution)/shard_map/ppermute | solution.py:386
  49.9 9.7 %copy-start.17 = (bf16[16,3072]{1,0:T(8,128)(2,1)S(1)}, bf16[16,3072]{1,0:T(8,128)(2,1)}, u32[]{:S(2)}) copy-start(bf16[16,3072]{1,0:T(8,128)(2,1)} %param.14) | copy-start | bytes 294916
  51.1 8.8 %copy-start.18 = (bf16[8,2048]{1,0:T(8,128)(2,1)S(1)}, bf16[8,2048]{1,0:T(8,128)(2,1)}, u32[]{:S(2)}) copy-start(bf16[8,2048]{1,0:T(8,128)(2,1)} %param.15) | copy-start | bytes 98308
  52.6 36.5 %collective-permute-start.8 = (bf16[4,2,32,2048]{3,2,1,0:T(8,128)(2,1)S(1)}, bf16[4,2,32,2048]{3,2,1,0:T(8,128)(2,1)}, u32[]{:S(2)}, u32[]{:S(2)}) collective-permute-start(bf16[4,2,32,2048]{3,2,1,0:T(8,128)(2,1)S(1)} %pad_maximum_fusion.refs_0_), channel_id=1, source_target_pairs={{0,64},{64,4},{4,68},{68,0},{1,65},{65,5},{5,69},{69,1},{2,66},{66... | collective-permute-start | bytes 3145736 | tf_op jit(solution)/shard_map/ppermute | solution.py:385
  52.7 36.4 %collective-permute-start.9 = (bf16[4,2,32,2048]{3,2,1,0:T(8,128)(2,1)S(1)}, bf16[4,2,32,2048]{3,2,1,0:T(8,128)(2,1)}, u32[]{:S(2)}, u32[]{:S(2)}) collective-permute-start(bf16[4,2,32,2048]{3,2,1,0:T(8,128)(2,1)S(1)} %pad_maximum_fusion.refs_0_), channel_id=1, source_target_pairs={{0,68},{64,0},{4,64},{68,4},{1,69},{65,1},{5,65},{69,5},{2,70},{66... | collective-permute-start | bytes 3145736 | tf_op jit(solution)/shard_map/ppermute | solution.py:385
  55.9 33.2 %collective-permute-start.10 = (bf16[4,2,32,2048]{3,2,1,0:T(8,128)(2,1)}, bf16[4,2,32,2048]{3,2,1,0:T(8,128)(2,1)}, u32[]{:S(2)}, u32[]{:S(2)}) collective-permute-start(bf16[4,2,32,2048]{3,2,1,0:T(8,128)(2,1)} %pad_maximum_fusion.1.refs_5_), channel_id=1, source_target_pairs={{0,8},{8,16},{16,24},{24,0},{1,9},{9,17},{17,25},{25,1},{2,10},{10... | collective-permute-start | bytes 3145736 | tf_op jit(solution)/shard_map/ppermute | solution.py:386
  56.9 32.2 %collective-permute-start.11 = (bf16[4,2,32,2048]{3,2,1,0:T(8,128)(2,1)}, bf16[4,2,32,2048]{3,2,1,0:T(8,128)(2,1)}, u32[]{:S(2)}, u32[]{:S(2)}) collective-permute-start(bf16[4,2,32,2048]{3,2,1,0:T(8,128)(2,1)} %pad_maximum_fusion.1.refs_5_), channel_id=1, source_target_pairs={{0,24},{8,0},{16,8},{24,16},{1,25},{9,1},{17,9},{25,17},{2,26},{10... | collective-permute-start | bytes 3145736 | tf_op jit(solution)/shard_map/ppermute | solution.py:386
  89.1 38.0 %copy-start.9 = (f32[2048]{0:T(1024)S(1)}, f32[2048]{0:T(1024)}, u32[]{:S(2)}) copy-start(f32[2048]{0:T(1024)} %param.13) | copy-start | bytes 24580
  89.2 8.9 %collective-permute-start.16 = (bf16[4,2,32,2048]{3,2,1,0:T(8,128)(2,1)S(1)}, bf16[4,2,32,2048]{3,2,1,0:T(8,128)(2,1)S(1)}, u32[]{:S(2)}, u32[]{:S(2)}) collective-permute-start(bf16[4,2,32,2048]{3,2,1,0:T(8,128)(2,1)S(1)} %pad_maximum_fusion.refs_0_), channel_id=1, source_target_pairs={{0,32},{32,0},{1,33},{33,1},{2,34},{34,2},{3,35},{35,3},{4,36},{36... | collective-permute-start | bytes 3145736 | tf_op jit(solution)/shard_map/ppermute | solution.py:405
  89.2 17.5 %collective-permute-start.21 = (bf16[4,2,32,2048]{3,2,1,0:T(8,128)(2,1)}, bf16[4,2,32,2048]{3,2,1,0:T(8,128)(2,1)S(1)}, u32[]{:S(2)}, u32[]{:S(2)}) collective-permute-start(bf16[4,2,32,2048]{3,2,1,0:T(8,128)(2,1)} %pad_maximum_fusion.1.refs_5_), channel_id=1, source_target_pairs={{0,32},{32,0},{1,33},{33,1},{2,34},{34,2},{3,35},{35,3},{4,36},{36... | collective-permute-start | bytes 3145736 | tf_op jit(solution)/shard_map/ppermute | solution.py:405
  90.8 15.4 %collective-permute-start.12 = (bf16[4,2,32,1024]{3,2,1,0:T(8,128)(2,1)S(1)}, bf16[4,2,32,1024]{3,2,1,0:T(8,128)(2,1)S(1)}, u32[]{:S(2)}, u32[]{:S(2)}) collective-permute-start(bf16[4,2,32,1024]{3,2,1,0:T(8,128)(2,1)S(1)} %slice.98), channel_id=1, source_target_pairs={{0,64},{64,4},{4,68},{68,0},{1,65},{65,5},{5,69},{69,1},{2,66},{66... | collective-permute-start | bytes 1572872 | tf_op jit(solution)/shard_map/ppermute | solution.py:385
  92.3 14.4 %collective-permute-start.13 = (bf16[4,2,32,1024]{3,2,1,0:T(8,128)(2,1)S(1)}, bf16[4,2,32,1024]{3,2,1,0:T(8,128)(2,1)S(1)}, u32[]{:S(2)}, u32[]{:S(2)}) collective-permute-start(bf16[4,2,32,1024]{3,2,1,0:T(8,128)(2,1)S(1)} %slice.99), channel_id=1, source_target_pairs={{0,68},{64,0},{4,64},{68,4},{1,69},{65,1},{5,65},{69,5},{2,70},{66... | collective-permute-start | bytes 1572872 | tf_op jit(solution)/shard_map/ppermute | solution.py:385
  96.4 23.3 %collective-permute-start.14 = (bf16[4,2,32,1024]{3,2,1,0:T(8,128)(2,1)S(1)}, bf16[4,2,32,1024]{3,2,1,0:T(8,128)(2,1)S(1)}, u32[]{:S(2)}, u32[]{:S(2)}) collective-permute-start(bf16[4,2,32,1024]{3,2,1,0:T(8,128)(2,1)S(1)} %slice.100), channel_id=1, source_target_pairs={{0,8},{8,16},{16,24},{24,0},{1,9},{9,17},{17,25},{25,1},{2,10},{10... | collective-permute-start | bytes 1572872 | tf_op jit(solution)/shard_map/ppermute | solution.py:386
  98.1 24.2 %copy-start.21 = (bf16[4,2,32,2048]{3,2,1,0:T(8,128)(2,1)}, bf16[4,2,32,2048]{3,2,1,0:T(8,128)(2,1)S(1)}, u32[]{:S(2)}) copy-start(bf16[4,2,32,2048]{3,2,1,0:T(8,128)(2,1)S(1)} %collective-permute-done.16.refs_10_) | copy-start | bytes 3145732
  98.1 21.6 %collective-permute-start.15 = (bf16[4,2,32,1024]{3,2,1,0:T(8,128)(2,1)S(1)}, bf16[4,2,32,1024]{3,2,1,0:T(8,128)(2,1)}, u32[]{:S(2)}, u32[]{:S(2)}) collective-permute-start(bf16[4,2,32,1024]{3,2,1,0:T(8,128)(2,1)S(1)} %slice.101), channel_id=1, source_target_pairs={{0,24},{8,0},{16,8},{24,16},{1,25},{9,1},{17,9},{25,17},{2,26},{10... | collective-permute-start | bytes 1572872 | tf_op jit(solution)/shard_map/ppermute | solution.py:386
  106.2 14.0 %collective-permute-start.19 = (bf16[4,2,32,1024]{3,2,1,0:T(8,128)(2,1)S(1)}, bf16[4,2,32,1024]{3,2,1,0:T(8,128)(2,1)S(1)}, u32[]{:S(2)}, u32[]{:S(2)}) collective-permute-start(bf16[4,2,32,1024]{3,2,1,0:T(8,128)(2,1)S(1)} %collective-permute-done.12.refs_3_), channel_id=1, source_target_pairs={{0,32},{32,0},{1,33},{33,1},{2,34},{34,2},{3,35},{35,3},{4,36},{36... | collective-permute-start | bytes 1572872 | tf_op jit(solution)/shard_map/ppermute | solution.py:405
  106.7 14.3 %collective-permute-start.20 = (bf16[4,2,32,1024]{3,2,1,0:T(8,128)(2,1)S(1)}, bf16[4,2,32,1024]{3,2,1,0:T(8,128)(2,1)S(1)}, u32[]{:S(2)}, u32[]{:S(2)}) collective-permute-start(bf16[4,2,32,1024]{3,2,1,0:T(8,128)(2,1)S(1)} %collective-permute-done.13.refs_4_), channel_id=1, source_target_pairs={{0,32},{32,0},{1,33},{33,1},{2,34},{34,2},{3,35},{35,3},{4,36},{36... | collective-permute-start | bytes 1572872 | tf_op jit(solution)/shard_map/ppermute | solution.py:405
  106.7 15.6 %copy-start.22 = (bf16[4,2,32,2048]{3,2,1,0:T(8,128)(2,1)}, bf16[4,2,32,2048]{3,2,1,0:T(8,128)(2,1)S(1)}, u32[]{:S(2)}) copy-start(bf16[4,2,32,2048]{3,2,1,0:T(8,128)(2,1)S(1)} %collective-permute-done.21.refs_15_) | copy-start | bytes 3145732
  106.7 20.4 %collective-permute-start.17 = (bf16[4,2,32,2048]{3,2,1,0:T(8,128)(2,1)}, bf16[4,2,32,2048]{3,2,1,0:T(8,128)(2,1)}, u32[]{:S(2)}, u32[]{:S(2)}) collective-permute-start(bf16[4,2,32,2048]{3,2,1,0:T(8,128)(2,1)} %collective-permute-done.8.refs_1_), channel_id=1, source_target_pairs={{0,32},{32,0},{1,33},{33,1},{2,34},{34,2},{3,35},{35,3},{4,36},{36... | collective-permute-start | bytes 3145736 | tf_op jit(solution)/shard_map/ppermute | solution.py:405
  119.7 2.7 %collective-permute-start.24 = (bf16[4,2,32,1024]{3,2,1,0:T(8,128)(2,1)S(1)}, bf16[4,2,32,1024]{3,2,1,0:T(8,128)(2,1)S(1)}, u32[]{:S(2)}, u32[]{:S(2)}) collective-permute-start(bf16[4,2,32,1024]{3,2,1,0:T(8,128)(2,1)S(1)} %collective-permute-done.14.refs_8_), channel_id=1, source_target_pairs={{0,32},{32,0},{1,33},{33,1},{2,34},{34,2},{3,35},{35,3},{4,36},{36... | collective-permute-start | bytes 1572872 | tf_op jit(solution)/shard_map/ppermute | solution.py:405
  119.7 7.4 %collective-permute-start.18 = (bf16[4,2,32,2048]{3,2,1,0:T(8,128)(2,1)}, bf16[4,2,32,2048]{3,2,1,0:T(8,128)(2,1)}, u32[]{:S(2)}, u32[]{:S(2)}) collective-permute-start(bf16[4,2,32,2048]{3,2,1,0:T(8,128)(2,1)} %collective-permute-done.9.refs_2_), channel_id=1, source_target_pairs={{0,32},{32,0},{1,33},{33,1},{2,34},{34,2},{3,35},{35,3},{4,36},{36... | collective-permute-start | bytes 3145736 | tf_op jit(solution)/shard_map/ppermute | solution.py:405
  120.2 0.8 copy-start.3
  121.0 6.2 %collective-permute-start.22 = (bf16[4,2,32,2048]{3,2,1,0:T(8,128)(2,1)}, bf16[4,2,32,2048]{3,2,1,0:T(8,128)(2,1)}, u32[]{:S(2)}, u32[]{:S(2)}) collective-permute-start(bf16[4,2,32,2048]{3,2,1,0:T(8,128)(2,1)} %collective-permute-done.10.refs_6_), channel_id=1, source_target_pairs={{0,32},{32,0},{1,33},{33,1},{2,34},{34,2},{3,35},{35,3},{4,36},{36... | collective-permute-start | bytes 3145736 | tf_op jit(solution)/shard_map/ppermute | solution.py:405
  121.1 0.8 copy-start.5
  121.9 5.3 %collective-permute-start.23 = (bf16[4,2,32,2048]{3,2,1,0:T(8,128)(2,1)}, bf16[4,2,32,2048]{3,2,1,0:T(8,128)(2,1)}, u32[]{:S(2)}, u32[]{:S(2)}) collective-permute-start(bf16[4,2,32,2048]{3,2,1,0:T(8,128)(2,1)} %collective-permute-done.11.refs_7_), channel_id=1, source_target_pairs={{0,32},{32,0},{1,33},{33,1},{2,34},{34,2},{3,35},{35,3},{4,36},{36... | collective-permute-start | bytes 3145736 | tf_op jit(solution)/shard_map/ppermute | solution.py:405
  122.3 0.8 copy-start.7
  123.1 4.0 %collective-permute-start.25 = (bf16[4,2,32,1024]{3,2,1,0:T(8,128)(2,1)}, bf16[4,2,32,1024]{3,2,1,0:T(8,128)(2,1)}, u32[]{:S(2)}, u32[]{:S(2)}) collective-permute-start(bf16[4,2,32,1024]{3,2,1,0:T(8,128)(2,1)} %collective-permute-done.15.refs_9_), channel_id=1, source_target_pairs={{0,32},{32,0},{1,33},{33,1},{2,34},{34,2},{3,35},{35,3},{4,36},{36... | collective-permute-start | bytes 1572872 | tf_op jit(solution)/shard_map/ppermute | solution.py:405
  127.2 1.1 copy-start.4
  128.3 1.0 copy-start.6
  129.4 1.0 copy-start.8
  164.2 37.5 %collective-permute-start.26 = (bf16[4,4,2,2,16,4096]{5,4,3,2,1,0:T(8,128)(2,1)}, bf16[4,4,2,2,16,4096]{5,4,3,2,1,0:T(8,128)(2,1)}, u32[]{:S(2)}, u32[]{:S(2)}) collective-permute-start(bf16[4,4,2,2,16,4096]{5,4,3,2,1,0:T(8,128)(2,1)} %bitcast.76), channel_id=1, source_target_pairs={{0,32},{32,0},{1,33},{33,1},{2,34},{34,2},{3,35},{35,3},{4,36},{36... | collective-permute-start | bytes 25165832 | tf_op jit(solution)/shard_map/ppermute | solution.py:405
  223.0 23.2 %all-to-all-start.1 = ((bf16[32,16,1024]{2,1,0:T(8,128)(2,1)}), bf16[32,16,1024]{2,1,0:T(8,128)(2,1)S(1)}, u32[]{:S(2)}, u32[]{:S(2)}) async-start(bf16[32,16,1024]{2,1,0:T(8,128)(2,1)} %bitcast.71), calls=%async_computation.1 | async-start | bytes 2097152 | tf_op jit(solution)/shard_map/all_to_all | solution.py:492
  246.2 1.0 copy-start.10
Sparse Core Ops, SparseCore 0:
  89.3 74.8 all-gather.4

commit v6 on v4

--- a/solution.py
+++ b/solution.py
@@ -19,7 +19,8 @@
 STEPS = WIDTH // PAIR
 SEQ = ("x", "yhi", "z")
 QKV_PART = 3 * WIDTH // 2
-PART = 2 * WIDTH
+OUT_PART = WIDTH // 2
+PART = QKV_PART + 2 * OUT_PART
 RELATIVE = ((0, 0, PART), (3, 0, PART), (1, 0, PART), (2, 0, PART // 2), (2, PART // 2, PART))
 STACKED = (0, 3, 1, 2)
 LOG2E = 1.4426950408889634
@@ -98,7 +99,7 @@
     )(core, x, gain)
 
 
-def start_copies(place_ref, pieces, sems, w_ref=None, o_ref=None):
+def start_copies(place_ref, pieces, sems, w_ref=None, o_ref=None, base=None):
     my_x, my_y = place_ref[1], place_ref[2]
 
     def block_of(part, stacked, ring):
@@ -114,18 +115,17 @@
             if outputs:
                 if high < PART:
                     continue
-                lanes, target = pl.ds(QKV_PART - low, PART - QKV_PART), None
+                lanes, target = pl.ds(base - low, OUT_PART), None
             else:
                 end = min(high, QKV_PART)
                 lanes, target = pl.ds(0, end - low), pl.ds(low, end - low)
             for k, stacked in enumerate(STACKED):
                 block = block_of(part, stacked, ring)
                 if outputs:
-                    width = PART - QKV_PART
-                    dst = o_ref.at[slot, block, :, :, pl.ds(part * width, width)]
+                    dst = o_ref.at[slot, block, :, :, pl.ds(part * OUT_PART, OUT_PART)]
                 else:
                     dst = w_ref.at[slot, part, block, :, :, target]
-                sem = sems.at[4 + slot if outputs else slot * 2 + part]
+                sem = sems.at[slot if outputs else slot * 2 + part]
                 pltpu.make_async_copy(src.at[k, :, :, lanes], dst, sem).start()
 
     for outputs, ref in ((False, w_ref), (True, o_ref)):
@@ -167,15 +167,24 @@
     return total
 
 
-def row_kernel(place_ref, x_ref, hid_ref, gain_ref, cos_ref, sin_ref, *refs):
-    pieces = refs[: 4 * len(RELATIVE)]
-    mid_ref, next_ref, w_ref, o_ref, att_ref, sems = refs[4 * len(RELATIVE) :]
-    core = place_ref[0]
-    start_copies(place_ref, pieces, sems, w_ref, o_ref)
+def row_kernel(hid_ref, cos_ref, sin_ref, own_plane, other_plane, out_ref, w_ref, sems):
     half = D // 2
+    triple = 3 * PAIR
+    for g in range(STEPS):
+        lanes = pl.ds(g * triple, triple)
+        for slot, plane in enumerate((own_plane, other_plane)):
+            for ylo in range(2):
+                for yhi in range(2):
+                    src = plane.at[:, :, ylo, yhi, :, lanes]
+                    dst = w_ref.at[g, slot, ylo, :, yhi]
+                    pltpu.make_async_copy(src, dst, sems.at[g]).start()
 
     def step(g, _):
-        weight = step_weights(w_ref, sems, g)
+        arrived(w_ref.at[g], sems.at[g])
+
+        def weight(slot, kind):
+            lanes = slice(kind * PAIR, (kind + 1) * PAIR)
+            return w_ref[g, slot, :, :, :, :, :, lanes].reshape(half, PAIR)
 
         def projected(kind):
             return dot(hid_ref[:, :half], weight(0, kind)) + dot(hid_ref[:, half:], weight(1, kind))
@@ -195,12 +204,41 @@
                 row = lax.broadcasted_iota(jnp.int32, scores.shape, 0) + b * size
                 keep = lax.broadcasted_iota(jnp.int32, scores.shape, 1) <= row
                 target = pl.ds(pl.multiple_of(g * PAIR + h * HEAD, HEAD), HEAD)
-                att_ref[b * size : end, target] = softmax_times(scores, keep, v[:end]).astype(jnp.bfloat16)
+                out_ref[b * size : end, target] = softmax_times(scores, keep, v[:end]).astype(jnp.bfloat16)
         return 0
 
     lax.fori_loop(0, STEPS, step, 0)
+
+
+def row_layer(hidden, tables, planes):
+    vmem = pl.BlockSpec(memory_space=pltpu.VMEM)
+    hbm = pl.BlockSpec(memory_space=pltpu.HBM)
+    return pl.pallas_call(
+        row_kernel,
+        out_shape=jax.ShapeDtypeStruct((C, WIDTH), jnp.bfloat16),
+        in_specs=[vmem] * 3 + [hbm] * 2,
+        out_specs=vmem,
+        scratch_shapes=[
+            pltpu.VMEM((STEPS, 2, 2, 4, 2, 4, 16, 3 * PAIR), jnp.bfloat16),
+            pltpu.SemaphoreType.DMA((STEPS,)),
+        ],
+        compiler_params=pltpu.CompilerParams(vmem_limit_bytes=56 * MIB),
+        cost_estimate=pl.CostEstimate(
+            flops=2 * C * D * 3 * WIDTH + 4 * C * C * WIDTH,
+            bytes_accessed=2 * (C * D + 3 * D * WIDTH + C * WIDTH),
+            transcendentals=C * C * HEADS,
+        ),
+    )(hidden, *tables, *planes)
+
+
+def middle_kernel(place_ref, att_ref, x_ref, gain_ref, *refs):
+    pieces = refs[: 4 * len(RELATIVE)]
+    mid_ref, next_ref, o_ref, sems = refs[4 * len(RELATIVE) :]
+    core = place_ref[0]
+    half = D // 2
+    start_copies(place_ref, pieces, sems, o_ref=o_ref, base=QKV_PART + OUT_PART)
     for slot in range(2):
-        arrived(o_ref.at[slot], sems.at[4 + slot])
+        arrived(o_ref.at[slot], sems.at[slot])
 
     def finish(i, _):
         rows = pl.ds(pl.multiple_of(i * 128, 128), 128)
@@ -223,30 +261,26 @@
     lax.fori_loop(0, C // 128, finish, 0)
 
 
-def row_layer(place, x, hidden, gain, tables, pieces):
+def middle_layer(place, attended, x, gain, pieces):
     vmem = pl.BlockSpec(memory_space=pltpu.VMEM)
     hbm = pl.BlockSpec(memory_space=pltpu.HBM)
     shape = jax.ShapeDtypeStruct((C, D), jnp.bfloat16)
     return pl.pallas_call(
-        row_kernel,
+        middle_kernel,
         out_shape=[shape, shape],
-        in_specs=[pl.BlockSpec(memory_space=pltpu.SMEM)]
-        + [vmem] * 5
-        + [hbm] * len(pieces),
+        in_specs=[pl.BlockSpec(memory_space=pltpu.SMEM)] + [vmem] * 3 + [hbm] * len(pieces),
         out_specs=[vmem, vmem],
         scratch_shapes=[
-            pltpu.VMEM((2, 2, 16, 2, 32, QKV_PART), jnp.bfloat16),
             pltpu.VMEM((2, 16, 2, 32, D // 2), jnp.bfloat16),
-            pltpu.VMEM((C, WIDTH), jnp.bfloat16),
-            pltpu.SemaphoreType.DMA((6,)),
+            pltpu.SemaphoreType.DMA((2,)),
         ],
-        compiler_params=pltpu.CompilerParams(vmem_limit_bytes=48 * MIB),
+        compiler_params=pltpu.CompilerParams(vmem_limit_bytes=54 * MIB),
         cost_estimate=pl.CostEstimate(
-            flops=2 * C * D * 4 * WIDTH + 4 * C * C * WIDTH,
-            bytes_accessed=2 * (4 * C * D + 4 * D * WIDTH),
-            transcendentals=C * C * HEADS,
+            flops=2 * C * D * WIDTH,
+            bytes_accessed=2 * (3 * C * D + D * WIDTH + C * WIDTH),
+            transcendentals=0,
         ),
-    )(place, x, hidden, gain, *tables, *pieces)
+    )(place, attended, x, gain, *pieces)
 
 
 def column_kernel(place_ref, x_ref, cos_ref, sin_ref, *refs):
@@ -316,7 +350,7 @@
             pltpu.VMEM((C, D), jnp.bfloat16),
             pltpu.SemaphoreType.DMA((4,)),
         ],
-        compiler_params=pltpu.CompilerParams(vmem_limit_bytes=40 * MIB),
+        compiler_params=pltpu.CompilerParams(vmem_limit_bytes=56 * MIB),
         cost_estimate=pl.CostEstimate(
             flops=2 * C * D * 3 * WIDTH + 4 * C * C * WIDTH,
             bytes_accessed=2 * (C * D + 3 * D * WIDTH + C * WIDTH),
@@ -333,9 +367,9 @@
 
     @pl.when(pl.program_id(0) == 0)
     def _():
-        start_copies(place_ref, pieces, sems, o_ref=o_ref)
+        start_copies(place_ref, pieces, sems, o_ref=o_ref, base=QKV_PART)
         for slot in range(2):
-            arrived(o_ref.at[slot], sems.at[4 + slot])
+            arrived(o_ref.at[slot], sems.at[slot])
 
     for h in range(2):
         lanes = slice(h * half, (h + 1) * half)
@@ -355,10 +389,10 @@
         out_specs=block(D),
         scratch_shapes=[
             pltpu.VMEM((2, 16, 2, 32, D // 2), jnp.bfloat16),
-            pltpu.SemaphoreType.DMA((6,)),
+            pltpu.SemaphoreType.DMA((2,)),
         ],
         compiler_params=pltpu.CompilerParams(
-            dimension_semantics=("arbitrary",), vmem_limit_bytes=24 * MIB
+            dimension_semantics=("arbitrary",), vmem_limit_bytes=54 * MIB
         ),
         cost_estimate=pl.CostEstimate(
             flops=2 * C * D * WIDTH,
@@ -402,17 +436,23 @@
     return inputs.reshape(-1, 3, STEPS, PAIR).transpose(0, 2, 1, 3).reshape(-1, 3 * WIDTH)
 
 
-def lines(inputs, output):
-    shard = jnp.concatenate([by_step(inputs), fold_output(output)], 1)
+def lines(inputs, *outputs):
+    shard = jnp.concatenate([by_step(inputs)] + [fold_output(output) for output in outputs], 1)
     rows = lax.all_gather(shard, "z", axis=0)
     qkv = rows[:, :, : 3 * WIDTH].reshape(2, 32, 3 * WIDTH)
-    out = rows[:, :, 3 * WIDTH :].reshape(4, 2, 8, WIDTH).transpose(1, 0, 2, 3).reshape(2, 32, WIDTH)
+    outs = rows[:, :, 3 * WIDTH :].reshape(4, 2, 8, len(outputs), WIDTH).transpose(3, 1, 0, 2, 4)
+    outs = outs.reshape(len(outputs), 2, 32, WIDTH)
     parts = []
     for p in range(2):
         lanes = slice(p * QKV_PART, (p + 1) * QKV_PART)
-        rest = slice(p * WIDTH // 2, (p + 1) * WIDTH // 2)
-        parts.append(jnp.concatenate([qkv[:, :, lanes], out[:, :, rest]], -1))
+        rest = slice(p * OUT_PART, (p + 1) * OUT_PART)
+        parts.append(jnp.concatenate([qkv[:, :, lanes]] + [out[:, :, rest] for out in outs], -1))
     return parts
+
+
+def row_plane(inputs):
+    line = lax.all_gather(by_step(inputs), ("ylo", "yhi"), axis=0)
+    return line, lax.all_gather(line, ("x", "z"), axis=0).reshape(4, 4, 2, 2, 16, 3 * WIDTH)
 
 
 def inner_rings(parts):
@@ -428,10 +468,9 @@
     return [forwards(hop, axis) for hop, axis in zip(hops, "yx")]
 
 
-def both_cores(parts, swapped):
+def both_cores(parts):
     own = [piece for part in parts for piece in part]
-    other = [swapped[index] if index in swapped else swap(piece) for index, piece in enumerate(own)]
-    return own + other
+    return own + [swap(piece) for piece in own]
 
 
 def shards(tokens, gain_first, inputs_first, output_first, gain_second, inputs_second, output_second, starts, band_edges):
@@ -452,20 +491,20 @@
 
     hidden = normed_slots(core_scalar, residual, gain_first.reshape(1, D))
 
-    first = inner_rings(lines(inputs_first, output_first))
-    first, hidden, row_tables, column_tables = lax.optimization_barrier((first, hidden, row_tables, column_tables))
-    first_hop = outer_hops(first)
-    swapped = {0: swap(first[0]), 5: swap(first[1])}
-    inputs_second, output_second, swapped = lax.optimization_barrier((inputs_second, output_second, swapped))
-    second = lines(inputs_second, output_second)
-    pieces = both_cores(outer_forwards(first_hop), swapped)
-    second = inner_rings(second)
-    second, place = lax.optimization_barrier((second, place))
-    second_hop = outer_hops(second)
-
-    middle, hidden = row_layer(place, residual, hidden, gain_second.reshape(1, D), row_tables, pieces)
-    second_hop, hidden = lax.optimization_barrier((second_hop, hidden))
-    pieces = both_cores(outer_forwards(second_hop), {})
+    line, plane = row_plane(inputs_first)
+    output_first, output_second, inputs_second, line = lax.optimization_barrier(
+        (output_first, output_second, inputs_second, line)
+    )
+    stacks = inner_rings(lines(inputs_second, output_second, output_first))
+    hops = outer_hops(stacks)
+    plane, hidden, row_tables, column_tables, _ = lax.optimization_barrier(
+        (plane, hidden, row_tables, column_tables, hops)
+    )
+    planes = (plane, swap(plane))
+    pieces = both_cores(outer_forwards(hops))
+
+    attended = row_layer(hidden, row_tables, planes)
+    middle, hidden = middle_layer(place, attended, residual, gain_second.reshape(1, D), pieces)
     hidden = lax.all_to_all(hidden, SEQ, split_axis=0, concat_axis=0, tiled=True)
     attended = column_layer(place, hidden, column_tables, pieces)
     attended = lax.all_to_all(attended, SEQ, split_axis=0, concat_axis=0, tiled=True)

time: 274 us -> 275 us (level)
  blocking collectives: 60.7 us -> 90.7 us
  starting transfers between devices: 56.1 us -> 26.8 us
  local copies, waits for them, and re-layouts: 35.9 us -> 11.4 us
  between operations: 2.29 us -> 15.1 us
  waiting for transfers between devices: 51.6 us -> 61.1 us
  Pallas kernels: 54.2 us -> 61.5 us
  other arithmetic: 12 us -> 6.78 us
    all_to_all x0 -> x1, blocking collectives: none -> 37.8 us  [shards(): lax.all_to_all(hidden, SEQ, split_axis=0, concat_axis=0, tiled=True)]
    ppermute x16 -> x8, waiting for transfers between devices: 12 us -> 41.9 us  [shift(): return lax.ppermute(value, axis, [(i, (i + by) % 4) for i in range(4)])]
    unnamed x114 -> x36, local copies, waits for them, and re-layouts: 18.3 us -> 2.86 us
    all_gather x0 -> x1, blocking collectives: none -> 15.2 us  [row_plane(): line = lax.all_gather(by_step(inputs), ('ylo', 'yhi'), axis=0)]
    all_to_all x1 -> x0, waiting for transfers between devices: 14.5 us -> none  [shards(): lax.all_to_all(hidden, SEQ, split_axis=0, concat_axis=0, tiled=True)]
    all_gather x2 -> x1, blocking collectives: 27.3 us -> 14.9 us  [lines(): rows = lax.all_gather(shard, 'z', axis=0)]
    all_to_all x1, blocking collectives: 33.4 us -> 22.8 us  [shards(): lax.all_to_all(attended, SEQ, split_axis=0, concat_axis=0, tiled=True)]
    all_to_all x1 -> x0, starting transfers between devices: 10.2 us -> none  [shards(): lax.all_to_all(hidden, SEQ, split_axis=0, concat_axis=0, tiled=True)]
  transfers between devices with their start and end apart: 53 -> 28, of which waited for: 12 -> 11; matrix products, arithmetic and copies ran while one was open for 9% -> 5% of each run, Pallas kernels for 10% -> 7%
where the time goes in v6:
time: 275 us; the launch traced here: 273 us
  blocking collectives  90.7 us (33%)
  Pallas kernels  61.5 us (22%)
  waiting for transfers between devices  61.1 us (22%)
  starting transfers between devices  26.8 us (10%)
  between operations  15.1 us (5%)
  local copies, waits for them, and re-layouts  11.4 us (4%)
  other arithmetic  6.78 us (2%)
    ppermute x8, waiting for transfers between devices, shift(): return lax.ppermute(value, axis, [(i, (i + by) % 4) for i in range(4)])  41.9 us
    all_to_all x1, blocking collectives, shards(): lax.all_to_all(hidden, SEQ, split_axis=0, concat_axis=0, tiled=True)  37.8 us
    pallas_call x1, Pallas kernels, column_layer(): pl.pallas_call(column_kernel, out_shape=jax.ShapeDtypeStruct((C, WIDTH),...  23.4 us
    all_to_all x1, blocking collectives, shards(): lax.all_to_all(attended, SEQ, split_axis=0, concat_axis=0, tiled=True)  22.8 us
    pallas_call x1, Pallas kernels, row_layer(): pl.pallas_call(row_kernel, out_shape=jax.ShapeDtypeStruct((C, WIDTH), jnp...  18.3 us
    all_gather x1, blocking collectives, row_plane(): line = lax.all_gather(by_step(inputs), ('ylo', 'yhi'), axis=0)  15.2 us
    all_gather x1, blocking collectives, lines(): rows = lax.all_gather(shard, 'z', axis=0)  14.9 us
    ppermute x8, waiting for transfers between devices, shift(): lax.ppermute(value, ('ylo', 'yhi'), [(where(y), where((y + by) % 4)) for...  14 us
  transfers between devices with their start and end apart: 28, of which 11 were waited for; matrix products, arithmetic and copies ran while one was open for 5% of the time, Pallas kernels for 7%

profile of v6, /device:TPU:0, one launch (start us, length us, event | category | flops | bytes accessed | tf_op | source)
XLA Modules:
  0.0 273.4 jit_solution(2695970728309398205)
XLA Ops:
  6.5 1.0 reshape.77
  7.6 0.1 all_gather_reshape.3
  7.7 15.2 %all_gather.15 = bf16[4,16,3072]{2,1,0:T(8,128)(2,1)} all-gather(bf16[1,16,3072]{2,1,0:T(8,128)(2,1)S(1)} %all_gather_reshape.3), channel_id=1, replica_groups=mesh['ylo'=2,'core'=2,'x'=4,'yhi'=2,'z'=4] {'ylo','yhi'}, dimensions={0}, use_global_device_ids=true | all-gather | bytes 491520 | tf_op jit(solution)/shard_map/all_gather | solution.py:454
  23.0 0.1 reshape.81
  23.2 14.9 %all-gather.1 = bf16[64,5120]{1,0:T(8,128)(2,1)S(1)} all-gather(bf16[16,5120]{1,0:T(8,128)(2,1)S(1)} %maximum_maximum_fusion), channel_id=3, replica_groups=mesh['ylo'=2,'core'=2,'x'=4,'yhi'=2,'z'=4] {'z'}, dimensions={0}, use_global_device_ids=true | all-gather | bytes 819200 | tf_op jit(solution)/shard_map/all_gather | solution.py:441
  38.2 0.2 reshape.83
  38.4 0.5 fusion.9
  39.1 0.8 collective-permute-start.6
  39.9 2.5 collective-permute-start.7
  42.4 1.6 collective-permute-start
  44.0 1.7 collective-permute-start.1
  45.7 3.5 %collective-permute-done.6 = bf16[2,32,2560]{2,1,0:T(8,128)(2,1)S(1)} collective-permute-done((bf16[2,32,2560]{2,1,0:T(8,128)(2,1)S(1)}, bf16[2,32,2560]{2,1,0:T(8,128)(2,1)S(1)}, u32[]{:S(2)}, u32[]{:S(2)}) %collective-permute-start.6) | collective-permute-done | bytes 327712 | tf_op jit(solution)/shard_map/ppermute | solution.py:408
  49.3 3.3 %collective-permute-start.9 = (bf16[2,32,1280]{2,1,0:T(8,128)(2,1)S(1)}, bf16[2,32,1280]{2,1,0:T(8,128)(2,1)S(1)}, u32[]{:S(2)}, u32[]{:S(2)}) collective-permute-start(bf16[2,32,1280]{2,1,0:T(8,128)(2,1)S(1)} %slice.101), channel_id=1, source_target_pairs={{0,68},{64,0},{4,64},{68,4},{1,69},{65,1},{5,65},{69,5},{2,70},{66... | collective-permute-start | bytes 491528 | tf_op jit(solution)/shard_map/ppermute | solution.py:408
  52.6 0.6 collective-permute-done
  53.2 1.1 collective-permute-start.2
  54.3 2.3 collective-permute-start.3
  56.6 0.2 pad_maximum_fusion.1.refs_5_
  56.8 0.7 collective-permute-start.10
  57.6 2.6 collective-permute-start.11
  60.1 1.5 collective-permute-done.2
  61.6 1.3 collective-permute-done.3
  63.0 1.2 pad_maximum_fusion.refs_0_
  64.3 3.9 %collective-permute-start.4 = (bf16[4,2,32,2560]{3,2,1,0:T(8,128)(2,1)}, bf16[4,2,32,2560]{3,2,1,0:T(8,128)(2,1)}, u32[]{:S(2)}, u32[]{:S(2)}) collective-permute-start(bf16[4,2,32,2560]{3,2,1,0:T(8,128)(2,1)} %pad_maximum_fusion.refs_0_), channel_id=1, source_target_pairs={{0,64},{64,4},{4,68},{68,0},{1,65},{65,5},{5,69},{69,1},{2,66},{66... | collective-permute-start | bytes 3932168 | tf_op jit(solution)/shard_map/ppermute | solution.py:408
  68.1 0.6 constant_dynamic-slice_fusion
  68.8 0.1 add_convert_fusion
  68.8 0.1 convert_element_type.35
  68.9 0.6 fusion.14
  70.7 2.1 shard_map.91.hid_ref
  72.9 0.6 add_convert_fusion.1
  73.5 1.9 fusion.4
  75.5 1.0 pad_maximum_fusion.6
  76.5 1.0 pad_maximum_fusion.4
  77.5 33.1 %collective-permute-done.10.refs_6_ = bf16[4,2,32,2560]{3,2,1,0:T(8,128)(2,1)} collective-permute-done((bf16[4,2,32,2560]{3,2,1,0:T(8,128)(2,1)S(1)}, bf16[4,2,32,2560]{3,2,1,0:T(8,128)(2,1)}, u32[]{:S(2)}, u32[]{:S(2)}) %collective-permute-start.10) | collective-permute-done | bytes 1310752 | tf_op jit(solution)/shard_map/ppermute | solution.py:409
  110.6 0.1 collective-permute-start.12
  110.7 0.5 collective-permute-start.22
  111.2 0.1 collective-permute-start.17
  111.3 1.1 slice.104
  112.6 1.1 slice.105
  113.7 3.3 %collective-permute-start.16 = (bf16[4,2,32,1280]{3,2,1,0:T(8,128)(2,1)S(1)}, bf16[4,2,32,1280]{3,2,1,0:T(8,128)(2,1)S(1)}, u32[]{:S(2)}, u32[]{:S(2)}) collective-permute-start(bf16[4,2,32,1280]{3,2,1,0:T(8,128)(2,1)S(1)} %slice.105), channel_id=1, source_target_pairs={{0,24},{8,0},{16,8},{24,16},{1,25},{9,1},{17,9},{25,17},{2,26},{10... | collective-permute-start | bytes 1966088 | tf_op jit(solution)/shard_map/ppermute | solution.py:409
  117.0 1.1 slice.102
  118.1 2.2 collective-permute-done.22.refs_15_
  120.3 1.6 slice.103
  121.9 3.0 %collective-permute-done.17.refs_10_ = bf16[4,2,32,2560]{3,2,1,0:T(8,128)(2,1)} collective-permute-done((bf16[4,2,32,2560]{3,2,1,0:T(8,128)(2,1)}, bf16[4,2,32,2560]{3,2,1,0:T(8,128)(2,1)}, u32[]{:S(2)}, u32[]{:S(2)}) %collective-permute-start.17) | collective-permute-done | bytes 1310752 | tf_op jit(solution)/shard_map/ppermute | solution.py:428
  125.0 1.0 collective-permute-start.14
  126.0 4.9 %collective-permute-done.15.refs_8_ = bf16[4,2,32,1280]{3,2,1,0:T(8,128)(2,1)S(1)} collective-permute-done((bf16[4,2,32,1280]{3,2,1,0:T(8,128)(2,1)S(1)}, bf16[4,2,32,1280]{3,2,1,0:T(8,128)(2,1)S(1)}, u32[]{:S(2)}, u32[]{:S(2)}) %collective-permute-start.15) | collective-permute-done | bytes 655392 | tf_op jit(solution)/shard_map/ppermute | solution.py:409
  130.8 0.5 collective-permute-done.16.refs_9_
  131.3 7.2 %collective-permute-done.13.refs_3_ = bf16[4,2,32,1280]{3,2,1,0:T(8,128)(2,1)S(1)} collective-permute-done((bf16[4,2,32,1280]{3,2,1,0:T(8,128)(2,1)S(1)}, bf16[4,2,32,1280]{3,2,1,0:T(8,128)(2,1)S(1)}, u32[]{:S(2)}, u32[]{:S(2)}) %collective-permute-start.13) | collective-permute-done | bytes 655392 | tf_op jit(solution)/shard_map/ppermute | solution.py:408
  138.6 3.3 %collective-permute-done.14.refs_4_ = bf16[4,2,32,1280]{3,2,1,0:T(8,128)(2,1)} collective-permute-done((bf16[4,2,32,1280]{3,2,1,0:T(8,128)(2,1)S(1)}, bf16[4,2,32,1280]{3,2,1,0:T(8,128)(2,1)}, u32[]{:S(2)}, u32[]{:S(2)}) %collective-permute-start.14) | collective-permute-done | bytes 655392 | tf_op jit(solution)/shard_map/ppermute | solution.py:408
  141.9 0.6 collective-permute-start.24
  142.5 0.1 collective-permute-start.18
  142.6 0.2 copy-done.9
  142.7 0.6 copy-done.10
  143.3 0.8 copy-done.11
  144.1 0.1 collective-permute-start.19
  144.3 0.6 pad_add_fusion.place_ref
  144.8 0.4 collective-permute-start.21
  145.2 18.3 %shard_map.92.att_ref = bf16[512,1024]{1,0:T(8,128)(2,1)} custom-call(bf16[512,2048]{1,0:T(8,128)(2,1)} %copy-done.1, f32[512,128]{1,0:T(8,128)} %get-tuple-element.20.cos_ref, f32[512,128]{1,0:T(8,128)} %get-tuple-element.21.sin_ref, bf16[4,4,2,2,16,3072]{5,4,3,2,1,0:T(8,128)(2,1)} %bitcast.65, ...), custom_call_target="tpu_custom_call" | custom-call | flops 7516192768 | bytes 15728640 | tf_op jit(solution)/shard_map/pallas_call | solution.py:216
  163.6 0.8 copy-done.12
  164.4 0.5 copy-done.5
  164.8 9.8 %shard_map.93 = (bf16[512,2048]{1,0:T(8,128)(2,1)}, bf16[512,2048]{1,0:T(8,128)(2,1)}) custom-call(s32[3]{0:T(128)} %pad_add_fusion.place_ref, bf16[512,1024]{1,0:T(8,128)(2,1)} %shard_map.92.att_ref, bf16[512,2048]{1,0:T(8,128)(2,1)} %bitcast.43, f32[1,2048]{1,0:T(1,128)} %bitcast.62, bf16[4,2,32,2560]{3,2,1,0:T(8,128)(2,1)} %pad_maximum_fusion.refs_0_, ...), custom_call_target="tpu_custom_call" | custom-call | flops 2147483648 | bytes 11534336 | tf_op jit(solution)/shard_map/pallas_call | solution.py:268
  174.7 37.8 %all_to_all.22 = bf16[32,16,2048]{2,1,0:T(8,128)(2,1)} all-to-all(bf16[32,16,2048]{2,1,0:T(8,128)(2,1)} %bitcast.50), channel_id=1, replica_groups=mesh['ylo'=2,'core'=2,'x'=4,'yhi'=2,'z'=4] {'x','yhi','z'}, dimensions={0} | all-to-all | bytes 4194304 | tf_op jit(solution)/shard_map/all_to_all | solution.py:508
  212.5 23.4 %shard_map.94 = bf16[512,1024]{1,0:T(8,128)(2,1)} custom-call(s32[3]{0:T(128)} %pad_add_fusion.place_ref, bf16[512,2048]{1,0:T(8,128)(2,1)} %bitcast.51, f32[512,128]{1,0:T(8,128)} %get-tuple-element.24.cos_ref, f32[512,128]{1,0:T(8,128)} %get-tuple-element.25.sin_ref, bf16[4,2,32,2560]{3,2,1,0:T(8,128)(2,1)} %pad_maximum_fusion.refs_0_, ...), custom_call_target="tpu_custom_call" | custom-call | flops 7516192768 | bytes 15728640 | tf_op jit(solution)/shard_map/pallas_call | solution.py:343
  235.9 22.8 %all_to_all.23 = bf16[32,16,1024]{2,1,0:T(8,128)(2,1)} all-to-all(bf16[32,16,1024]{2,1,0:T(8,128)(2,1)} %bitcast.53), channel_id=1, replica_groups=mesh['ylo'=2,'core'=2,'x'=4,'yhi'=2,'z'=4] {'x','yhi','z'}, dimensions={0} | all-to-all | bytes 2097152 | tf_op jit(solution)/shard_map/all_to_all | solution.py:510
  258.8 7.8 %shard_map.95 = bf16[512,2048]{1,0:T(8,128)(2,1)} custom-call(s32[3]{0:T(128)} %pad_add_fusion.place_ref, bf16[512,1024]{1,0:T(8,128)(2,1)} %bitcast.46, bf16[512,2048]{1,0:T(8,128)(2,1)} %get-tuple-element.26.x_ref, bf16[4,2,32,2560]{3,2,1,0:T(8,128)(2,1)} %pad_maximum_fusion.refs_0_, bf16[4,2,32,2560]{3,2,1,0:T(8,128)(2,1)} %collective-permute-done.4.refs_1_, ...), custom_call_target="tpu_custom_call" | custom-call | flops 2147483648 | bytes 9437184 | tf_op jit(solution)/shard_map/pallas_call | solution.py:384
  (80 shorter events, 0.9 us)
Async XLA Ops:
  6.5 16.6 %copy-start.15 = (bf16[8,2048]{1,0:T(8,128)(2,1)S(1)}, bf16[8,2048]{1,0:T(8,128)(2,1)}, u32[]{:S(2)}) copy-start(bf16[8,2048]{1,0:T(8,128)(2,1)} %param.12) | copy-start | bytes 98308
  6.5 16.4 %copy-start.13 = (bf16[16,3072]{1,0:T(8,128)(2,1)S(1)}, bf16[16,3072]{1,0:T(8,128)(2,1)}, u32[]{:S(2)}) copy-start(bf16[16,3072]{1,0:T(8,128)(2,1)} %param.14) | copy-start | bytes 294916
  6.5 16.6 %copy-start.14 = (bf16[8,2048]{1,0:T(8,128)(2,1)S(1)}, bf16[8,2048]{1,0:T(8,128)(2,1)}, u32[]{:S(2)}) copy-start(bf16[8,2048]{1,0:T(8,128)(2,1)} %param.15) | copy-start | bytes 98308
  6.5 104.1 %all-gather.4.cloned.1.call-start = ((), (), s32[]{:S(2)}) async-start(), calls=%async_computation.2 | async-start | bytes 6684672 | tf_op jit(solution)/shard_map/all_gather | solution.py:455
  39.1 10.1 %collective-permute-start.6 = (bf16[2,32,2560]{2,1,0:T(8,128)(2,1)S(1)}, bf16[2,32,2560]{2,1,0:T(8,128)(2,1)S(1)}, u32[]{:S(2)}, u32[]{:S(2)}) collective-permute-start(bf16[2,32,2560]{2,1,0:T(8,128)(2,1)S(1)} %get-tuple-element.30), channel_id=1, source_target_pairs={{0,64},{64,4},{4,68},{68,0},{1,65},{65,5},{5,69},{69,1},{2,66},{66... | collective-permute-start | bytes 983048 | tf_op jit(solution)/shard_map/ppermute | solution.py:408
  39.9 9.4 %collective-permute-start.7 = (bf16[2,32,2560]{2,1,0:T(8,128)(2,1)S(1)}, bf16[2,32,2560]{2,1,0:T(8,128)(2,1)S(1)}, u32[]{:S(2)}, u32[]{:S(2)}) collective-permute-start(bf16[2,32,2560]{2,1,0:T(8,128)(2,1)S(1)} %get-tuple-element.30), channel_id=1, source_target_pairs={{0,68},{64,0},{4,64},{68,4},{1,69},{65,1},{5,65},{69,5},{2,70},{66... | collective-permute-start | bytes 983048 | tf_op jit(solution)/shard_map/ppermute | solution.py:408
  42.4 10.8 %collective-permute-start = (bf16[2,32,2560]{2,1,0:T(8,128)(2,1)S(1)}, bf16[2,32,2560]{2,1,0:T(8,128)(2,1)S(1)}, u32[]{:S(2)}, u32[]{:S(2)}) collective-permute-start(bf16[2,32,2560]{2,1,0:T(8,128)(2,1)S(1)} %get-tuple-element.32), channel_id=1, source_target_pairs={{0,8},{8,16},{16,24},{24,0},{1,9},{9,17},{17,25},{25,1},{2,10},{10... | collective-permute-start | bytes 983048 | tf_op jit(solution)/shard_map/ppermute | solution.py:409
  44.0 10.3 %collective-permute-start.1 = (bf16[2,32,2560]{2,1,0:T(8,128)(2,1)S(1)}, bf16[2,32,2560]{2,1,0:T(8,128)(2,1)S(1)}, u32[]{:S(2)}, u32[]{:S(2)}) collective-permute-start(bf16[2,32,2560]{2,1,0:T(8,128)(2,1)S(1)} %get-tuple-element.32), channel_id=1, source_target_pairs={{0,24},{8,0},{16,8},{24,16},{1,25},{9,1},{17,9},{25,17},{2,26},{10... | collective-permute-start | bytes 983048 | tf_op jit(solution)/shard_map/ppermute | solution.py:409
  49.2 7.4 %collective-permute-start.8 = (bf16[2,32,1280]{2,1,0:T(8,128)(2,1)S(1)}, bf16[2,32,1280]{2,1,0:T(8,128)(2,1)S(1)}, u32[]{:S(2)}, u32[]{:S(2)}) collective-permute-start(bf16[2,32,1280]{2,1,0:T(8,128)(2,1)S(1)} %slice.100), channel_id=1, source_target_pairs={{0,64},{64,4},{4,68},{68,0},{1,65},{65,5},{5,69},{69,1},{2,66},{66... | collective-permute-start | bytes 491528 | tf_op jit(solution)/shard_map/ppermute | solution.py:408
  49.3 7.3 %collective-permute-start.9 = (bf16[2,32,1280]{2,1,0:T(8,128)(2,1)S(1)}, bf16[2,32,1280]{2,1,0:T(8,128)(2,1)S(1)}, u32[]{:S(2)}, u32[]{:S(2)}) collective-permute-start(bf16[2,32,1280]{2,1,0:T(8,128)(2,1)S(1)} %slice.101), channel_id=1, source_target_pairs={{0,68},{64,0},{4,64},{68,4},{1,69},{65,1},{5,65},{69,5},{2,70},{66... | collective-permute-start | bytes 491528 | tf_op jit(solution)/shard_map/ppermute | solution.py:408
  53.2 8.4 %collective-permute-start.2 = (bf16[2,32,1280]{2,1,0:T(8,128)(2,1)S(1)}, bf16[2,32,1280]{2,1,0:T(8,128)(2,1)S(1)}, u32[]{:S(2)}, u32[]{:S(2)}) collective-permute-start(bf16[2,32,1280]{2,1,0:T(8,128)(2,1)S(1)} %slice.95), channel_id=1, source_target_pairs={{0,8},{8,16},{16,24},{24,0},{1,9},{9,17},{17,25},{25,1},{2,10},{10... | collective-permute-start | bytes 491528 | tf_op jit(solution)/shard_map/ppermute | solution.py:409
  54.3 8.7 %collective-permute-start.3 = (bf16[2,32,1280]{2,1,0:T(8,128)(2,1)S(1)}, bf16[2,32,1280]{2,1,0:T(8,128)(2,1)S(1)}, u32[]{:S(2)}, u32[]{:S(2)}) collective-permute-start(bf16[2,32,1280]{2,1,0:T(8,128)(2,1)S(1)} %slice.96), channel_id=1, source_target_pairs={{0,24},{8,0},{16,8},{24,16},{1,25},{9,1},{17,9},{25,17},{2,26},{10... | collective-permute-start | bytes 491528 | tf_op jit(solution)/shard_map/ppermute | solution.py:409
  56.8 53.9 %copy-start.3 = (bf16[4,2,32,2560]{3,2,1,0:T(8,128)(2,1)}, bf16[4,2,32,2560]{3,2,1,0:T(8,128)(2,1)S(1)}, u32[]{:S(2)}) copy-start(bf16[4,2,32,2560]{3,2,1,0:T(8,128)(2,1)S(1)} %pad_maximum_fusion.1.refs_5_) | copy-start | bytes 3932164
  56.8 53.8 %collective-permute-start.10 = (bf16[4,2,32,2560]{3,2,1,0:T(8,128)(2,1)S(1)}, bf16[4,2,32,2560]{3,2,1,0:T(8,128)(2,1)}, u32[]{:S(2)}, u32[]{:S(2)}) collective-permute-start(bf16[4,2,32,2560]{3,2,1,0:T(8,128)(2,1)S(1)} %pad_maximum_fusion.1.refs_5_), channel_id=1, source_target_pairs={{0,8},{8,16},{16,24},{24,0},{1,9},{9,17},{17,25},{25,1},{2,10},{10... | collective-permute-start | bytes 3932168 | tf_op jit(solution)/shard_map/ppermute | solution.py:409
  57.6 53.0 %collective-permute-start.11 = (bf16[4,2,32,2560]{3,2,1,0:T(8,128)(2,1)S(1)}, bf16[4,2,32,2560]{3,2,1,0:T(8,128)(2,1)}, u32[]{:S(2)}, u32[]{:S(2)}) collective-permute-start(bf16[4,2,32,2560]{3,2,1,0:T(8,128)(2,1)S(1)} %pad_maximum_fusion.1.refs_5_), channel_id=1, source_target_pairs={{0,24},{8,0},{16,8},{24,16},{1,25},{9,1},{17,9},{25,17},{2,26},{10... | collective-permute-start | bytes 3932168 | tf_op jit(solution)/shard_map/ppermute | solution.py:409
  63.0 5.1 %copy-start.17 = (s32[1,32]{1,0:T(1,128)S(1)}, s32[1,32]{1,0:T(1,128)}, u32[]{:S(2)}) copy-start(s32[1,32]{1,0:T(1,128)} %param.16) | copy-start | bytes 388
  63.0 5.9 %copy-start.16 = (s32[2]{0:T(128)S(1)}, s32[2]{0:T(128)}, u32[]{:S(2)}) copy-start(s32[2]{0:T(128)} %param.17) | copy-start | bytes 28
  63.0 7.7 %copy-start = (bf16[1,512,2048]{2,1,0:T(8,128)(2,1)S(1)}, bf16[1,512,2048]{2,1,0:T(8,128)(2,1)}, u32[]{:S(2)}) copy-start(bf16[1,512,2048]{2,1,0:T(8,128)(2,1)} %param.9) | copy-start | bytes 6291460
  63.0 7.7 %copy-start.2 = (f32[2048]{0:T(1024)S(1)}, f32[2048]{0:T(1024)}, u32[]{:S(2)}) copy-start(f32[2048]{0:T(1024)} %param.10) | copy-start | bytes 24580
  64.3 46.3 %collective-permute-start.4 = (bf16[4,2,32,2560]{3,2,1,0:T(8,128)(2,1)}, bf16[4,2,32,2560]{3,2,1,0:T(8,128)(2,1)}, u32[]{:S(2)}, u32[]{:S(2)}) collective-permute-start(bf16[4,2,32,2560]{3,2,1,0:T(8,128)(2,1)} %pad_maximum_fusion.refs_0_), channel_id=1, source_target_pairs={{0,64},{64,4},{4,68},{68,0},{1,65},{65,5},{5,69},{69,1},{2,66},{66... | collective-permute-start | bytes 3932168 | tf_op jit(solution)/shard_map/ppermute | solution.py:408
  68.1 42.5 %collective-permute-start.5 = (bf16[4,2,32,2560]{3,2,1,0:T(8,128)(2,1)}, bf16[4,2,32,2560]{3,2,1,0:T(8,128)(2,1)}, u32[]{:S(2)}, u32[]{:S(2)}) collective-permute-start(bf16[4,2,32,2560]{3,2,1,0:T(8,128)(2,1)} %pad_maximum_fusion.refs_0_), channel_id=1, source_target_pairs={{0,68},{64,0},{4,64},{68,4},{1,69},{65,1},{5,65},{69,5},{2,70},{66... | collective-permute-start | bytes 3932168 | tf_op jit(solution)/shard_map/ppermute | solution.py:408
  72.9 3.6 %copy-start.1 = (bf16[512,2048]{1,0:T(8,128)(2,1)}, bf16[512,2048]{1,0:T(8,128)(2,1)S(1)}, u32[]{:S(2)}) copy-start(bf16[512,2048]{1,0:T(8,128)(2,1)S(1)} %shard_map.91.hid_ref) | copy-start | bytes 6291460
  110.6 34.2 %collective-permute-start.12 = (bf16[4,4,2,2,16,3072]{5,4,3,2,1,0:T(8,128)(2,1)}, bf16[4,4,2,2,16,3072]{5,4,3,2,1,0:T(8,128)(2,1)}, u32[]{:S(2)}, u32[]{:S(2)}) collective-permute-start(bf16[4,4,2,2,16,3072]{5,4,3,2,1,0:T(8,128)(2,1)} %bitcast.64), channel_id=1, source_target_pairs={{0,32},{32,0},{1,33},{33,1},{2,34},{34,2},{3,35},{35,3},{4,36},{36... | collective-permute-start | bytes 18874376 | tf_op jit(solution)/shard_map/ppermute | solution.py:428
  110.7 9.6 %collective-permute-start.22 = (bf16[4,2,32,2560]{3,2,1,0:T(8,128)(2,1)S(1)}, bf16[4,2,32,2560]{3,2,1,0:T(8,128)(2,1)S(1)}, u32[]{:S(2)}, u32[]{:S(2)}) collective-permute-start(bf16[4,2,32,2560]{3,2,1,0:T(8,128)(2,1)S(1)} %pad_maximum_fusion.1.refs_5_), channel_id=1, source_target_pairs={{0,32},{32,0},{1,33},{33,1},{2,34},{34,2},{3,35},{35,3},{4,36},{36... | collective-permute-start | bytes 3932168 | tf_op jit(solution)/shard_map/ppermute | solution.py:428
  111.2 13.7 %collective-permute-start.17 = (bf16[4,2,32,2560]{3,2,1,0:T(8,128)(2,1)}, bf16[4,2,32,2560]{3,2,1,0:T(8,128)(2,1)}, u32[]{:S(2)}, u32[]{:S(2)}) collective-permute-start(bf16[4,2,32,2560]{3,2,1,0:T(8,128)(2,1)} %pad_maximum_fusion.refs_0_), channel_id=1, source_target_pairs={{0,32},{32,0},{1,33},{33,1},{2,34},{34,2},{3,35},{35,3},{4,36},{36... | collective-permute-start | bytes 3932168 | tf_op jit(solution)/shard_map/ppermute | solution.py:428
  112.5 18.3 %collective-permute-start.15 = (bf16[4,2,32,1280]{3,2,1,0:T(8,128)(2,1)S(1)}, bf16[4,2,32,1280]{3,2,1,0:T(8,128)(2,1)S(1)}, u32[]{:S(2)}, u32[]{:S(2)}) collective-permute-start(bf16[4,2,32,1280]{3,2,1,0:T(8,128)(2,1)S(1)} %slice.104), channel_id=1, source_target_pairs={{0,8},{8,16},{16,24},{24,0},{1,9},{9,17},{17,25},{25,1},{2,10},{10... | collective-permute-start | bytes 1966088 | tf_op jit(solution)/shard_map/ppermute | solution.py:409
  113.7 17.6 %collective-permute-start.16 = (bf16[4,2,32,1280]{3,2,1,0:T(8,128)(2,1)S(1)}, bf16[4,2,32,1280]{3,2,1,0:T(8,128)(2,1)S(1)}, u32[]{:S(2)}, u32[]{:S(2)}) collective-permute-start(bf16[4,2,32,1280]{3,2,1,0:T(8,128)(2,1)S(1)} %slice.105), channel_id=1, source_target_pairs={{0,24},{8,0},{16,8},{24,16},{1,25},{9,1},{17,9},{25,17},{2,26},{10... | collective-permute-start | bytes 1966088 | tf_op jit(solution)/shard_map/ppermute | solution.py:409
  120.3 43.2 %copy-start.4 = (bf16[4,2,32,2560]{3,2,1,0:T(8,128)(2,1)}, bf16[4,2,32,2560]{3,2,1,0:T(8,128)(2,1)S(1)}, u32[]{:S(2)}) copy-start(bf16[4,2,32,2560]{3,2,1,0:T(8,128)(2,1)S(1)} %collective-permute-done.22.refs_15_) | copy-start | bytes 3932164
  120.3 18.2 %collective-permute-start.13 = (bf16[4,2,32,1280]{3,2,1,0:T(8,128)(2,1)S(1)}, bf16[4,2,32,1280]{3,2,1,0:T(8,128)(2,1)S(1)}, u32[]{:S(2)}, u32[]{:S(2)}) collective-permute-start(bf16[4,2,32,1280]{3,2,1,0:T(8,128)(2,1)S(1)} %slice.102), channel_id=1, source_target_pairs={{0,64},{64,4},{4,68},{68,0},{1,65},{65,5},{5,69},{69,1},{2,66},{66... | collective-permute-start | bytes 1966088 | tf_op jit(solution)/shard_map/ppermute | solution.py:408
  125.0 16.9 %collective-permute-start.14 = (bf16[4,2,32,1280]{3,2,1,0:T(8,128)(2,1)S(1)}, bf16[4,2,32,1280]{3,2,1,0:T(8,128)(2,1)}, u32[]{:S(2)}, u32[]{:S(2)}) collective-permute-start(bf16[4,2,32,1280]{3,2,1,0:T(8,128)(2,1)S(1)} %slice.103), channel_id=1, source_target_pairs={{0,68},{64,0},{4,64},{68,4},{1,69},{65,1},{5,65},{69,5},{2,70},{66... | collective-permute-start | bytes 1966088 | tf_op jit(solution)/shard_map/ppermute | solution.py:408
  130.8 7.7 %copy-start.6 = (bf16[4,2,32,1280]{3,2,1,0:T(8,128)(2,1)}, bf16[4,2,32,1280]{3,2,1,0:T(8,128)(2,1)S(1)}, u32[]{:S(2)}) copy-start(bf16[4,2,32,1280]{3,2,1,0:T(8,128)(2,1)S(1)} %collective-permute-done.15.refs_8_) | copy-start | bytes 1966084
  130.8 11.0 %collective-permute-start.25 = (bf16[4,2,32,1280]{3,2,1,0:T(8,128)(2,1)S(1)}, bf16[4,2,32,1280]{3,2,1,0:T(8,128)(2,1)S(1)}, u32[]{:S(2)}, u32[]{:S(2)}) collective-permute-start(bf16[4,2,32,1280]{3,2,1,0:T(8,128)(2,1)S(1)} %collective-permute-done.15.refs_8_), channel_id=1, source_target_pairs={{0,32},{32,0},{1,33},{33,1},{2,34},{34,2},{3,35},{35,3},{4,36},{36... | collective-permute-start | bytes 1966088 | tf_op jit(solution)/shard_map/ppermute | solution.py:428
  131.3 10.6 %copy-start.7 = (bf16[4,2,32,1280]{3,2,1,0:T(8,128)(2,1)}, bf16[4,2,32,1280]{3,2,1,0:T(8,128)(2,1)S(1)}, u32[]{:S(2)}) copy-start(bf16[4,2,32,1280]{3,2,1,0:T(8,128)(2,1)S(1)} %collective-permute-done.16.refs_9_) | copy-start | bytes 1966084
  131.3 11.2 %collective-permute-start.26 = (bf16[4,2,32,1280]{3,2,1,0:T(8,128)(2,1)S(1)}, bf16[4,2,32,1280]{3,2,1,0:T(8,128)(2,1)S(1)}, u32[]{:S(2)}, u32[]{:S(2)}) collective-permute-start(bf16[4,2,32,1280]{3,2,1,0:T(8,128)(2,1)S(1)} %collective-permute-done.16.refs_9_), channel_id=1, source_target_pairs={{0,32},{32,0},{1,33},{33,1},{2,34},{34,2},{3,35},{35,3},{4,36},{36... | collective-permute-start | bytes 1966088 | tf_op jit(solution)/shard_map/ppermute | solution.py:428
  138.6 25.0 %copy-start.8 = (bf16[4,2,32,1280]{3,2,1,0:T(8,128)(2,1)}, bf16[4,2,32,1280]{3,2,1,0:T(8,128)(2,1)S(1)}, u32[]{:S(2)}) copy-start(bf16[4,2,32,1280]{3,2,1,0:T(8,128)(2,1)S(1)} %collective-permute-done.13.refs_3_) | copy-start | bytes 1966084
  138.6 4.0 %collective-permute-start.20 = (bf16[4,2,32,1280]{3,2,1,0:T(8,128)(2,1)S(1)}, bf16[4,2,32,1280]{3,2,1,0:T(8,128)(2,1)S(1)}, u32[]{:S(2)}, u32[]{:S(2)}) collective-permute-start(bf16[4,2,32,1280]{3,2,1,0:T(8,128)(2,1)S(1)} %collective-permute-done.13.refs_3_), channel_id=1, source_target_pairs={{0,32},{32,0},{1,33},{33,1},{2,34},{34,2},{3,35},{35,3},{4,36},{36... | collective-permute-start | bytes 1966088 | tf_op jit(solution)/shard_map/ppermute | solution.py:428
  141.9 21.7 %collective-permute-start.23 = (bf16[4,2,32,2560]{3,2,1,0:T(8,128)(2,1)}, bf16[4,2,32,2560]{3,2,1,0:T(8,128)(2,1)S(1)}, u32[]{:S(2)}, u32[]{:S(2)}) collective-permute-start(bf16[4,2,32,2560]{3,2,1,0:T(8,128)(2,1)} %collective-permute-done.10.refs_6_), channel_id=1, source_target_pairs={{0,32},{32,0},{1,33},{33,1},{2,34},{34,2},{3,35},{35,3},{4,36},{36... | collective-permute-start | bytes 3932168 | tf_op jit(solution)/shard_map/ppermute | solution.py:428
  141.9 0.9 copy-start.9
  141.9 21.7 %collective-permute-start.24 = (bf16[4,2,32,2560]{3,2,1,0:T(8,128)(2,1)}, bf16[4,2,32,2560]{3,2,1,0:T(8,128)(2,1)}, u32[]{:S(2)}, u32[]{:S(2)}) collective-permute-start(bf16[4,2,32,2560]{3,2,1,0:T(8,128)(2,1)} %collective-permute-done.11.refs_7_), channel_id=1, source_target_pairs={{0,32},{32,0},{1,33},{33,1},{2,34},{34,2},{3,35},{35,3},{4,36},{36... | collective-permute-start | bytes 3932168 | tf_op jit(solution)/shard_map/ppermute | solution.py:428
  142.5 0.9 copy-start.10
  142.5 21.1 %collective-permute-start.18 = (bf16[4,2,32,2560]{3,2,1,0:T(8,128)(2,1)}, bf16[4,2,32,2560]{3,2,1,0:T(8,128)(2,1)}, u32[]{:S(2)}, u32[]{:S(2)}) collective-permute-start(bf16[4,2,32,2560]{3,2,1,0:T(8,128)(2,1)} %collective-permute-done.4.refs_1_), channel_id=1, source_target_pairs={{0,32},{32,0},{1,33},{33,1},{2,34},{34,2},{3,35},{35,3},{4,36},{36... | collective-permute-start | bytes 3932168 | tf_op jit(solution)/shard_map/ppermute | solution.py:428
  143.3 0.8 copy-start.11
  144.1 19.5 %collective-permute-start.19 = (bf16[4,2,32,2560]{3,2,1,0:T(8,128)(2,1)}, bf16[4,2,32,2560]{3,2,1,0:T(8,128)(2,1)}, u32[]{:S(2)}, u32[]{:S(2)}) collective-permute-start(bf16[4,2,32,2560]{3,2,1,0:T(8,128)(2,1)} %collective-permute-done.5.refs_2_), channel_id=1, source_target_pairs={{0,32},{32,0},{1,33},{33,1},{2,34},{34,2},{3,35},{35,3},{4,36},{36... | collective-permute-start | bytes 3932168 | tf_op jit(solution)/shard_map/ppermute | solution.py:428
  144.8 18.7 %collective-permute-start.21 = (bf16[4,2,32,1280]{3,2,1,0:T(8,128)(2,1)}, bf16[4,2,32,1280]{3,2,1,0:T(8,128)(2,1)S(1)}, u32[]{:S(2)}, u32[]{:S(2)}) collective-permute-start(bf16[4,2,32,1280]{3,2,1,0:T(8,128)(2,1)} %collective-permute-done.14.refs_4_), channel_id=1, source_target_pairs={{0,32},{32,0},{1,33},{33,1},{2,34},{34,2},{3,35},{35,3},{4,36},{36... | collective-permute-start | bytes 1966088 | tf_op jit(solution)/shard_map/ppermute | solution.py:428
  163.5 0.8 copy-start.12
  163.6 1.3 copy-start.5
Sparse Core Ops, SparseCore 0:
  23.0 87.0 all-gather.3

commit v7 on v5

--- a/solution.py
+++ b/solution.py
@@ -20,8 +20,8 @@
 SEQ = ("x", "yhi", "z")
 QKV_PART = 3 * WIDTH // 2
 PART = 2 * WIDTH
-RELATIVE = ((0, 0, PART), (3, 0, PART), (1, 0, PART), (2, 0, PART // 2), (2, PART // 2, PART))
-STACKED = (0, 3, 1, 2)
+RELATIVE = (0, 3, 1, 2)
+PIECES = 2 * 2 * 2 * len(RELATIVE)
 LOG2E = 1.4426950408889634
 MIB = 1 << 20
 
@@ -108,25 +108,27 @@
         return lax.rem(y, 2) * 8 + x * 2 + y // 2
 
     def move(slot, part, outputs):
-        first = (slot * 2 + part) * len(RELATIVE)
-        for index, (ring, low, high) in enumerate(RELATIVE):
-            src = pieces[first + index]
-            if outputs:
-                if high < PART:
-                    continue
-                lanes, target = pl.ds(QKV_PART - low, PART - QKV_PART), None
-            else:
-                end = min(high, QKV_PART)
-                lanes, target = pl.ds(0, end - low), pl.ds(low, end - low)
-            for k, stacked in enumerate(STACKED):
-                block = block_of(part, stacked, ring)
+        cut = QKV_PART - WIDTH
+        for half in range(2):
+            first = ((slot * 2 + part) * 2 + half) * len(RELATIVE)
+            for index, ring in enumerate(RELATIVE):
+                src = pieces[first + index]
                 if outputs:
-                    width = PART - QKV_PART
-                    dst = o_ref.at[slot, block, :, :, pl.ds(part * width, width)]
+                    if half == 0:
+                        continue
+                    lanes = pl.ds(cut, WIDTH - cut)
                 else:
-                    dst = w_ref.at[slot, part, block, :, :, target]
-                sem = sems.at[4 + slot if outputs else slot * 2 + part]
-                pltpu.make_async_copy(src.at[k, :, :, lanes], dst, sem).start()
+                    width = cut if half else WIDTH
+                    lanes, target = pl.ds(0, width), pl.ds(half * WIDTH, width)
+                for k, stacked in enumerate(RELATIVE):
+                    block = block_of(part, stacked, ring)
+                    if outputs:
+                        width = WIDTH - cut
+                        dst = o_ref.at[slot, block, :, :, pl.ds(part * width, width)]
+                    else:
+                        dst = w_ref.at[slot, part, block, :, :, target]
+                    sem = sems.at[4 + slot if outputs else slot * 2 + part]
+                    pltpu.make_async_copy(src.at[k, :, :, lanes], dst, sem).start()
 
     for outputs, ref in ((False, w_ref), (True, o_ref)):
         if ref is not None:
@@ -168,8 +170,8 @@
 
 
 def row_kernel(place_ref, x_ref, hid_ref, gain_ref, cos_ref, sin_ref, *refs):
-    pieces = refs[: 4 * len(RELATIVE)]
-    mid_ref, next_ref, w_ref, o_ref, att_ref, sems = refs[4 * len(RELATIVE) :]
+    pieces = refs[: PIECES]
+    mid_ref, next_ref, w_ref, o_ref, att_ref, sems = refs[PIECES :]
     core = place_ref[0]
     start_copies(place_ref, pieces, sems, w_ref, o_ref)
     half = D // 2
@@ -386,19 +388,32 @@
     return lax.ppermute(value, axis, [(i, (i + by) % 4) for i in range(4)])
 
 
-def first_hops(value, axis):
-    return [value, shift(value, axis, 1), shift(value, axis, -1)]
-
-
-def forwards(hops, axis):
-    own, left, right = hops
-    half = own.shape[-1] // 2
-    return hops + [shift(left[..., :half], axis, 1), shift(right[..., half:], axis, -1)]
-
-
-def stack(pieces):
-    own, left, right, low, high = pieces
-    return jnp.stack([own, left, right, jnp.concatenate([low, high], -1)])
+def inner_ring(part, axis):
+    half = part.shape[-1] // 2
+    left = shift(part, axis, 1)
+    right = shift(part, axis, -1)
+    opposite = (shift(left[..., :half], axis, 1), shift(right[..., half:], axis, -1))
+    lanes = (slice(0, half), slice(half, 2 * half))
+    return [
+        jnp.stack([part[..., lanes[h]], left[..., lanes[h]], right[..., lanes[h]], opposite[h]])
+        for h in range(2)
+    ]
+
+
+def outer_hops(stacks):
+    return [
+        [(stack, shift(stack, axis, 1), shift(stack, axis, -1)) for stack in part]
+        for part, axis in zip(stacks, "yx")
+    ]
+
+
+def outer_pieces(hops):
+    pieces = []
+    for part, axis in zip(hops, "yx"):
+        for half, (own, left, right) in enumerate(part):
+            far = shift(right, axis, -1) if half else shift(left, axis, 1)
+            pieces += [own, left, right, far]
+    return pieces
 
 
 def swap(value):
@@ -426,27 +441,9 @@
     return parts
 
 
-def inner_rings(parts):
-    hops = [first_hops(part, axis) for part, axis in zip(parts, "xy")]
-    return [stack(forwards(hop, axis)) for hop, axis in zip(hops, "xy")]
-
-
-def outer_hops(stacks):
-    return [first_hops(part, axis) for part, axis in zip(stacks, "yx")]
-
-
-def outer_forwards(hops):
-    return [forwards(hop, axis) for hop, axis in zip(hops, "yx")]
-
-
-def both_cores(parts):
-    own = [piece for part in parts for piece in part]
-    return own + [swap(piece) for piece in own]
-
-
 def column_line(inputs, output):
     shard = jnp.concatenate([by_step(inputs), fold_output(output)], 1)
-    return lax.all_gather(shard, ("ylo", "yhi"), axis=0)
+    return lax.all_gather(jnp.concatenate([shard, shard], 1), ("ylo", "yhi"), axis=0)[:, :, : 4 * WIDTH]
 
 
 def column_plane(line):
@@ -477,12 +474,13 @@
     hidden = normed_slots(core_scalar, residual, gain_first.reshape(1, D))
 
     line = column_line(inputs_second, output_second)
-    first = inner_rings(lines(inputs_first, output_first))
+    first = [inner_ring(part, axis) for part, axis in zip(lines(inputs_first, output_first), "xy")]
     first, hidden, row_tables, column_tables = lax.optimization_barrier((first, hidden, row_tables, column_tables))
     first_hop = outer_hops(first)
     line, _ = lax.optimization_barrier((line, first_hop))
     plane = column_plane(line)
-    pieces = both_cores(outer_forwards(first_hop))
+    pieces = outer_pieces(first_hop)
+    pieces = pieces + [swap(piece) for piece in pieces]
 
     middle, hidden = row_layer(place, residual, hidden, gain_second.reshape(1, D), row_tables, pieces)
     plane, hidden = lax.optimization_barrier((plane, hidden))

time: 262 us -> 273 us (1.042)
  waiting for transfers between devices: 43.1 us -> 85.7 us
  blocking collectives: 80.8 us -> 51.7 us
  local copies, waits for them, and re-layouts: 23.8 us -> 20.2 us
    all_gather x1 -> x0, blocking collectives: 29.2 us -> none  [column_line(): return lax.all_gather(shard, ('ylo', 'yhi'), axis=0)]
    ppermute x8 -> x10, waiting for transfers between devices: 5.84 us -> 28.7 us  [shift(): lax.ppermute(value, ('ylo', 'yhi'), [(where(y), where((y + by) % 4)) for...]
    ppermute x8 -> x10, waiting for transfers between devices: 12.9 us -> 27.8 us  [shift(): return lax.ppermute(value, axis, [(i, (i + by) % 4) for i in range(4)])]
    slice x8 -> x1, local copies, waits for them, and re-layouts: 7.05 us -> 1.88 us  [column_line(): lax.all_gather(jnp.concatenate([shard, shard], 1), ('ylo', 'yhi'), axis=0)]
    another operation x0 -> x5, local copies, waits for them, and re-layouts: none -> 4.51 us  [inner_ring(): jnp.stack([part[..., lanes[h]], left[..., lanes[h]], right[..., lanes[h]]...]
    another operation x6 -> x5, other arithmetic: 4.97 us -> 1.75 us  [inner_ring(): jnp.stack([part[..., lanes[h]], left[..., lanes[h]], right[..., lanes[h]]...]
    unnamed x46, local copies, waits for them, and re-layouts: 6.68 us -> 3.82 us
    ppermute x11 -> x17, waiting for transfers between devices: 3.93 us -> 6.55 us  [swap(): return lax.ppermute(value, 'core', [(0, 1), (1, 0)])]
  transfers between devices with their start and end apart: 29 -> 40, of which waited for: 8 -> 16; matrix products, arithmetic and copies ran while one was open for 8% -> 8% of each run, Pallas kernels for 10% -> 10%
where the time goes in v7:
time: 273 us; the launch traced here: 272 us
  waiting for transfers between devices  85.7 us (31%)
  Pallas kernels  54.7 us (20%)
  blocking collectives  51.7 us (19%)
  starting transfers between devices  37 us (14%)
  local copies, waits for them, and re-layouts  20.2 us (7%)
  between operations  15.1 us (6%)
  other arithmetic  7.91 us (3%)
    all_to_all x1, blocking collectives, shards(): lax.all_to_all(hidden, SEQ, split_axis=0, concat_axis=0, tiled=True)  37.5 us
    ppermute x10, waiting for transfers between devices, shift(): lax.ppermute(value, ('ylo', 'yhi'), [(where(y), where((y + by) % 4)) for...  28.7 us
    ppermute x10, waiting for transfers between devices, shift(): return lax.ppermute(value, axis, [(i, (i + by) % 4) for i in range(4)])  27.8 us
    pallas_call x1, Pallas kernels, row_layer(): pl.pallas_call(row_kernel, out_shape=[shape, shape], in_specs=[pl.BlockSp...  24.4 us
    pallas_call x1, Pallas kernels, column_layer(): pl.pallas_call(column_kernel, out_shape=jax.ShapeDtypeStruct((C, WIDTH),...  21.3 us
    ppermute x10, starting transfers between devices, shift(): return lax.ppermute(value, axis, [(i, (i + by) % 4) for i in range(4)])  14.2 us
    all_gather x1, blocking collectives, lines(): rows = lax.all_gather(shard, 'z', axis=0)  14.2 us
    ppermute x10, starting transfers between devices, shift(): lax.ppermute(value, ('ylo', 'yhi'), [(where(y), where((y + by) % 4)) for...  14.1 us
  transfers between devices with their start and end apart: 40, of which 16 were waited for; matrix products, arithmetic and copies ran while one was open for 8% of the time, Pallas kernels for 10%

profile of v7, /device:TPU:0, one launch (start us, length us, event | category | flops | bytes accessed | tf_op | source)
XLA Modules:
  0.0 272.3 jit_solution(3289629872629990126)
XLA Ops:
  6.5 0.7 fusion.12
  7.3 0.9 reshape.95
  8.4 14.2 %all-gather.1 = bf16[64,4096]{1,0:T(8,128)(2,1)S(1)} all-gather(bf16[16,4096]{1,0:T(8,128)(2,1)S(1)} %maximum_maximum_fusion.1), channel_id=3, replica_groups=mesh['ylo'=2,'core'=2,'x'=4,'yhi'=2,'z'=4] {'z'}, dimensions={0}, use_global_device_ids=true | all-gather | bytes 655360 | tf_op jit(solution)/shard_map/all_gather | solution.py:433
  22.8 0.7 pad_maximum_fusion.5
  23.5 3.0 %collective-permute-start.5 = (bf16[2,32,2048]{2,1,0:T(8,128)(2,1)}, bf16[2,32,2048]{2,1,0:T(8,128)(2,1)}, u32[]{:S(2)}, u32[]{:S(2)}) collective-permute-start(bf16[2,32,2048]{2,1,0:T(8,128)(2,1)} %pad_maximum_fusion.5), channel_id=1, source_target_pairs={{0,68},{64,0},{4,64},{68,4},{1,69},{65,1},{5,65},{69,5},{2,70},{66... | collective-permute-start | bytes 786440 | tf_op jit(solution)/shard_map/ppermute | solution.py:387
  26.5 0.7 pad_maximum_fusion.4
  27.2 2.8 %collective-permute-start.1 = (bf16[2,32,2048]{2,1,0:T(8,128)(2,1)}, bf16[2,32,2048]{2,1,0:T(8,128)(2,1)}, u32[]{:S(2)}, u32[]{:S(2)}) collective-permute-start(bf16[2,32,2048]{2,1,0:T(8,128)(2,1)} %pad_maximum_fusion.4), channel_id=1, source_target_pairs={{0,24},{8,0},{16,8},{24,16},{1,25},{9,1},{17,9},{25,17},{2,26},{10... | collective-permute-start | bytes 786440 | tf_op jit(solution)/shard_map/ppermute | solution.py:388
  30.3 0.7 maximum_maximum_fusion
  31.1 0.6 constant_dynamic-slice_fusion
  31.7 0.6 add_convert_fusion.1
  32.5 0.6 fusion.14
  34.4 1.9 fusion.8
  36.6 1.0 pad_maximum_fusion.8
  37.6 0.7 fusion.5
  38.3 2.1 shard_map.91.hid_ref
  40.4 1.5 slice_bitcast_fusion.9
  41.9 3.3 %collective-permute-start.7 = (bf16[2,32,1024]{2,1,0:T(8,128)(2,1)S(1)}, bf16[2,32,1024]{2,1,0:T(8,128)(2,1)S(1)}, u32[]{:S(2)}, u32[]{:S(2)}) collective-permute-start(bf16[2,32,1024]{2,1,0:T(8,128)(2,1)S(1)} %get-tuple-element.41), channel_id=1, source_target_pairs={{0,68},{64,0},{4,64},{68,4},{1,69},{65,1},{5,65},{69,5},{2,70},{66... | collective-permute-start | bytes 393224 | tf_op jit(solution)/shard_map/ppermute | solution.py:387
  45.3 1.0 slice_bitcast_fusion.11
  46.3 3.3 %collective-permute-start.3 = (bf16[2,32,1024]{2,1,0:T(8,128)(2,1)S(1)}, bf16[2,32,1024]{2,1,0:T(8,128)(2,1)S(1)}, u32[]{:S(2)}, u32[]{:S(2)}) collective-permute-start(bf16[2,32,1024]{2,1,0:T(8,128)(2,1)S(1)} %get-tuple-element.47), channel_id=1, source_target_pairs={{0,24},{8,0},{16,8},{24,16},{1,25},{9,1},{17,9},{25,17},{2,26},{10... | collective-permute-start | bytes 393224 | tf_op jit(solution)/shard_map/ppermute | solution.py:388
  49.6 1.0 slice_bitcast_fusion.2
  50.7 1.0 slice_bitcast_fusion.5
  51.7 1.8 collective-permute-done.7
  53.5 0.9 pad_maximum_fusion.3.refs_12_
  54.5 8.1 %collective-permute-done.6 = bf16[2,32,1024]{2,1,0:T(8,128)(2,1)S(1)} collective-permute-done((bf16[2,32,1024]{2,1,0:T(8,128)(2,1)S(1)}, bf16[2,32,1024]{2,1,0:T(8,128)(2,1)S(1)}, u32[]{:S(2)}, u32[]{:S(2)}) %collective-permute-start.6) | collective-permute-done | bytes 131104 | tf_op jit(solution)/shard_map/ppermute | solution.py:387
  62.8 3.2 %collective-permute-start.11 = (bf16[4,2,32,1024]{3,2,1,0:T(8,128)(2,1)S(1)}, bf16[4,2,32,1024]{3,2,1,0:T(8,128)(2,1)S(1)}, u32[]{:S(2)}, u32[]{:S(2)}) collective-permute-start(bf16[4,2,32,1024]{3,2,1,0:T(8,128)(2,1)S(1)} %pad_maximum_fusion.1.refs_4_), channel_id=1, source_target_pairs={{0,68},{64,0},{4,64},{68,4},{1,69},{65,1},{5,65},{69,5},{2,70},{66... | collective-permute-start | bytes 1572872 | tf_op jit(solution)/shard_map/ppermute | solution.py:387
  66.1 2.0 collective-permute-start.10
  68.1 10.8 %collective-permute-done.8.refs_1_ = bf16[4,2,32,1024]{3,2,1,0:T(8,128)(2,1)S(1)} collective-permute-done((bf16[4,2,32,1024]{3,2,1,0:T(8,128)(2,1)S(1)}, bf16[4,2,32,1024]{3,2,1,0:T(8,128)(2,1)S(1)}, u32[]{:S(2)}, u32[]{:S(2)}) %collective-permute-start.8) | collective-permute-done | bytes 524320 | tf_op jit(solution)/shard_map/ppermute | solution.py:387
  78.9 2.2 collective-permute-start.15
  81.0 1.0 collective-permute-start.13
  82.0 0.8 copy-done.3
  82.8 1.0 collective-permute-start.14
  83.9 1.9 slice.114
  85.8 8.3 %collective-permute-done.15.refs_14_ = bf16[4,2,32,1024]{3,2,1,0:T(8,128)(2,1)} collective-permute-done((bf16[4,2,32,1024]{3,2,1,0:T(8,128)(2,1)}, bf16[4,2,32,1024]{3,2,1,0:T(8,128)(2,1)}, u32[]{:S(2)}, u32[]{:S(2)}) %collective-permute-start.15) | collective-permute-done | bytes 524320 | tf_op jit(solution)/shard_map/ppermute | solution.py:388
  94.0 8.1 %collective-permute-done.13.refs_10_ = bf16[4,2,32,1024]{3,2,1,0:T(8,128)(2,1)} collective-permute-done((bf16[4,2,32,1024]{3,2,1,0:T(8,128)(2,1)S(1)}, bf16[4,2,32,1024]{3,2,1,0:T(8,128)(2,1)}, u32[]{:S(2)}, u32[]{:S(2)}) %collective-permute-start.13) | collective-permute-done | bytes 524320 | tf_op jit(solution)/shard_map/ppermute | solution.py:388
  102.3 0.5 collective-permute-start.24
  102.9 0.4 collective-permute-start.32
  103.3 0.9 collective-permute-done.20.refs_16_
  104.2 2.4 collective-permute-start.17
  106.6 1.3 collective-permute-start.18
  107.9 2.6 collective-permute-start.19
  110.5 8.1 %collective-permute-done.16.refs_3_ = bf16[4,2,32,1024]{3,2,1,0:T(8,128)(2,1)} collective-permute-done((bf16[4,2,32,1024]{3,2,1,0:T(8,128)(2,1)S(1)}, bf16[4,2,32,1024]{3,2,1,0:T(8,128)(2,1)}, u32[]{:S(2)}, u32[]{:S(2)}) %collective-permute-start.16) | collective-permute-done | bytes 524320 | tf_op jit(solution)/shard_map/ppermute | solution.py:387
  118.6 0.5 collective-permute-start.25
  119.1 10.5 %collective-permute-done.18.refs_11_ = bf16[4,2,32,1024]{3,2,1,0:T(8,128)(2,1)} collective-permute-done((bf16[4,2,32,1024]{3,2,1,0:T(8,128)(2,1)}, bf16[4,2,32,1024]{3,2,1,0:T(8,128)(2,1)}, u32[]{:S(2)}, u32[]{:S(2)}) %collective-permute-start.18) | collective-permute-done | bytes 524320 | tf_op jit(solution)/shard_map/ppermute | solution.py:388
  129.5 0.9 collective-permute-done.19.refs_15_
  130.5 0.5 collective-permute-start.30
  131.7 0.9 collective-permute-done.29.refs_25_
  132.7 1.4 collective-permute-done.30.refs_26_
  134.2 1.4 collective-permute-done.33.refs_29_
  135.6 0.8 copy-done.22
  136.6 0.6 collective-permute-done.31.refs_27_
  137.2 1.4 collective-permute-done.35.refs_31_
  138.7 1.1 copy-done.4
  139.8 24.4 %shard_map.92 = (bf16[512,2048]{1,0:T(8,128)(2,1)}, bf16[512,2048]{1,0:T(8,128)(2,1)}) custom-call(s32[3]{0:T(128)S(1)} %pad_add_fusion.place_ref, bf16[512,2048]{1,0:T(8,128)(2,1)} %bitcast.74, bf16[512,2048]{1,0:T(8,128)(2,1)} %copy-done.1, f32[1,2048]{1,0:T(1,128)S(1)} %bitcast.77, f32[512,128]{1,0:T(8,128)S(1)} %get-tuple-element.25.cos_ref, ...), custom_call_target="tpu_custom_call" | custom-call | flops 9663676416 | bytes 25165824 | tf_op jit(solution)/shard_map/pallas_call | solution.py:232
  164.2 11.4 %all-gather.8.cloned.1.call-done = bf16[64,16,4096]{2,1,0:T(8,128)(2,1)} async-done(((bf16[4,16,4096]{2,1,0:T(8,128)(2,1)}), bf16[64,16,4096]{2,1,0:T(8,128)(2,1)}) %all-gather.8.cloned.1.call-update) | async-done | bytes 8388624 | tf_op jit(solution)/shard_map/all_gather | solution.py:450
  175.6 37.5 %all_to_all.22 = bf16[32,16,2048]{2,1,0:T(8,128)(2,1)} all-to-all(bf16[32,16,2048]{2,1,0:T(8,128)(2,1)} %bitcast.85), channel_id=1, replica_groups=mesh['ylo'=2,'core'=2,'x'=4,'yhi'=2,'z'=4] {'x','yhi','z'}, dimensions={0} | all-to-all | bytes 4194304 | tf_op jit(solution)/shard_map/all_to_all | solution.py:488
  213.1 21.3 %shard_map.93 = bf16[512,1024]{1,0:T(8,128)(2,1)} custom-call(s32[1]{0:T(128)} %bitcast.core_ref, bf16[512,2048]{1,0:T(8,128)(2,1)} %bitcast.86, f32[512,128]{1,0:T(8,128)} %get-tuple-element.29.cos_ref, f32[512,128]{1,0:T(8,128)} %get-tuple-element.30.sin_ref, bf16[4,4,2,2,16,4096]{5,4,3,2,1,0:T(8,128)(2,1)} %bitcast.91, ...), custom_call_target="tpu_custom_call" | custom-call | flops 7516192768 | bytes 15728640 | tf_op jit(solution)/shard_map/pallas_call | solution.py:322
  234.4 5.5 %all-to-all-start.1 = ((bf16[32,16,1024]{2,1,0:T(8,128)(2,1)}), bf16[32,16,1024]{2,1,0:T(8,128)(2,1)S(1)}, u32[]{:S(2)}, u32[]{:S(2)}) async-start(bf16[32,16,1024]{2,1,0:T(8,128)(2,1)} %bitcast.87), calls=%async_computation.1 | async-start | bytes 2097152 | tf_op jit(solution)/shard_map/all_to_all | solution.py:490
  239.9 1.8 slice_bitcast_fusion.1
  241.7 1.5 copy.18
  243.2 1.8 slice_bitcast_fusion
  244.9 1.5 copy.19
  246.5 11.1 %all-to-all-done.1 = bf16[32,16,1024]{2,1,0:T(8,128)(2,1)S(1)} async-done(((bf16[32,16,1024]{2,1,0:T(8,128)(2,1)}), bf16[32,16,1024]{2,1,0:T(8,128)(2,1)S(1)}, u32[]{:S(2)}, u32[]{:S(2)}) %all-to-all-start.1) | async-done | bytes 1048608 | tf_op jit(solution)/shard_map/all_to_all | solution.py:490
  257.6 1.0 copy-done.6
  258.6 6.9 %shard_map.94 = bf16[512,2048]{1,0:T(8,128)(2,1)} custom-call(s32[1]{0:T(128)} %bitcast.core_ref, bf16[512,1024]{1,0:T(8,128)(2,1)} %bitcast.80, bf16[512,2048]{1,0:T(8,128)(2,1)} %bitcast.78, bf16[512,2048]{1,0:T(8,128)(2,1)} %bitcast.79, bf16[512,2048]{1,0:T(8,128)(2,1)} %get-tuple-element.32.resid_ref), custom_call_target="tpu_custom_call" | custom-call | flops 2147483648 | bytes 9437184 | tf_op jit(solution)/shard_map/pallas_call | solution.py:361
  (112 shorter events, 2.9 us)
Async XLA Ops:
  6.5 77.4 %all-gather.6.cloned.1.call-start = ((), (), s32[]{:S(2)}) async-start(), calls=%async_computation.2 | async-start | bytes 1310720 | tf_op jit(solution)/shard_map/all_gather | solution.py:446
  8.3 21.7 %copy-start.9 = (bf16[8,2048]{1,0:T(8,128)(2,1)S(1)}, bf16[8,2048]{1,0:T(8,128)(2,1)}, u32[]{:S(2)}) copy-start(bf16[8,2048]{1,0:T(8,128)(2,1)} %param.15) | copy-start | bytes 98308
  8.4 21.6 %copy-start.8 = (bf16[16,3072]{1,0:T(8,128)(2,1)S(1)}, bf16[16,3072]{1,0:T(8,128)(2,1)}, u32[]{:S(2)}) copy-start(bf16[16,3072]{1,0:T(8,128)(2,1)} %param.14) | copy-start | bytes 294916
  22.7 8.4 %copy-start.11 = (s32[1,32]{1,0:T(1,128)S(1)}, s32[1,32]{1,0:T(1,128)}, u32[]{:S(2)}) copy-start(s32[1,32]{1,0:T(1,128)} %param.16) | copy-start | bytes 388
  22.7 9.8 %copy-start.10 = (s32[2]{0:T(128)S(1)}, s32[2]{0:T(128)}, u32[]{:S(2)}) copy-start(s32[2]{0:T(128)} %param.17) | copy-start | bytes 28
  23.5 16.9 %collective-permute-start.5 = (bf16[2,32,2048]{2,1,0:T(8,128)(2,1)}, bf16[2,32,2048]{2,1,0:T(8,128)(2,1)}, u32[]{:S(2)}, u32[]{:S(2)}) collective-permute-start(bf16[2,32,2048]{2,1,0:T(8,128)(2,1)} %pad_maximum_fusion.5), channel_id=1, source_target_pairs={{0,68},{64,0},{4,64},{68,4},{1,69},{65,1},{5,65},{69,5},{2,70},{66... | collective-permute-start | bytes 786440 | tf_op jit(solution)/shard_map/ppermute | solution.py:387
  26.5 23.1 %collective-permute-start.4 = (bf16[2,32,2048]{2,1,0:T(8,128)(2,1)}, bf16[2,32,2048]{2,1,0:T(8,128)(2,1)}, u32[]{:S(2)}, u32[]{:S(2)}) collective-permute-start(bf16[2,32,2048]{2,1,0:T(8,128)(2,1)} %pad_maximum_fusion.5), channel_id=1, source_target_pairs={{0,64},{64,4},{4,68},{68,0},{1,65},{65,5},{5,69},{69,1},{2,66},{66... | collective-permute-start | bytes 786440 | tf_op jit(solution)/shard_map/ppermute | solution.py:387
  27.2 18.0 %collective-permute-start.1 = (bf16[2,32,2048]{2,1,0:T(8,128)(2,1)}, bf16[2,32,2048]{2,1,0:T(8,128)(2,1)}, u32[]{:S(2)}, u32[]{:S(2)}) collective-permute-start(bf16[2,32,2048]{2,1,0:T(8,128)(2,1)} %pad_maximum_fusion.4), channel_id=1, source_target_pairs={{0,24},{8,0},{16,8},{24,16},{1,25},{9,1},{17,9},{25,17},{2,26},{10... | collective-permute-start | bytes 786440 | tf_op jit(solution)/shard_map/ppermute | solution.py:388
  30.0 20.6 %collective-permute-start = (bf16[2,32,2048]{2,1,0:T(8,128)(2,1)}, bf16[2,32,2048]{2,1,0:T(8,128)(2,1)}, u32[]{:S(2)}, u32[]{:S(2)}) collective-permute-start(bf16[2,32,2048]{2,1,0:T(8,128)(2,1)} %pad_maximum_fusion.4), channel_id=1, source_target_pairs={{0,8},{8,16},{16,24},{24,0},{1,9},{9,17},{17,25},{25,1},{2,10},{10... | collective-permute-start | bytes 786440 | tf_op jit(solution)/shard_map/ppermute | solution.py:388
  31.0 144.6 %all-gather.8.cloned.1.call-start = ((), (), s32[]{:S(2)}) async-start(), calls=%async_computation.3 | async-start | bytes 8912896 | tf_op jit(solution)/shard_map/all_gather | solution.py:450
  36.4 1.9 copy-start
  36.4 1.9 copy-start.2
  40.4 14.1 %copy-start.1 = (bf16[512,2048]{1,0:T(8,128)(2,1)}, bf16[512,2048]{1,0:T(8,128)(2,1)S(1)}, u32[]{:S(2)}) copy-start(bf16[512,2048]{1,0:T(8,128)(2,1)S(1)} %shard_map.91.hid_ref) | copy-start | bytes 6291460
  40.4 13.1 %copy-start.7 = (bf16[1,2,32,1024]{3,2,1,0:T(8,128)(2,1)S(1)}, bf16[1,2,32,1024]{3,2,1,0:T(8,128)(2,1)}, u32[]{:S(2)}) copy-start(bf16[1,2,32,1024]{3,2,1,0:T(8,128)(2,1)} %get-tuple-element.66) | copy-start | bytes 393220
  41.9 11.6 %collective-permute-start.7 = (bf16[2,32,1024]{2,1,0:T(8,128)(2,1)S(1)}, bf16[2,32,1024]{2,1,0:T(8,128)(2,1)S(1)}, u32[]{:S(2)}, u32[]{:S(2)}) collective-permute-start(bf16[2,32,1024]{2,1,0:T(8,128)(2,1)S(1)} %get-tuple-element.41), channel_id=1, source_target_pairs={{0,68},{64,0},{4,64},{68,4},{1,69},{65,1},{5,65},{69,5},{2,70},{66... | collective-permute-start | bytes 393224 | tf_op jit(solution)/shard_map/ppermute | solution.py:387
  46.3 8.1 %collective-permute-start.3 = (bf16[2,32,1024]{2,1,0:T(8,128)(2,1)S(1)}, bf16[2,32,1024]{2,1,0:T(8,128)(2,1)S(1)}, u32[]{:S(2)}, u32[]{:S(2)}) collective-permute-start(bf16[2,32,1024]{2,1,0:T(8,128)(2,1)S(1)} %get-tuple-element.47), channel_id=1, source_target_pairs={{0,24},{8,0},{16,8},{24,16},{1,25},{9,1},{17,9},{25,17},{2,26},{10... | collective-permute-start | bytes 393224 | tf_op jit(solution)/shard_map/ppermute | solution.py:388
  50.6 12.0 %collective-permute-start.6 = (bf16[2,32,1024]{2,1,0:T(8,128)(2,1)S(1)}, bf16[2,32,1024]{2,1,0:T(8,128)(2,1)S(1)}, u32[]{:S(2)}, u32[]{:S(2)}) collective-permute-start(bf16[2,32,1024]{2,1,0:T(8,128)(2,1)S(1)} %get-tuple-element.39), channel_id=1, source_target_pairs={{0,64},{64,4},{4,68},{68,0},{1,65},{65,5},{5,69},{69,1},{2,66},{66... | collective-permute-start | bytes 393224 | tf_op jit(solution)/shard_map/ppermute | solution.py:387
  51.7 11.0 %collective-permute-start.2 = (bf16[2,32,1024]{2,1,0:T(8,128)(2,1)S(1)}, bf16[2,32,1024]{2,1,0:T(8,128)(2,1)S(1)}, u32[]{:S(2)}, u32[]{:S(2)}) collective-permute-start(bf16[2,32,1024]{2,1,0:T(8,128)(2,1)S(1)} %get-tuple-element.45), channel_id=1, source_target_pairs={{0,8},{8,16},{16,24},{24,0},{1,9},{9,17},{17,25},{25,1},{2,10},{10... | collective-permute-start | bytes 393224 | tf_op jit(solution)/shard_map/ppermute | solution.py:388
  54.5 84.2 %copy-start.5 = (f32[2048]{0:T(1024)S(1)}, f32[2048]{0:T(1024)}, u32[]{:S(2)}) copy-start(f32[2048]{0:T(1024)} %param.13) | copy-start | bytes 24580
  62.7 16.1 %collective-permute-start.8 = (bf16[4,2,32,1024]{3,2,1,0:T(8,128)(2,1)S(1)}, bf16[4,2,32,1024]{3,2,1,0:T(8,128)(2,1)S(1)}, u32[]{:S(2)}, u32[]{:S(2)}) collective-permute-start(bf16[4,2,32,1024]{3,2,1,0:T(8,128)(2,1)S(1)} %pad_maximum_fusion.refs_0_), channel_id=1, source_target_pairs={{0,64},{64,4},{4,68},{68,0},{1,65},{65,5},{5,69},{69,1},{2,66},{66... | collective-permute-start | bytes 1572872 | tf_op jit(solution)/shard_map/ppermute | solution.py:387
  62.8 18.2 %collective-permute-start.11 = (bf16[4,2,32,1024]{3,2,1,0:T(8,128)(2,1)S(1)}, bf16[4,2,32,1024]{3,2,1,0:T(8,128)(2,1)S(1)}, u32[]{:S(2)}, u32[]{:S(2)}) collective-permute-start(bf16[4,2,32,1024]{3,2,1,0:T(8,128)(2,1)S(1)} %pad_maximum_fusion.1.refs_4_), channel_id=1, source_target_pairs={{0,68},{64,0},{4,64},{68,4},{1,69},{65,1},{5,65},{69,5},{2,70},{66... | collective-permute-start | bytes 1572872 | tf_op jit(solution)/shard_map/ppermute | solution.py:387
  66.0 16.0 %collective-permute-start.12 = (bf16[4,2,32,1024]{3,2,1,0:T(8,128)(2,1)S(1)}, bf16[4,2,32,1024]{3,2,1,0:T(8,128)(2,1)S(1)}, u32[]{:S(2)}, u32[]{:S(2)}) collective-permute-start(bf16[4,2,32,1024]{3,2,1,0:T(8,128)(2,1)S(1)} %pad_maximum_fusion.2.refs_8_), channel_id=1, source_target_pairs={{0,8},{8,16},{16,24},{24,0},{1,9},{9,17},{17,25},{25,1},{2,10},{10... | collective-permute-start | bytes 1572872 | tf_op jit(solution)/shard_map/ppermute | solution.py:388
  66.0 28.0 %collective-permute-start.9 = (bf16[4,2,32,1024]{3,2,1,0:T(8,128)(2,1)S(1)}, bf16[4,2,32,1024]{3,2,1,0:T(8,128)(2,1)}, u32[]{:S(2)}, u32[]{:S(2)}) collective-permute-start(bf16[4,2,32,1024]{3,2,1,0:T(8,128)(2,1)S(1)} %pad_maximum_fusion.refs_0_), channel_id=1, source_target_pairs={{0,68},{64,0},{4,64},{68,4},{1,69},{65,1},{5,65},{69,5},{2,70},{66... | collective-permute-start | bytes 1572872 | tf_op jit(solution)/shard_map/ppermute | solution.py:387
  66.1 28.0 %collective-permute-start.10 = (bf16[4,2,32,1024]{3,2,1,0:T(8,128)(2,1)S(1)}, bf16[4,2,32,1024]{3,2,1,0:T(8,128)(2,1)}, u32[]{:S(2)}, u32[]{:S(2)}) collective-permute-start(bf16[4,2,32,1024]{3,2,1,0:T(8,128)(2,1)S(1)} %pad_maximum_fusion.1.refs_4_), channel_id=1, source_target_pairs={{0,64},{64,4},{4,68},{68,0},{1,65},{65,5},{5,69},{69,1},{2,66},{66... | collective-permute-start | bytes 1572872 | tf_op jit(solution)/shard_map/ppermute | solution.py:387
  78.9 15.2 %collective-permute-start.15 = (bf16[4,2,32,1024]{3,2,1,0:T(8,128)(2,1)}, bf16[4,2,32,1024]{3,2,1,0:T(8,128)(2,1)}, u32[]{:S(2)}, u32[]{:S(2)}) collective-permute-start(bf16[4,2,32,1024]{3,2,1,0:T(8,128)(2,1)} %pad_maximum_fusion.3.refs_12_), channel_id=1, source_target_pairs={{0,24},{8,0},{16,8},{24,16},{1,25},{9,1},{17,9},{25,17},{2,26},{10... | collective-permute-start | bytes 1572872 | tf_op jit(solution)/shard_map/ppermute | solution.py:388
  81.0 21.1 %collective-permute-start.13 = (bf16[4,2,32,1024]{3,2,1,0:T(8,128)(2,1)S(1)}, bf16[4,2,32,1024]{3,2,1,0:T(8,128)(2,1)}, u32[]{:S(2)}, u32[]{:S(2)}) collective-permute-start(bf16[4,2,32,1024]{3,2,1,0:T(8,128)(2,1)S(1)} %pad_maximum_fusion.2.refs_8_), channel_id=1, source_target_pairs={{0,24},{8,0},{16,8},{24,16},{1,25},{9,1},{17,9},{25,17},{2,26},{10... | collective-permute-start | bytes 1572872 | tf_op jit(solution)/shard_map/ppermute | solution.py:388
  82.0 0.8 copy-start.3
  82.8 19.3 %collective-permute-start.14 = (bf16[4,2,32,1024]{3,2,1,0:T(8,128)(2,1)}, bf16[4,2,32,1024]{3,2,1,0:T(8,128)(2,1)}, u32[]{:S(2)}, u32[]{:S(2)}) collective-permute-start(bf16[4,2,32,1024]{3,2,1,0:T(8,128)(2,1)} %pad_maximum_fusion.3.refs_12_), channel_id=1, source_target_pairs={{0,8},{8,16},{16,24},{24,0},{1,9},{9,17},{17,25},{25,1},{2,10},{10... | collective-permute-start | bytes 1572872 | tf_op jit(solution)/shard_map/ppermute | solution.py:388
  102.2 2.0 collective-permute-start.20
  102.3 4.3 %collective-permute-start.24 = (bf16[4,2,32,1024]{3,2,1,0:T(8,128)(2,1)S(1)}, bf16[4,2,32,1024]{3,2,1,0:T(8,128)(2,1)S(1)}, u32[]{:S(2)}, u32[]{:S(2)}) collective-permute-start(bf16[4,2,32,1024]{3,2,1,0:T(8,128)(2,1)S(1)} %pad_maximum_fusion.1.refs_4_), channel_id=1, source_target_pairs={{0,32},{32,0},{1,33},{33,1},{2,34},{34,2},{3,35},{35,3},{4,36},{36... | collective-permute-start | bytes 1572872 | tf_op jit(solution)/shard_map/ppermute | solution.py:420
  102.8 5.1 %collective-permute-start.28 = (bf16[4,2,32,1024]{3,2,1,0:T(8,128)(2,1)S(1)}, bf16[4,2,32,1024]{3,2,1,0:T(8,128)(2,1)S(1)}, u32[]{:S(2)}, u32[]{:S(2)}) collective-permute-start(bf16[4,2,32,1024]{3,2,1,0:T(8,128)(2,1)S(1)} %pad_maximum_fusion.2.refs_8_), channel_id=1, source_target_pairs={{0,32},{32,0},{1,33},{33,1},{2,34},{34,2},{3,35},{35,3},{4,36},{36... | collective-permute-start | bytes 1572872 | tf_op jit(solution)/shard_map/ppermute | solution.py:420
  102.9 7.6 %collective-permute-start.32 = (bf16[4,2,32,1024]{3,2,1,0:T(8,128)(2,1)}, bf16[4,2,32,1024]{3,2,1,0:T(8,128)(2,1)S(1)}, u32[]{:S(2)}, u32[]{:S(2)}) collective-permute-start(bf16[4,2,32,1024]{3,2,1,0:T(8,128)(2,1)} %pad_maximum_fusion.3.refs_12_), channel_id=1, source_target_pairs={{0,32},{32,0},{1,33},{33,1},{2,34},{34,2},{3,35},{35,3},{4,36},{36... | collective-permute-start | bytes 1572872 | tf_op jit(solution)/shard_map/ppermute | solution.py:420
  103.3 15.2 %collective-permute-start.16 = (bf16[4,2,32,1024]{3,2,1,0:T(8,128)(2,1)S(1)}, bf16[4,2,32,1024]{3,2,1,0:T(8,128)(2,1)}, u32[]{:S(2)}, u32[]{:S(2)}) collective-permute-start(bf16[4,2,32,1024]{3,2,1,0:T(8,128)(2,1)S(1)} %collective-permute-done.8.refs_1_), channel_id=1, source_target_pairs={{0,64},{64,4},{4,68},{68,0},{1,65},{65,5},{5,69},{69,1},{2,66},{66... | collective-permute-start | bytes 1572872 | tf_op jit(solution)/shard_map/ppermute | solution.py:387
  104.2 27.3 %copy-start.12 = (bf16[4,2,32,1024]{3,2,1,0:T(8,128)(2,1)}, bf16[4,2,32,1024]{3,2,1,0:T(8,128)(2,1)S(1)}, u32[]{:S(2)}) copy-start(bf16[4,2,32,1024]{3,2,1,0:T(8,128)(2,1)S(1)} %collective-permute-done.20.refs_16_) | copy-start | bytes 1572868
  104.2 14.4 %collective-permute-start.17 = (bf16[4,2,32,1024]{3,2,1,0:T(8,128)(2,1)S(1)}, bf16[4,2,32,1024]{3,2,1,0:T(8,128)(2,1)}, u32[]{:S(2)}, u32[]{:S(2)}) collective-permute-start(bf16[4,2,32,1024]{3,2,1,0:T(8,128)(2,1)S(1)} %collective-permute-done.11.refs_6_), channel_id=1, source_target_pairs={{0,68},{64,0},{4,64},{68,4},{1,69},{65,1},{5,65},{69,5},{2,70},{66... | collective-permute-start | bytes 1572872 | tf_op jit(solution)/shard_map/ppermute | solution.py:387
  106.6 25.1 %copy-start.13 = (bf16[4,2,32,1024]{3,2,1,0:T(8,128)(2,1)}, bf16[4,2,32,1024]{3,2,1,0:T(8,128)(2,1)S(1)}, u32[]{:S(2)}) copy-start(bf16[4,2,32,1024]{3,2,1,0:T(8,128)(2,1)S(1)} %collective-permute-done.24.refs_20_) | copy-start | bytes 1572868
  106.6 23.0 %collective-permute-start.18 = (bf16[4,2,32,1024]{3,2,1,0:T(8,128)(2,1)}, bf16[4,2,32,1024]{3,2,1,0:T(8,128)(2,1)}, u32[]{:S(2)}, u32[]{:S(2)}) collective-permute-start(bf16[4,2,32,1024]{3,2,1,0:T(8,128)(2,1)} %copy-done.3), channel_id=1, source_target_pairs={{0,8},{8,16},{16,24},{24,0},{1,9},{9,17},{17,25},{25,1},{2,10},{10... | collective-permute-start | bytes 1572872 | tf_op jit(solution)/shard_map/ppermute | solution.py:388
  107.9 24.7 %copy-start.14 = (bf16[4,2,32,1024]{3,2,1,0:T(8,128)(2,1)}, bf16[4,2,32,1024]{3,2,1,0:T(8,128)(2,1)S(1)}, u32[]{:S(2)}) copy-start(bf16[4,2,32,1024]{3,2,1,0:T(8,128)(2,1)S(1)} %collective-permute-done.28.refs_24_) | copy-start | bytes 1572868
  107.9 22.6 %collective-permute-start.19 = (bf16[4,2,32,1024]{3,2,1,0:T(8,128)(2,1)}, bf16[4,2,32,1024]{3,2,1,0:T(8,128)(2,1)}, u32[]{:S(2)}, u32[]{:S(2)}) collective-permute-start(bf16[4,2,32,1024]{3,2,1,0:T(8,128)(2,1)} %collective-permute-done.15.refs_14_), channel_id=1, source_target_pairs={{0,24},{8,0},{16,8},{24,16},{1,25},{9,1},{17,9},{25,17},{2,26},{10... | collective-permute-start | bytes 1572872 | tf_op jit(solution)/shard_map/ppermute | solution.py:388
  110.5 22.3 %copy-start.15 = (bf16[4,2,32,1024]{3,2,1,0:T(8,128)(2,1)}, bf16[4,2,32,1024]{3,2,1,0:T(8,128)(2,1)S(1)}, u32[]{:S(2)}) copy-start(bf16[4,2,32,1024]{3,2,1,0:T(8,128)(2,1)S(1)} %collective-permute-done.32.refs_28_) | copy-start | bytes 1572868
  110.5 20.0 %collective-permute-start.21 = (bf16[4,2,32,1024]{3,2,1,0:T(8,128)(2,1)S(1)}, bf16[4,2,32,1024]{3,2,1,0:T(8,128)(2,1)S(1)}, u32[]{:S(2)}, u32[]{:S(2)}) collective-permute-start(bf16[4,2,32,1024]{3,2,1,0:T(8,128)(2,1)S(1)} %collective-permute-done.8.refs_1_), channel_id=1, source_target_pairs={{0,32},{32,0},{1,33},{33,1},{2,34},{34,2},{3,35},{35,3},{4,36},{36... | collective-permute-start | bytes 1572872 | tf_op jit(solution)/shard_map/ppermute | solution.py:420
  118.5 12.4 %collective-permute-start.22 = (bf16[4,2,32,1024]{3,2,1,0:T(8,128)(2,1)}, bf16[4,2,32,1024]{3,2,1,0:T(8,128)(2,1)S(1)}, u32[]{:S(2)}, u32[]{:S(2)}) collective-permute-start(bf16[4,2,32,1024]{3,2,1,0:T(8,128)(2,1)} %collective-permute-done.9.refs_2_), channel_id=1, source_target_pairs={{0,32},{32,0},{1,33},{33,1},{2,34},{34,2},{3,35},{35,3},{4,36},{36... | collective-permute-start | bytes 1572872 | tf_op jit(solution)/shard_map/ppermute | solution.py:420
  118.6 12.5 %collective-permute-start.25 = (bf16[4,2,32,1024]{3,2,1,0:T(8,128)(2,1)}, bf16[4,2,32,1024]{3,2,1,0:T(8,128)(2,1)S(1)}, u32[]{:S(2)}, u32[]{:S(2)}) collective-permute-start(bf16[4,2,32,1024]{3,2,1,0:T(8,128)(2,1)} %collective-permute-done.10.refs_5_), channel_id=1, source_target_pairs={{0,32},{32,0},{1,33},{33,1},{2,34},{34,2},{3,35},{35,3},{4,36},{36... | collective-permute-start | bytes 1572872 | tf_op jit(solution)/shard_map/ppermute | solution.py:420
  129.5 2.0 collective-permute-start.26
  130.5 2.1 collective-permute-start.29
  130.5 3.6 %copy-start.16 = (bf16[4,2,32,1024]{3,2,1,0:T(8,128)(2,1)}, bf16[4,2,32,1024]{3,2,1,0:T(8,128)(2,1)S(1)}, u32[]{:S(2)}) copy-start(bf16[4,2,32,1024]{3,2,1,0:T(8,128)(2,1)S(1)} %collective-permute-done.21.refs_17_) | copy-start | bytes 1572868
  130.5 3.6 %collective-permute-start.30 = (bf16[4,2,32,1024]{3,2,1,0:T(8,128)(2,1)}, bf16[4,2,32,1024]{3,2,1,0:T(8,128)(2,1)S(1)}, u32[]{:S(2)}, u32[]{:S(2)}) collective-permute-start(bf16[4,2,32,1024]{3,2,1,0:T(8,128)(2,1)} %collective-permute-done.13.refs_10_), channel_id=1, source_target_pairs={{0,32},{32,0},{1,33},{33,1},{2,34},{34,2},{3,35},{35,3},{4,36},{36... | collective-permute-start | bytes 1572872 | tf_op jit(solution)/shard_map/ppermute | solution.py:420
  131.0 3.2 %copy-start.17 = (bf16[4,2,32,1024]{3,2,1,0:T(8,128)(2,1)}, bf16[4,2,32,1024]{3,2,1,0:T(8,128)(2,1)S(1)}, u32[]{:S(2)}) copy-start(bf16[4,2,32,1024]{3,2,1,0:T(8,128)(2,1)S(1)} %collective-permute-done.22.refs_18_) | copy-start | bytes 1572868
  131.0 4.6 %collective-permute-start.33 = (bf16[4,2,32,1024]{3,2,1,0:T(8,128)(2,1)}, bf16[4,2,32,1024]{3,2,1,0:T(8,128)(2,1)S(1)}, u32[]{:S(2)}, u32[]{:S(2)}) collective-permute-start(bf16[4,2,32,1024]{3,2,1,0:T(8,128)(2,1)} %collective-permute-done.14.refs_13_), channel_id=1, source_target_pairs={{0,32},{32,0},{1,33},{33,1},{2,34},{34,2},{3,35},{35,3},{4,36},{36... | collective-permute-start | bytes 1572872 | tf_op jit(solution)/shard_map/ppermute | solution.py:420
  131.1 4.5 %copy-start.18 = (bf16[4,2,32,1024]{3,2,1,0:T(8,128)(2,1)}, bf16[4,2,32,1024]{3,2,1,0:T(8,128)(2,1)S(1)}, u32[]{:S(2)}) copy-start(bf16[4,2,32,1024]{3,2,1,0:T(8,128)(2,1)S(1)} %collective-permute-done.25.refs_21_) | copy-start | bytes 1572868
  131.1 5.5 %collective-permute-start.34 = (bf16[4,2,32,1024]{3,2,1,0:T(8,128)(2,1)}, bf16[4,2,32,1024]{3,2,1,0:T(8,128)(2,1)}, u32[]{:S(2)}, u32[]{:S(2)}) collective-permute-start(bf16[4,2,32,1024]{3,2,1,0:T(8,128)(2,1)} %collective-permute-done.15.refs_14_), channel_id=1, source_target_pairs={{0,32},{32,0},{1,33},{33,1},{2,34},{34,2},{3,35},{35,3},{4,36},{36... | collective-permute-start | bytes 1572872 | tf_op jit(solution)/shard_map/ppermute | solution.py:420
  131.5 4.1 %copy-start.19 = (bf16[4,2,32,1024]{3,2,1,0:T(8,128)(2,1)}, bf16[4,2,32,1024]{3,2,1,0:T(8,128)(2,1)S(1)}, u32[]{:S(2)}) copy-start(bf16[4,2,32,1024]{3,2,1,0:T(8,128)(2,1)S(1)} %collective-permute-done.26.refs_22_) | copy-start | bytes 1572868
  131.5 5.1 %collective-permute-start.23 = (bf16[4,2,32,1024]{3,2,1,0:T(8,128)(2,1)}, bf16[4,2,32,1024]{3,2,1,0:T(8,128)(2,1)}, u32[]{:S(2)}, u32[]{:S(2)}) collective-permute-start(bf16[4,2,32,1024]{3,2,1,0:T(8,128)(2,1)} %collective-permute-done.16.refs_3_), channel_id=1, source_target_pairs={{0,32},{32,0},{1,33},{33,1},{2,34},{34,2},{3,35},{35,3},{4,36},{36... | collective-permute-start | bytes 1572872 | tf_op jit(solution)/shard_map/ppermute | solution.py:420
  132.6 3.0 %copy-start.20 = (bf16[4,2,32,1024]{3,2,1,0:T(8,128)(2,1)}, bf16[4,2,32,1024]{3,2,1,0:T(8,128)(2,1)S(1)}, u32[]{:S(2)}) copy-start(bf16[4,2,32,1024]{3,2,1,0:T(8,128)(2,1)S(1)} %collective-permute-done.29.refs_25_) | copy-start | bytes 1572868
  132.6 4.0 %collective-permute-start.27 = (bf16[4,2,32,1024]{3,2,1,0:T(8,128)(2,1)}, bf16[4,2,32,1024]{3,2,1,0:T(8,128)(2,1)}, u32[]{:S(2)}, u32[]{:S(2)}) collective-permute-start(bf16[4,2,32,1024]{3,2,1,0:T(8,128)(2,1)} %collective-permute-done.17.refs_7_), channel_id=1, source_target_pairs={{0,32},{32,0},{1,33},{33,1},{2,34},{34,2},{3,35},{35,3},{4,36},{36... | collective-permute-start | bytes 1572872 | tf_op jit(solution)/shard_map/ppermute | solution.py:420
  134.1 1.5 copy-start.21
  134.1 3.1 %collective-permute-start.31 = (bf16[4,2,32,1024]{3,2,1,0:T(8,128)(2,1)}, bf16[4,2,32,1024]{3,2,1,0:T(8,128)(2,1)}, u32[]{:S(2)}, u32[]{:S(2)}) collective-permute-start(bf16[4,2,32,1024]{3,2,1,0:T(8,128)(2,1)} %collective-permute-done.18.refs_11_), channel_id=1, source_target_pairs={{0,32},{32,0},{1,33},{33,1},{2,34},{34,2},{3,35},{35,3},{4,36},{36... | collective-permute-start | bytes 1572872 | tf_op jit(solution)/shard_map/ppermute | solution.py:420
  135.6 0.8 copy-start.22
  136.4 2.3 collective-permute-start.35
  138.7 1.1 copy-start.4
  175.6 37.5 %collective-permute-start.36 = (bf16[4,4,2,2,16,4096]{5,4,3,2,1,0:T(8,128)(2,1)}, bf16[4,4,2,2,16,4096]{5,4,3,2,1,0:T(8,128)(2,1)}, u32[]{:S(2)}, u32[]{:S(2)}) collective-permute-start(bf16[4,4,2,2,16,4096]{5,4,3,2,1,0:T(8,128)(2,1)} %bitcast.90), channel_id=1, source_target_pairs={{0,32},{32,0},{1,33},{33,1},{2,34},{34,2},{3,35},{35,3},{4,36},{36... | collective-permute-start | bytes 25165832 | tf_op jit(solution)/shard_map/ppermute | solution.py:420
  234.4 23.2 %all-to-all-start.1 = ((bf16[32,16,1024]{2,1,0:T(8,128)(2,1)}), bf16[32,16,1024]{2,1,0:T(8,128)(2,1)S(1)}, u32[]{:S(2)}, u32[]{:S(2)}) async-start(bf16[32,16,1024]{2,1,0:T(8,128)(2,1)} %bitcast.87), calls=%async_computation.1 | async-start | bytes 2097152 | tf_op jit(solution)/shard_map/all_to_all | solution.py:490
  257.6 1.0 copy-start.6
Sparse Core Ops, SparseCore 0:
  31.1 36.4 all-gather.5
  102.3 73.2 all-gather.7

commit v8 on v5

--- a/solution.py
+++ b/solution.py
@@ -1,3 +1,4 @@
+import functools
 import math
 
 import jax
@@ -14,7 +15,8 @@
 D = 2048
 WIDTH = HEADS * HEAD
 N_SEQ = 32
-COLS = C // N_SEQ
+ROWS = C // 2
+COLS = ROWS // N_SEQ
 PAIR = 2 * HEAD
 STEPS = WIDTH // PAIR
 SEQ = ("x", "yhi", "z")
@@ -167,9 +169,12 @@
     return total
 
 
-def row_kernel(place_ref, x_ref, hid_ref, gain_ref, cos_ref, sin_ref, *refs):
+def row_kernel(first, place_ref, x_ref, hid_ref, gain_ref, cos_ref, sin_ref, *refs):
     pieces = refs[: 4 * len(RELATIVE)]
-    mid_ref, next_ref, w_ref, o_ref, att_ref, sems = refs[4 * len(RELATIVE) :]
+    key_ref, value_ref, mid_ref, next_ref = refs[4 * len(RELATIVE) : -4]
+    if first:
+        mid_ref, next_ref, key_ref, value_ref = refs[4 * len(RELATIVE) : -4]
+    w_ref, o_ref, att_ref, sems = refs[-4:]
     core = place_ref[0]
     start_copies(place_ref, pieces, sems, w_ref, o_ref)
     half = D // 2
@@ -188,14 +193,17 @@
             q = rotate(q2[:, lanes], cos_ref[...], sin_ref[...]).astype(jnp.bfloat16)
             k = rotate(k2[:, lanes], cos_ref[...], sin_ref[...]).astype(jnp.bfloat16)
             v = v2[:, lanes]
-            size = 256
-            for b in range(C // size):
-                end = (b + 1) * size
-                scores = dot_t(q[b * size : end], k[:end])
-                row = lax.broadcasted_iota(jnp.int32, scores.shape, 0) + b * size
-                keep = lax.broadcasted_iota(jnp.int32, scores.shape, 1) <= row
-                target = pl.ds(pl.multiple_of(g * PAIR + h * HEAD, HEAD), HEAD)
-                att_ref[b * size : end, target] = softmax_times(scores, keep, v[:end]).astype(jnp.bfloat16)
+            target = pl.ds(pl.multiple_of(g * PAIR + h * HEAD, HEAD), HEAD)
+            if first:
+                key_ref[:, target] = k
+                value_ref[:, target] = v
+            else:
+                k = jnp.concatenate([key_ref[:, target], k], 0)
+                v = jnp.concatenate([value_ref[:, target], v], 0)
+            scores = dot_t(q, k)
+            row = lax.broadcasted_iota(jnp.int32, scores.shape, 0) + (k.shape[0] - ROWS)
+            keep = lax.broadcasted_iota(jnp.int32, scores.shape, 1) <= row
+            att_ref[:, target] = softmax_times(scores, keep, v).astype(jnp.bfloat16)
         return 0
 
     lax.fori_loop(0, STEPS, step, 0)
@@ -220,33 +228,38 @@
             next_ref[rows, lanes] = (halves[h] * inv * gain_ref[:, lanes]).astype(jnp.bfloat16)
         return 0
 
-    lax.fori_loop(0, C // 128, finish, 0)
-
-
-def row_layer(place, x, hidden, gain, tables, pieces):
-    vmem = pl.BlockSpec(memory_space=pltpu.VMEM)
+    lax.fori_loop(0, ROWS // 128, finish, 0)
+
+
+def row_layer(place, x, hidden, gain, tables, pieces, kept):
+    first = kept is None
     hbm = pl.BlockSpec(memory_space=pltpu.HBM)
-    shape = jax.ShapeDtypeStruct((C, D), jnp.bfloat16)
+    mine = lambda width: pl.BlockSpec((ROWS, width), lambda i: (0 if first else 1, 0), pipeline_mode=pl.Buffered(1))
+    whole = lambda rows, width: pl.BlockSpec((rows, width), lambda i: (0, 0), pipeline_mode=pl.Buffered(1))
+    state = whole(ROWS, WIDTH)
+    wide = whole(ROWS, D)
+    shape = lambda width: jax.ShapeDtypeStruct((ROWS, width), jnp.bfloat16)
     return pl.pallas_call(
-        row_kernel,
-        out_shape=[shape, shape],
-        in_specs=[pl.BlockSpec(memory_space=pltpu.SMEM)]
-        + [vmem] * 5
-        + [hbm] * len(pieces),
-        out_specs=[vmem, vmem],
+        functools.partial(row_kernel, first),
+        grid=(1,),
+        out_shape=[shape(D), shape(D)] + [shape(WIDTH)] * (2 if first else 0),
+        in_specs=[pl.BlockSpec(memory_space=pltpu.SMEM), mine(D), mine(D), whole(1, D), mine(HEAD), mine(HEAD)]
+        + [hbm] * len(pieces)
+        + ([] if first else [state, state]),
+        out_specs=[wide, wide] + ([state, state] if first else []),
         scratch_shapes=[
             pltpu.VMEM((2, 2, 16, 2, 32, QKV_PART), jnp.bfloat16),
             pltpu.VMEM((2, 16, 2, 32, D // 2), jnp.bfloat16),
-            pltpu.VMEM((C, WIDTH), jnp.bfloat16),
+            pltpu.VMEM((ROWS, WIDTH), jnp.bfloat16),
             pltpu.SemaphoreType.DMA((6,)),
         ],
         compiler_params=pltpu.CompilerParams(vmem_limit_bytes=48 * MIB),
         cost_estimate=pl.CostEstimate(
-            flops=2 * C * D * 4 * WIDTH + 4 * C * C * WIDTH,
-            bytes_accessed=2 * (4 * C * D + 4 * D * WIDTH),
-            transcendentals=C * C * HEADS,
+            flops=C * D * 4 * WIDTH + 2 * C * C * WIDTH,
+            bytes_accessed=2 * (2 * C * D + 4 * D * WIDTH),
+            transcendentals=C * C * HEADS // 2,
         ),
-    )(place, x, hidden, gain, *tables, *pieces)
+    )(place, x, hidden, gain, *tables, *pieces, *([] if first else kept))
 
 
 def column_kernel(core_ref, x_ref, cos_ref, sin_ref, own_plane, other_plane, out_ref, w_ref, hid_ref, sems):
@@ -264,8 +277,8 @@
                     pltpu.make_async_copy(src, dst, sems.at[g]).start()
 
     def selection(transposed):
-        a = lax.broadcasted_iota(jnp.int32, (C, C), 1 if transposed else 0)
-        b = lax.broadcasted_iota(jnp.int32, (C, C), 0 if transposed else 1)
+        a = lax.broadcasted_iota(jnp.int32, (ROWS, ROWS), 1 if transposed else 0)
+        b = lax.broadcasted_iota(jnp.int32, (ROWS, ROWS), 0 if transposed else 1)
         same = (a // N_SEQ == lax.rem(b, COLS)) & (lax.rem(a, N_SEQ) == b // COLS)
         return jnp.where(same, 1.0, 0.0).astype(jnp.bfloat16)
 
@@ -302,7 +315,7 @@
             k = rotate(k2[:, lanes], cos_ref[...], sin_ref[...]).astype(jnp.bfloat16)
             v = v2[:, lanes]
             blocks = []
-            for b in range(C // size):
+            for b in range(ROWS // size):
                 rows = slice(b * size, (b + 1) * size)
                 blocks.append(softmax_times(dot_t(q[rows], k[rows]), keep, v[rows]).astype(jnp.bfloat16))
             heads.append(jnp.concatenate(blocks, 0))
@@ -319,19 +332,19 @@
     hbm = pl.BlockSpec(memory_space=pltpu.HBM)
     return pl.pallas_call(
         column_kernel,
-        out_shape=jax.ShapeDtypeStruct((C, WIDTH), jnp.bfloat16),
+        out_shape=jax.ShapeDtypeStruct((ROWS, WIDTH), jnp.bfloat16),
         in_specs=[pl.BlockSpec(memory_space=pltpu.SMEM)] + [vmem] * 3 + [hbm] * 2,
         out_specs=vmem,
         scratch_shapes=[
             pltpu.VMEM((STEPS, 2, 2, 4, 2, 4, 16, 3 * PAIR), jnp.bfloat16),
-            pltpu.VMEM((C, D), jnp.bfloat16),
+            pltpu.VMEM((ROWS, D), jnp.bfloat16),
             pltpu.SemaphoreType.DMA((STEPS,)),
         ],
         compiler_params=pltpu.CompilerParams(vmem_limit_bytes=56 * MIB),
         cost_estimate=pl.CostEstimate(
-            flops=2 * C * D * 3 * WIDTH + 4 * C * C * WIDTH,
+            flops=C * D * 3 * WIDTH + C * C * WIDTH,
             bytes_accessed=2 * (C * D + 3 * D * WIDTH + C * WIDTH),
-            transcendentals=C * C * HEADS,
+            transcendentals=C * C * HEADS // 4,
         ),
     )(core, x, *tables, *planes)
 
@@ -348,17 +361,20 @@
     return total
 
 
-def final_kernel(core_ref, att_ref, own_ref, other_ref, resid_ref, out_ref):
+def final_kernel(core_ref, att_ref, own_ref, other_ref, resid_ref, *refs):
+    out_ref = refs[-1]
     out_ref[...] = branch_sum(core_ref[0], att_ref, own_ref, other_ref, resid_ref).astype(jnp.bfloat16)
 
 
-def output_layer(core, attended, own, other, resid):
+def output_layer(core, attended, own, other, resid, out):
     size = 128
+    second = out is not None
+    start = ROWS // size if second else 0
     block = lambda width: pl.BlockSpec((size, width), lambda i: (i, 0))
     whole = lambda shape: pl.BlockSpec(shape, lambda i: (0, 0), pipeline_mode=pl.Buffered(1))
     return pl.pallas_call(
         final_kernel,
-        grid=(C // size,),
+        grid=(ROWS // size,),
         out_shape=jax.ShapeDtypeStruct((C, D), jnp.bfloat16),
         in_specs=[
             pl.BlockSpec(memory_space=pltpu.SMEM),
@@ -366,17 +382,19 @@
             whole(own.shape),
             whole(other.shape),
             block(D),
-        ],
-        out_specs=block(D),
+        ]
+        + ([pl.BlockSpec(memory_space=pl.ANY)] if second else []),
+        out_specs=pl.BlockSpec((size, D), lambda i: (start + i, 0)),
+        input_output_aliases={5: 0} if second else {},
         compiler_params=pltpu.CompilerParams(
             dimension_semantics=("arbitrary",), vmem_limit_bytes=54 * MIB
         ),
         cost_estimate=pl.CostEstimate(
-            flops=2 * C * D * WIDTH,
-            bytes_accessed=2 * (2 * C * D + D * WIDTH + C * WIDTH),
+            flops=C * D * WIDTH,
+            bytes_accessed=2 * (C * D + D * WIDTH + C * WIDTH // 2),
             transcendentals=0,
         ),
-    )(core, attended, own, other, resid)
+    )(core, attended, own, other, resid, *([out] if second else []))
 
 
 def shift(value, axis, by):
@@ -446,7 +464,7 @@
 
 def column_line(inputs, output):
     shard = jnp.concatenate([by_step(inputs), fold_output(output)], 1)
-    return lax.all_gather(shard, ("ylo", "yhi"), axis=0)
+    return lax.all_gather(jnp.concatenate([shard, shard], 1), ("ylo", "yhi"), axis=0)[:, :, : 4 * WIDTH]
 
 
 def column_plane(line):
@@ -470,27 +488,36 @@
     block_starts = starts[0]
     own_start = lax.dynamic_index_in_dim(block_starts, seq, 0, keepdims=False)
     row_tables = rotary_tables(own_start + jnp.arange(C, dtype=jnp.int32), frequency)
-    columns = seq.astype(jnp.int32) * COLS + jnp.arange(COLS, dtype=jnp.int32)
-    column_positions = (columns[:, None] + block_starts[None, :]).reshape(C)
-    column_tables = rotary_tables(column_positions, frequency)
-
+    column_tables = []
+    for half in range(2):
+        columns = half * ROWS + seq.astype(jnp.int32) * COLS + jnp.arange(COLS, dtype=jnp.int32)
+        positions = (columns[:, None] + block_starts[None, :]).reshape(ROWS)
+        column_tables.append(rotary_tables(positions, frequency))
     hidden = normed_slots(core_scalar, residual, gain_first.reshape(1, D))
 
     line = column_line(inputs_second, output_second)
     first = inner_rings(lines(inputs_first, output_first))
-    first, hidden, row_tables, column_tables = lax.optimization_barrier((first, hidden, row_tables, column_tables))
-    first_hop = outer_hops(first)
-    line, _ = lax.optimization_barrier((line, first_hop))
+    first, line = lax.optimization_barrier((first, line))
     plane = column_plane(line)
-    pieces = both_cores(outer_forwards(first_hop))
-
-    middle, hidden = row_layer(place, residual, hidden, gain_second.reshape(1, D), row_tables, pieces)
-    plane, hidden = lax.optimization_barrier((plane, hidden))
+    hops = outer_hops(first)
+    hops, hidden, row_tables, column_tables = lax.optimization_barrier((hops, hidden, row_tables, column_tables))
+    pieces = both_cores(outer_forwards(hops))
+    gain = gain_second.reshape(1, D)
+    exchange = lambda value: lax.all_to_all(value, SEQ, split_axis=0, concat_axis=0, tiled=True)
+
+    middle_a, next_a, *kept = row_layer(place, residual, hidden, gain, row_tables, pieces, None)
+    plane, next_a = lax.optimization_barrier((plane, next_a))
     planes = (plane, swap(plane))
-    hidden = lax.all_to_all(hidden, SEQ, split_axis=0, concat_axis=0, tiled=True)
-    attended = column_layer(core_scalar, hidden, column_tables, planes)
-    attended = lax.all_to_all(attended, SEQ, split_axis=0, concat_axis=0, tiled=True)
-    return output_layer(core_scalar, attended, *[column_output(p) for p in planes], middle)[None]
+    middle_b, next_b = row_layer(place, residual, hidden, gain, row_tables, pieces, kept)
+    next_a = exchange(next_a)
+    next_b = exchange(next_b)
+    attended_a = column_layer(core_scalar, next_a, column_tables[0], planes)
+    attended_b = column_layer(core_scalar, next_b, column_tables[1], planes)
+    attended_a = exchange(attended_a)
+    attended_b = exchange(attended_b)
+    output = [column_output(p) for p in planes]
+    out = output_layer(core_scalar, attended_a, *output, middle_a, None)
+    return output_layer(core_scalar, attended_b, *output, middle_b, out)[None]
 
 
 def solution(mesh):

time: 262 us -> 271 us (1.034)
  blocking collectives: 80.8 us -> 14.1 us
  waiting for transfers between devices: 43.1 us -> 83.1 us
  starting transfers between devices: 34.5 us -> 59.1 us
  Pallas kernels: 54.7 us -> 65.5 us
    all_to_all x1 -> x0, blocking collectives: 37.5 us -> none  [shards(): lax.all_to_all(hidden, SEQ, split_axis=0, concat_axis=0, tiled=True)]
    all_gather x1 -> x0, blocking collectives: 29.2 us -> none  [column_line(): return lax.all_gather(shard, ('ylo', 'yhi'), axis=0)]
    ppermute x8, waiting for transfers between devices: 5.84 us -> 33.2 us  [shift(): lax.ppermute(value, ('ylo', 'yhi'), [(where(y), where((y + by) % 4)) for...]
    ppermute x8, waiting for transfers between devices: 12.9 us -> 37.3 us  [shift(): return lax.ppermute(value, axis, [(i, (i + by) % 4) for i in range(4)])]
    all_to_all x1 -> x4, starting transfers between devices: 5.48 us -> 29.6 us  [shards(): lax.all_to_all(value, SEQ, split_axis=0, concat_axis=0, tiled=True)]
    pallas_call x3 -> x6, Pallas kernels: 52.6 us -> 63.4 us  [the longest x2 28.6 us: row_layer(): pl.pallas_call(functools.partial(row_kernel, first), grid=(1,), out_shape...]
    all_gather x1, waiting for transfers between devices: 9.39 us -> 0.01 us  [column_plane(): lax.all_gather(line, ('x', 'z'), axis=0).reshape(4, 4, 2, 2, 16, 4 * WIDTH)]
    all_to_all x1 -> x4, waiting for transfers between devices: 11.1 us -> 6.22 us  [shards(): lax.all_to_all(value, SEQ, split_axis=0, concat_axis=0, tiled=True)]
  transfers between devices with their start and end apart: 29 -> 33, of which waited for: 8 -> 16; matrix products, arithmetic and copies ran while one was open for 8% -> 7% of each run, Pallas kernels for 10% -> 23%
where the time goes in v8:
time: 271 us; the launch traced here: 269 us
  waiting for transfers between devices  83.1 us (31%)
  Pallas kernels  65.5 us (24%)
  starting transfers between devices  59.1 us (22%)
  local copies, waits for them, and re-layouts  23.9 us (9%)
  between operations  15.2 us (6%)
  blocking collectives  14.1 us (5%)
  other arithmetic  8.25 us (3%)
    ppermute x8, waiting for transfers between devices, shift(): return lax.ppermute(value, axis, [(i, (i + by) % 4) for i in range(4)])  37.3 us
    ppermute x8, waiting for transfers between devices, shift(): lax.ppermute(value, ('ylo', 'yhi'), [(where(y), where((y + by) % 4)) for...  33.2 us
    all_to_all x4, starting transfers between devices, shards(): lax.all_to_all(value, SEQ, split_axis=0, concat_axis=0, tiled=True)  29.6 us
    pallas_call x2, Pallas kernels, row_layer(): pl.pallas_call(functools.partial(row_kernel, first), grid=(1,), out_shape...  28.6 us
    pallas_call x2, Pallas kernels, column_layer(): pl.pallas_call(column_kernel, out_shape=jax.ShapeDtypeStruct((ROWS, WIDTH...  25.3 us
    all_gather x1, blocking collectives, lines(): rows = lax.all_gather(shard, 'z', axis=0)  14.1 us
    ppermute x8, starting transfers between devices, shift(): return lax.ppermute(value, axis, [(i, (i + by) % 4) for i in range(4)])  13.7 us
    ppermute x8, starting transfers between devices, shift(): lax.ppermute(value, ('ylo', 'yhi'), [(where(y), where((y + by) % 4)) for...  13.6 us
  transfers between devices with their start and end apart: 33, of which 16 were waited for; matrix products, arithmetic and copies ran while one was open for 7% of the time, Pallas kernels for 23%

profile of v8, /device:TPU:0, one launch (start us, length us, event | category | flops | bytes accessed | tf_op | source)
XLA Modules:
  0.0 269.1 jit_solution(5473704560085072446)
XLA Ops:
  6.5 0.7 fusion.13
  7.3 0.9 reshape.121
  8.4 0.7 maximum_maximum_fusion
  9.2 0.7 fusion.14
  9.9 0.9 reshape.116
  11.1 14.1 %all-gather = bf16[64,4096]{1,0:T(8,128)(2,1)S(1)} all-gather(bf16[16,4096]{1,0:T(8,128)(2,1)S(1)} %maximum_maximum_fusion.1), channel_id=2, replica_groups=mesh['ylo'=2,'core'=2,'x'=4,'yhi'=2,'z'=4] {'z'}, dimensions={0}, use_global_device_ids=true | all-gather | bytes 655360 | tf_op jit(solution)/shard_map/all_gather | solution.py:436
  25.3 2.8 %collective-permute-start.1 = (bf16[2,32,2048]{2,1,0:T(8,128)(2,1)S(1)}, bf16[2,32,2048]{2,1,0:T(8,128)(2,1)S(1)}, u32[]{:S(2)}, u32[]{:S(2)}) collective-permute-start(bf16[2,32,2048]{2,1,0:T(8,128)(2,1)S(1)} %get-tuple-element.58), channel_id=1, source_target_pairs={{0,24},{8,0},{16,8},{24,16},{1,25},{9,1},{17,9},{25,17},{2,26},{10... | collective-permute-start | bytes 786440 | tf_op jit(solution)/shard_map/ppermute | solution.py:404
  28.2 3.1 %collective-permute-start.5 = (bf16[2,32,2048]{2,1,0:T(8,128)(2,1)S(1)}, bf16[2,32,2048]{2,1,0:T(8,128)(2,1)S(1)}, u32[]{:S(2)}, u32[]{:S(2)}) collective-permute-start(bf16[2,32,2048]{2,1,0:T(8,128)(2,1)S(1)} %get-tuple-element.56), channel_id=1, source_target_pairs={{0,68},{64,0},{4,64},{68,4},{1,69},{65,1},{5,65},{69,5},{2,70},{66... | collective-permute-start | bytes 786440 | tf_op jit(solution)/shard_map/ppermute | solution.py:403
  31.3 1.0 collective-permute-done.1
  32.3 3.8 %collective-permute-start.3 = (bf16[2,32,1024]{2,1,0:T(8,128)(2,1)S(1)}, bf16[2,32,1024]{2,1,0:T(8,128)(2,1)S(1)}, u32[]{:S(2)}, u32[]{:S(2)}) collective-permute-start(bf16[2,32,1024]{2,1,0:T(8,128)(2,1)S(1)} %slice.97), channel_id=1, source_target_pairs={{0,24},{8,0},{16,8},{24,16},{1,25},{9,1},{17,9},{25,17},{2,26},{10... | collective-permute-start | bytes 393224 | tf_op jit(solution)/shard_map/ppermute | solution.py:404
  36.1 9.6 %collective-permute-done.5 = bf16[2,32,2048]{2,1,0:T(8,128)(2,1)S(1)} collective-permute-done((bf16[2,32,2048]{2,1,0:T(8,128)(2,1)S(1)}, bf16[2,32,2048]{2,1,0:T(8,128)(2,1)S(1)}, u32[]{:S(2)}, u32[]{:S(2)}) %collective-permute-start.5) | collective-permute-done | bytes 262176 | tf_op jit(solution)/shard_map/ppermute | solution.py:403
  45.8 3.8 %collective-permute-start.7 = (bf16[2,32,1024]{2,1,0:T(8,128)(2,1)S(1)}, bf16[2,32,1024]{2,1,0:T(8,128)(2,1)S(1)}, u32[]{:S(2)}, u32[]{:S(2)}) collective-permute-start(bf16[2,32,1024]{2,1,0:T(8,128)(2,1)S(1)} %slice.101), channel_id=1, source_target_pairs={{0,68},{64,0},{4,64},{68,4},{1,69},{65,1},{5,65},{69,5},{2,70},{66... | collective-permute-start | bytes 393224 | tf_op jit(solution)/shard_map/ppermute | solution.py:403
  49.7 2.4 collective-permute-done.7
  52.1 3.7 %collective-permute-done.6 = bf16[2,32,1024]{2,1,0:T(8,128)(2,1)S(1)} collective-permute-done((bf16[2,32,1024]{2,1,0:T(8,128)(2,1)S(1)}, bf16[2,32,1024]{2,1,0:T(8,128)(2,1)S(1)}, u32[]{:S(2)}, u32[]{:S(2)}) %collective-permute-start.6) | collective-permute-done | bytes 131104 | tf_op jit(solution)/shard_map/ppermute | solution.py:403
  55.8 1.1 pad_maximum_fusion.refs_0_
  57.1 2.4 slice.102
  61.5 0.7 constant_dynamic-slice_fusion
  62.4 2.1 shard_map.91.hid_ref
  64.5 0.7 add_convert_fusion.2
  65.3 3.2 %collective-permute-start.9 = (bf16[4,2,32,2048]{3,2,1,0:T(8,128)(2,1)}, bf16[4,2,32,2048]{3,2,1,0:T(8,128)(2,1)S(1)}, u32[]{:S(2)}, u32[]{:S(2)}) collective-permute-start(bf16[4,2,32,2048]{3,2,1,0:T(8,128)(2,1)} %pad_maximum_fusion.refs_0_), channel_id=1, source_target_pairs={{0,68},{64,0},{4,64},{68,4},{1,69},{65,1},{5,65},{69,5},{2,70},{66... | collective-permute-start | bytes 3145736 | tf_op jit(solution)/shard_map/ppermute | solution.py:403
  68.5 1.2 collective-permute-start.10
  69.7 2.0 collective-permute-start.11
  71.8 1.0 fusion.7
  72.8 0.8 pad_maximum_fusion.6.cos_ref
  73.6 0.8 pad_maximum_fusion.8.cos_ref
  74.3 0.8 pad_maximum_fusion.7.sin_ref
  75.1 0.7 pad_maximum_fusion.9.sin_ref
  75.8 1.0 fusion.6
  77.1 12.4 %collective-permute-done.8.refs_1_ = bf16[4,2,32,2048]{3,2,1,0:T(8,128)(2,1)S(1)} collective-permute-done((bf16[4,2,32,2048]{3,2,1,0:T(8,128)(2,1)}, bf16[4,2,32,2048]{3,2,1,0:T(8,128)(2,1)S(1)}, u32[]{:S(2)}, u32[]{:S(2)}) %collective-permute-start.8) | collective-permute-done | bytes 1048608 | tf_op jit(solution)/shard_map/ppermute | solution.py:403
  89.5 11.5 %collective-permute-done.10.refs_6_ = bf16[4,2,32,2048]{3,2,1,0:T(8,128)(2,1)} collective-permute-done((bf16[4,2,32,2048]{3,2,1,0:T(8,128)(2,1)S(1)}, bf16[4,2,32,2048]{3,2,1,0:T(8,128)(2,1)}, u32[]{:S(2)}, u32[]{:S(2)}) %collective-permute-start.10) | collective-permute-done | bytes 1048608 | tf_op jit(solution)/shard_map/ppermute | solution.py:404
  100.9 2.6 collective-permute-done.11.refs_7_
  103.7 3.3 %collective-permute-start.13 = (bf16[4,2,32,1024]{3,2,1,0:T(8,128)(2,1)S(1)}, bf16[4,2,32,1024]{3,2,1,0:T(8,128)(2,1)S(1)}, u32[]{:S(2)}, u32[]{:S(2)}) collective-permute-start(bf16[4,2,32,1024]{3,2,1,0:T(8,128)(2,1)S(1)} %slice.87), channel_id=1, source_target_pairs={{0,68},{64,0},{4,64},{68,4},{1,69},{65,1},{5,65},{69,5},{2,70},{66... | collective-permute-start | bytes 1572872 | tf_op jit(solution)/shard_map/ppermute | solution.py:403
  107.5 1.1 slice.88
  108.6 1.1 slice.89
  109.8 5.0 %collective-permute-done.12.refs_3_ = bf16[4,2,32,1024]{3,2,1,0:T(8,128)(2,1)S(1)} collective-permute-done((bf16[4,2,32,1024]{3,2,1,0:T(8,128)(2,1)S(1)}, bf16[4,2,32,1024]{3,2,1,0:T(8,128)(2,1)S(1)}, u32[]{:S(2)}, u32[]{:S(2)}) %collective-permute-start.12) | collective-permute-done | bytes 524320 | tf_op jit(solution)/shard_map/ppermute | solution.py:403
  114.9 3.6 %collective-permute-start.15 = (bf16[4,2,32,1024]{3,2,1,0:T(8,128)(2,1)S(1)}, bf16[4,2,32,1024]{3,2,1,0:T(8,128)(2,1)S(1)}, u32[]{:S(2)}, u32[]{:S(2)}) collective-permute-start(bf16[4,2,32,1024]{3,2,1,0:T(8,128)(2,1)S(1)} %slice.89), channel_id=1, source_target_pairs={{0,24},{8,0},{16,8},{24,16},{1,25},{9,1},{17,9},{25,17},{2,26},{10... | collective-permute-start | bytes 1572872 | tf_op jit(solution)/shard_map/ppermute | solution.py:404
  118.6 22.3 %collective-permute-done.14.refs_8_ = bf16[4,2,32,1024]{3,2,1,0:T(8,128)(2,1)S(1)} collective-permute-done((bf16[4,2,32,1024]{3,2,1,0:T(8,128)(2,1)S(1)}, bf16[4,2,32,1024]{3,2,1,0:T(8,128)(2,1)S(1)}, u32[]{:S(2)}, u32[]{:S(2)}) %collective-permute-start.14) | collective-permute-done | bytes 524320 | tf_op jit(solution)/shard_map/ppermute | solution.py:404
  142.1 2.8 %collective-permute-done.19.refs_13_ = bf16[4,2,32,1024]{3,2,1,0:T(8,128)(2,1)S(1)} collective-permute-done((bf16[4,2,32,1024]{3,2,1,0:T(8,128)(2,1)S(1)}, bf16[4,2,32,1024]{3,2,1,0:T(8,128)(2,1)S(1)}, u32[]{:S(2)}, u32[]{:S(2)}) %collective-permute-start.19) | collective-permute-done | bytes 524320 | tf_op jit(solution)/shard_map/ppermute | solution.py:423
  145.1 1.4 collective-permute-done.20.refs_14_
  146.5 0.8 copy-done.2
  147.5 1.6 collective-permute-done.21.refs_15_
  149.6 1.0 copy-done.3
  150.7 13.9 %shard_map.92 = (bf16[256,2048]{1,0:T(8,128)(2,1)}, bf16[256,2048]{1,0:T(8,128)(2,1)}, bf16[256,1024]{1,0:T(8,128)(2,1)S(1)}, bf16[256,1024]{1,0:T(8,128)(2,1)S(1)}) custom-call(s32[3]{0:T(128)S(1)} %pad_add_fusion.place_ref, bf16[512,2048]{1,0:T(8,128)(2,1)} %bitcast.62, bf16[512,2048]{1,0:T(8,128)(2,1)} %copy-done.1, f32[1,2048]{1,0:T(1,128)S(1)} %bitcast.65, ...), custom_call_target="tpu_custom_call" | custom-call | flops 4831838208 | bytes 20971520 | tf_op jit(solution)/shard_map/pallas_call | solution.py:242
  164.5 0.8 copy-done.5
  165.4 0.8 copy-done.7
  166.3 5.6 %all-to-all-start.2 = ((bf16[32,8,2048]{2,1,0:T(8,128)(2,1)}), bf16[32,8,2048]{2,1,0:T(8,128)(2,1)}, u32[]{:S(2)}, u32[]{:S(2)}) async-start(bf16[32,8,2048]{2,1,0:T(8,128)(2,1)} %bitcast.85), calls=%async_computation.2 | async-start | bytes 2097152 | tf_op jit(solution)/shard_map/all_to_all | solution.py:506
  171.9 1.0 copy-done.4
  172.9 1.0 copy-done.6
  174.0 1.0 copy-done.8
  175.0 14.7 %shard_map.93 = (bf16[256,2048]{1,0:T(8,128)(2,1)}, bf16[256,2048]{1,0:T(8,128)(2,1)}) custom-call(s32[3]{0:T(128)S(1)} %pad_add_fusion.place_ref, bf16[512,2048]{1,0:T(8,128)(2,1)} %bitcast.63, bf16[512,2048]{1,0:T(8,128)(2,1)} %copy-done.1, f32[1,2048]{1,0:T(1,128)S(1)} %bitcast.66, f32[512,128]{1,0:T(8,128)S(1)} %get-tuple-element.32.cos_ref, ...), custom_call_target="tpu_custom_call" | custom-call | flops 4831838208 | bytes 20971520 | tf_op jit(solution)/shard_map/pallas_call | solution.py:242
  189.9 9.6 %all-to-all-start = ((bf16[32,8,2048]{2,1,0:T(8,128)(2,1)}), bf16[32,8,2048]{2,1,0:T(8,128)(2,1)S(1)}, u32[]{:S(2)}, u32[]{:S(2)}) async-start(bf16[32,8,2048]{2,1,0:T(8,128)(2,1)} %bitcast.84), calls=%async_computation | async-start | bytes 2097152 | tf_op jit(solution)/shard_map/all_to_all | solution.py:506
  199.5 12.6 %shard_map.95 = bf16[256,1024]{1,0:T(8,128)(2,1)} custom-call(s32[1]{0:T(128)} %bitcast.core_ref, bf16[256,2048]{1,0:T(8,128)(2,1)} %bitcast.40.x_ref, f32[256,128]{1,0:T(8,128)} %pad_maximum_fusion.6.cos_ref, f32[256,128]{1,0:T(8,128)} %pad_maximum_fusion.7.sin_ref, bf16[4,4,2,2,16,4096]{5,4,3,2,1,0:T(8,128)(2,1)} %bitcast.69, ...), custom_call_target="tpu_custom_call" | custom-call | flops 3489660928 | bytes 15728640 | tf_op jit(solution)/shard_map/pallas_call | solution.py:333
  212.1 5.3 %all-to-all-done = bf16[32,8,2048]{2,1,0:T(8,128)(2,1)S(1)} async-done(((bf16[32,8,2048]{2,1,0:T(8,128)(2,1)}), bf16[32,8,2048]{2,1,0:T(8,128)(2,1)S(1)}, u32[]{:S(2)}, u32[]{:S(2)}) %all-to-all-start) | async-done | bytes 1048608 | tf_op jit(solution)/shard_map/all_to_all | solution.py:506
  217.5 4.8 %all-to-all-start.3 = ((bf16[32,8,1024]{2,1,0:T(8,128)(2,1)}), bf16[32,8,1024]{2,1,0:T(8,128)(2,1)S(1)}, u32[]{:S(2)}, u32[]{:S(2)}) async-start(bf16[32,8,1024]{2,1,0:T(8,128)(2,1)} %bitcast.80), calls=%async_computation.3 | async-start | bytes 1048576 | tf_op jit(solution)/shard_map/all_to_all | solution.py:506
  222.3 12.7 %shard_map.94 = bf16[256,1024]{1,0:T(8,128)(2,1)} custom-call(s32[1]{0:T(128)} %bitcast.core_ref, bf16[256,2048]{1,0:T(8,128)(2,1)} %bitcast.76, f32[256,128]{1,0:T(8,128)} %pad_maximum_fusion.8.cos_ref, f32[256,128]{1,0:T(8,128)} %pad_maximum_fusion.9.sin_ref, bf16[4,4,2,2,16,4096]{5,4,3,2,1,0:T(8,128)(2,1)} %bitcast.70, ...), custom_call_target="tpu_custom_call" | custom-call | flops 3489660928 | bytes 15728640 | tf_op jit(solution)/shard_map/pallas_call | solution.py:333
  235.0 9.6 %all-to-all-start.1 = ((bf16[32,8,1024]{2,1,0:T(8,128)(2,1)}), bf16[32,8,1024]{2,1,0:T(8,128)(2,1)S(1)}, u32[]{:S(2)}, u32[]{:S(2)}) async-start(bf16[32,8,1024]{2,1,0:T(8,128)(2,1)} %bitcast.78), calls=%async_computation.1 | async-start | bytes 1048576 | tf_op jit(solution)/shard_map/all_to_all | solution.py:506
  244.6 1.8 slice_bitcast_fusion.1
  246.4 1.5 copy.19
  247.9 1.8 slice_bitcast_fusion
  249.6 1.5 copy.20
  251.1 4.8 %shard_map.96.refs_0_ = bf16[512,2048]{1,0:T(8,128)(2,1)} custom-call(s32[1]{0:T(128)} %bitcast.core_ref, bf16[256,1024]{1,0:T(8,128)(2,1)} %bitcast.77, bf16[512,2048]{1,0:T(8,128)(2,1)} %bitcast.72, bf16[512,2048]{1,0:T(8,128)(2,1)} %bitcast.74, bf16[256,2048]{1,0:T(8,128)(2,1)} %get-tuple-element.52.resid_ref), custom_call_target="tpu_custom_call" | custom-call | flops 1073741824 | bytes 6815744 | tf_op jit(solution)/shard_map/pallas_call | solution.py:375
  255.9 0.8 all-to-all-done.1
  256.7 0.8 copy-done.19
  257.5 4.8 %shard_map.97 = bf16[512,2048]{1,0:T(8,128)(2,1)} custom-call(s32[1]{0:T(128)} %bitcast.core_ref, bf16[256,1024]{1,0:T(8,128)(2,1)} %bitcast.79, bf16[512,2048]{1,0:T(8,128)(2,1)} %bitcast.73, bf16[512,2048]{1,0:T(8,128)(2,1)} %bitcast.75, bf16[256,2048]{1,0:T(8,128)(2,1)} %get-tuple-element.48.resid_ref, ...), custom_call_target="tpu_custom_call", output_to_operand_aliasing={{}: (5, {})} | custom-call | flops 1073741824 | bytes 6815744 | tf_op jit(solution)/shard_map/pallas_call | solution.py:375
  (105 shorter events, 5.5 us)
Async XLA Ops:
  6.5 50.6 %all-gather.6.cloned.1.call-start = ((), (), s32[]{:S(2)}) async-start(), calls=%async_computation.4 | async-start | bytes 1310720 | tf_op jit(solution)/shard_map/all_gather | solution.py:467
  9.1 157.0 %all-gather.8.cloned.1.call-start = ((), (), s32[]{:S(2)}) async-start(), calls=%async_computation.5 | async-start | bytes 8912896 | tf_op jit(solution)/shard_map/all_gather | solution.py:471
  25.3 7.0 %collective-permute-start.1 = (bf16[2,32,2048]{2,1,0:T(8,128)(2,1)S(1)}, bf16[2,32,2048]{2,1,0:T(8,128)(2,1)S(1)}, u32[]{:S(2)}, u32[]{:S(2)}) collective-permute-start(bf16[2,32,2048]{2,1,0:T(8,128)(2,1)S(1)} %get-tuple-element.58), channel_id=1, source_target_pairs={{0,24},{8,0},{16,8},{24,16},{1,25},{9,1},{17,9},{25,17},{2,26},{10... | collective-permute-start | bytes 786440 | tf_op jit(solution)/shard_map/ppermute | solution.py:404
  28.1 7.9 %collective-permute-start = (bf16[2,32,2048]{2,1,0:T(8,128)(2,1)S(1)}, bf16[2,32,2048]{2,1,0:T(8,128)(2,1)S(1)}, u32[]{:S(2)}, u32[]{:S(2)}) collective-permute-start(bf16[2,32,2048]{2,1,0:T(8,128)(2,1)S(1)} %get-tuple-element.58), channel_id=1, source_target_pairs={{0,8},{8,16},{16,24},{24,0},{1,9},{9,17},{17,25},{25,1},{2,10},{10... | collective-permute-start | bytes 786440 | tf_op jit(solution)/shard_map/ppermute | solution.py:404
  28.2 17.6 %collective-permute-start.5 = (bf16[2,32,2048]{2,1,0:T(8,128)(2,1)S(1)}, bf16[2,32,2048]{2,1,0:T(8,128)(2,1)S(1)}, u32[]{:S(2)}, u32[]{:S(2)}) collective-permute-start(bf16[2,32,2048]{2,1,0:T(8,128)(2,1)S(1)} %get-tuple-element.56), channel_id=1, source_target_pairs={{0,68},{64,0},{4,64},{68,4},{1,69},{65,1},{5,65},{69,5},{2,70},{66... | collective-permute-start | bytes 786440 | tf_op jit(solution)/shard_map/ppermute | solution.py:403
  31.3 18.3 %collective-permute-start.4 = (bf16[2,32,2048]{2,1,0:T(8,128)(2,1)S(1)}, bf16[2,32,2048]{2,1,0:T(8,128)(2,1)S(1)}, u32[]{:S(2)}, u32[]{:S(2)}) collective-permute-start(bf16[2,32,2048]{2,1,0:T(8,128)(2,1)S(1)} %get-tuple-element.56), channel_id=1, source_target_pairs={{0,64},{64,4},{4,68},{68,0},{1,65},{65,5},{5,69},{69,1},{2,66},{66... | collective-permute-start | bytes 786440 | tf_op jit(solution)/shard_map/ppermute | solution.py:403
  32.3 17.4 %collective-permute-start.3 = (bf16[2,32,1024]{2,1,0:T(8,128)(2,1)S(1)}, bf16[2,32,1024]{2,1,0:T(8,128)(2,1)S(1)}, u32[]{:S(2)}, u32[]{:S(2)}) collective-permute-start(bf16[2,32,1024]{2,1,0:T(8,128)(2,1)S(1)} %slice.97), channel_id=1, source_target_pairs={{0,24},{8,0},{16,8},{24,16},{1,25},{9,1},{17,9},{25,17},{2,26},{10... | collective-permute-start | bytes 393224 | tf_op jit(solution)/shard_map/ppermute | solution.py:404
  36.1 13.6 %collective-permute-start.2 = (bf16[2,32,1024]{2,1,0:T(8,128)(2,1)S(1)}, bf16[2,32,1024]{2,1,0:T(8,128)(2,1)S(1)}, u32[]{:S(2)}, u32[]{:S(2)}) collective-permute-start(bf16[2,32,1024]{2,1,0:T(8,128)(2,1)S(1)} %slice.96), channel_id=1, source_target_pairs={{0,8},{8,16},{16,24},{24,0},{1,9},{9,17},{17,25},{25,1},{2,10},{10... | collective-permute-start | bytes 393224 | tf_op jit(solution)/shard_map/ppermute | solution.py:404
  45.8 6.3 %collective-permute-start.7 = (bf16[2,32,1024]{2,1,0:T(8,128)(2,1)S(1)}, bf16[2,32,1024]{2,1,0:T(8,128)(2,1)S(1)}, u32[]{:S(2)}, u32[]{:S(2)}) collective-permute-start(bf16[2,32,1024]{2,1,0:T(8,128)(2,1)S(1)} %slice.101), channel_id=1, source_target_pairs={{0,68},{64,0},{4,64},{68,4},{1,69},{65,1},{5,65},{69,5},{2,70},{66... | collective-permute-start | bytes 393224 | tf_op jit(solution)/shard_map/ppermute | solution.py:403
  49.6 6.2 %collective-permute-start.6 = (bf16[2,32,1024]{2,1,0:T(8,128)(2,1)S(1)}, bf16[2,32,1024]{2,1,0:T(8,128)(2,1)S(1)}, u32[]{:S(2)}, u32[]{:S(2)}) collective-permute-start(bf16[2,32,1024]{2,1,0:T(8,128)(2,1)S(1)} %slice.100), channel_id=1, source_target_pairs={{0,64},{64,4},{4,68},{68,0},{1,65},{65,5},{5,69},{69,1},{2,66},{66... | collective-permute-start | bytes 393224 | tf_op jit(solution)/shard_map/ppermute | solution.py:403
  57.0 2.6 copy-start.20
  57.0 4.5 %copy-start.21 = (s32[1,32]{1,0:T(1,128)S(1)}, s32[1,32]{1,0:T(1,128)}, u32[]{:S(2)}) copy-start(s32[1,32]{1,0:T(1,128)} %param.16) | copy-start | bytes 388
  57.0 5.4 %copy-start = (bf16[1,512,2048]{2,1,0:T(8,128)(2,1)S(1)}, bf16[1,512,2048]{2,1,0:T(8,128)(2,1)}, u32[]{:S(2)}) copy-start(bf16[1,512,2048]{2,1,0:T(8,128)(2,1)} %param.9) | copy-start | bytes 6291460
  57.0 5.4 %copy-start.10 = (f32[2048]{0:T(1024)S(1)}, f32[2048]{0:T(1024)}, u32[]{:S(2)}) copy-start(f32[2048]{0:T(1024)} %param.10) | copy-start | bytes 24580
  57.1 51.5 %copy-start.11 = (bf16[4,2,32,2048]{3,2,1,0:T(8,128)(2,1)}, bf16[4,2,32,2048]{3,2,1,0:T(8,128)(2,1)S(1)}, u32[]{:S(2)}) copy-start(bf16[4,2,32,2048]{3,2,1,0:T(8,128)(2,1)S(1)} %pad_maximum_fusion.1.refs_5_) | copy-start | bytes 3145732
  64.5 12.6 %copy-start.1 = (bf16[512,2048]{1,0:T(8,128)(2,1)}, bf16[512,2048]{1,0:T(8,128)(2,1)S(1)}, u32[]{:S(2)}) copy-start(bf16[512,2048]{1,0:T(8,128)(2,1)S(1)} %shard_map.91.hid_ref) | copy-start | bytes 6291460
  65.2 24.2 %collective-permute-start.8 = (bf16[4,2,32,2048]{3,2,1,0:T(8,128)(2,1)}, bf16[4,2,32,2048]{3,2,1,0:T(8,128)(2,1)S(1)}, u32[]{:S(2)}, u32[]{:S(2)}) collective-permute-start(bf16[4,2,32,2048]{3,2,1,0:T(8,128)(2,1)} %pad_maximum_fusion.refs_0_), channel_id=1, source_target_pairs={{0,64},{64,4},{4,68},{68,0},{1,65},{65,5},{5,69},{69,1},{2,66},{66... | collective-permute-start | bytes 3145736 | tf_op jit(solution)/shard_map/ppermute | solution.py:403
  65.3 24.1 %collective-permute-start.9 = (bf16[4,2,32,2048]{3,2,1,0:T(8,128)(2,1)}, bf16[4,2,32,2048]{3,2,1,0:T(8,128)(2,1)S(1)}, u32[]{:S(2)}, u32[]{:S(2)}) collective-permute-start(bf16[4,2,32,2048]{3,2,1,0:T(8,128)(2,1)} %pad_maximum_fusion.refs_0_), channel_id=1, source_target_pairs={{0,68},{64,0},{4,64},{68,4},{1,69},{65,1},{5,65},{69,5},{2,70},{66... | collective-permute-start | bytes 3145736 | tf_op jit(solution)/shard_map/ppermute | solution.py:403
  68.5 32.4 %collective-permute-start.10 = (bf16[4,2,32,2048]{3,2,1,0:T(8,128)(2,1)S(1)}, bf16[4,2,32,2048]{3,2,1,0:T(8,128)(2,1)}, u32[]{:S(2)}, u32[]{:S(2)}) collective-permute-start(bf16[4,2,32,2048]{3,2,1,0:T(8,128)(2,1)S(1)} %pad_maximum_fusion.1.refs_5_), channel_id=1, source_target_pairs={{0,8},{8,16},{16,24},{24,0},{1,9},{9,17},{17,25},{25,1},{2,10},{10... | collective-permute-start | bytes 3145736 | tf_op jit(solution)/shard_map/ppermute | solution.py:404
  69.7 33.8 %collective-permute-start.11 = (bf16[4,2,32,2048]{3,2,1,0:T(8,128)(2,1)S(1)}, bf16[4,2,32,2048]{3,2,1,0:T(8,128)(2,1)}, u32[]{:S(2)}, u32[]{:S(2)}) collective-permute-start(bf16[4,2,32,2048]{3,2,1,0:T(8,128)(2,1)S(1)} %pad_maximum_fusion.1.refs_5_), channel_id=1, source_target_pairs={{0,24},{8,0},{16,8},{24,16},{1,25},{9,1},{17,9},{25,17},{2,26},{10... | collective-permute-start | bytes 3145736 | tf_op jit(solution)/shard_map/ppermute | solution.py:404
  89.5 20.3 %copy-start.12 = (bf16[4,2,32,2048]{3,2,1,0:T(8,128)(2,1)}, bf16[4,2,32,2048]{3,2,1,0:T(8,128)(2,1)S(1)}, u32[]{:S(2)}) copy-start(bf16[4,2,32,2048]{3,2,1,0:T(8,128)(2,1)S(1)} %collective-permute-done.8.refs_1_) | copy-start | bytes 3145732
  89.5 20.3 %copy-start.13 = (bf16[4,2,32,2048]{3,2,1,0:T(8,128)(2,1)}, bf16[4,2,32,2048]{3,2,1,0:T(8,128)(2,1)S(1)}, u32[]{:S(2)}) copy-start(bf16[4,2,32,2048]{3,2,1,0:T(8,128)(2,1)S(1)} %collective-permute-done.9.refs_2_) | copy-start | bytes 3145732
  103.5 46.1 %copy-start.9 = (f32[2048]{0:T(1024)S(1)}, f32[2048]{0:T(1024)}, u32[]{:S(2)}) copy-start(f32[2048]{0:T(1024)} %param.13) | copy-start | bytes 24580
  103.6 11.2 %collective-permute-start.12 = (bf16[4,2,32,1024]{3,2,1,0:T(8,128)(2,1)S(1)}, bf16[4,2,32,1024]{3,2,1,0:T(8,128)(2,1)S(1)}, u32[]{:S(2)}, u32[]{:S(2)}) collective-permute-start(bf16[4,2,32,1024]{3,2,1,0:T(8,128)(2,1)S(1)} %slice.86), channel_id=1, source_target_pairs={{0,64},{64,4},{4,68},{68,0},{1,65},{65,5},{5,69},{69,1},{2,66},{66... | collective-permute-start | bytes 1572872 | tf_op jit(solution)/shard_map/ppermute | solution.py:403
  103.7 11.2 %collective-permute-start.13 = (bf16[4,2,32,1024]{3,2,1,0:T(8,128)(2,1)S(1)}, bf16[4,2,32,1024]{3,2,1,0:T(8,128)(2,1)S(1)}, u32[]{:S(2)}, u32[]{:S(2)}) collective-permute-start(bf16[4,2,32,1024]{3,2,1,0:T(8,128)(2,1)S(1)} %slice.87), channel_id=1, source_target_pairs={{0,68},{64,0},{4,64},{68,4},{1,69},{65,1},{5,65},{69,5},{2,70},{66... | collective-permute-start | bytes 1572872 | tf_op jit(solution)/shard_map/ppermute | solution.py:403
  107.0 34.3 %collective-permute-start.16 = (bf16[4,2,32,2048]{3,2,1,0:T(8,128)(2,1)}, bf16[4,2,32,2048]{3,2,1,0:T(8,128)(2,1)S(1)}, u32[]{:S(2)}, u32[]{:S(2)}) collective-permute-start(bf16[4,2,32,2048]{3,2,1,0:T(8,128)(2,1)} %pad_maximum_fusion.refs_0_), channel_id=1, source_target_pairs={{0,32},{32,0},{1,33},{33,1},{2,34},{34,2},{3,35},{35,3},{4,36},{36... | collective-permute-start | bytes 3145736 | tf_op jit(solution)/shard_map/ppermute | solution.py:423
  107.0 34.6 %collective-permute-start.17 = (bf16[4,2,32,2048]{3,2,1,0:T(8,128)(2,1)S(1)}, bf16[4,2,32,2048]{3,2,1,0:T(8,128)(2,1)S(1)}, u32[]{:S(2)}, u32[]{:S(2)}) collective-permute-start(bf16[4,2,32,2048]{3,2,1,0:T(8,128)(2,1)S(1)} %collective-permute-done.8.refs_1_), channel_id=1, source_target_pairs={{0,32},{32,0},{1,33},{33,1},{2,34},{34,2},{3,35},{35,3},{4,36},{36... | collective-permute-start | bytes 3145736 | tf_op jit(solution)/shard_map/ppermute | solution.py:423
  107.5 34.4 %collective-permute-start.18 = (bf16[4,2,32,2048]{3,2,1,0:T(8,128)(2,1)S(1)}, bf16[4,2,32,2048]{3,2,1,0:T(8,128)(2,1)S(1)}, u32[]{:S(2)}, u32[]{:S(2)}) collective-permute-start(bf16[4,2,32,2048]{3,2,1,0:T(8,128)(2,1)S(1)} %collective-permute-done.9.refs_2_), channel_id=1, source_target_pairs={{0,32},{32,0},{1,33},{33,1},{2,34},{34,2},{3,35},{35,3},{4,36},{36... | collective-permute-start | bytes 3145736 | tf_op jit(solution)/shard_map/ppermute | solution.py:423
  114.8 26.1 %collective-permute-start.14 = (bf16[4,2,32,1024]{3,2,1,0:T(8,128)(2,1)S(1)}, bf16[4,2,32,1024]{3,2,1,0:T(8,128)(2,1)S(1)}, u32[]{:S(2)}, u32[]{:S(2)}) collective-permute-start(bf16[4,2,32,1024]{3,2,1,0:T(8,128)(2,1)S(1)} %slice.88), channel_id=1, source_target_pairs={{0,8},{8,16},{16,24},{24,0},{1,9},{9,17},{17,25},{25,1},{2,10},{10... | collective-permute-start | bytes 1572872 | tf_op jit(solution)/shard_map/ppermute | solution.py:404
  114.9 25.9 %collective-permute-start.15 = (bf16[4,2,32,1024]{3,2,1,0:T(8,128)(2,1)S(1)}, bf16[4,2,32,1024]{3,2,1,0:T(8,128)(2,1)S(1)}, u32[]{:S(2)}, u32[]{:S(2)}) collective-permute-start(bf16[4,2,32,1024]{3,2,1,0:T(8,128)(2,1)S(1)} %slice.89), channel_id=1, source_target_pairs={{0,24},{8,0},{16,8},{24,16},{1,25},{9,1},{17,9},{25,17},{2,26},{10... | collective-permute-start | bytes 1572872 | tf_op jit(solution)/shard_map/ppermute | solution.py:404
  140.8 8.3 %collective-permute-start.22 = (bf16[4,2,32,2048]{3,2,1,0:T(8,128)(2,1)}, bf16[4,2,32,2048]{3,2,1,0:T(8,128)(2,1)}, u32[]{:S(2)}, u32[]{:S(2)}) collective-permute-start(bf16[4,2,32,2048]{3,2,1,0:T(8,128)(2,1)} %collective-permute-done.10.refs_6_), channel_id=1, source_target_pairs={{0,32},{32,0},{1,33},{33,1},{2,34},{34,2},{3,35},{35,3},{4,36},{36... | collective-permute-start | bytes 3145736 | tf_op jit(solution)/shard_map/ppermute | solution.py:423
  140.8 8.3 %collective-permute-start.23 = (bf16[4,2,32,2048]{3,2,1,0:T(8,128)(2,1)}, bf16[4,2,32,2048]{3,2,1,0:T(8,128)(2,1)}, u32[]{:S(2)}, u32[]{:S(2)}) collective-permute-start(bf16[4,2,32,2048]{3,2,1,0:T(8,128)(2,1)} %collective-permute-done.11.refs_7_), channel_id=1, source_target_pairs={{0,32},{32,0},{1,33},{33,1},{2,34},{34,2},{3,35},{35,3},{4,36},{36... | collective-permute-start | bytes 3145736 | tf_op jit(solution)/shard_map/ppermute | solution.py:423
  141.3 5.1 %copy-start.14 = (bf16[4,2,32,2048]{3,2,1,0:T(8,128)(2,1)}, bf16[4,2,32,2048]{3,2,1,0:T(8,128)(2,1)S(1)}, u32[]{:S(2)}) copy-start(bf16[4,2,32,2048]{3,2,1,0:T(8,128)(2,1)S(1)} %collective-permute-done.16.refs_10_) | copy-start | bytes 3145732
  141.3 7.7 %collective-permute-start.21 = (bf16[4,2,32,2048]{3,2,1,0:T(8,128)(2,1)}, bf16[4,2,32,2048]{3,2,1,0:T(8,128)(2,1)}, u32[]{:S(2)}, u32[]{:S(2)}) collective-permute-start(bf16[4,2,32,2048]{3,2,1,0:T(8,128)(2,1)} %copy-done.11), channel_id=1, source_target_pairs={{0,32},{32,0},{1,33},{33,1},{2,34},{34,2},{3,35},{35,3},{4,36},{36... | collective-permute-start | bytes 3145736 | tf_op jit(solution)/shard_map/ppermute | solution.py:423
  141.6 4.9 %copy-start.15 = (bf16[4,2,32,2048]{3,2,1,0:T(8,128)(2,1)}, bf16[4,2,32,2048]{3,2,1,0:T(8,128)(2,1)S(1)}, u32[]{:S(2)}) copy-start(bf16[4,2,32,2048]{3,2,1,0:T(8,128)(2,1)S(1)} %collective-permute-done.17.refs_11_) | copy-start | bytes 3145732
  141.6 3.4 %collective-permute-start.19 = (bf16[4,2,32,1024]{3,2,1,0:T(8,128)(2,1)S(1)}, bf16[4,2,32,1024]{3,2,1,0:T(8,128)(2,1)S(1)}, u32[]{:S(2)}, u32[]{:S(2)}) collective-permute-start(bf16[4,2,32,1024]{3,2,1,0:T(8,128)(2,1)S(1)} %collective-permute-done.12.refs_3_), channel_id=1, source_target_pairs={{0,32},{32,0},{1,33},{33,1},{2,34},{34,2},{3,35},{35,3},{4,36},{36... | collective-permute-start | bytes 1572872 | tf_op jit(solution)/shard_map/ppermute | solution.py:423
  141.9 4.6 %copy-start.16 = (bf16[4,2,32,2048]{3,2,1,0:T(8,128)(2,1)}, bf16[4,2,32,2048]{3,2,1,0:T(8,128)(2,1)S(1)}, u32[]{:S(2)}) copy-start(bf16[4,2,32,2048]{3,2,1,0:T(8,128)(2,1)S(1)} %collective-permute-done.18.refs_12_) | copy-start | bytes 3145732
  141.9 4.6 %collective-permute-start.20 = (bf16[4,2,32,1024]{3,2,1,0:T(8,128)(2,1)S(1)}, bf16[4,2,32,1024]{3,2,1,0:T(8,128)(2,1)S(1)}, u32[]{:S(2)}, u32[]{:S(2)}) collective-permute-start(bf16[4,2,32,1024]{3,2,1,0:T(8,128)(2,1)S(1)} %collective-permute-done.13.refs_4_), channel_id=1, source_target_pairs={{0,32},{32,0},{1,33},{33,1},{2,34},{34,2},{3,35},{35,3},{4,36},{36... | collective-permute-start | bytes 1572872 | tf_op jit(solution)/shard_map/ppermute | solution.py:423
  145.0 4.1 %collective-permute-start.24 = (bf16[4,2,32,1024]{3,2,1,0:T(8,128)(2,1)S(1)}, bf16[4,2,32,1024]{3,2,1,0:T(8,128)(2,1)}, u32[]{:S(2)}, u32[]{:S(2)}) collective-permute-start(bf16[4,2,32,1024]{3,2,1,0:T(8,128)(2,1)S(1)} %collective-permute-done.14.refs_8_), channel_id=1, source_target_pairs={{0,32},{32,0},{1,33},{33,1},{2,34},{34,2},{3,35},{35,3},{4,36},{36... | collective-permute-start | bytes 1572872 | tf_op jit(solution)/shard_map/ppermute | solution.py:423
  146.5 0.8 copy-start.2
  147.3 2.3 collective-permute-start.25
  149.6 1.0 copy-start.3
  164.5 0.8 copy-start.5
  165.4 0.8 copy-start.7
  166.1 33.3 %collective-permute-start.26 = (bf16[4,4,2,2,16,4096]{5,4,3,2,1,0:T(8,128)(2,1)}, bf16[4,4,2,2,16,4096]{5,4,3,2,1,0:T(8,128)(2,1)}, u32[]{:S(2)}, u32[]{:S(2)}) collective-permute-start(bf16[4,4,2,2,16,4096]{5,4,3,2,1,0:T(8,128)(2,1)} %bitcast.68), channel_id=1, source_target_pairs={{0,32},{32,0},{1,33},{33,1},{2,34},{34,2},{3,35},{35,3},{4,36},{36... | collective-permute-start | bytes 25165832 | tf_op jit(solution)/shard_map/ppermute | solution.py:423
  166.3 23.6 %all-to-all-start.2 = ((bf16[32,8,2048]{2,1,0:T(8,128)(2,1)}), bf16[32,8,2048]{2,1,0:T(8,128)(2,1)}, u32[]{:S(2)}, u32[]{:S(2)}) async-start(bf16[32,8,2048]{2,1,0:T(8,128)(2,1)} %bitcast.85), calls=%async_computation.2 | async-start | bytes 2097152 | tf_op jit(solution)/shard_map/all_to_all | solution.py:506
  171.9 1.0 copy-start.4
  172.9 1.0 copy-start.6
  174.0 1.0 copy-start.8
  189.9 27.6 %all-to-all-start = ((bf16[32,8,2048]{2,1,0:T(8,128)(2,1)}), bf16[32,8,2048]{2,1,0:T(8,128)(2,1)S(1)}, u32[]{:S(2)}, u32[]{:S(2)}) async-start(bf16[32,8,2048]{2,1,0:T(8,128)(2,1)} %bitcast.84), calls=%async_computation | async-start | bytes 2097152 | tf_op jit(solution)/shard_map/all_to_all | solution.py:506
  217.5 4.8 %copy-start.17 = (bf16[32,8,2048]{2,1,0:T(8,128)(2,1)}, bf16[32,8,2048]{2,1,0:T(8,128)(2,1)S(1)}, u32[]{:S(2)}) copy-start(bf16[32,8,2048]{2,1,0:T(8,128)(2,1)S(1)} %all-to-all-done) | copy-start | bytes 3145732
  217.5 17.5 %all-to-all-start.3 = ((bf16[32,8,1024]{2,1,0:T(8,128)(2,1)}), bf16[32,8,1024]{2,1,0:T(8,128)(2,1)S(1)}, u32[]{:S(2)}, u32[]{:S(2)}) async-start(bf16[32,8,1024]{2,1,0:T(8,128)(2,1)} %bitcast.80), calls=%async_computation.3 | async-start | bytes 1048576 | tf_op jit(solution)/shard_map/all_to_all | solution.py:506
  235.0 11.4 %copy-start.18 = (bf16[32,8,1024]{2,1,0:T(8,128)(2,1)}, bf16[32,8,1024]{2,1,0:T(8,128)(2,1)S(1)}, u32[]{:S(2)}) copy-start(bf16[32,8,1024]{2,1,0:T(8,128)(2,1)S(1)} %all-to-all-done.3) | copy-start | bytes 1572868
  235.0 21.7 %all-to-all-start.1 = ((bf16[32,8,1024]{2,1,0:T(8,128)(2,1)}), bf16[32,8,1024]{2,1,0:T(8,128)(2,1)S(1)}, u32[]{:S(2)}, u32[]{:S(2)}) async-start(bf16[32,8,1024]{2,1,0:T(8,128)(2,1)} %bitcast.78), calls=%async_computation.1 | async-start | bytes 1048576 | tf_op jit(solution)/shard_map/all_to_all | solution.py:506
  256.7 0.8 copy-start.19
Sparse Core Ops, SparseCore 0:
  9.3 38.0 all-gather.5
  59.7 86.3 all-gather.7

commit v9 on v5

--- a/solution.py
+++ b/solution.py
@@ -18,10 +18,10 @@
 PAIR = 2 * HEAD
 STEPS = WIDTH // PAIR
 SEQ = ("x", "yhi", "z")
-QKV_PART = 3 * WIDTH // 2
-PART = 2 * WIDTH
+QKV_HALF = 3 * WIDTH // 2
+PART = 4 * WIDTH
 RELATIVE = ((0, 0, PART), (3, 0, PART), (1, 0, PART), (2, 0, PART // 2), (2, PART // 2, PART))
-STACKED = (0, 3, 1, 2)
+RINGS = (0, 3, 1, 2)
 LOG2E = 1.4426950408889634
 MIB = 1 << 20
 
@@ -98,41 +98,35 @@
     )(core, x, gain)
 
 
-def start_copies(place_ref, pieces, sems, w_ref=None, o_ref=None):
+def start_copies(place_ref, pieces, sems, w_ref, o_ref):
     my_x, my_y = place_ref[1], place_ref[2]
 
-    def block_of(part, stacked, ring):
-        x, y = (stacked, ring) if part == 0 else (ring, stacked)
-        x = lax.rem(my_x + x, 4)
-        y = lax.rem(my_y + y, 4)
+    def block_of(stacked, ring):
+        x = lax.rem(my_x + stacked, 4)
+        y = lax.rem(my_y + ring, 4)
         return lax.rem(y, 2) * 8 + x * 2 + y // 2
 
-    def move(slot, part, outputs):
-        first = (slot * 2 + part) * len(RELATIVE)
+    def move(slot, first, last, dst_of, sem):
         for index, (ring, low, high) in enumerate(RELATIVE):
-            src = pieces[first + index]
-            if outputs:
-                if high < PART:
-                    continue
-                lanes, target = pl.ds(QKV_PART - low, PART - QKV_PART), None
-            else:
-                end = min(high, QKV_PART)
-                lanes, target = pl.ds(0, end - low), pl.ds(low, end - low)
-            for k, stacked in enumerate(STACKED):
-                block = block_of(part, stacked, ring)
-                if outputs:
-                    width = PART - QKV_PART
-                    dst = o_ref.at[slot, block, :, :, pl.ds(part * width, width)]
-                else:
-                    dst = w_ref.at[slot, part, block, :, :, target]
-                sem = sems.at[4 + slot if outputs else slot * 2 + part]
-                pltpu.make_async_copy(src.at[k, :, :, lanes], dst, sem).start()
-
-    for outputs, ref in ((False, w_ref), (True, o_ref)):
-        if ref is not None:
-            for part in range(2):
-                for slot in range(2):
-                    move(slot, part, outputs)
+            begin, end = max(low, first), min(high, last)
+            if begin >= end:
+                continue
+            src = pieces[slot * len(RELATIVE) + index]
+            for k, stacked in enumerate(RINGS):
+                dst = dst_of(block_of(stacked, ring)).at[:, :, pl.ds(begin - first, end - begin)]
+                pltpu.make_async_copy(src.at[k, :, :, pl.ds(begin - low, end - begin)], dst, sem).start()
+
+    for group in range(2):
+        for slot in range(2):
+            move(
+                slot,
+                group * QKV_HALF,
+                (group + 1) * QKV_HALF,
+                lambda block: w_ref.at[slot, group, block],
+                sems.at[slot * 2 + group],
+            )
+    for slot in range(2):
+        move(slot, 2 * QKV_HALF, PART, lambda block: o_ref.at[slot, block], sems.at[4 + slot])
 
 
 def arrived(ref, sem):
@@ -168,8 +162,8 @@
 
 
 def row_kernel(place_ref, x_ref, hid_ref, gain_ref, cos_ref, sin_ref, *refs):
-    pieces = refs[: 4 * len(RELATIVE)]
-    mid_ref, next_ref, w_ref, o_ref, att_ref, sems = refs[4 * len(RELATIVE) :]
+    pieces = refs[: 2 * len(RELATIVE)]
+    mid_ref, next_ref, w_ref, o_ref, att_ref, sems = refs[2 * len(RELATIVE) :]
     core = place_ref[0]
     start_copies(place_ref, pieces, sems, w_ref, o_ref)
     half = D // 2
@@ -235,7 +229,7 @@
         + [hbm] * len(pieces),
         out_specs=[vmem, vmem],
         scratch_shapes=[
-            pltpu.VMEM((2, 2, 16, 2, 32, QKV_PART), jnp.bfloat16),
+            pltpu.VMEM((2, 2, 16, 2, 32, QKV_HALF), jnp.bfloat16),
             pltpu.VMEM((2, 16, 2, 32, D // 2), jnp.bfloat16),
             pltpu.VMEM((C, WIDTH), jnp.bfloat16),
             pltpu.SemaphoreType.DMA((6,)),
@@ -369,7 +363,7 @@
         ],
         out_specs=block(D),
         compiler_params=pltpu.CompilerParams(
-            dimension_semantics=("arbitrary",), vmem_limit_bytes=54 * MIB
+            dimension_semantics=("arbitrary",), vmem_limit_bytes=40 * MIB
         ),
         cost_estimate=pl.CostEstimate(
             flops=2 * C * D * WIDTH,
@@ -413,35 +407,12 @@
     return inputs.reshape(-1, 3, STEPS, PAIR).transpose(0, 2, 1, 3).reshape(-1, 3 * WIDTH)
 
 
-def lines(inputs, output):
+def row_stack(inputs, output):
     shard = jnp.concatenate([by_step(inputs), fold_output(output)], 1)
     rows = lax.all_gather(shard, "z", axis=0)
     qkv = rows[:, :, : 3 * WIDTH].reshape(2, 32, 3 * WIDTH)
     out = rows[:, :, 3 * WIDTH :].reshape(4, 2, 8, WIDTH).transpose(1, 0, 2, 3).reshape(2, 32, WIDTH)
-    parts = []
-    for p in range(2):
-        lanes = slice(p * QKV_PART, (p + 1) * QKV_PART)
-        rest = slice(p * WIDTH // 2, (p + 1) * WIDTH // 2)
-        parts.append(jnp.concatenate([qkv[:, :, lanes], out[:, :, rest]], -1))
-    return parts
-
-
-def inner_rings(parts):
-    hops = [first_hops(part, axis) for part, axis in zip(parts, "xy")]
-    return [stack(forwards(hop, axis)) for hop, axis in zip(hops, "xy")]
-
-
-def outer_hops(stacks):
-    return [first_hops(part, axis) for part, axis in zip(stacks, "yx")]
-
-
-def outer_forwards(hops):
-    return [forwards(hop, axis) for hop, axis in zip(hops, "yx")]
-
-
-def both_cores(parts):
-    own = [piece for part in parts for piece in part]
-    return own + [swap(piece) for piece in own]
+    return stack(forwards(first_hops(jnp.concatenate([qkv, out], -1), "x"), "x"))
 
 
 def column_line(inputs, output):
@@ -477,12 +448,14 @@
     hidden = normed_slots(core_scalar, residual, gain_first.reshape(1, D))
 
     line = column_line(inputs_second, output_second)
-    first = inner_rings(lines(inputs_first, output_first))
-    first, hidden, row_tables, column_tables = lax.optimization_barrier((first, hidden, row_tables, column_tables))
-    first_hop = outer_hops(first)
-    line, _ = lax.optimization_barrier((line, first_hop))
+    inputs_first, output_first, line = lax.optimization_barrier((inputs_first, output_first, line))
     plane = column_plane(line)
-    pieces = both_cores(outer_forwards(first_hop))
+    own_stack = row_stack(inputs_first, output_first)
+    pieces = forwards(first_hops(own_stack, "y"), "y")
+    own_stack, hidden, row_tables, column_tables = lax.optimization_barrier(
+        (own_stack, hidden, row_tables, column_tables)
+    )
+    pieces = pieces + [swap(own_stack)] + [swap(piece) for piece in pieces[1:]]
 
     middle, hidden = row_layer(place, residual, hidden, gain_second.reshape(1, D), row_tables, pieces)
     plane, hidden = lax.optimization_barrier((plane, hidden))

time: 262 us -> 263 us (level)
  waiting for transfers between devices: 43.1 us -> 87.1 us
  starting transfers between devices: 34.5 us -> 19.4 us
  blocking collectives: 80.8 us -> 67.8 us
  local copies, waits for them, and re-layouts: 23.8 us -> 14.5 us
  other arithmetic: 8.98 us -> 5.72 us
  Pallas kernels: 54.7 us -> 51.9 us
    ppermute x8 -> x4, waiting for transfers between devices: 5.84 us -> 44.5 us  [shift(): lax.ppermute(value, ('ylo', 'yhi'), [(where(y), where((y + by) % 4)) for...]
    ppermute x8 -> x4, waiting for transfers between devices: 12.9 us -> 26.9 us  [shift(): return lax.ppermute(value, axis, [(i, (i + by) % 4) for i in range(4)])]
    all_gather x1, blocking collectives: 29.2 us -> 16 us  [column_line(): return lax.all_gather(shard, ('ylo', 'yhi'), axis=0)]
    all_gather x1, waiting for transfers between devices: 9.39 us -> 0.02 us  [column_plane(): lax.all_gather(line, ('x', 'z'), axis=0).reshape(4, 4, 2, 2, 16, 4 * WIDTH)]
    ppermute x8 -> x4, starting transfers between devices: 13.6 us -> 6.68 us  [shift(): return lax.ppermute(value, axis, [(i, (i + by) % 4) for i in range(4)])]
    ppermute x8 -> x4, starting transfers between devices: 13.2 us -> 6.61 us  [shift(): lax.ppermute(value, ('ylo', 'yhi'), [(where(y), where((y + by) % 4)) for...]
    unnamed x46 -> x20, local copies, waits for them, and re-layouts: 6.68 us -> 3.22 us
    another operation x6 -> x3, other arithmetic: 4.97 us -> 1.75 us  [stack(): return jnp.stack([own, left, right, jnp.concatenate([low, high], -1)])]
  transfers between devices with their start and end apart: 29 -> 16, of which waited for: 8 -> 9; matrix products, arithmetic and copies ran while one was open for 8% -> 6% of each run, Pallas kernels for 10% -> 10%
where the time goes in v9:
time: 263 us; the launch traced here: 261 us
  waiting for transfers between devices  87.1 us (33%)
  blocking collectives  67.8 us (26%)
  Pallas kernels  51.9 us (20%)
  starting transfers between devices  19.4 us (7%)
  between operations  15 us (6%)
  local copies, waits for them, and re-layouts  14.5 us (6%)
  other arithmetic  5.72 us (2%)
    ppermute x4, waiting for transfers between devices, shift(): lax.ppermute(value, ('ylo', 'yhi'), [(where(y), where((y + by) % 4)) for...  44.5 us
    all_to_all x1, blocking collectives, shards(): lax.all_to_all(hidden, SEQ, split_axis=0, concat_axis=0, tiled=True)  37.1 us
    ppermute x4, waiting for transfers between devices, shift(): return lax.ppermute(value, axis, [(i, (i + by) % 4) for i in range(4)])  26.9 us
    pallas_call x1, Pallas kernels, row_layer(): pl.pallas_call(row_kernel, out_shape=[shape, shape], in_specs=[pl.BlockSp...  24.6 us
    pallas_call x1, Pallas kernels, column_layer(): pl.pallas_call(column_kernel, out_shape=jax.ShapeDtypeStruct((C, WIDTH),...  21.4 us
    all_gather x1, blocking collectives, column_line(): return lax.all_gather(shard, ('ylo', 'yhi'), axis=0)  16 us
    all_gather x1, blocking collectives, row_stack(): rows = lax.all_gather(shard, 'z', axis=0)  14.6 us
    all_to_all x1, waiting for transfers between devices, shards(): lax.all_to_all(attended, SEQ, split_axis=0, concat_axis=0, tiled=True)  12.4 us
  transfers between devices with their start and end apart: 16, of which 9 were waited for; matrix products, arithmetic and copies ran while one was open for 6% of the time, Pallas kernels for 10%

profile of v9, /device:TPU:0, one launch (start us, length us, event | category | flops | bytes accessed | tf_op | source)
XLA Modules:
  0.0 261.4 jit_solution(7494709166541204930)
XLA Ops:
  6.5 0.8 fusion.8
  7.3 0.9 reshape.93
  8.3 0.1 copy.24
  8.3 0.1 reshape.94
  8.4 16.0 %all-gather = bf16[64,4096]{1,0:T(8,128)(2,1)} all-gather(bf16[16,4096]{1,0:T(8,128)(2,1)S(1)} %maximum_maximum_fusion), channel_id=2, replica_groups=mesh['ylo'=2,'core'=2,'x'=4,'yhi'=2,'z'=4] {'ylo','yhi'}, dimensions={0}, use_global_device_ids=true | all-gather | bytes 655360 | tf_op jit(solution)/shard_map/all_gather | solution.py:420
  24.5 0.0 all-gather.5.cloned.1.call-update
  24.5 0.1 copy.23
  24.6 0.1 reshape.97
  24.8 14.6 %all-gather.2 = bf16[64,4096]{1,0:T(8,128)(2,1)S(1)} all-gather(bf16[16,4096]{1,0:T(8,128)(2,1)S(1)} %maximum_maximum_fusion.1), channel_id=4, replica_groups=mesh['ylo'=2,'core'=2,'x'=4,'yhi'=2,'z'=4] {'z'}, dimensions={0}, use_global_device_ids=true | all-gather | bytes 655360 | tf_op jit(solution)/shard_map/all_gather | solution.py:412
  39.5 0.1 fusion.6
  39.5 1.6 collective-permute-start
  41.1 1.7 collective-permute-start.1
  42.8 17.7 %collective-permute-done = bf16[2,32,4096]{2,1,0:T(8,128)(2,1)S(1)} collective-permute-done((bf16[2,32,4096]{2,1,0:T(8,128)(2,1)S(1)}, bf16[2,32,4096]{2,1,0:T(8,128)(2,1)S(1)}, u32[]{:S(2)}, u32[]{:S(2)}) %collective-permute-start) | collective-permute-done | bytes 524320 | tf_op jit(solution)/shard_map/ppermute | solution.py:380
  60.6 0.2 collective-permute-start.2
  60.8 0.0 collective-permute-done.1
  60.8 3.2 %collective-permute-start.3 = (bf16[2,32,2048]{2,1,0:T(8,128)(2,1)S(1)}, bf16[2,32,2048]{2,1,0:T(8,128)(2,1)S(1)}, u32[]{:S(2)}, u32[]{:S(2)}) collective-permute-start(bf16[2,32,2048]{2,1,0:T(8,128)(2,1)S(1)} %slice.59), channel_id=1, source_target_pairs={{0,24},{8,0},{16,8},{24,16},{1,25},{9,1},{17,9},{25,17},{2,26},{10... | collective-permute-start | bytes 786440 | tf_op jit(solution)/shard_map/ppermute | solution.py:380
  64.0 5.9 %collective-permute-done.2 = bf16[2,32,2048]{2,1,0:T(8,128)(2,1)S(1)} collective-permute-done((bf16[2,32,2048]{2,1,0:T(8,128)(2,1)S(1)}, bf16[2,32,2048]{2,1,0:T(8,128)(2,1)S(1)}, u32[]{:S(2)}, u32[]{:S(2)}) %collective-permute-start.2) | collective-permute-done | bytes 262176 | tf_op jit(solution)/shard_map/ppermute | solution.py:380
  69.8 3.3 %collective-permute-done.3 = bf16[2,32,2048]{2,1,0:T(8,128)(2,1)S(1)} collective-permute-done((bf16[2,32,2048]{2,1,0:T(8,128)(2,1)S(1)}, bf16[2,32,2048]{2,1,0:T(8,128)(2,1)S(1)}, u32[]{:S(2)}, u32[]{:S(2)}) %collective-permute-start.3) | collective-permute-done | bytes 262176 | tf_op jit(solution)/shard_map/ppermute | solution.py:380
  73.2 0.0 copy-start.9
  73.2 0.0 copy-start.8
  73.2 0.0 copy-start.2
  73.2 0.0 copy-start.4
  73.2 1.6 pad_maximum_fusion.refs_0_
  74.9 0.8 collective-permute-start.4
  75.7 2.5 collective-permute-start.5
  78.1 0.6 constant_dynamic-slice_fusion
  78.7 0.1 add_convert_fusion
  78.8 0.1 convert_element_type.35
  78.9 0.6 fusion.9
  80.9 2.1 shard_map.91.hid_ref
  83.0 0.0 copy-start.3
  83.0 0.6 add_convert_fusion.1
  83.7 1.9 fusion.4
  85.6 0.2 pad_maximum_fusion.2
  85.8 1.0 pad_maximum_fusion.4
  86.8 0.0 collective-permute-start.8
  86.8 32.7 %collective-permute-done.4.refs_1_ = bf16[4,2,32,4096]{3,2,1,0:T(8,128)(2,1)} collective-permute-done((bf16[4,2,32,4096]{3,2,1,0:T(8,128)(2,1)}, bf16[4,2,32,4096]{3,2,1,0:T(8,128)(2,1)}, u32[]{:S(2)}, u32[]{:S(2)}) %collective-permute-start.4) | collective-permute-done | bytes 2097184 | tf_op jit(solution)/shard_map/ppermute | solution.py:379
  119.5 1.3 slice.60
  120.8 0.2 collective-permute-start.6
  121.0 1.3 slice.61
  122.3 3.2 %collective-permute-start.7 = (bf16[4,2,32,2048]{3,2,1,0:T(8,128)(2,1)S(1)}, bf16[4,2,32,2048]{3,2,1,0:T(8,128)(2,1)S(1)}, u32[]{:S(2)}, u32[]{:S(2)}) collective-permute-start(bf16[4,2,32,2048]{3,2,1,0:T(8,128)(2,1)S(1)} %slice.61), channel_id=1, source_target_pairs={{0,68},{64,0},{4,64},{68,4},{1,69},{65,1},{5,65},{69,5},{2,70},{66... | collective-permute-start | bytes 3145736 | tf_op jit(solution)/shard_map/ppermute | solution.py:379
  125.5 0.0 collective-permute-start.10
  125.5 0.5 collective-permute-start.9
  126.0 10.9 %collective-permute-done.6.refs_3_ = bf16[4,2,32,2048]{3,2,1,0:T(8,128)(2,1)S(1)} collective-permute-done((bf16[4,2,32,2048]{3,2,1,0:T(8,128)(2,1)S(1)}, bf16[4,2,32,2048]{3,2,1,0:T(8,128)(2,1)S(1)}, u32[]{:S(2)}, u32[]{:S(2)}) %collective-permute-start.6) | collective-permute-done | bytes 1048608 | tf_op jit(solution)/shard_map/ppermute | solution.py:379
  136.9 0.9 collective-permute-done.7.refs_4_
  137.8 0.0 collective-permute-start.12
  137.8 0.1 pad_add_fusion.place_ref
  137.9 1.8 collective-permute-done.11.refs_8_
  139.7 1.5 collective-permute-done.12.refs_9_
  141.2 24.6 %shard_map.92 = (bf16[512,2048]{1,0:T(8,128)(2,1)}, bf16[512,2048]{1,0:T(8,128)(2,1)}) custom-call(s32[3]{0:T(128)S(1)} %pad_add_fusion.place_ref, bf16[512,2048]{1,0:T(8,128)(2,1)} %bitcast.55, bf16[512,2048]{1,0:T(8,128)(2,1)} %copy-done.3, f32[1,2048]{1,0:T(1,128)S(1)} %bitcast.58, f32[512,128]{1,0:T(8,128)S(1)} %get-tuple-element.22.cos_ref, ...), custom_call_target="tpu_custom_call" | custom-call | flops 9663676416 | bytes 25165824 | tf_op jit(solution)/shard_map/pallas_call | solution.py:224
  165.8 0.0 all-gather.5.cloned.1.call-done
  165.8 0.2 collective-permute-start.13
  166.0 37.1 %all_to_all.22 = bf16[32,16,2048]{2,1,0:T(8,128)(2,1)} all-to-all(bf16[32,16,2048]{2,1,0:T(8,128)(2,1)} %bitcast.62), channel_id=1, replica_groups=mesh['ylo'=2,'core'=2,'x'=4,'yhi'=2,'z'=4] {'x','yhi','z'}, dimensions={0} | all-to-all | bytes 4194304 | tf_op jit(solution)/shard_map/all_to_all | solution.py:463
  203.2 0.0 collective-permute-done.13.other_plane
  203.2 21.4 %shard_map.93 = bf16[512,1024]{1,0:T(8,128)(2,1)} custom-call(s32[1]{0:T(128)} %bitcast.core_ref, bf16[512,2048]{1,0:T(8,128)(2,1)} %bitcast.63, f32[512,128]{1,0:T(8,128)} %get-tuple-element.27.cos_ref, f32[512,128]{1,0:T(8,128)} %get-tuple-element.28.sin_ref, bf16[4,4,2,2,16,4096]{5,4,3,2,1,0:T(8,128)(2,1)} %bitcast.71, ...), custom_call_target="tpu_custom_call" | custom-call | flops 7516192768 | bytes 15728640 | tf_op jit(solution)/shard_map/pallas_call | solution.py:314
  224.6 5.4 %all-to-all-start.1 = ((bf16[32,16,1024]{2,1,0:T(8,128)(2,1)}), bf16[32,16,1024]{2,1,0:T(8,128)(2,1)S(1)}, u32[]{:S(2)}, u32[]{:S(2)}) async-start(bf16[32,16,1024]{2,1,0:T(8,128)(2,1)} %bitcast.67), calls=%async_computation.1 | async-start | bytes 2097152 | tf_op jit(solution)/shard_map/all_to_all | solution.py:465
  230.0 1.8 slice_bitcast_fusion.1
  231.8 0.2 copy.18
  232.0 1.8 slice_bitcast_fusion
  233.7 1.5 copy.19
  235.2 12.4 %all-to-all-done.1 = bf16[32,16,1024]{2,1,0:T(8,128)(2,1)S(1)} async-done(((bf16[32,16,1024]{2,1,0:T(8,128)(2,1)}), bf16[32,16,1024]{2,1,0:T(8,128)(2,1)S(1)}, u32[]{:S(2)}, u32[]{:S(2)}) %all-to-all-start.1) | async-done | bytes 1048608 | tf_op jit(solution)/shard_map/all_to_all | solution.py:465
  247.6 1.6 copy-done
  249.2 1.6 copy-done.1
  250.8 3.8 %shard_map.94 = bf16[512,2048]{1,0:T(8,128)(2,1)} custom-call(s32[1]{0:T(128)} %bitcast.core_ref, bf16[512,1024]{1,0:T(8,128)(2,1)S(1)} %bitcast.54, bf16[512,2048]{1,0:T(8,128)(2,1)S(1)} %bitcast.52, bf16[512,2048]{1,0:T(8,128)(2,1)S(1)} %bitcast.53, bf16[512,2048]{1,0:T(8,128)(2,1)S(1)} %copy-done.1), custom_call_target="tpu_custom_call" | custom-call | flops 2147483648 | bytes 9437184 | tf_op jit(solution)/shard_map/pallas_call | solution.py:353
  (30 shorter events, 0.2 us)
Async XLA Ops:
  6.5 17.9 %copy-start.6 = (bf16[16,3072]{1,0:T(8,128)(2,1)S(1)}, bf16[16,3072]{1,0:T(8,128)(2,1)}, u32[]{:S(2)}) copy-start(bf16[16,3072]{1,0:T(8,128)(2,1)} %param.11) | copy-start | bytes 294916
  6.5 18.2 %copy-start.7 = (bf16[8,2048]{1,0:T(8,128)(2,1)S(1)}, bf16[8,2048]{1,0:T(8,128)(2,1)}, u32[]{:S(2)}) copy-start(bf16[8,2048]{1,0:T(8,128)(2,1)} %param.12) | copy-start | bytes 98308
  6.5 159.3 %all-gather.5.cloned.1.call-start = ((), (), s32[]{:S(2)}) async-start(), calls=%async_computation.2 | async-start | bytes 8912896 | tf_op jit(solution)/shard_map/all_gather | solution.py:424
  39.5 21.0 %collective-permute-start = (bf16[2,32,4096]{2,1,0:T(8,128)(2,1)S(1)}, bf16[2,32,4096]{2,1,0:T(8,128)(2,1)S(1)}, u32[]{:S(2)}, u32[]{:S(2)}) collective-permute-start(bf16[2,32,4096]{2,1,0:T(8,128)(2,1)S(1)} %get-tuple-element.32), channel_id=1, source_target_pairs={{0,8},{8,16},{16,24},{24,0},{1,9},{9,17},{17,25},{25,1},{2,10},{10... | collective-permute-start | bytes 1572872 | tf_op jit(solution)/shard_map/ppermute | solution.py:380
  41.1 19.7 %collective-permute-start.1 = (bf16[2,32,4096]{2,1,0:T(8,128)(2,1)S(1)}, bf16[2,32,4096]{2,1,0:T(8,128)(2,1)S(1)}, u32[]{:S(2)}, u32[]{:S(2)}) collective-permute-start(bf16[2,32,4096]{2,1,0:T(8,128)(2,1)S(1)} %get-tuple-element.32), channel_id=1, source_target_pairs={{0,24},{8,0},{16,8},{24,16},{1,25},{9,1},{17,9},{25,17},{2,26},{10... | collective-permute-start | bytes 1572872 | tf_op jit(solution)/shard_map/ppermute | solution.py:380
  60.6 9.3 %collective-permute-start.2 = (bf16[2,32,2048]{2,1,0:T(8,128)(2,1)S(1)}, bf16[2,32,2048]{2,1,0:T(8,128)(2,1)S(1)}, u32[]{:S(2)}, u32[]{:S(2)}) collective-permute-start(bf16[2,32,2048]{2,1,0:T(8,128)(2,1)S(1)} %slice.58), channel_id=1, source_target_pairs={{0,8},{8,16},{16,24},{24,0},{1,9},{9,17},{17,25},{25,1},{2,10},{10... | collective-permute-start | bytes 786440 | tf_op jit(solution)/shard_map/ppermute | solution.py:380
  60.8 12.3 %collective-permute-start.3 = (bf16[2,32,2048]{2,1,0:T(8,128)(2,1)S(1)}, bf16[2,32,2048]{2,1,0:T(8,128)(2,1)S(1)}, u32[]{:S(2)}, u32[]{:S(2)}) collective-permute-start(bf16[2,32,2048]{2,1,0:T(8,128)(2,1)S(1)} %slice.59), channel_id=1, source_target_pairs={{0,24},{8,0},{16,8},{24,16},{1,25},{9,1},{17,9},{25,17},{2,26},{10... | collective-permute-start | bytes 786440 | tf_op jit(solution)/shard_map/ppermute | solution.py:380
  73.2 4.9 %copy-start.9 = (s32[1,32]{1,0:T(1,128)S(1)}, s32[1,32]{1,0:T(1,128)}, u32[]{:S(2)}) copy-start(s32[1,32]{1,0:T(1,128)} %param.16) | copy-start | bytes 388
  73.2 5.7 %copy-start.8 = (s32[2]{0:T(128)S(1)}, s32[2]{0:T(128)}, u32[]{:S(2)}) copy-start(s32[2]{0:T(128)} %param.17) | copy-start | bytes 28
  73.2 7.6 %copy-start.2 = (bf16[1,512,2048]{2,1,0:T(8,128)(2,1)S(1)}, bf16[1,512,2048]{2,1,0:T(8,128)(2,1)}, u32[]{:S(2)}) copy-start(bf16[1,512,2048]{2,1,0:T(8,128)(2,1)} %param.9) | copy-start | bytes 6291460
  73.2 7.6 %copy-start.4 = (f32[2048]{0:T(1024)S(1)}, f32[2048]{0:T(1024)}, u32[]{:S(2)}) copy-start(f32[2048]{0:T(1024)} %param.10) | copy-start | bytes 24580
  74.9 44.6 %collective-permute-start.4 = (bf16[4,2,32,4096]{3,2,1,0:T(8,128)(2,1)}, bf16[4,2,32,4096]{3,2,1,0:T(8,128)(2,1)}, u32[]{:S(2)}, u32[]{:S(2)}) collective-permute-start(bf16[4,2,32,4096]{3,2,1,0:T(8,128)(2,1)} %pad_maximum_fusion.refs_0_), channel_id=1, source_target_pairs={{0,64},{64,4},{4,68},{68,0},{1,65},{65,5},{5,69},{69,1},{2,66},{66... | collective-permute-start | bytes 6291464 | tf_op jit(solution)/shard_map/ppermute | solution.py:379
  75.7 45.3 %collective-permute-start.5 = (bf16[4,2,32,4096]{3,2,1,0:T(8,128)(2,1)}, bf16[4,2,32,4096]{3,2,1,0:T(8,128)(2,1)}, u32[]{:S(2)}, u32[]{:S(2)}) collective-permute-start(bf16[4,2,32,4096]{3,2,1,0:T(8,128)(2,1)} %pad_maximum_fusion.refs_0_), channel_id=1, source_target_pairs={{0,68},{64,0},{4,64},{68,4},{1,69},{65,1},{5,65},{69,5},{2,70},{66... | collective-permute-start | bytes 6291464 | tf_op jit(solution)/shard_map/ppermute | solution.py:379
  83.0 3.8 %copy-start.3 = (bf16[512,2048]{1,0:T(8,128)(2,1)}, bf16[512,2048]{1,0:T(8,128)(2,1)S(1)}, u32[]{:S(2)}) copy-start(bf16[512,2048]{1,0:T(8,128)(2,1)S(1)} %shard_map.91.hid_ref) | copy-start | bytes 6291460
  86.8 54.4 %copy-start.5 = (f32[2048]{0:T(1024)S(1)}, f32[2048]{0:T(1024)}, u32[]{:S(2)}) copy-start(f32[2048]{0:T(1024)} %param.13) | copy-start | bytes 24580
  86.8 51.1 %collective-permute-start.8 = (bf16[4,2,32,4096]{3,2,1,0:T(8,128)(2,1)}, bf16[4,2,32,4096]{3,2,1,0:T(8,128)(2,1)}, u32[]{:S(2)}, u32[]{:S(2)}) collective-permute-start(bf16[4,2,32,4096]{3,2,1,0:T(8,128)(2,1)} %pad_maximum_fusion.refs_0_), channel_id=1, source_target_pairs={{0,32},{32,0},{1,33},{33,1},{2,34},{34,2},{3,35},{35,3},{4,36},{36... | collective-permute-start | bytes 6291464 | tf_op jit(solution)/shard_map/ppermute | solution.py:399
  120.8 16.1 %collective-permute-start.6 = (bf16[4,2,32,2048]{3,2,1,0:T(8,128)(2,1)S(1)}, bf16[4,2,32,2048]{3,2,1,0:T(8,128)(2,1)S(1)}, u32[]{:S(2)}, u32[]{:S(2)}) collective-permute-start(bf16[4,2,32,2048]{3,2,1,0:T(8,128)(2,1)S(1)} %slice.60), channel_id=1, source_target_pairs={{0,64},{64,4},{4,68},{68,0},{1,65},{65,5},{5,69},{69,1},{2,66},{66... | collective-permute-start | bytes 3145736 | tf_op jit(solution)/shard_map/ppermute | solution.py:379
  122.3 15.5 %collective-permute-start.7 = (bf16[4,2,32,2048]{3,2,1,0:T(8,128)(2,1)S(1)}, bf16[4,2,32,2048]{3,2,1,0:T(8,128)(2,1)S(1)}, u32[]{:S(2)}, u32[]{:S(2)}) collective-permute-start(bf16[4,2,32,2048]{3,2,1,0:T(8,128)(2,1)S(1)} %slice.61), channel_id=1, source_target_pairs={{0,68},{64,0},{4,64},{68,4},{1,69},{65,1},{5,65},{69,5},{2,70},{66... | collective-permute-start | bytes 3145736 | tf_op jit(solution)/shard_map/ppermute | solution.py:379
  125.5 15.7 %collective-permute-start.10 = (bf16[4,2,32,4096]{3,2,1,0:T(8,128)(2,1)}, bf16[4,2,32,4096]{3,2,1,0:T(8,128)(2,1)}, u32[]{:S(2)}, u32[]{:S(2)}) collective-permute-start(bf16[4,2,32,4096]{3,2,1,0:T(8,128)(2,1)} %collective-permute-done.5.refs_2_), channel_id=1, source_target_pairs={{0,32},{32,0},{1,33},{33,1},{2,34},{34,2},{3,35},{35,3},{4,36},{36... | collective-permute-start | bytes 6291464 | tf_op jit(solution)/shard_map/ppermute | solution.py:399
  125.5 15.7 %collective-permute-start.9 = (bf16[4,2,32,4096]{3,2,1,0:T(8,128)(2,1)}, bf16[4,2,32,4096]{3,2,1,0:T(8,128)(2,1)}, u32[]{:S(2)}, u32[]{:S(2)}) collective-permute-start(bf16[4,2,32,4096]{3,2,1,0:T(8,128)(2,1)} %collective-permute-done.4.refs_1_), channel_id=1, source_target_pairs={{0,32},{32,0},{1,33},{33,1},{2,34},{34,2},{3,35},{35,3},{4,36},{36... | collective-permute-start | bytes 6291464 | tf_op jit(solution)/shard_map/ppermute | solution.py:399
  136.9 2.8 %collective-permute-start.11 = (bf16[4,2,32,2048]{3,2,1,0:T(8,128)(2,1)S(1)}, bf16[4,2,32,2048]{3,2,1,0:T(8,128)(2,1)}, u32[]{:S(2)}, u32[]{:S(2)}) collective-permute-start(bf16[4,2,32,2048]{3,2,1,0:T(8,128)(2,1)S(1)} %collective-permute-done.6.refs_3_), channel_id=1, source_target_pairs={{0,32},{32,0},{1,33},{33,1},{2,34},{34,2},{3,35},{35,3},{4,36},{36... | collective-permute-start | bytes 3145736 | tf_op jit(solution)/shard_map/ppermute | solution.py:399
  137.8 3.4 %collective-permute-start.12 = (bf16[4,2,32,2048]{3,2,1,0:T(8,128)(2,1)S(1)}, bf16[4,2,32,2048]{3,2,1,0:T(8,128)(2,1)}, u32[]{:S(2)}, u32[]{:S(2)}) collective-permute-start(bf16[4,2,32,2048]{3,2,1,0:T(8,128)(2,1)S(1)} %collective-permute-done.7.refs_4_), channel_id=1, source_target_pairs={{0,32},{32,0},{1,33},{33,1},{2,34},{34,2},{3,35},{35,3},{4,36},{36... | collective-permute-start | bytes 3145736 | tf_op jit(solution)/shard_map/ppermute | solution.py:399
  165.8 37.3 %collective-permute-start.13 = (bf16[4,4,2,2,16,4096]{5,4,3,2,1,0:T(8,128)(2,1)}, bf16[4,4,2,2,16,4096]{5,4,3,2,1,0:T(8,128)(2,1)}, u32[]{:S(2)}, u32[]{:S(2)}) collective-permute-start(bf16[4,4,2,2,16,4096]{5,4,3,2,1,0:T(8,128)(2,1)} %bitcast.70), channel_id=1, source_target_pairs={{0,32},{32,0},{1,33},{33,1},{2,34},{34,2},{3,35},{35,3},{4,36},{36... | collective-permute-start | bytes 25165832 | tf_op jit(solution)/shard_map/ppermute | solution.py:399
  224.6 23.0 %all-to-all-start.1 = ((bf16[32,16,1024]{2,1,0:T(8,128)(2,1)}), bf16[32,16,1024]{2,1,0:T(8,128)(2,1)S(1)}, u32[]{:S(2)}, u32[]{:S(2)}) async-start(bf16[32,16,1024]{2,1,0:T(8,128)(2,1)} %bitcast.67), calls=%async_computation.1 | async-start | bytes 2097152 | tf_op jit(solution)/shard_map/all_to_all | solution.py:465
  247.6 1.6 copy-start
  249.2 1.6 copy-start.1
Sparse Core Ops, SparseCore 0:
  24.6 77.7 all-gather.4

commit v10 on v6

--- a/solution.py
+++ b/solution.py
@@ -18,11 +18,9 @@
 PAIR = 2 * HEAD
 STEPS = WIDTH // PAIR
 SEQ = ("x", "yhi", "z")
-QKV_PART = 3 * WIDTH // 2
-OUT_PART = WIDTH // 2
-PART = QKV_PART + 2 * OUT_PART
-RELATIVE = ((0, 0, PART), (3, 0, PART), (1, 0, PART), (2, 0, PART // 2), (2, PART // 2, PART))
-STACKED = (0, 3, 1, 2)
+QKV_HALF = 3 * WIDTH // 2
+PIECES = 2 * 5
+RINGS = (0, 3, 1, 2)
 LOG2E = 1.4426950408889634
 MIB = 1 << 20
 
@@ -99,40 +97,27 @@
     )(core, x, gain)
 
 
-def start_copies(place_ref, pieces, sems, w_ref=None, o_ref=None, base=None):
+def start_copies(place_ref, pieces, width, targets):
     my_x, my_y = place_ref[1], place_ref[2]
-
-    def block_of(part, stacked, ring):
-        x, y = (stacked, ring) if part == 0 else (ring, stacked)
-        x = lax.rem(my_x + x, 4)
-        y = lax.rem(my_y + y, 4)
-        return lax.rem(y, 2) * 8 + x * 2 + y // 2
-
-    def move(slot, part, outputs):
-        first = (slot * 2 + part) * len(RELATIVE)
-        for index, (ring, low, high) in enumerate(RELATIVE):
-            src = pieces[first + index]
-            if outputs:
-                if high < PART:
-                    continue
-                lanes, target = pl.ds(base - low, OUT_PART), None
-            else:
-                end = min(high, QKV_PART)
-                lanes, target = pl.ds(0, end - low), pl.ds(low, end - low)
-            for k, stacked in enumerate(STACKED):
-                block = block_of(part, stacked, ring)
-                if outputs:
-                    dst = o_ref.at[slot, block, :, :, pl.ds(part * OUT_PART, OUT_PART)]
-                else:
-                    dst = w_ref.at[slot, part, block, :, :, target]
-                sem = sems.at[slot if outputs else slot * 2 + part]
-                pltpu.make_async_copy(src.at[k, :, :, lanes], dst, sem).start()
-
-    for outputs, ref in ((False, w_ref), (True, o_ref)):
-        if ref is not None:
-            for part in range(2):
-                for slot in range(2):
-                    move(slot, part, outputs)
+    held = (
+        (0, 0, width),
+        (3, 0, width),
+        (1, 0, width),
+        (2, 0, width // 2),
+        (2, width // 2, width),
+    )
+    for slot, first, last, ref, sem in targets:
+        for index, (ring, low, high) in enumerate(held):
+            begin, end = max(low, first), min(high, last)
+            if begin >= end:
+                continue
+            src = pieces[slot * len(held) + index]
+            for k, stacked in enumerate(RINGS):
+                x = lax.rem(my_x + stacked, 4)
+                y = lax.rem(my_y + ring, 4)
+                block = lax.rem(y, 2) * 8 + x * 2 + y // 2
+                dst = ref.at[block, :, :, pl.ds(begin - first, end - begin)]
+                pltpu.make_async_copy(src.at[k, :, :, pl.ds(begin - low, end - begin)], dst, sem).start()
 
 
 def arrived(ref, sem):
@@ -232,11 +217,12 @@
 
 
 def middle_kernel(place_ref, att_ref, x_ref, gain_ref, *refs):
-    pieces = refs[: 4 * len(RELATIVE)]
-    mid_ref, next_ref, o_ref, sems = refs[4 * len(RELATIVE) :]
+    pieces = refs[: PIECES]
+    mid_ref, next_ref, o_ref, sems = refs[PIECES :]
     core = place_ref[0]
     half = D // 2
-    start_copies(place_ref, pieces, sems, o_ref=o_ref, base=QKV_PART + OUT_PART)
+    targets = [(slot, WIDTH, 2 * WIDTH, o_ref.at[slot], sems.at[slot]) for slot in range(2)]
+    start_copies(place_ref, pieces, 2 * WIDTH, targets)
     for slot in range(2):
         arrived(o_ref.at[slot], sems.at[slot])
 
@@ -284,11 +270,16 @@
 
 
 def column_kernel(place_ref, x_ref, cos_ref, sin_ref, *refs):
-    pieces = refs[: 4 * len(RELATIVE)]
-    out_ref, w_ref, hid_ref, sems = refs[4 * len(RELATIVE) :]
+    pieces = refs[: PIECES]
+    out_ref, w_ref, hid_ref, sems = refs[PIECES :]
     core = place_ref[0]
     half = D // 2
-    start_copies(place_ref, pieces, sems, w_ref)
+    targets = [
+        (slot, group * QKV_HALF, (group + 1) * QKV_HALF, w_ref.at[slot, group], sems.at[slot * 2 + group])
+        for group in range(2)
+        for slot in range(2)
+    ]
+    start_copies(place_ref, pieces, 3 * WIDTH, targets)
 
     def selection(transposed):
         a = lax.broadcasted_iota(jnp.int32, (C, C), 1 if transposed else 0)
@@ -346,7 +337,7 @@
         in_specs=[pl.BlockSpec(memory_space=pltpu.SMEM)] + [vmem] * 3 + [hbm] * len(pieces),
         out_specs=vmem,
         scratch_shapes=[
-            pltpu.VMEM((2, 2, 16, 2, 32, QKV_PART), jnp.bfloat16),
+            pltpu.VMEM((2, 2, 16, 2, 32, QKV_HALF), jnp.bfloat16),
             pltpu.VMEM((C, D), jnp.bfloat16),
             pltpu.SemaphoreType.DMA((4,)),
         ],
@@ -360,14 +351,15 @@
 
 
 def final_kernel(place_ref, att_ref, x_ref, *refs):
-    pieces = refs[: 4 * len(RELATIVE)]
-    out_ref, o_ref, sems = refs[4 * len(RELATIVE) :]
+    pieces = refs[: PIECES]
+    out_ref, o_ref, sems = refs[PIECES :]
     core = place_ref[0]
     half = D // 2
 
     @pl.when(pl.program_id(0) == 0)
     def _():
-        start_copies(place_ref, pieces, sems, o_ref=o_ref, base=QKV_PART)
+        targets = [(slot, 0, WIDTH, o_ref.at[slot], sems.at[slot]) for slot in range(2)]
+        start_copies(place_ref, pieces, 2 * WIDTH, targets)
         for slot in range(2):
             arrived(o_ref.at[slot], sems.at[slot])
 
@@ -436,41 +428,18 @@
     return inputs.reshape(-1, 3, STEPS, PAIR).transpose(0, 2, 1, 3).reshape(-1, 3 * WIDTH)
 
 
-def lines(inputs, *outputs):
+def line_stack(inputs, *outputs):
     shard = jnp.concatenate([by_step(inputs)] + [fold_output(output) for output in outputs], 1)
     rows = lax.all_gather(shard, "z", axis=0)
     qkv = rows[:, :, : 3 * WIDTH].reshape(2, 32, 3 * WIDTH)
-    outs = rows[:, :, 3 * WIDTH :].reshape(4, 2, 8, len(outputs), WIDTH).transpose(3, 1, 0, 2, 4)
-    outs = outs.reshape(len(outputs), 2, 32, WIDTH)
-    parts = []
-    for p in range(2):
-        lanes = slice(p * QKV_PART, (p + 1) * QKV_PART)
-        rest = slice(p * OUT_PART, (p + 1) * OUT_PART)
-        parts.append(jnp.concatenate([qkv[:, :, lanes]] + [out[:, :, rest] for out in outs], -1))
-    return parts
+    outs = rows[:, :, 3 * WIDTH :].reshape(4, 2, 8, len(outputs) * WIDTH).transpose(1, 0, 2, 3)
+    outs = outs.reshape(2, 32, len(outputs) * WIDTH)
+    return stack(forwards(first_hops(jnp.concatenate([qkv, outs], -1), "x"), "x"))
 
 
 def row_plane(inputs):
     line = lax.all_gather(by_step(inputs), ("ylo", "yhi"), axis=0)
     return line, lax.all_gather(line, ("x", "z"), axis=0).reshape(4, 4, 2, 2, 16, 3 * WIDTH)
-
-
-def inner_rings(parts):
-    hops = [first_hops(part, axis) for part, axis in zip(parts, "xy")]
-    return [stack(forwards(hop, axis)) for hop, axis in zip(hops, "xy")]
-
-
-def outer_hops(stacks):
-    return [first_hops(part, axis) for part, axis in zip(stacks, "yx")]
-
-
-def outer_forwards(hops):
-    return [forwards(hop, axis) for hop, axis in zip(hops, "yx")]
-
-
-def both_cores(parts):
-    own = [piece for part in parts for piece in part]
-    return own + [swap(piece) for piece in own]
 
 
 def shards(tokens, gain_first, inputs_first, output_first, gain_second, inputs_second, output_second, starts, band_edges):
@@ -495,20 +464,27 @@
     output_first, output_second, inputs_second, line = lax.optimization_barrier(
         (output_first, output_second, inputs_second, line)
     )
-    stacks = inner_rings(lines(inputs_second, output_second, output_first))
-    hops = outer_hops(stacks)
+    gathered = line_stack(inputs_second, output_second, output_first)
+    second, small = gathered[..., : 3 * WIDTH], gathered[..., 3 * WIDTH :]
+    small_hop = first_hops(small, "y")
     plane, hidden, row_tables, column_tables, _ = lax.optimization_barrier(
-        (plane, hidden, row_tables, column_tables, hops)
+        (plane, hidden, row_tables, column_tables, small_hop)
     )
     planes = (plane, swap(plane))
-    pieces = both_cores(outer_forwards(hops))
+    small = forwards(small_hop, "y")
+    small = small + [swap(piece) for piece in small]
+    second, small = lax.optimization_barrier((second, small))
+    second_hop = first_hops(second, "y")
 
     attended = row_layer(hidden, row_tables, planes)
-    middle, hidden = middle_layer(place, attended, residual, gain_second.reshape(1, D), pieces)
+    middle, hidden = middle_layer(place, attended, residual, gain_second.reshape(1, D), small)
+    second_hop, _ = lax.optimization_barrier((second_hop, hidden))
+    pieces = forwards(second_hop, "y")
+    pieces = pieces + [swap(piece) for piece in pieces]
     hidden = lax.all_to_all(hidden, SEQ, split_axis=0, concat_axis=0, tiled=True)
     attended = column_layer(place, hidden, column_tables, pieces)
     attended = lax.all_to_all(attended, SEQ, split_axis=0, concat_axis=0, tiled=True)
-    return final_layer(place, attended, middle, pieces)[None]
+    return final_layer(place, attended, middle, small)[None]
 
 
 def solution(mesh):

time: 275 us -> 281 us (1.022)
  blocking collectives: 90.7 us -> 56.6 us
  waiting for transfers between devices: 61.1 us -> 94.5 us
  other arithmetic: 6.78 us -> 10.3 us
    ppermute x8, waiting for transfers between devices: 14 us -> 58.3 us  [shift(): lax.ppermute(value, ('ylo', 'yhi'), [(where(y), where((y + by) % 4)) for...]
    all_to_all x1 -> x0, blocking collectives: 37.8 us -> none  [shards(): lax.all_to_all(hidden, SEQ, split_axis=0, concat_axis=0, tiled=True)]
    ppermute x8 -> x4, waiting for transfers between devices: 41.9 us -> 29.2 us  [shift(): return lax.ppermute(value, axis, [(i, (i + by) % 4) for i in range(4)])]
    all_to_all x0 -> x1, starting transfers between devices: none -> 9.45 us  [shards(): lax.all_to_all(hidden, SEQ, split_axis=0, concat_axis=0, tiled=True)]
    ppermute x8 -> x4, starting transfers between devices: 13.3 us -> 5.01 us  [shift(): return lax.ppermute(value, axis, [(i, (i + by) % 4) for i in range(4)])]
    all_to_all x1, blocking collectives: 22.8 us -> 26.5 us  [shards(): lax.all_to_all(attended, SEQ, split_axis=0, concat_axis=0, tiled=True)]
  transfers between devices with their start and end apart: 28 -> 25, of which waited for: 11 -> 10; matrix products, arithmetic and copies ran while one was open for 5% -> 6% of each run, Pallas kernels for 7% -> 11%
where the time goes in v10:
time: 281 us; the launch traced here: 280 us
  waiting for transfers between devices  94.5 us (34%)
  Pallas kernels  61.7 us (22%)
  blocking collectives  56.6 us (20%)
  starting transfers between devices  29.2 us (10%)
  between operations  15.2 us (5%)
  local copies, waits for them, and re-layouts  12.6 us (4%)
  other arithmetic  10.3 us (4%)
    ppermute x8, waiting for transfers between devices, shift(): lax.ppermute(value, ('ylo', 'yhi'), [(where(y), where((y + by) % 4)) for...  58.3 us
    ppermute x4, waiting for transfers between devices, shift(): return lax.ppermute(value, axis, [(i, (i + by) % 4) for i in range(4)])  29.2 us
    all_to_all x1, blocking collectives, shards(): lax.all_to_all(attended, SEQ, split_axis=0, concat_axis=0, tiled=True)  26.5 us
    pallas_call x1, Pallas kernels, column_layer(): pl.pallas_call(column_kernel, out_shape=jax.ShapeDtypeStruct((C, WIDTH),...  23.6 us
    pallas_call x1, Pallas kernels, row_layer(): pl.pallas_call(row_kernel, out_shape=jax.ShapeDtypeStruct((C, WIDTH), jnp...  18.4 us
    all_gather x1, blocking collectives, row_plane(): line = lax.all_gather(by_step(inputs), ('ylo', 'yhi'), axis=0)  15.2 us
    all_gather x1, blocking collectives, line_stack(): rows = lax.all_gather(shard, 'z', axis=0)  14.9 us
    ppermute x8, starting transfers between devices, shift(): lax.ppermute(value, ('ylo', 'yhi'), [(where(y), where((y + by) % 4)) for...  12.5 us
  transfers between devices with their start and end apart: 25, of which 10 were waited for; matrix products, arithmetic and copies ran while one was open for 6% of the time, Pallas kernels for 11%

profile of v10, /device:TPU:0, one launch (start us, length us, event | category | flops | bytes accessed | tf_op | source)
XLA Modules:
  0.0 280.1 jit_solution(12574221684578110317)
XLA Ops:
  6.5 0.9 reshape.75
  7.5 0.1 copy.21
  7.6 0.1 all_gather_reshape.3
  7.7 15.2 %all_gather.15 = bf16[4,16,3072]{2,1,0:T(8,128)(2,1)} all-gather(bf16[1,16,3072]{2,1,0:T(8,128)(2,1)S(1)} %all_gather_reshape.3), channel_id=1, replica_groups=mesh['ylo'=2,'core'=2,'x'=4,'yhi'=2,'z'=4] {'ylo','yhi'}, dimensions={0}, use_global_device_ids=true | all-gather | bytes 491520 | tf_op jit(solution)/shard_map/all_gather | solution.py:441
  22.9 0.9 reshape.78
  23.9 0.1 reshape.79
  24.1 14.9 %all-gather.1 = bf16[64,5120]{1,0:T(8,128)(2,1)S(1)} all-gather(bf16[16,5120]{1,0:T(8,128)(2,1)S(1)} %maximum_maximum_fusion), channel_id=3, replica_groups=mesh['ylo'=2,'core'=2,'x'=4,'yhi'=2,'z'=4] {'z'}, dimensions={0}, use_global_device_ids=true | all-gather | bytes 819200 | tf_op jit(solution)/shard_map/all_gather | solution.py:433
  39.1 1.0 fusion.6
  40.0 2.8 %collective-permute-start.1 = (bf16[2,32,5120]{2,1,0:T(8,128)(2,1)S(1)}, bf16[2,32,5120]{2,1,0:T(8,128)(2,1)S(1)}, u32[]{:S(2)}, u32[]{:S(2)}) collective-permute-start(bf16[2,32,5120]{2,1,0:T(8,128)(2,1)S(1)} %get-tuple-element.56), channel_id=1, source_target_pairs={{0,24},{8,0},{16,8},{24,16},{1,25},{9,1},{17,9},{25,17},{2,26},{10... | collective-permute-start | bytes 1966088 | tf_op jit(solution)/shard_map/ppermute | solution.py:401
  42.9 15.3 %collective-permute-done.1 = bf16[2,32,5120]{2,1,0:T(8,128)(2,1)S(1)} collective-permute-done((bf16[2,32,5120]{2,1,0:T(8,128)(2,1)S(1)}, bf16[2,32,5120]{2,1,0:T(8,128)(2,1)S(1)}, u32[]{:S(2)}, u32[]{:S(2)}) %collective-permute-start.1) | collective-permute-done | bytes 655392 | tf_op jit(solution)/shard_map/ppermute | solution.py:401
  58.2 2.0 collective-permute-start.3
  60.2 0.9 copy-done.9
  61.1 0.1 collective-permute-start.2
  61.3 0.7 fusion.9
  63.3 8.8 %collective-permute-done.3 = bf16[2,32,2560]{2,1,0:T(8,128)(2,1)S(1)} collective-permute-done((bf16[2,32,2560]{2,1,0:T(8,128)(2,1)S(1)}, bf16[2,32,2560]{2,1,0:T(8,128)(2,1)S(1)}, u32[]{:S(2)}, u32[]{:S(2)}) %collective-permute-start.3) | collective-permute-done | bytes 327712 | tf_op jit(solution)/shard_map/ppermute | solution.py:401
  72.1 5.0 %collective-permute-done.2 = bf16[2,32,2560]{2,1,0:T(8,128)(2,1)S(1)} collective-permute-done((bf16[2,32,2560]{2,1,0:T(8,128)(2,1)S(1)}, bf16[2,32,2560]{2,1,0:T(8,128)(2,1)S(1)}, u32[]{:S(2)}, u32[]{:S(2)}) %collective-permute-start.2) | collective-permute-done | bytes 327712 | tf_op jit(solution)/shard_map/ppermute | solution.py:401
  77.2 1.5 pad_maximum_fusion.3.refs_0_
  78.7 2.3 collective-permute-start.4
  81.1 1.0 collective-permute-start.5
  82.0 0.1 add_convert_fusion
  82.1 0.1 convert_element_type.35
  82.2 0.6 constant_dynamic-slice_fusion
  82.8 2.1 shard_map.91.hid_ref
  85.0 0.6 add_convert_fusion.1
  85.6 1.9 fusion.4
  87.6 1.0 pad_maximum_fusion.5
  88.6 1.0 pad_maximum_fusion.7
  89.6 7.7 %collective-permute-done.4.refs_1_ = bf16[4,2,32,2048]{3,2,1,0:T(8,128)(2,1)} collective-permute-done((bf16[4,2,32,2048]{3,2,1,0:T(8,128)(2,1)S(1)}, bf16[4,2,32,2048]{3,2,1,0:T(8,128)(2,1)}, u32[]{:S(2)}, u32[]{:S(2)}) %collective-permute-start.4) | collective-permute-done | bytes 1048608 | tf_op jit(solution)/shard_map/ppermute | solution.py:400
  97.3 1.9 collective-permute-done.5.refs_2_
  99.3 0.5 collective-permute-start.9
  99.8 1.1 slice.68
  100.9 0.4 collective-permute-start.7
  101.3 1.1 slice.69
  102.4 0.1 collective-permute-start.10
  102.5 0.5 collective-permute-start.11
  103.0 5.2 %collective-permute-done.9.refs_5_ = bf16[4,2,32,2048]{3,2,1,0:T(8,128)(2,1)S(1)} collective-permute-done((bf16[4,2,32,2048]{3,2,1,0:T(8,128)(2,1)S(1)}, bf16[4,2,32,2048]{3,2,1,0:T(8,128)(2,1)S(1)}, u32[]{:S(2)}, u32[]{:S(2)}) %collective-permute-start.9) | collective-permute-done | bytes 1048608 | tf_op jit(solution)/shard_map/ppermute | solution.py:420
  108.1 1.5 collective-permute-start.8
  109.7 6.4 %collective-permute-done.7.refs_3_ = bf16[4,2,32,1024]{3,2,1,0:T(8,128)(2,1)S(1)} collective-permute-done((bf16[4,2,32,1024]{3,2,1,0:T(8,128)(2,1)S(1)}, bf16[4,2,32,1024]{3,2,1,0:T(8,128)(2,1)S(1)}, u32[]{:S(2)}, u32[]{:S(2)}) %collective-permute-start.7) | collective-permute-done | bytes 524320 | tf_op jit(solution)/shard_map/ppermute | solution.py:400
  116.1 6.3 %collective-permute-done.8.refs_4_ = bf16[4,2,32,1024]{3,2,1,0:T(8,128)(2,1)S(1)} collective-permute-done((bf16[4,2,32,1024]{3,2,1,0:T(8,128)(2,1)S(1)}, bf16[4,2,32,1024]{3,2,1,0:T(8,128)(2,1)S(1)}, u32[]{:S(2)}, u32[]{:S(2)}) %collective-permute-start.8) | collective-permute-done | bytes 524320 | tf_op jit(solution)/shard_map/ppermute | solution.py:400
  122.4 2.6 pad_maximum_fusion.refs_0_
  125.0 0.8 copy-done.14
  125.8 0.4 collective-permute-start.14
  126.2 2.9 %collective-permute-start.15 = (bf16[4,2,32,3072]{3,2,1,0:T(8,128)(2,1)}, bf16[4,2,32,3072]{3,2,1,0:T(8,128)(2,1)}, u32[]{:S(2)}, u32[]{:S(2)}) collective-permute-start(bf16[4,2,32,3072]{3,2,1,0:T(8,128)(2,1)} %pad_maximum_fusion.refs_0_), channel_id=1, source_target_pairs={{0,68},{64,0},{4,64},{68,4},{1,69},{65,1},{5,65},{69,5},{2,70},{66... | collective-permute-start | bytes 4718600 | tf_op jit(solution)/shard_map/ppermute | solution.py:400
  129.1 0.6 pad_add_fusion.place_ref
  129.7 18.4 %shard_map.92.att_ref = bf16[512,1024]{1,0:T(8,128)(2,1)} custom-call(bf16[512,2048]{1,0:T(8,128)(2,1)} %copy-done.1, f32[512,128]{1,0:T(8,128)} %get-tuple-element.34.cos_ref, f32[512,128]{1,0:T(8,128)} %get-tuple-element.35.sin_ref, bf16[4,4,2,2,16,3072]{5,4,3,2,1,0:T(8,128)(2,1)} %bitcast.56, ...), custom_call_target="tpu_custom_call" | custom-call | flops 7516192768 | bytes 15728640 | tf_op jit(solution)/shard_map/pallas_call | solution.py:201
  148.1 9.8 %shard_map.93 = (bf16[512,2048]{1,0:T(8,128)(2,1)}, bf16[512,2048]{1,0:T(8,128)(2,1)}) custom-call(s32[3]{0:T(128)} %pad_add_fusion.place_ref, bf16[512,1024]{1,0:T(8,128)(2,1)} %shard_map.92.att_ref, bf16[512,2048]{1,0:T(8,128)(2,1)} %bitcast.37, f32[1,2048]{1,0:T(1,128)} %bitcast.53, bf16[4,2,32,2048]{3,2,1,0:T(8,128)(2,1)} %copy-done.3, ...), custom_call_target="tpu_custom_call" | custom-call | flops 2147483648 | bytes 11534336 | tf_op jit(solution)/shard_map/pallas_call | solution.py:254
  157.9 9.5 %all-to-all-start = ((bf16[32,16,2048]{2,1,0:T(8,128)(2,1)}), bf16[32,16,2048]{2,1,0:T(8,128)(2,1)S(1)}, u32[]{:S(2)}, u32[]{:S(2)}) async-start(bf16[32,16,2048]{2,1,0:T(8,128)(2,1)} %bitcast.48), calls=%async_computation | async-start | bytes 4194304 | tf_op jit(solution)/shard_map/all_to_all | solution.py:484
  167.4 1.2 slice.62
  168.6 0.1 collective-permute-start.19
  168.7 1.5 collective-permute-start.16
  170.2 0.2 collective-permute-start.18
  170.3 1.2 slice.63
  171.5 0.4 collective-permute-start.20
  172.0 2.5 collective-permute-start.17
  174.5 35.9 %collective-permute-done.16.refs_3_ = bf16[4,2,32,1536]{3,2,1,0:T(8,128)(2,1)S(1)} collective-permute-done((bf16[4,2,32,1536]{3,2,1,0:T(8,128)(2,1)S(1)}, bf16[4,2,32,1536]{3,2,1,0:T(8,128)(2,1)S(1)}, u32[]{:S(2)}, u32[]{:S(2)}) %collective-permute-start.16) | collective-permute-done | bytes 786464 | tf_op jit(solution)/shard_map/ppermute | solution.py:400
  210.4 0.1 collective-permute-start.21
  210.5 0.4 collective-permute-start.22
  211.0 1.9 collective-permute-done.21.refs_8_
  212.8 0.3 copy-done.21
  213.2 0.9 copy-done.24
  214.1 1.3 copy-done.10
  215.4 23.6 %shard_map.94 = bf16[512,1024]{1,0:T(8,128)(2,1)} custom-call(s32[3]{0:T(128)} %pad_add_fusion.place_ref, bf16[512,2048]{1,0:T(8,128)(2,1)} %bitcast.47, f32[512,128]{1,0:T(8,128)} %get-tuple-element.48.cos_ref, f32[512,128]{1,0:T(8,128)} %get-tuple-element.49.sin_ref, bf16[4,2,32,3072]{3,2,1,0:T(8,128)(2,1)} %pad_maximum_fusion.refs_0_, ...), custom_call_target="tpu_custom_call" | custom-call | flops 7516192768 | bytes 15728640 | tf_op jit(solution)/shard_map/pallas_call | solution.py:334
  239.0 26.5 %all_to_all.22 = bf16[32,16,1024]{2,1,0:T(8,128)(2,1)} all-to-all(bf16[32,16,1024]{2,1,0:T(8,128)(2,1)} %bitcast.50), channel_id=1, replica_groups=mesh['ylo'=2,'core'=2,'x'=4,'yhi'=2,'z'=4] {'x','yhi','z'}, dimensions={0} | all-to-all | bytes 2097152 | tf_op jit(solution)/shard_map/all_to_all | solution.py:486
  265.5 7.8 %shard_map.95 = bf16[512,2048]{1,0:T(8,128)(2,1)} custom-call(s32[3]{0:T(128)} %pad_add_fusion.place_ref, bf16[512,1024]{1,0:T(8,128)(2,1)} %bitcast.40, bf16[512,2048]{1,0:T(8,128)(2,1)} %get-tuple-element.54.x_ref, bf16[4,2,32,2048]{3,2,1,0:T(8,128)(2,1)} %copy-done.3, bf16[4,2,32,2048]{3,2,1,0:T(8,128)(2,1)} %collective-permute-done.4.refs_1_, ...), custom_call_target="tpu_custom_call" | custom-call | flops 2147483648 | bytes 9437184 | tf_op jit(solution)/shard_map/pallas_call | solution.py:376
  (76 shorter events, 0.4 us)
Async XLA Ops:
  6.5 17.5 %copy-start.16 = (bf16[8,2048]{1,0:T(8,128)(2,1)S(1)}, bf16[8,2048]{1,0:T(8,128)(2,1)}, u32[]{:S(2)}) copy-start(bf16[8,2048]{1,0:T(8,128)(2,1)} %param.12) | copy-start | bytes 98308
  6.5 17.5 %copy-start.15 = (bf16[8,2048]{1,0:T(8,128)(2,1)S(1)}, bf16[8,2048]{1,0:T(8,128)(2,1)}, u32[]{:S(2)}) copy-start(bf16[8,2048]{1,0:T(8,128)(2,1)} %param.15) | copy-start | bytes 98308
  6.5 92.7 %all-gather.4.cloned.1.call-start = ((), (), s32[]{:S(2)}) async-start(), calls=%async_computation.2 | async-start | bytes 6684672 | tf_op jit(solution)/shard_map/all_gather | solution.py:442
  39.0 22.3 %copy-start.17 = (s32[2]{0:T(128)S(1)}, s32[2]{0:T(128)}, u32[]{:S(2)}) copy-start(s32[2]{0:T(128)} %param.17) | copy-start | bytes 28
  40.0 18.2 %collective-permute-start.1 = (bf16[2,32,5120]{2,1,0:T(8,128)(2,1)S(1)}, bf16[2,32,5120]{2,1,0:T(8,128)(2,1)S(1)}, u32[]{:S(2)}, u32[]{:S(2)}) collective-permute-start(bf16[2,32,5120]{2,1,0:T(8,128)(2,1)S(1)} %get-tuple-element.56), channel_id=1, source_target_pairs={{0,24},{8,0},{16,8},{24,16},{1,25},{9,1},{17,9},{25,17},{2,26},{10... | collective-permute-start | bytes 1966088 | tf_op jit(solution)/shard_map/ppermute | solution.py:401
  42.9 17.4 %collective-permute-start = (bf16[2,32,5120]{2,1,0:T(8,128)(2,1)S(1)}, bf16[2,32,5120]{2,1,0:T(8,128)(2,1)S(1)}, u32[]{:S(2)}, u32[]{:S(2)}) collective-permute-start(bf16[2,32,5120]{2,1,0:T(8,128)(2,1)S(1)} %get-tuple-element.56), channel_id=1, source_target_pairs={{0,8},{8,16},{16,24},{24,0},{1,9},{9,17},{17,25},{25,1},{2,10},{10... | collective-permute-start | bytes 1966088 | tf_op jit(solution)/shard_map/ppermute | solution.py:401
  58.2 19.0 %copy-start.8 = (bf16[2,32,5120]{2,1,0:T(8,128)(2,1)}, bf16[2,32,5120]{2,1,0:T(8,128)(2,1)S(1)}, u32[]{:S(2)}) copy-start(bf16[2,32,5120]{2,1,0:T(8,128)(2,1)S(1)} %collective-permute-done.1) | copy-start | bytes 1966084
  58.2 13.9 %collective-permute-start.3 = (bf16[2,32,2560]{2,1,0:T(8,128)(2,1)S(1)}, bf16[2,32,2560]{2,1,0:T(8,128)(2,1)S(1)}, u32[]{:S(2)}, u32[]{:S(2)}) collective-permute-start(bf16[2,32,2560]{2,1,0:T(8,128)(2,1)S(1)} %slice.67), channel_id=1, source_target_pairs={{0,24},{8,0},{16,8},{24,16},{1,25},{9,1},{17,9},{25,17},{2,26},{10... | collective-permute-start | bytes 983048 | tf_op jit(solution)/shard_map/ppermute | solution.py:401
  60.2 0.9 copy-start.9
  61.1 16.0 %collective-permute-start.2 = (bf16[2,32,2560]{2,1,0:T(8,128)(2,1)S(1)}, bf16[2,32,2560]{2,1,0:T(8,128)(2,1)S(1)}, u32[]{:S(2)}, u32[]{:S(2)}) collective-permute-start(bf16[2,32,2560]{2,1,0:T(8,128)(2,1)S(1)} %slice.66), channel_id=1, source_target_pairs={{0,8},{8,16},{16,24},{24,0},{1,9},{9,17},{17,25},{25,1},{2,10},{10... | collective-permute-start | bytes 983048 | tf_op jit(solution)/shard_map/ppermute | solution.py:401
  77.2 1.5 copy-start.4
  77.2 4.9 %copy-start.18 = (s32[1,32]{1,0:T(1,128)S(1)}, s32[1,32]{1,0:T(1,128)}, u32[]{:S(2)}) copy-start(s32[1,32]{1,0:T(1,128)} %param.16) | copy-start | bytes 388
  77.2 5.6 %copy-start = (bf16[1,512,2048]{2,1,0:T(8,128)(2,1)S(1)}, bf16[1,512,2048]{2,1,0:T(8,128)(2,1)}, u32[]{:S(2)}) copy-start(bf16[1,512,2048]{2,1,0:T(8,128)(2,1)} %param.9) | copy-start | bytes 6291460
  77.2 5.6 %copy-start.2 = (f32[2048]{0:T(1024)S(1)}, f32[2048]{0:T(1024)}, u32[]{:S(2)}) copy-start(f32[2048]{0:T(1024)} %param.10) | copy-start | bytes 24580
  78.7 20.6 %copy-start.3 = (bf16[4,2,32,2048]{3,2,1,0:T(8,128)(2,1)}, bf16[4,2,32,2048]{3,2,1,0:T(8,128)(2,1)S(1)}, u32[]{:S(2)}) copy-start(bf16[4,2,32,2048]{3,2,1,0:T(8,128)(2,1)S(1)} %pad_maximum_fusion.3.refs_0_) | copy-start | bytes 3145732
  78.7 18.6 %collective-permute-start.4 = (bf16[4,2,32,2048]{3,2,1,0:T(8,128)(2,1)S(1)}, bf16[4,2,32,2048]{3,2,1,0:T(8,128)(2,1)}, u32[]{:S(2)}, u32[]{:S(2)}) collective-permute-start(bf16[4,2,32,2048]{3,2,1,0:T(8,128)(2,1)S(1)} %pad_maximum_fusion.3.refs_0_), channel_id=1, source_target_pairs={{0,64},{64,4},{4,68},{68,0},{1,65},{65,5},{5,69},{69,1},{2,66},{66... | collective-permute-start | bytes 3145736 | tf_op jit(solution)/shard_map/ppermute | solution.py:400
  81.1 18.2 %collective-permute-start.5 = (bf16[4,2,32,2048]{3,2,1,0:T(8,128)(2,1)S(1)}, bf16[4,2,32,2048]{3,2,1,0:T(8,128)(2,1)}, u32[]{:S(2)}, u32[]{:S(2)}) collective-permute-start(bf16[4,2,32,2048]{3,2,1,0:T(8,128)(2,1)S(1)} %pad_maximum_fusion.3.refs_0_), channel_id=1, source_target_pairs={{0,68},{64,0},{4,64},{68,4},{1,69},{65,1},{5,65},{69,5},{2,70},{66... | collective-permute-start | bytes 3145736 | tf_op jit(solution)/shard_map/ppermute | solution.py:400
  84.9 4.7 %copy-start.1 = (bf16[512,2048]{1,0:T(8,128)(2,1)}, bf16[512,2048]{1,0:T(8,128)(2,1)S(1)}, u32[]{:S(2)}) copy-start(bf16[512,2048]{1,0:T(8,128)(2,1)S(1)} %shard_map.91.hid_ref) | copy-start | bytes 6291460
  87.6 34.8 %copy-start.5 = (bf16[1,2,32,5120]{3,2,1,0:T(8,128)(2,1)S(1)}, bf16[1,2,32,5120]{3,2,1,0:T(8,128)(2,1)}, u32[]{:S(2)}) copy-start(bf16[1,2,32,5120]{3,2,1,0:T(8,128)(2,1)} %copy-done.4) | copy-start | bytes 1966084
  87.6 34.8 %copy-start.6 = (bf16[1,2,32,5120]{3,2,1,0:T(8,128)(2,1)S(1)}, bf16[1,2,32,5120]{3,2,1,0:T(8,128)(2,1)}, u32[]{:S(2)}) copy-start(bf16[1,2,32,5120]{3,2,1,0:T(8,128)(2,1)} %get-tuple-element.55) | copy-start | bytes 1966084
  99.3 30.4 %collective-permute-start.6 = (bf16[4,4,2,2,16,3072]{5,4,3,2,1,0:T(8,128)(2,1)}, bf16[4,4,2,2,16,3072]{5,4,3,2,1,0:T(8,128)(2,1)}, u32[]{:S(2)}, u32[]{:S(2)}) collective-permute-start(bf16[4,4,2,2,16,3072]{5,4,3,2,1,0:T(8,128)(2,1)} %bitcast.55), channel_id=1, source_target_pairs={{0,32},{32,0},{1,33},{33,1},{2,34},{34,2},{3,35},{35,3},{4,36},{36... | collective-permute-start | bytes 18874376 | tf_op jit(solution)/shard_map/ppermute | solution.py:420
  99.3 8.9 %collective-permute-start.9 = (bf16[4,2,32,2048]{3,2,1,0:T(8,128)(2,1)S(1)}, bf16[4,2,32,2048]{3,2,1,0:T(8,128)(2,1)S(1)}, u32[]{:S(2)}, u32[]{:S(2)}) collective-permute-start(bf16[4,2,32,2048]{3,2,1,0:T(8,128)(2,1)S(1)} %pad_maximum_fusion.3.refs_0_), channel_id=1, source_target_pairs={{0,32},{32,0},{1,33},{33,1},{2,34},{34,2},{3,35},{35,3},{4,36},{36... | collective-permute-start | bytes 3145736 | tf_op jit(solution)/shard_map/ppermute | solution.py:420
  100.9 15.2 %collective-permute-start.7 = (bf16[4,2,32,1024]{3,2,1,0:T(8,128)(2,1)S(1)}, bf16[4,2,32,1024]{3,2,1,0:T(8,128)(2,1)S(1)}, u32[]{:S(2)}, u32[]{:S(2)}) collective-permute-start(bf16[4,2,32,1024]{3,2,1,0:T(8,128)(2,1)S(1)} %slice.68), channel_id=1, source_target_pairs={{0,64},{64,4},{4,68},{68,0},{1,65},{65,5},{5,69},{69,1},{2,66},{66... | collective-permute-start | bytes 1572872 | tf_op jit(solution)/shard_map/ppermute | solution.py:400
  102.4 22.6 %collective-permute-start.10 = (bf16[4,2,32,2048]{3,2,1,0:T(8,128)(2,1)}, bf16[4,2,32,2048]{3,2,1,0:T(8,128)(2,1)}, u32[]{:S(2)}, u32[]{:S(2)}) collective-permute-start(bf16[4,2,32,2048]{3,2,1,0:T(8,128)(2,1)} %collective-permute-done.4.refs_1_), channel_id=1, source_target_pairs={{0,32},{32,0},{1,33},{33,1},{2,34},{34,2},{3,35},{35,3},{4,36},{36... | collective-permute-start | bytes 3145736 | tf_op jit(solution)/shard_map/ppermute | solution.py:420
  102.5 22.5 %collective-permute-start.11 = (bf16[4,2,32,2048]{3,2,1,0:T(8,128)(2,1)}, bf16[4,2,32,2048]{3,2,1,0:T(8,128)(2,1)}, u32[]{:S(2)}, u32[]{:S(2)}) collective-permute-start(bf16[4,2,32,2048]{3,2,1,0:T(8,128)(2,1)} %collective-permute-done.5.refs_2_), channel_id=1, source_target_pairs={{0,32},{32,0},{1,33},{33,1},{2,34},{34,2},{3,35},{35,3},{4,36},{36... | collective-permute-start | bytes 3145736 | tf_op jit(solution)/shard_map/ppermute | solution.py:420
  108.1 20.9 %copy-start.7 = (bf16[4,2,32,2048]{3,2,1,0:T(8,128)(2,1)}, bf16[4,2,32,2048]{3,2,1,0:T(8,128)(2,1)S(1)}, u32[]{:S(2)}) copy-start(bf16[4,2,32,2048]{3,2,1,0:T(8,128)(2,1)S(1)} %collective-permute-done.9.refs_5_) | copy-start | bytes 3145732
  108.1 14.2 %collective-permute-start.8 = (bf16[4,2,32,1024]{3,2,1,0:T(8,128)(2,1)S(1)}, bf16[4,2,32,1024]{3,2,1,0:T(8,128)(2,1)S(1)}, u32[]{:S(2)}, u32[]{:S(2)}) collective-permute-start(bf16[4,2,32,1024]{3,2,1,0:T(8,128)(2,1)S(1)} %slice.69), channel_id=1, source_target_pairs={{0,68},{64,0},{4,64},{68,4},{1,69},{65,1},{5,65},{69,5},{2,70},{66... | collective-permute-start | bytes 1572872 | tf_op jit(solution)/shard_map/ppermute | solution.py:400
  116.0 8.9 %copy-start.11 = (bf16[4,2,32,1024]{3,2,1,0:T(8,128)(2,1)}, bf16[4,2,32,1024]{3,2,1,0:T(8,128)(2,1)S(1)}, u32[]{:S(2)}) copy-start(bf16[4,2,32,1024]{3,2,1,0:T(8,128)(2,1)S(1)} %collective-permute-done.7.refs_3_) | copy-start | bytes 1572868
  116.1 8.9 %collective-permute-start.12 = (bf16[4,2,32,1024]{3,2,1,0:T(8,128)(2,1)S(1)}, bf16[4,2,32,1024]{3,2,1,0:T(8,128)(2,1)S(1)}, u32[]{:S(2)}, u32[]{:S(2)}) collective-permute-start(bf16[4,2,32,1024]{3,2,1,0:T(8,128)(2,1)S(1)} %collective-permute-done.7.refs_3_), channel_id=1, source_target_pairs={{0,32},{32,0},{1,33},{33,1},{2,34},{34,2},{3,35},{35,3},{4,36},{36... | collective-permute-start | bytes 1572872 | tf_op jit(solution)/shard_map/ppermute | solution.py:420
  122.3 6.7 %copy-start.12 = (bf16[4,2,32,1024]{3,2,1,0:T(8,128)(2,1)}, bf16[4,2,32,1024]{3,2,1,0:T(8,128)(2,1)S(1)}, u32[]{:S(2)}) copy-start(bf16[4,2,32,1024]{3,2,1,0:T(8,128)(2,1)S(1)} %collective-permute-done.8.refs_4_) | copy-start | bytes 1572868
  122.3 2.6 collective-permute-start.13
  125.0 23.2 %copy-start.13 = (bf16[4,2,32,1024]{3,2,1,0:T(8,128)(2,1)}, bf16[4,2,32,1024]{3,2,1,0:T(8,128)(2,1)S(1)}, u32[]{:S(2)}) copy-start(bf16[4,2,32,1024]{3,2,1,0:T(8,128)(2,1)S(1)} %collective-permute-done.12.refs_8_) | copy-start | bytes 1572868
  125.0 0.9 copy-start.14
  125.8 41.6 %collective-permute-start.14 = (bf16[4,2,32,3072]{3,2,1,0:T(8,128)(2,1)}, bf16[4,2,32,3072]{3,2,1,0:T(8,128)(2,1)}, u32[]{:S(2)}, u32[]{:S(2)}) collective-permute-start(bf16[4,2,32,3072]{3,2,1,0:T(8,128)(2,1)} %pad_maximum_fusion.refs_0_), channel_id=1, source_target_pairs={{0,64},{64,4},{4,68},{68,0},{1,65},{65,5},{5,69},{69,1},{2,66},{66... | collective-permute-start | bytes 4718600 | tf_op jit(solution)/shard_map/ppermute | solution.py:400
  126.2 41.2 %collective-permute-start.15 = (bf16[4,2,32,3072]{3,2,1,0:T(8,128)(2,1)}, bf16[4,2,32,3072]{3,2,1,0:T(8,128)(2,1)}, u32[]{:S(2)}, u32[]{:S(2)}) collective-permute-start(bf16[4,2,32,3072]{3,2,1,0:T(8,128)(2,1)} %pad_maximum_fusion.refs_0_), channel_id=1, source_target_pairs={{0,68},{64,0},{4,64},{68,4},{1,69},{65,1},{5,65},{69,5},{2,70},{66... | collective-permute-start | bytes 4718600 | tf_op jit(solution)/shard_map/ppermute | solution.py:400
  157.9 56.1 %all-to-all-start = ((bf16[32,16,2048]{2,1,0:T(8,128)(2,1)}), bf16[32,16,2048]{2,1,0:T(8,128)(2,1)S(1)}, u32[]{:S(2)}, u32[]{:S(2)}) async-start(bf16[32,16,2048]{2,1,0:T(8,128)(2,1)} %bitcast.48), calls=%async_computation | async-start | bytes 4194304 | tf_op jit(solution)/shard_map/all_to_all | solution.py:484
  168.6 42.3 %collective-permute-start.19 = (bf16[4,2,32,3072]{3,2,1,0:T(8,128)(2,1)}, bf16[4,2,32,3072]{3,2,1,0:T(8,128)(2,1)S(1)}, u32[]{:S(2)}, u32[]{:S(2)}) collective-permute-start(bf16[4,2,32,3072]{3,2,1,0:T(8,128)(2,1)} %collective-permute-done.14.refs_1_), channel_id=1, source_target_pairs={{0,32},{32,0},{1,33},{33,1},{2,34},{34,2},{3,35},{35,3},{4,36},{36... | collective-permute-start | bytes 4718600 | tf_op jit(solution)/shard_map/ppermute | solution.py:420
  168.7 41.7 %collective-permute-start.16 = (bf16[4,2,32,1536]{3,2,1,0:T(8,128)(2,1)S(1)}, bf16[4,2,32,1536]{3,2,1,0:T(8,128)(2,1)S(1)}, u32[]{:S(2)}, u32[]{:S(2)}) collective-permute-start(bf16[4,2,32,1536]{3,2,1,0:T(8,128)(2,1)S(1)} %slice.62), channel_id=1, source_target_pairs={{0,64},{64,4},{4,68},{68,0},{1,65},{65,5},{5,69},{69,1},{2,66},{66... | collective-permute-start | bytes 2359304 | tf_op jit(solution)/shard_map/ppermute | solution.py:400
  170.2 40.8 %collective-permute-start.18 = (bf16[4,2,32,3072]{3,2,1,0:T(8,128)(2,1)}, bf16[4,2,32,3072]{3,2,1,0:T(8,128)(2,1)S(1)}, u32[]{:S(2)}, u32[]{:S(2)}) collective-permute-start(bf16[4,2,32,3072]{3,2,1,0:T(8,128)(2,1)} %pad_maximum_fusion.refs_0_), channel_id=1, source_target_pairs={{0,32},{32,0},{1,33},{33,1},{2,34},{34,2},{3,35},{35,3},{4,36},{36... | collective-permute-start | bytes 4718600 | tf_op jit(solution)/shard_map/ppermute | solution.py:420
  171.5 39.4 %collective-permute-start.20 = (bf16[4,2,32,3072]{3,2,1,0:T(8,128)(2,1)}, bf16[4,2,32,3072]{3,2,1,0:T(8,128)(2,1)S(1)}, u32[]{:S(2)}, u32[]{:S(2)}) collective-permute-start(bf16[4,2,32,3072]{3,2,1,0:T(8,128)(2,1)} %collective-permute-done.15.refs_2_), channel_id=1, source_target_pairs={{0,32},{32,0},{1,33},{33,1},{2,34},{34,2},{3,35},{35,3},{4,36},{36... | collective-permute-start | bytes 4718600 | tf_op jit(solution)/shard_map/ppermute | solution.py:420
  172.0 38.5 %collective-permute-start.17 = (bf16[4,2,32,1536]{3,2,1,0:T(8,128)(2,1)S(1)}, bf16[4,2,32,1536]{3,2,1,0:T(8,128)(2,1)S(1)}, u32[]{:S(2)}, u32[]{:S(2)}) collective-permute-start(bf16[4,2,32,1536]{3,2,1,0:T(8,128)(2,1)S(1)} %slice.63), channel_id=1, source_target_pairs={{0,68},{64,0},{4,64},{68,4},{1,69},{65,1},{5,65},{69,5},{2,70},{66... | collective-permute-start | bytes 2359304 | tf_op jit(solution)/shard_map/ppermute | solution.py:400
  210.4 3.6 %copy-start.22 = (bf16[4,2,32,1536]{3,2,1,0:T(8,128)(2,1)}, bf16[4,2,32,1536]{3,2,1,0:T(8,128)(2,1)S(1)}, u32[]{:S(2)}) copy-start(bf16[4,2,32,1536]{3,2,1,0:T(8,128)(2,1)S(1)} %collective-permute-done.16.refs_3_) | copy-start | bytes 2359300
  210.4 2.4 collective-permute-start.21
  210.5 2.3 copy-start.23
  210.5 3.5 %collective-permute-start.22 = (bf16[4,2,32,1536]{3,2,1,0:T(8,128)(2,1)S(1)}, bf16[4,2,32,1536]{3,2,1,0:T(8,128)(2,1)}, u32[]{:S(2)}, u32[]{:S(2)}) collective-permute-start(bf16[4,2,32,1536]{3,2,1,0:T(8,128)(2,1)S(1)} %collective-permute-done.17.refs_4_), channel_id=1, source_target_pairs={{0,32},{32,0},{1,33},{33,1},{2,34},{34,2},{3,35},{35,3},{4,36},{36... | collective-permute-start | bytes 2359304 | tf_op jit(solution)/shard_map/ppermute | solution.py:420
  210.9 1.9 copy-start.20
  210.9 1.9 copy-start.19
  211.0 2.2 copy-start.21
  213.2 0.9 copy-start.24
  214.0 1.3 copy-start.10
Sparse Core Ops, SparseCore 0:
  23.0 71.0 all-gather.3

commit v11 on v3

--- a/solution.py
+++ b/solution.py
@@ -301,14 +301,14 @@
     return pl.pallas_call(
         column_kernel,
         out_shape=jax.ShapeDtypeStruct((C, WIDTH), jnp.bfloat16),
-        in_specs=[pl.BlockSpec(memory_space=pltpu.SMEM)] + [vmem] * 3 + [pl.BlockSpec(memory_space=pl.ANY)] * 2,
+        in_specs=[pl.BlockSpec(memory_space=pltpu.SMEM)] + [vmem] * 3 + [pl.BlockSpec(memory_space=pltpu.HBM)] * 2,
         out_specs=vmem,
         scratch_shapes=[
             pltpu.VMEM((STEPS, 2, 2, 4, 2, 4, 16, 3 * PAIR), jnp.bfloat16),
             pltpu.VMEM((C, D), jnp.bfloat16),
             pltpu.SemaphoreType.DMA((STEPS,)),
         ],
-        compiler_params=pltpu.CompilerParams(vmem_limit_bytes=40 * MIB),
+        compiler_params=pltpu.CompilerParams(vmem_limit_bytes=56 * MIB),
         cost_estimate=pl.CostEstimate(
             flops=2 * C * D * 3 * WIDTH + 4 * C * C * WIDTH,
             bytes_accessed=2 * (C * D + 3 * D * WIDTH + C * WIDTH),
@@ -430,11 +430,6 @@
     place = jnp.stack([core, lax.axis_index("x").astype(jnp.int32), my_y.astype(jnp.int32)])
 
     line = column_line(inputs_second, output_second)
-    own, line = row_weights(inputs_first, output_first, line)
-    plane = column_plane(line)
-    pieces = [piece for part in own for piece in part]
-    pieces = pieces + [swap(piece) for piece in pieces]
-
     frequency = frequencies(band_edges, HEAD // 2)
     block_starts = starts[0]
     own_start = lax.dynamic_index_in_dim(block_starts, seq, 0, keepdims=False)
@@ -444,6 +439,14 @@
     column_tables = rotary_tables(column_positions, frequency)
 
     hidden = normed_slots(core_scalar, residual, gain_first.reshape(1, D))
+    own, line = row_weights(inputs_first, output_first, line)
+    plane = column_plane(line)
+    pieces = [piece for part in own for piece in part]
+    early, hidden, row_tables, column_tables = lax.optimization_barrier(
+        (own[0][1], hidden, row_tables, column_tables)
+    )
+    other = [swap(early if index == 1 else piece) for index, piece in enumerate(pieces)]
+    pieces = pieces + other
     middle, hidden = row_layer(place, residual, hidden, gain_second.reshape(1, D), row_tables, pieces)
     plane, hidden = lax.optimization_barrier((plane, hidden))
     planes = (plane, swap(plane))

time: 253 us -> 257 us (1.016)
  blocking collectives: 14.1 us -> 49.5 us
  waiting for transfers between devices: 104 us -> 75.9 us
  starting transfers between devices: 40.1 us -> 33.9 us
    all_to_all x0 -> x1, blocking collectives: none -> 35.5 us  [shards(): lax.all_to_all(hidden, SEQ, split_axis=0, concat_axis=0, tiled=True)]
    all_to_all x1 -> x0, waiting for transfers between devices: 29.1 us -> none  [shards(): lax.all_to_all(hidden, SEQ, split_axis=0, concat_axis=0, tiled=True)]
    all_to_all x1 -> x0, starting transfers between devices: 6.53 us -> none  [shards(): lax.all_to_all(hidden, SEQ, split_axis=0, concat_axis=0, tiled=True)]
    ppermute x11, waiting for transfers between devices: 0.03 us -> 4.6 us  [swap(): return lax.ppermute(value, 'core', [(0, 1), (1, 0)])]
    ppermute x8, waiting for transfers between devices: 33.6 us -> 29.8 us  [shift(): lax.ppermute(value, ('ylo', 'yhi'), [(where(y), where((y + by) % 4)) for...]
    unnamed x32 -> x26, local copies, waits for them, and re-layouts: 8.84 us -> 7.01 us
  transfers between devices with their start and end apart: 31 -> 30, of which waited for: 9 -> 11; matrix products, arithmetic and copies ran while one was open for 6% -> 7% of each run, Pallas kernels for 11% -> 10%
where the time goes in v11:
time: 257 us; the launch traced here: 256 us
  waiting for transfers between devices  75.9 us (30%)
  Pallas kernels  51.3 us (20%)
  blocking collectives  49.5 us (19%)
  starting transfers between devices  33.9 us (13%)
  local copies, waits for them, and re-layouts  23.9 us (9%)
  between operations  15 us (6%)
  other arithmetic  6.07 us (2%)
    all_to_all x1, blocking collectives, shards(): lax.all_to_all(hidden, SEQ, split_axis=0, concat_axis=0, tiled=True)  35.5 us
    ppermute x8, waiting for transfers between devices, shift(): lax.ppermute(value, ('ylo', 'yhi'), [(where(y), where((y + by) % 4)) for...  29.8 us
    ppermute x8, waiting for transfers between devices, shift(): return lax.ppermute(value, axis, [(i, (i + by) % 4) for i in range(4)])  29.1 us
    pallas_call x1, Pallas kernels, row_layer(): pl.pallas_call(row_kernel, out_shape=[shape, shape], in_specs=[pl.BlockSp...  24.1 us
    pallas_call x1, Pallas kernels, column_layer(): pl.pallas_call(column_kernel, out_shape=jax.ShapeDtypeStruct((C, WIDTH),...  21.3 us
    all_gather x1, blocking collectives, row_weights(): rows = lax.all_gather(shard, 'z', axis=0)  14.1 us
    ppermute x8, starting transfers between devices, shift(): lax.ppermute(value, ('ylo', 'yhi'), [(where(y), where((y + by) % 4)) for...  13.2 us
    ppermute x8, starting transfers between devices, shift(): return lax.ppermute(value, axis, [(i, (i + by) % 4) for i in range(4)])  13.2 us
  transfers between devices with their start and end apart: 30, of which 11 were waited for; matrix products, arithmetic and copies ran while one was open for 7% of the time, Pallas kernels for 10%

profile of v11, /device:TPU:0, one launch (start us, length us, event | category | flops | bytes accessed | tf_op | source)
XLA Modules:
  0.0 255.7 jit_solution(14873802829215246883)
XLA Ops:
  6.5 0.7 fusion.10
  7.3 0.9 reshape.98
  8.4 0.7 maximum_maximum_fusion
  9.2 0.7 fusion.11
  9.9 0.9 reshape.93
  11.1 14.1 %all-gather = bf16[64,4096]{1,0:T(8,128)(2,1)S(1)} all-gather(bf16[16,4096]{1,0:T(8,128)(2,1)S(1)} %maximum_maximum_fusion.1), channel_id=2, replica_groups=mesh['ylo'=2,'core'=2,'x'=4,'yhi'=2,'z'=4] {'z'}, dimensions={0}, use_global_device_ids=true | all-gather | bytes 655360 | tf_op jit(solution)/shard_map/all_gather | solution.py:396
  25.3 1.6 collective-permute-start.4
  26.9 1.7 collective-permute-start.5
  28.6 1.6 collective-permute-start
  30.2 1.7 collective-permute-start.1
  31.9 14.4 %collective-permute-done.4 = bf16[2,32,2048]{2,1,0:T(8,128)(2,1)S(1)} collective-permute-done((bf16[2,32,2048]{2,1,0:T(8,128)(2,1)S(1)}, bf16[2,32,2048]{2,1,0:T(8,128)(2,1)S(1)}, u32[]{:S(2)}, u32[]{:S(2)}) %collective-permute-start.4) | collective-permute-done | bytes 262176 | tf_op jit(solution)/shard_map/ppermute | solution.py:366
  46.5 3.3 %collective-permute-start.7 = (bf16[2,32,1024]{2,1,0:T(8,128)(2,1)S(1)}, bf16[2,32,1024]{2,1,0:T(8,128)(2,1)S(1)}, u32[]{:S(2)}, u32[]{:S(2)}) collective-permute-start(bf16[2,32,1024]{2,1,0:T(8,128)(2,1)S(1)} %slice.101), channel_id=1, source_target_pairs={{0,68},{64,0},{4,64},{68,4},{1,69},{65,1},{5,65},{69,5},{2,70},{66... | collective-permute-start | bytes 393224 | tf_op jit(solution)/shard_map/ppermute | solution.py:366
  49.8 1.6 collective-permute-start.2
  51.4 1.8 collective-permute-start.3
  53.2 2.8 %collective-permute-done.2 = bf16[2,32,1024]{2,1,0:T(8,128)(2,1)S(1)} collective-permute-done((bf16[2,32,1024]{2,1,0:T(8,128)(2,1)S(1)}, bf16[2,32,1024]{2,1,0:T(8,128)(2,1)S(1)}, u32[]{:S(2)}, u32[]{:S(2)}) %collective-permute-start.2) | collective-permute-done | bytes 131104 | tf_op jit(solution)/shard_map/ppermute | solution.py:367
  56.0 0.4 collective-permute-done.3
  56.4 1.1 pad_maximum_fusion.1.refs_5_
  57.5 0.1 pad_maximum_fusion.refs_0_
  57.7 2.1 slice.83
  59.9 0.7 fusion.12
  61.9 0.7 constant_dynamic-slice_fusion
  62.5 3.2 %collective-permute-start.9 = (bf16[4,2,32,2048]{3,2,1,0:T(8,128)(2,1)S(1)}, bf16[4,2,32,2048]{3,2,1,0:T(8,128)(2,1)}, u32[]{:S(2)}, u32[]{:S(2)}) collective-permute-start(bf16[4,2,32,2048]{3,2,1,0:T(8,128)(2,1)S(1)} %pad_maximum_fusion.refs_0_), channel_id=1, source_target_pairs={{0,68},{64,0},{4,64},{68,4},{1,69},{65,1},{5,65},{69,5},{2,70},{66... | collective-permute-start | bytes 3145736 | tf_op jit(solution)/shard_map/ppermute | solution.py:366
  65.7 0.6 add_convert_fusion.1
  66.4 1.5 collective-permute-start.12
  67.9 1.8 collective-permute-start.13
  69.7 13.1 %collective-permute-done.8.refs_1_ = bf16[4,2,32,2048]{3,2,1,0:T(8,128)(2,1)} collective-permute-done((bf16[4,2,32,2048]{3,2,1,0:T(8,128)(2,1)S(1)}, bf16[4,2,32,2048]{3,2,1,0:T(8,128)(2,1)}, u32[]{:S(2)}, u32[]{:S(2)}) %collective-permute-start.8) | collective-permute-done | bytes 1048608 | tf_op jit(solution)/shard_map/ppermute | solution.py:366
  82.8 2.1 shard_map.91.hid_ref
  85.0 1.9 fusion.4
  86.9 0.2 pad_maximum_fusion.4
  87.1 1.0 pad_maximum_fusion.6
  88.2 0.6 collective-permute-start.17
  88.8 1.1 slice.102
  89.8 1.1 slice.103
  90.9 6.5 %collective-permute-done.12.refs_6_ = bf16[4,2,32,2048]{3,2,1,0:T(8,128)(2,1)} collective-permute-done((bf16[4,2,32,2048]{3,2,1,0:T(8,128)(2,1)}, bf16[4,2,32,2048]{3,2,1,0:T(8,128)(2,1)}, u32[]{:S(2)}, u32[]{:S(2)}) %collective-permute-start.12) | collective-permute-done | bytes 1048608 | tf_op jit(solution)/shard_map/ppermute | solution.py:367
  97.4 1.2 slice.104
  98.7 3.3 %collective-permute-start.11 = (bf16[4,2,32,1024]{3,2,1,0:T(8,128)(2,1)S(1)}, bf16[4,2,32,1024]{3,2,1,0:T(8,128)(2,1)S(1)}, u32[]{:S(2)}, u32[]{:S(2)}) collective-permute-start(bf16[4,2,32,1024]{3,2,1,0:T(8,128)(2,1)S(1)} %slice.103), channel_id=1, source_target_pairs={{0,68},{64,0},{4,64},{68,4},{1,69},{65,1},{5,65},{69,5},{2,70},{66... | collective-permute-start | bytes 1572872 | tf_op jit(solution)/shard_map/ppermute | solution.py:366
  102.0 1.1 slice.105
  103.1 0.1 collective-permute-start.14
  103.2 3.2 %collective-permute-start.15 = (bf16[4,2,32,1024]{3,2,1,0:T(8,128)(2,1)S(1)}, bf16[4,2,32,1024]{3,2,1,0:T(8,128)(2,1)}, u32[]{:S(2)}, u32[]{:S(2)}) collective-permute-start(bf16[4,2,32,1024]{3,2,1,0:T(8,128)(2,1)S(1)} %slice.105), channel_id=1, source_target_pairs={{0,24},{8,0},{16,8},{24,16},{1,25},{9,1},{17,9},{25,17},{2,26},{10... | collective-permute-start | bytes 1572872 | tf_op jit(solution)/shard_map/ppermute | solution.py:367
  106.4 1.4 collective-permute-done.10.refs_3_
  107.8 0.9 collective-permute-done.11.refs_4_
  108.7 19.4 %collective-permute-done.14.refs_8_ = bf16[4,2,32,1024]{3,2,1,0:T(8,128)(2,1)S(1)} collective-permute-done((bf16[4,2,32,1024]{3,2,1,0:T(8,128)(2,1)S(1)}, bf16[4,2,32,1024]{3,2,1,0:T(8,128)(2,1)S(1)}, u32[]{:S(2)}, u32[]{:S(2)}) %collective-permute-start.14) | collective-permute-done | bytes 524320 | tf_op jit(solution)/shard_map/ppermute | solution.py:367
  128.1 0.5 collective-permute-start.22
  128.7 0.9 copy-done.5
  129.6 0.3 collective-permute-start.24
  130.0 0.8 copy-done.7
  130.8 0.2 collective-permute-start.25
  131.0 2.9 %collective-permute-done.24.refs_18_ = bf16[4,2,32,1024]{3,2,1,0:T(8,128)(2,1)} collective-permute-done((bf16[4,2,32,1024]{3,2,1,0:T(8,128)(2,1)S(1)}, bf16[4,2,32,1024]{3,2,1,0:T(8,128)(2,1)}, u32[]{:S(2)}, u32[]{:S(2)}) %collective-permute-start.24) | collective-permute-done | bytes 524320 | tf_op jit(solution)/shard_map/ppermute | solution.py:383
  133.9 1.7 collective-permute-done.25.refs_19_
  135.7 1.0 copy-done.6
  136.7 1.0 copy-done.8
  137.7 24.1 %shard_map.92 = (bf16[512,2048]{1,0:T(8,128)(2,1)}, bf16[512,2048]{1,0:T(8,128)(2,1)}) custom-call(s32[3]{0:T(128)S(1)} %pad_add_fusion.place_ref, bf16[512,2048]{1,0:T(8,128)(2,1)} %bitcast.61, bf16[512,2048]{1,0:T(8,128)(2,1)} %copy-done.3, f32[1,2048]{1,0:T(1,128)S(1)} %bitcast.64, f32[512,128]{1,0:T(8,128)S(1)} %get-tuple-element.21.cos_ref, ...), custom_call_target="tpu_custom_call" | custom-call | flops 9663676416 | bytes 25165824 | tf_op jit(solution)/shard_map/pallas_call | solution.py:212
  161.9 0.2 collective-permute-start.26
  162.1 35.5 %all_to_all.22 = bf16[32,16,2048]{2,1,0:T(8,128)(2,1)} all-to-all(bf16[32,16,2048]{2,1,0:T(8,128)(2,1)} %bitcast.67), channel_id=1, replica_groups=mesh['ylo'=2,'core'=2,'x'=4,'yhi'=2,'z'=4] {'x','yhi','z'}, dimensions={0} | all-to-all | bytes 4194304 | tf_op jit(solution)/shard_map/all_to_all | solution.py:453
  197.6 21.3 %shard_map.93 = bf16[512,1024]{1,0:T(8,128)(2,1)} custom-call(s32[1]{0:T(128)} %bitcast.core_ref, bf16[512,2048]{1,0:T(8,128)(2,1)} %bitcast.68, f32[512,128]{1,0:T(8,128)} %get-tuple-element.27.cos_ref, f32[512,128]{1,0:T(8,128)} %get-tuple-element.28.sin_ref, bf16[4,4,2,2,16,4096]{5,4,3,2,1,0:T(8,128)(2,1)} %bitcast.78, ...), custom_call_target="tpu_custom_call" | custom-call | flops 7516192768 | bytes 15728640 | tf_op jit(solution)/shard_map/pallas_call | solution.py:301
  218.9 5.4 %all-to-all-start.1 = ((bf16[32,16,1024]{2,1,0:T(8,128)(2,1)}), bf16[32,16,1024]{2,1,0:T(8,128)(2,1)S(1)}, u32[]{:S(2)}, u32[]{:S(2)}) async-start(bf16[32,16,1024]{2,1,0:T(8,128)(2,1)} %bitcast.70), calls=%async_computation.1 | async-start | bytes 2097152 | tf_op jit(solution)/shard_map/all_to_all | solution.py:455
  224.3 1.8 slice_bitcast_fusion.1
  226.1 0.2 copy.18
  226.3 1.8 slice_bitcast_fusion
  228.1 1.5 copy.19
  229.5 12.3 %all-to-all-done.1 = bf16[32,16,1024]{2,1,0:T(8,128)(2,1)S(1)} async-done(((bf16[32,16,1024]{2,1,0:T(8,128)(2,1)}), bf16[32,16,1024]{2,1,0:T(8,128)(2,1)S(1)}, u32[]{:S(2)}, u32[]{:S(2)}) %all-to-all-start.1) | async-done | bytes 1048608 | tf_op jit(solution)/shard_map/all_to_all | solution.py:455
  241.9 1.6 copy-done
  243.5 1.6 copy-done.1
  245.0 3.8 %shard_map.94 = bf16[512,2048]{1,0:T(8,128)(2,1)} custom-call(s32[1]{0:T(128)} %bitcast.core_ref, bf16[512,1024]{1,0:T(8,128)(2,1)S(1)} %bitcast.60, bf16[512,2048]{1,0:T(8,128)(2,1)S(1)} %bitcast.58, bf16[512,2048]{1,0:T(8,128)(2,1)S(1)} %bitcast.59, bf16[512,2048]{1,0:T(8,128)(2,1)S(1)} %copy-done.1), custom_call_target="tpu_custom_call" | custom-call | flops 2147483648 | bytes 9437184 | tf_op jit(solution)/shard_map/pallas_call | solution.py:340
  (74 shorter events, 1.3 us)
Async XLA Ops:
  6.5 51.2 %all-gather.6.cloned.1.call-start = ((), (), s32[]{:S(2)}) async-start(), calls=%async_computation.2 | async-start | bytes 1310720 | tf_op jit(solution)/shard_map/all_gather | solution.py:412
  9.1 152.8 %all-gather.8.cloned.1.call-start = ((), (), s32[]{:S(2)}) async-start(), calls=%async_computation.3 | async-start | bytes 8912896 | tf_op jit(solution)/shard_map/all_gather | solution.py:416
  25.3 21.1 %collective-permute-start.4 = (bf16[2,32,2048]{2,1,0:T(8,128)(2,1)S(1)}, bf16[2,32,2048]{2,1,0:T(8,128)(2,1)S(1)}, u32[]{:S(2)}, u32[]{:S(2)}) collective-permute-start(bf16[2,32,2048]{2,1,0:T(8,128)(2,1)S(1)} %get-tuple-element.34), channel_id=1, source_target_pairs={{0,64},{64,4},{4,68},{68,0},{1,65},{65,5},{5,69},{69,1},{2,66},{66... | collective-permute-start | bytes 786440 | tf_op jit(solution)/shard_map/ppermute | solution.py:366
  26.9 19.5 %collective-permute-start.5 = (bf16[2,32,2048]{2,1,0:T(8,128)(2,1)S(1)}, bf16[2,32,2048]{2,1,0:T(8,128)(2,1)S(1)}, u32[]{:S(2)}, u32[]{:S(2)}) collective-permute-start(bf16[2,32,2048]{2,1,0:T(8,128)(2,1)S(1)} %get-tuple-element.34), channel_id=1, source_target_pairs={{0,68},{64,0},{4,64},{68,4},{1,69},{65,1},{5,65},{69,5},{2,70},{66... | collective-permute-start | bytes 786440 | tf_op jit(solution)/shard_map/ppermute | solution.py:366
  28.6 21.1 %collective-permute-start = (bf16[2,32,2048]{2,1,0:T(8,128)(2,1)S(1)}, bf16[2,32,2048]{2,1,0:T(8,128)(2,1)S(1)}, u32[]{:S(2)}, u32[]{:S(2)}) collective-permute-start(bf16[2,32,2048]{2,1,0:T(8,128)(2,1)S(1)} %get-tuple-element.36), channel_id=1, source_target_pairs={{0,8},{8,16},{16,24},{24,0},{1,9},{9,17},{17,25},{25,1},{2,10},{10... | collective-permute-start | bytes 786440 | tf_op jit(solution)/shard_map/ppermute | solution.py:367
  30.2 21.2 %collective-permute-start.1 = (bf16[2,32,2048]{2,1,0:T(8,128)(2,1)S(1)}, bf16[2,32,2048]{2,1,0:T(8,128)(2,1)S(1)}, u32[]{:S(2)}, u32[]{:S(2)}) collective-permute-start(bf16[2,32,2048]{2,1,0:T(8,128)(2,1)S(1)} %get-tuple-element.36), channel_id=1, source_target_pairs={{0,24},{8,0},{16,8},{24,16},{1,25},{9,1},{17,9},{25,17},{2,26},{10... | collective-permute-start | bytes 786440 | tf_op jit(solution)/shard_map/ppermute | solution.py:367
  46.4 6.8 %collective-permute-start.6 = (bf16[2,32,1024]{2,1,0:T(8,128)(2,1)S(1)}, bf16[2,32,1024]{2,1,0:T(8,128)(2,1)S(1)}, u32[]{:S(2)}, u32[]{:S(2)}) collective-permute-start(bf16[2,32,1024]{2,1,0:T(8,128)(2,1)S(1)} %slice.100), channel_id=1, source_target_pairs={{0,64},{64,4},{4,68},{68,0},{1,65},{65,5},{5,69},{69,1},{2,66},{66... | collective-permute-start | bytes 393224 | tf_op jit(solution)/shard_map/ppermute | solution.py:366
  46.5 6.7 %collective-permute-start.7 = (bf16[2,32,1024]{2,1,0:T(8,128)(2,1)S(1)}, bf16[2,32,1024]{2,1,0:T(8,128)(2,1)S(1)}, u32[]{:S(2)}, u32[]{:S(2)}) collective-permute-start(bf16[2,32,1024]{2,1,0:T(8,128)(2,1)S(1)} %slice.101), channel_id=1, source_target_pairs={{0,68},{64,0},{4,64},{68,4},{1,69},{65,1},{5,65},{69,5},{2,70},{66... | collective-permute-start | bytes 393224 | tf_op jit(solution)/shard_map/ppermute | solution.py:366
  49.8 6.2 %collective-permute-start.2 = (bf16[2,32,1024]{2,1,0:T(8,128)(2,1)S(1)}, bf16[2,32,1024]{2,1,0:T(8,128)(2,1)S(1)}, u32[]{:S(2)}, u32[]{:S(2)}) collective-permute-start(bf16[2,32,1024]{2,1,0:T(8,128)(2,1)S(1)} %slice.96), channel_id=1, source_target_pairs={{0,8},{8,16},{16,24},{24,0},{1,9},{9,17},{17,25},{25,1},{2,10},{10... | collective-permute-start | bytes 393224 | tf_op jit(solution)/shard_map/ppermute | solution.py:367
  51.4 5.0 %collective-permute-start.3 = (bf16[2,32,1024]{2,1,0:T(8,128)(2,1)S(1)}, bf16[2,32,1024]{2,1,0:T(8,128)(2,1)S(1)}, u32[]{:S(2)}, u32[]{:S(2)}) collective-permute-start(bf16[2,32,1024]{2,1,0:T(8,128)(2,1)S(1)} %slice.97), channel_id=1, source_target_pairs={{0,24},{8,0},{16,8},{24,16},{1,25},{9,1},{17,9},{25,17},{2,26},{10... | collective-permute-start | bytes 393224 | tf_op jit(solution)/shard_map/ppermute | solution.py:367
  57.5 2.4 copy-start.10
  57.5 4.3 %copy-start.11 = (s32[1,32]{1,0:T(1,128)S(1)}, s32[1,32]{1,0:T(1,128)}, u32[]{:S(2)}) copy-start(s32[1,32]{1,0:T(1,128)} %param.16) | copy-start | bytes 388
  57.5 25.3 %copy-start.2 = (bf16[1,512,2048]{2,1,0:T(8,128)(2,1)S(1)}, bf16[1,512,2048]{2,1,0:T(8,128)(2,1)}, u32[]{:S(2)}) copy-start(bf16[1,512,2048]{2,1,0:T(8,128)(2,1)} %param.9) | copy-start | bytes 6291460
  57.5 25.3 %copy-start.4 = (f32[2048]{0:T(1024)S(1)}, f32[2048]{0:T(1024)}, u32[]{:S(2)}) copy-start(f32[2048]{0:T(1024)} %param.10) | copy-start | bytes 24580
  59.8 22.9 %collective-permute-start.8 = (bf16[4,2,32,2048]{3,2,1,0:T(8,128)(2,1)S(1)}, bf16[4,2,32,2048]{3,2,1,0:T(8,128)(2,1)}, u32[]{:S(2)}, u32[]{:S(2)}) collective-permute-start(bf16[4,2,32,2048]{3,2,1,0:T(8,128)(2,1)S(1)} %pad_maximum_fusion.refs_0_), channel_id=1, source_target_pairs={{0,64},{64,4},{4,68},{68,0},{1,65},{65,5},{5,69},{69,1},{2,66},{66... | collective-permute-start | bytes 3145736 | tf_op jit(solution)/shard_map/ppermute | solution.py:366
  62.5 25.7 %collective-permute-start.9 = (bf16[4,2,32,2048]{3,2,1,0:T(8,128)(2,1)S(1)}, bf16[4,2,32,2048]{3,2,1,0:T(8,128)(2,1)}, u32[]{:S(2)}, u32[]{:S(2)}) collective-permute-start(bf16[4,2,32,2048]{3,2,1,0:T(8,128)(2,1)S(1)} %pad_maximum_fusion.refs_0_), channel_id=1, source_target_pairs={{0,68},{64,0},{4,64},{68,4},{1,69},{65,1},{5,65},{69,5},{2,70},{66... | collective-permute-start | bytes 3145736 | tf_op jit(solution)/shard_map/ppermute | solution.py:366
  66.4 31.0 %collective-permute-start.12 = (bf16[4,2,32,2048]{3,2,1,0:T(8,128)(2,1)}, bf16[4,2,32,2048]{3,2,1,0:T(8,128)(2,1)}, u32[]{:S(2)}, u32[]{:S(2)}) collective-permute-start(bf16[4,2,32,2048]{3,2,1,0:T(8,128)(2,1)} %pad_maximum_fusion.1.refs_5_), channel_id=1, source_target_pairs={{0,8},{8,16},{16,24},{24,0},{1,9},{9,17},{17,25},{25,1},{2,10},{10... | collective-permute-start | bytes 3145736 | tf_op jit(solution)/shard_map/ppermute | solution.py:367
  67.9 30.7 %collective-permute-start.13 = (bf16[4,2,32,2048]{3,2,1,0:T(8,128)(2,1)}, bf16[4,2,32,2048]{3,2,1,0:T(8,128)(2,1)}, u32[]{:S(2)}, u32[]{:S(2)}) collective-permute-start(bf16[4,2,32,2048]{3,2,1,0:T(8,128)(2,1)} %pad_maximum_fusion.1.refs_5_), channel_id=1, source_target_pairs={{0,24},{8,0},{16,8},{24,16},{1,25},{9,1},{17,9},{25,17},{2,26},{10... | collective-permute-start | bytes 3145736 | tf_op jit(solution)/shard_map/ppermute | solution.py:367
  69.7 33.4 %collective-permute-start.16 = (bf16[4,2,32,2048]{3,2,1,0:T(8,128)(2,1)S(1)}, bf16[4,2,32,2048]{3,2,1,0:T(8,128)(2,1)}, u32[]{:S(2)}, u32[]{:S(2)}) collective-permute-start(bf16[4,2,32,2048]{3,2,1,0:T(8,128)(2,1)S(1)} %pad_maximum_fusion.refs_0_), channel_id=1, source_target_pairs={{0,32},{32,0},{1,33},{33,1},{2,34},{34,2},{3,35},{35,3},{4,36},{36... | collective-permute-start | bytes 3145736 | tf_op jit(solution)/shard_map/ppermute | solution.py:383
  82.7 20.5 %collective-permute-start.21 = (bf16[4,2,32,2048]{3,2,1,0:T(8,128)(2,1)}, bf16[4,2,32,2048]{3,2,1,0:T(8,128)(2,1)}, u32[]{:S(2)}, u32[]{:S(2)}) collective-permute-start(bf16[4,2,32,2048]{3,2,1,0:T(8,128)(2,1)} %pad_maximum_fusion.1.refs_5_), channel_id=1, source_target_pairs={{0,32},{32,0},{1,33},{33,1},{2,34},{34,2},{3,35},{35,3},{4,36},{36... | collective-permute-start | bytes 3145736 | tf_op jit(solution)/shard_map/ppermute | solution.py:383
  85.0 3.2 %copy-start.3 = (bf16[512,2048]{1,0:T(8,128)(2,1)}, bf16[512,2048]{1,0:T(8,128)(2,1)S(1)}, u32[]{:S(2)}) copy-start(bf16[512,2048]{1,0:T(8,128)(2,1)S(1)} %shard_map.91.hid_ref) | copy-start | bytes 6291460
  88.2 47.5 %copy-start.9 = (f32[2048]{0:T(1024)S(1)}, f32[2048]{0:T(1024)}, u32[]{:S(2)}) copy-start(f32[2048]{0:T(1024)} %param.13) | copy-start | bytes 24580
  88.2 40.5 %collective-permute-start.17 = (bf16[4,2,32,2048]{3,2,1,0:T(8,128)(2,1)}, bf16[4,2,32,2048]{3,2,1,0:T(8,128)(2,1)S(1)}, u32[]{:S(2)}, u32[]{:S(2)}) collective-permute-start(bf16[4,2,32,2048]{3,2,1,0:T(8,128)(2,1)} %collective-permute-done.8.refs_1_), channel_id=1, source_target_pairs={{0,32},{32,0},{1,33},{33,1},{2,34},{34,2},{3,35},{35,3},{4,36},{36... | collective-permute-start | bytes 3145736 | tf_op jit(solution)/shard_map/ppermute | solution.py:383
  97.4 10.4 %collective-permute-start.10 = (bf16[4,2,32,1024]{3,2,1,0:T(8,128)(2,1)S(1)}, bf16[4,2,32,1024]{3,2,1,0:T(8,128)(2,1)S(1)}, u32[]{:S(2)}, u32[]{:S(2)}) collective-permute-start(bf16[4,2,32,1024]{3,2,1,0:T(8,128)(2,1)S(1)} %slice.102), channel_id=1, source_target_pairs={{0,64},{64,4},{4,68},{68,0},{1,65},{65,5},{5,69},{69,1},{2,66},{66... | collective-permute-start | bytes 1572872 | tf_op jit(solution)/shard_map/ppermute | solution.py:366
  98.7 10.0 %collective-permute-start.11 = (bf16[4,2,32,1024]{3,2,1,0:T(8,128)(2,1)S(1)}, bf16[4,2,32,1024]{3,2,1,0:T(8,128)(2,1)S(1)}, u32[]{:S(2)}, u32[]{:S(2)}) collective-permute-start(bf16[4,2,32,1024]{3,2,1,0:T(8,128)(2,1)S(1)} %slice.103), channel_id=1, source_target_pairs={{0,68},{64,0},{4,64},{68,4},{1,69},{65,1},{5,65},{69,5},{2,70},{66... | collective-permute-start | bytes 1572872 | tf_op jit(solution)/shard_map/ppermute | solution.py:366
  103.1 25.0 %collective-permute-start.14 = (bf16[4,2,32,1024]{3,2,1,0:T(8,128)(2,1)S(1)}, bf16[4,2,32,1024]{3,2,1,0:T(8,128)(2,1)S(1)}, u32[]{:S(2)}, u32[]{:S(2)}) collective-permute-start(bf16[4,2,32,1024]{3,2,1,0:T(8,128)(2,1)S(1)} %slice.104), channel_id=1, source_target_pairs={{0,8},{8,16},{16,24},{24,0},{1,9},{9,17},{17,25},{25,1},{2,10},{10... | collective-permute-start | bytes 1572872 | tf_op jit(solution)/shard_map/ppermute | solution.py:367
  103.2 24.9 %collective-permute-start.15 = (bf16[4,2,32,1024]{3,2,1,0:T(8,128)(2,1)S(1)}, bf16[4,2,32,1024]{3,2,1,0:T(8,128)(2,1)}, u32[]{:S(2)}, u32[]{:S(2)}) collective-permute-start(bf16[4,2,32,1024]{3,2,1,0:T(8,128)(2,1)S(1)} %slice.105), channel_id=1, source_target_pairs={{0,24},{8,0},{16,8},{24,16},{1,25},{9,1},{17,9},{25,17},{2,26},{10... | collective-permute-start | bytes 1572872 | tf_op jit(solution)/shard_map/ppermute | solution.py:367
  107.8 20.9 %collective-permute-start.19 = (bf16[4,2,32,1024]{3,2,1,0:T(8,128)(2,1)S(1)}, bf16[4,2,32,1024]{3,2,1,0:T(8,128)(2,1)S(1)}, u32[]{:S(2)}, u32[]{:S(2)}) collective-permute-start(bf16[4,2,32,1024]{3,2,1,0:T(8,128)(2,1)S(1)} %collective-permute-done.10.refs_3_), channel_id=1, source_target_pairs={{0,32},{32,0},{1,33},{33,1},{2,34},{34,2},{3,35},{35,3},{4,36},{36... | collective-permute-start | bytes 1572872 | tf_op jit(solution)/shard_map/ppermute | solution.py:383
  108.7 21.3 %collective-permute-start.20 = (bf16[4,2,32,1024]{3,2,1,0:T(8,128)(2,1)S(1)}, bf16[4,2,32,1024]{3,2,1,0:T(8,128)(2,1)S(1)}, u32[]{:S(2)}, u32[]{:S(2)}) collective-permute-start(bf16[4,2,32,1024]{3,2,1,0:T(8,128)(2,1)S(1)} %collective-permute-done.11.refs_4_), channel_id=1, source_target_pairs={{0,32},{32,0},{1,33},{33,1},{2,34},{34,2},{3,35},{35,3},{4,36},{36... | collective-permute-start | bytes 1572872 | tf_op jit(solution)/shard_map/ppermute | solution.py:383
  128.1 7.5 %collective-permute-start.18 = (bf16[4,2,32,2048]{3,2,1,0:T(8,128)(2,1)}, bf16[4,2,32,2048]{3,2,1,0:T(8,128)(2,1)}, u32[]{:S(2)}, u32[]{:S(2)}) collective-permute-start(bf16[4,2,32,2048]{3,2,1,0:T(8,128)(2,1)} %collective-permute-done.9.refs_2_), channel_id=1, source_target_pairs={{0,32},{32,0},{1,33},{33,1},{2,34},{34,2},{3,35},{35,3},{4,36},{36... | collective-permute-start | bytes 3145736 | tf_op jit(solution)/shard_map/ppermute | solution.py:383
  128.1 7.5 %collective-permute-start.22 = (bf16[4,2,32,2048]{3,2,1,0:T(8,128)(2,1)}, bf16[4,2,32,2048]{3,2,1,0:T(8,128)(2,1)}, u32[]{:S(2)}, u32[]{:S(2)}) collective-permute-start(bf16[4,2,32,2048]{3,2,1,0:T(8,128)(2,1)} %collective-permute-done.12.refs_6_), channel_id=1, source_target_pairs={{0,32},{32,0},{1,33},{33,1},{2,34},{34,2},{3,35},{35,3},{4,36},{36... | collective-permute-start | bytes 3145736 | tf_op jit(solution)/shard_map/ppermute | solution.py:383
  128.6 1.3 copy-start.12
  128.6 7.0 %collective-permute-start.23 = (bf16[4,2,32,2048]{3,2,1,0:T(8,128)(2,1)}, bf16[4,2,32,2048]{3,2,1,0:T(8,128)(2,1)}, u32[]{:S(2)}, u32[]{:S(2)}) collective-permute-start(bf16[4,2,32,2048]{3,2,1,0:T(8,128)(2,1)} %collective-permute-done.13.refs_7_), channel_id=1, source_target_pairs={{0,32},{32,0},{1,33},{33,1},{2,34},{34,2},{3,35},{35,3},{4,36},{36... | collective-permute-start | bytes 3145736 | tf_op jit(solution)/shard_map/ppermute | solution.py:383
  128.7 0.9 copy-start.5
  129.6 4.3 %collective-permute-start.24 = (bf16[4,2,32,1024]{3,2,1,0:T(8,128)(2,1)S(1)}, bf16[4,2,32,1024]{3,2,1,0:T(8,128)(2,1)}, u32[]{:S(2)}, u32[]{:S(2)}) collective-permute-start(bf16[4,2,32,1024]{3,2,1,0:T(8,128)(2,1)S(1)} %collective-permute-done.14.refs_8_), channel_id=1, source_target_pairs={{0,32},{32,0},{1,33},{33,1},{2,34},{34,2},{3,35},{35,3},{4,36},{36... | collective-permute-start | bytes 1572872 | tf_op jit(solution)/shard_map/ppermute | solution.py:383
  130.0 0.8 copy-start.7
  130.8 4.8 %collective-permute-start.25 = (bf16[4,2,32,1024]{3,2,1,0:T(8,128)(2,1)}, bf16[4,2,32,1024]{3,2,1,0:T(8,128)(2,1)}, u32[]{:S(2)}, u32[]{:S(2)}) collective-permute-start(bf16[4,2,32,1024]{3,2,1,0:T(8,128)(2,1)} %collective-permute-done.15.refs_9_), channel_id=1, source_target_pairs={{0,32},{32,0},{1,33},{33,1},{2,34},{34,2},{3,35},{35,3},{4,36},{36... | collective-permute-start | bytes 1572872 | tf_op jit(solution)/shard_map/ppermute | solution.py:383
  135.6 1.1 copy-start.6
  136.7 1.0 copy-start.8
  161.9 35.7 %collective-permute-start.26 = (bf16[4,4,2,2,16,4096]{5,4,3,2,1,0:T(8,128)(2,1)}, bf16[4,4,2,2,16,4096]{5,4,3,2,1,0:T(8,128)(2,1)}, u32[]{:S(2)}, u32[]{:S(2)}) collective-permute-start(bf16[4,4,2,2,16,4096]{5,4,3,2,1,0:T(8,128)(2,1)} %bitcast.77), channel_id=1, source_target_pairs={{0,32},{32,0},{1,33},{33,1},{2,34},{34,2},{3,35},{35,3},{4,36},{36... | collective-permute-start | bytes 25165832 | tf_op jit(solution)/shard_map/ppermute | solution.py:383
  218.9 23.0 %all-to-all-start.1 = ((bf16[32,16,1024]{2,1,0:T(8,128)(2,1)}), bf16[32,16,1024]{2,1,0:T(8,128)(2,1)S(1)}, u32[]{:S(2)}, u32[]{:S(2)}) async-start(bf16[32,16,1024]{2,1,0:T(8,128)(2,1)} %bitcast.70), calls=%async_computation.1 | async-start | bytes 2097152 | tf_op jit(solution)/shard_map/all_to_all | solution.py:455
  241.9 1.6 copy-start
  243.5 1.6 copy-start.1
Sparse Core Ops, SparseCore 0:
  9.3 38.7 all-gather.5
  59.9 86.6 all-gather.7

commit v12 on v9

--- a/solution.py
+++ b/solution.py
@@ -447,10 +447,9 @@
 
     hidden = normed_slots(core_scalar, residual, gain_first.reshape(1, D))
 
-    line = column_line(inputs_second, output_second)
-    inputs_first, output_first, line = lax.optimization_barrier((inputs_first, output_first, line))
-    plane = column_plane(line)
     own_stack = row_stack(inputs_first, output_first)
+    inputs_second, output_second, own_stack = lax.optimization_barrier((inputs_second, output_second, own_stack))
+    plane = column_plane(column_line(inputs_second, output_second))
     pieces = forwards(first_hops(own_stack, "y"), "y")
     own_stack, hidden, row_tables, column_tables = lax.optimization_barrier(
         (own_stack, hidden, row_tables, column_tables)

time: 263 us -> 254 us (0.966)
  waiting for transfers between devices: 87.1 us -> 78.8 us
    ppermute x4, waiting for transfers between devices: 26.9 us -> 14.5 us  [shift(): return lax.ppermute(value, axis, [(i, (i + by) % 4) for i in range(4)])]
    ppermute x4, waiting for transfers between devices: 44.5 us -> 48.3 us  [shift(): lax.ppermute(value, ('ylo', 'yhi'), [(where(y), where((y + by) % 4)) for...]
  transfers between devices with their start and end apart: 16 -> 16, of which waited for: 9 -> 8; matrix products, arithmetic and copies ran while one was open for 6% -> 5% of each run, Pallas kernels for 10% -> 11%
where the time goes in v12:
time: 254 us; the launch traced here: 253 us
  waiting for transfers between devices  78.8 us (31%)
  blocking collectives  67.3 us (26%)
  Pallas kernels  51.9 us (20%)
  starting transfers between devices  19.7 us (8%)
  between operations  15 us (6%)
  local copies, waits for them, and re-layouts  14.5 us (6%)
  other arithmetic  5.71 us (2%)
    ppermute x4, waiting for transfers between devices, shift(): lax.ppermute(value, ('ylo', 'yhi'), [(where(y), where((y + by) % 4)) for...  48.3 us
    all_to_all x1, blocking collectives, shards(): lax.all_to_all(hidden, SEQ, split_axis=0, concat_axis=0, tiled=True)  36.1 us
    pallas_call x1, Pallas kernels, row_layer(): pl.pallas_call(row_kernel, out_shape=[shape, shape], in_specs=[pl.BlockSp...  24.6 us
    pallas_call x1, Pallas kernels, column_layer(): pl.pallas_call(column_kernel, out_shape=jax.ShapeDtypeStruct((C, WIDTH),...  21.4 us
    all_gather x1, blocking collectives, column_line(): return lax.all_gather(shard, ('ylo', 'yhi'), axis=0)  17.2 us
    ppermute x4, waiting for transfers between devices, shift(): return lax.ppermute(value, axis, [(i, (i + by) % 4) for i in range(4)])  14.5 us
    all_gather x1, blocking collectives, row_stack(): rows = lax.all_gather(shard, 'z', axis=0)  14.1 us
    all_to_all x1, waiting for transfers between devices, shards(): lax.all_to_all(attended, SEQ, split_axis=0, concat_axis=0, tiled=True)  12.4 us
  transfers between devices with their start and end apart: 16, of which 8 were waited for; matrix products, arithmetic and copies ran while one was open for 5% of the time, Pallas kernels for 11%

profile of v12, /device:TPU:0, one launch (start us, length us, event | category | flops | bytes accessed | tf_op | source)
XLA Modules:
  0.0 252.9 jit_solution(15657107154972760647)
XLA Ops:
  6.5 0.7 fusion.8
  7.3 0.9 reshape.93
  8.2 0.1 copy.24
  8.3 0.1 reshape.94
  8.4 14.1 %all-gather = bf16[64,4096]{1,0:T(8,128)(2,1)S(1)} all-gather(bf16[16,4096]{1,0:T(8,128)(2,1)S(1)} %maximum_maximum_fusion), channel_id=2, replica_groups=mesh['ylo'=2,'core'=2,'x'=4,'yhi'=2,'z'=4] {'z'}, dimensions={0}, use_global_device_ids=true | all-gather | bytes 655360 | tf_op jit(solution)/shard_map/all_gather | solution.py:412
  22.5 0.1 fusion.6
  22.6 1.6 collective-permute-start
  24.2 1.7 collective-permute-start.1
  25.9 10.2 %collective-permute-done = bf16[2,32,4096]{2,1,0:T(8,128)(2,1)S(1)} collective-permute-done((bf16[2,32,4096]{2,1,0:T(8,128)(2,1)S(1)}, bf16[2,32,4096]{2,1,0:T(8,128)(2,1)S(1)}, u32[]{:S(2)}, u32[]{:S(2)}) %collective-permute-start) | collective-permute-done | bytes 524320 | tf_op jit(solution)/shard_map/ppermute | solution.py:380
  36.1 0.3 collective-permute-start.2
  36.5 0.0 collective-permute-done.1
  36.5 3.0 %collective-permute-start.3 = (bf16[2,32,2048]{2,1,0:T(8,128)(2,1)S(1)}, bf16[2,32,2048]{2,1,0:T(8,128)(2,1)S(1)}, u32[]{:S(2)}, u32[]{:S(2)}) collective-permute-start(bf16[2,32,2048]{2,1,0:T(8,128)(2,1)S(1)} %slice.59), channel_id=1, source_target_pairs={{0,24},{8,0},{16,8},{24,16},{1,25},{9,1},{17,9},{25,17},{2,26},{10... | collective-permute-start | bytes 786440 | tf_op jit(solution)/shard_map/ppermute | solution.py:380
  39.5 4.3 %collective-permute-done.2 = bf16[2,32,2048]{2,1,0:T(8,128)(2,1)S(1)} collective-permute-done((bf16[2,32,2048]{2,1,0:T(8,128)(2,1)S(1)}, bf16[2,32,2048]{2,1,0:T(8,128)(2,1)S(1)}, u32[]{:S(2)}, u32[]{:S(2)}) %collective-permute-start.2) | collective-permute-done | bytes 262176 | tf_op jit(solution)/shard_map/ppermute | solution.py:380
  43.8 0.0 collective-permute-done.3
  43.8 0.0 copy-start.7
  43.9 0.0 copy-start.6
  43.9 1.6 pad_maximum_fusion.refs_0_
  45.5 0.0 copy-start.4
  45.6 0.1 copy.23
  45.7 0.1 reshape.99
  45.8 17.2 %all-gather.1 = bf16[64,4096]{1,0:T(8,128)(2,1)} all-gather(bf16[16,4096]{1,0:T(8,128)(2,1)S(1)} %maximum_maximum_fusion.1), channel_id=3, replica_groups=mesh['ylo'=2,'core'=2,'x'=4,'yhi'=2,'z'=4] {'ylo','yhi'}, dimensions={0}, use_global_device_ids=true | all-gather | bytes 655360 | tf_op jit(solution)/shard_map/all_gather | solution.py:420
  63.0 0.0 all-gather.5.cloned.1.call-update
  63.0 0.3 collective-permute-start.4
  63.4 3.0 %collective-permute-start.5 = (bf16[4,2,32,4096]{3,2,1,0:T(8,128)(2,1)}, bf16[4,2,32,4096]{3,2,1,0:T(8,128)(2,1)}, u32[]{:S(2)}, u32[]{:S(2)}) collective-permute-start(bf16[4,2,32,4096]{3,2,1,0:T(8,128)(2,1)} %pad_maximum_fusion.refs_0_), channel_id=1, source_target_pairs={{0,68},{64,0},{4,64},{68,4},{1,69},{65,1},{5,65},{69,5},{2,70},{66... | collective-permute-start | bytes 6291464 | tf_op jit(solution)/shard_map/ppermute | solution.py:379
  66.3 0.6 constant_dynamic-slice_fusion
  66.9 0.1 add_convert_fusion
  67.0 0.1 convert_element_type.35
  67.1 0.6 fusion.9
  69.1 2.1 shard_map.91.hid_ref
  71.2 0.0 copy-start.3
  71.2 0.6 add_convert_fusion.1
  71.9 1.9 fusion.4
  73.8 0.2 pad_maximum_fusion.2
  74.0 1.0 pad_maximum_fusion.4
  75.0 0.0 collective-permute-start.8
  75.0 32.7 %collective-permute-done.4.refs_1_ = bf16[4,2,32,4096]{3,2,1,0:T(8,128)(2,1)} collective-permute-done((bf16[4,2,32,4096]{3,2,1,0:T(8,128)(2,1)}, bf16[4,2,32,4096]{3,2,1,0:T(8,128)(2,1)}, u32[]{:S(2)}, u32[]{:S(2)}) %collective-permute-start.4) | collective-permute-done | bytes 2097184 | tf_op jit(solution)/shard_map/ppermute | solution.py:379
  107.7 1.3 slice.60
  109.0 0.1 collective-permute-start.6
  109.1 0.0 collective-permute-done.5.refs_2_
  109.1 1.3 slice.61
  110.5 3.3 %collective-permute-start.7 = (bf16[4,2,32,2048]{3,2,1,0:T(8,128)(2,1)S(1)}, bf16[4,2,32,2048]{3,2,1,0:T(8,128)(2,1)S(1)}, u32[]{:S(2)}, u32[]{:S(2)}) collective-permute-start(bf16[4,2,32,2048]{3,2,1,0:T(8,128)(2,1)S(1)} %slice.61), channel_id=1, source_target_pairs={{0,68},{64,0},{4,64},{68,4},{1,69},{65,1},{5,65},{69,5},{2,70},{66... | collective-permute-start | bytes 3145736 | tf_op jit(solution)/shard_map/ppermute | solution.py:379
  113.8 0.5 collective-permute-start.9
  114.3 15.2 %collective-permute-done.6.refs_3_ = bf16[4,2,32,2048]{3,2,1,0:T(8,128)(2,1)S(1)} collective-permute-done((bf16[4,2,32,2048]{3,2,1,0:T(8,128)(2,1)S(1)}, bf16[4,2,32,2048]{3,2,1,0:T(8,128)(2,1)S(1)}, u32[]{:S(2)}, u32[]{:S(2)}) %collective-permute-start.6) | collective-permute-done | bytes 1048608 | tf_op jit(solution)/shard_map/ppermute | solution.py:379
  129.5 0.0 collective-permute-start.11
  129.5 0.4 collective-permute-done.7.refs_4_
  129.8 0.2 collective-permute-start.12
  130.0 0.1 pad_add_fusion.place_ref
  130.1 2.2 collective-permute-done.11.refs_8_
  132.3 1.5 collective-permute-done.12.refs_9_
  133.8 0.0 collective-permute-done.9.refs_6_
  133.8 24.6 %shard_map.92 = (bf16[512,2048]{1,0:T(8,128)(2,1)}, bf16[512,2048]{1,0:T(8,128)(2,1)}) custom-call(s32[3]{0:T(128)S(1)} %pad_add_fusion.place_ref, bf16[512,2048]{1,0:T(8,128)(2,1)} %bitcast.55, bf16[512,2048]{1,0:T(8,128)(2,1)} %copy-done.3, f32[1,2048]{1,0:T(1,128)S(1)} %bitcast.58, f32[512,128]{1,0:T(8,128)S(1)} %get-tuple-element.22.cos_ref, ...), custom_call_target="tpu_custom_call" | custom-call | flops 9663676416 | bytes 25165824 | tf_op jit(solution)/shard_map/pallas_call | solution.py:224
  158.4 0.0 all-gather.5.cloned.1.call-done
  158.4 0.2 collective-permute-start.13
  158.6 36.1 %all_to_all.22 = bf16[32,16,2048]{2,1,0:T(8,128)(2,1)} all-to-all(bf16[32,16,2048]{2,1,0:T(8,128)(2,1)} %bitcast.62), channel_id=1, replica_groups=mesh['ylo'=2,'core'=2,'x'=4,'yhi'=2,'z'=4] {'x','yhi','z'}, dimensions={0} | all-to-all | bytes 4194304 | tf_op jit(solution)/shard_map/all_to_all | solution.py:462
  194.7 21.4 %shard_map.93 = bf16[512,1024]{1,0:T(8,128)(2,1)} custom-call(s32[1]{0:T(128)} %bitcast.core_ref, bf16[512,2048]{1,0:T(8,128)(2,1)} %bitcast.63, f32[512,128]{1,0:T(8,128)} %get-tuple-element.27.cos_ref, f32[512,128]{1,0:T(8,128)} %get-tuple-element.28.sin_ref, bf16[4,4,2,2,16,4096]{5,4,3,2,1,0:T(8,128)(2,1)} %bitcast.71, ...), custom_call_target="tpu_custom_call" | custom-call | flops 7516192768 | bytes 15728640 | tf_op jit(solution)/shard_map/pallas_call | solution.py:314
  216.1 5.5 %all-to-all-start.1 = ((bf16[32,16,1024]{2,1,0:T(8,128)(2,1)}), bf16[32,16,1024]{2,1,0:T(8,128)(2,1)S(1)}, u32[]{:S(2)}, u32[]{:S(2)}) async-start(bf16[32,16,1024]{2,1,0:T(8,128)(2,1)} %bitcast.67), calls=%async_computation.1 | async-start | bytes 2097152 | tf_op jit(solution)/shard_map/all_to_all | solution.py:464
  221.5 1.8 slice_bitcast_fusion.1
  223.3 0.2 copy.18
  223.5 1.8 slice_bitcast_fusion
  225.3 1.5 copy.19
  226.8 12.4 %all-to-all-done.1 = bf16[32,16,1024]{2,1,0:T(8,128)(2,1)S(1)} async-done(((bf16[32,16,1024]{2,1,0:T(8,128)(2,1)}), bf16[32,16,1024]{2,1,0:T(8,128)(2,1)S(1)}, u32[]{:S(2)}, u32[]{:S(2)}) %all-to-all-start.1) | async-done | bytes 1048608 | tf_op jit(solution)/shard_map/all_to_all | solution.py:464
  239.1 1.6 copy-done
  240.7 1.6 copy-done.1
  242.3 3.8 %shard_map.94 = bf16[512,2048]{1,0:T(8,128)(2,1)} custom-call(s32[1]{0:T(128)} %bitcast.core_ref, bf16[512,1024]{1,0:T(8,128)(2,1)S(1)} %bitcast.54, bf16[512,2048]{1,0:T(8,128)(2,1)S(1)} %bitcast.52, bf16[512,2048]{1,0:T(8,128)(2,1)S(1)} %bitcast.53, bf16[512,2048]{1,0:T(8,128)(2,1)S(1)} %copy-done.1), custom_call_target="tpu_custom_call" | custom-call | flops 2147483648 | bytes 9437184 | tf_op jit(solution)/shard_map/pallas_call | solution.py:353
  (30 shorter events, 0.2 us)
Async XLA Ops:
  6.5 151.9 %all-gather.5.cloned.1.call-start = ((), (), s32[]{:S(2)}) async-start(), calls=%async_computation.2 | async-start | bytes 8912896 | tf_op jit(solution)/shard_map/all_gather | solution.py:424
  22.6 13.5 %collective-permute-start = (bf16[2,32,4096]{2,1,0:T(8,128)(2,1)S(1)}, bf16[2,32,4096]{2,1,0:T(8,128)(2,1)S(1)}, u32[]{:S(2)}, u32[]{:S(2)}) collective-permute-start(bf16[2,32,4096]{2,1,0:T(8,128)(2,1)S(1)} %get-tuple-element.32), channel_id=1, source_target_pairs={{0,8},{8,16},{16,24},{24,0},{1,9},{9,17},{17,25},{25,1},{2,10},{10... | collective-permute-start | bytes 1572872 | tf_op jit(solution)/shard_map/ppermute | solution.py:380
  24.2 12.3 %collective-permute-start.1 = (bf16[2,32,4096]{2,1,0:T(8,128)(2,1)S(1)}, bf16[2,32,4096]{2,1,0:T(8,128)(2,1)S(1)}, u32[]{:S(2)}, u32[]{:S(2)}) collective-permute-start(bf16[2,32,4096]{2,1,0:T(8,128)(2,1)S(1)} %get-tuple-element.32), channel_id=1, source_target_pairs={{0,24},{8,0},{16,8},{24,16},{1,25},{9,1},{17,9},{25,17},{2,26},{10... | collective-permute-start | bytes 1572872 | tf_op jit(solution)/shard_map/ppermute | solution.py:380
  36.1 7.7 %collective-permute-start.2 = (bf16[2,32,2048]{2,1,0:T(8,128)(2,1)S(1)}, bf16[2,32,2048]{2,1,0:T(8,128)(2,1)S(1)}, u32[]{:S(2)}, u32[]{:S(2)}) collective-permute-start(bf16[2,32,2048]{2,1,0:T(8,128)(2,1)S(1)} %slice.58), channel_id=1, source_target_pairs={{0,8},{8,16},{16,24},{24,0},{1,9},{9,17},{17,25},{25,1},{2,10},{10... | collective-permute-start | bytes 786440 | tf_op jit(solution)/shard_map/ppermute | solution.py:380
  36.5 7.3 %collective-permute-start.3 = (bf16[2,32,2048]{2,1,0:T(8,128)(2,1)S(1)}, bf16[2,32,2048]{2,1,0:T(8,128)(2,1)S(1)}, u32[]{:S(2)}, u32[]{:S(2)}) collective-permute-start(bf16[2,32,2048]{2,1,0:T(8,128)(2,1)S(1)} %slice.59), channel_id=1, source_target_pairs={{0,24},{8,0},{16,8},{24,16},{1,25},{9,1},{17,9},{25,17},{2,26},{10... | collective-permute-start | bytes 786440 | tf_op jit(solution)/shard_map/ppermute | solution.py:380
  43.8 1.7 copy-start.7
  43.9 1.7 copy-start.6
  45.5 20.8 %copy-start.9 = (s32[1,32]{1,0:T(1,128)S(1)}, s32[1,32]{1,0:T(1,128)}, u32[]{:S(2)}) copy-start(s32[1,32]{1,0:T(1,128)} %param.16) | copy-start | bytes 388
  45.5 21.6 %copy-start.8 = (s32[2]{0:T(128)S(1)}, s32[2]{0:T(128)}, u32[]{:S(2)}) copy-start(s32[2]{0:T(128)} %param.17) | copy-start | bytes 28
  45.5 23.6 %copy-start.2 = (bf16[1,512,2048]{2,1,0:T(8,128)(2,1)S(1)}, bf16[1,512,2048]{2,1,0:T(8,128)(2,1)}, u32[]{:S(2)}) copy-start(bf16[1,512,2048]{2,1,0:T(8,128)(2,1)} %param.9) | copy-start | bytes 6291460
  45.5 23.6 %copy-start.4 = (f32[2048]{0:T(1024)S(1)}, f32[2048]{0:T(1024)}, u32[]{:S(2)}) copy-start(f32[2048]{0:T(1024)} %param.10) | copy-start | bytes 24580
  63.0 44.7 %collective-permute-start.4 = (bf16[4,2,32,4096]{3,2,1,0:T(8,128)(2,1)}, bf16[4,2,32,4096]{3,2,1,0:T(8,128)(2,1)}, u32[]{:S(2)}, u32[]{:S(2)}) collective-permute-start(bf16[4,2,32,4096]{3,2,1,0:T(8,128)(2,1)} %pad_maximum_fusion.refs_0_), channel_id=1, source_target_pairs={{0,64},{64,4},{4,68},{68,0},{1,65},{65,5},{5,69},{69,1},{2,66},{66... | collective-permute-start | bytes 6291464 | tf_op jit(solution)/shard_map/ppermute | solution.py:379
  63.4 45.8 %collective-permute-start.5 = (bf16[4,2,32,4096]{3,2,1,0:T(8,128)(2,1)}, bf16[4,2,32,4096]{3,2,1,0:T(8,128)(2,1)}, u32[]{:S(2)}, u32[]{:S(2)}) collective-permute-start(bf16[4,2,32,4096]{3,2,1,0:T(8,128)(2,1)} %pad_maximum_fusion.refs_0_), channel_id=1, source_target_pairs={{0,68},{64,0},{4,64},{68,4},{1,69},{65,1},{5,65},{69,5},{2,70},{66... | collective-permute-start | bytes 6291464 | tf_op jit(solution)/shard_map/ppermute | solution.py:379
  71.2 3.8 %copy-start.3 = (bf16[512,2048]{1,0:T(8,128)(2,1)}, bf16[512,2048]{1,0:T(8,128)(2,1)S(1)}, u32[]{:S(2)}) copy-start(bf16[512,2048]{1,0:T(8,128)(2,1)S(1)} %shard_map.91.hid_ref) | copy-start | bytes 6291460
  75.0 58.7 %copy-start.5 = (f32[2048]{0:T(1024)S(1)}, f32[2048]{0:T(1024)}, u32[]{:S(2)}) copy-start(f32[2048]{0:T(1024)} %param.13) | copy-start | bytes 24580
  75.0 55.0 %collective-permute-start.8 = (bf16[4,2,32,4096]{3,2,1,0:T(8,128)(2,1)}, bf16[4,2,32,4096]{3,2,1,0:T(8,128)(2,1)}, u32[]{:S(2)}, u32[]{:S(2)}) collective-permute-start(bf16[4,2,32,4096]{3,2,1,0:T(8,128)(2,1)} %pad_maximum_fusion.refs_0_), channel_id=1, source_target_pairs={{0,32},{32,0},{1,33},{33,1},{2,34},{34,2},{3,35},{35,3},{4,36},{36... | collective-permute-start | bytes 6291464 | tf_op jit(solution)/shard_map/ppermute | solution.py:399
  109.0 20.4 %collective-permute-start.6 = (bf16[4,2,32,2048]{3,2,1,0:T(8,128)(2,1)S(1)}, bf16[4,2,32,2048]{3,2,1,0:T(8,128)(2,1)S(1)}, u32[]{:S(2)}, u32[]{:S(2)}) collective-permute-start(bf16[4,2,32,2048]{3,2,1,0:T(8,128)(2,1)S(1)} %slice.60), channel_id=1, source_target_pairs={{0,64},{64,4},{4,68},{68,0},{1,65},{65,5},{5,69},{69,1},{2,66},{66... | collective-permute-start | bytes 3145736 | tf_op jit(solution)/shard_map/ppermute | solution.py:379
  110.5 19.4 %collective-permute-start.7 = (bf16[4,2,32,2048]{3,2,1,0:T(8,128)(2,1)S(1)}, bf16[4,2,32,2048]{3,2,1,0:T(8,128)(2,1)S(1)}, u32[]{:S(2)}, u32[]{:S(2)}) collective-permute-start(bf16[4,2,32,2048]{3,2,1,0:T(8,128)(2,1)S(1)} %slice.61), channel_id=1, source_target_pairs={{0,68},{64,0},{4,64},{68,4},{1,69},{65,1},{5,65},{69,5},{2,70},{66... | collective-permute-start | bytes 3145736 | tf_op jit(solution)/shard_map/ppermute | solution.py:379
  113.8 20.0 %collective-permute-start.10 = (bf16[4,2,32,4096]{3,2,1,0:T(8,128)(2,1)}, bf16[4,2,32,4096]{3,2,1,0:T(8,128)(2,1)}, u32[]{:S(2)}, u32[]{:S(2)}) collective-permute-start(bf16[4,2,32,4096]{3,2,1,0:T(8,128)(2,1)} %collective-permute-done.5.refs_2_), channel_id=1, source_target_pairs={{0,32},{32,0},{1,33},{33,1},{2,34},{34,2},{3,35},{35,3},{4,36},{36... | collective-permute-start | bytes 6291464 | tf_op jit(solution)/shard_map/ppermute | solution.py:399
  113.8 20.0 %collective-permute-start.9 = (bf16[4,2,32,4096]{3,2,1,0:T(8,128)(2,1)}, bf16[4,2,32,4096]{3,2,1,0:T(8,128)(2,1)}, u32[]{:S(2)}, u32[]{:S(2)}) collective-permute-start(bf16[4,2,32,4096]{3,2,1,0:T(8,128)(2,1)} %collective-permute-done.4.refs_1_), channel_id=1, source_target_pairs={{0,32},{32,0},{1,33},{33,1},{2,34},{34,2},{3,35},{35,3},{4,36},{36... | collective-permute-start | bytes 6291464 | tf_op jit(solution)/shard_map/ppermute | solution.py:399
  129.5 2.8 %collective-permute-start.11 = (bf16[4,2,32,2048]{3,2,1,0:T(8,128)(2,1)S(1)}, bf16[4,2,32,2048]{3,2,1,0:T(8,128)(2,1)}, u32[]{:S(2)}, u32[]{:S(2)}) collective-permute-start(bf16[4,2,32,2048]{3,2,1,0:T(8,128)(2,1)S(1)} %collective-permute-done.6.refs_3_), channel_id=1, source_target_pairs={{0,32},{32,0},{1,33},{33,1},{2,34},{34,2},{3,35},{35,3},{4,36},{36... | collective-permute-start | bytes 3145736 | tf_op jit(solution)/shard_map/ppermute | solution.py:399
  129.8 3.9 %collective-permute-start.12 = (bf16[4,2,32,2048]{3,2,1,0:T(8,128)(2,1)S(1)}, bf16[4,2,32,2048]{3,2,1,0:T(8,128)(2,1)}, u32[]{:S(2)}, u32[]{:S(2)}) collective-permute-start(bf16[4,2,32,2048]{3,2,1,0:T(8,128)(2,1)S(1)} %collective-permute-done.7.refs_4_), channel_id=1, source_target_pairs={{0,32},{32,0},{1,33},{33,1},{2,34},{34,2},{3,35},{35,3},{4,36},{36... | collective-permute-start | bytes 3145736 | tf_op jit(solution)/shard_map/ppermute | solution.py:399
  158.4 36.3 %collective-permute-start.13 = (bf16[4,4,2,2,16,4096]{5,4,3,2,1,0:T(8,128)(2,1)}, bf16[4,4,2,2,16,4096]{5,4,3,2,1,0:T(8,128)(2,1)}, u32[]{:S(2)}, u32[]{:S(2)}) collective-permute-start(bf16[4,4,2,2,16,4096]{5,4,3,2,1,0:T(8,128)(2,1)} %bitcast.70), channel_id=1, source_target_pairs={{0,32},{32,0},{1,33},{33,1},{2,34},{34,2},{3,35},{35,3},{4,36},{36... | collective-permute-start | bytes 25165832 | tf_op jit(solution)/shard_map/ppermute | solution.py:399
  216.1 23.0 %all-to-all-start.1 = ((bf16[32,16,1024]{2,1,0:T(8,128)(2,1)}), bf16[32,16,1024]{2,1,0:T(8,128)(2,1)S(1)}, u32[]{:S(2)}, u32[]{:S(2)}) async-start(bf16[32,16,1024]{2,1,0:T(8,128)(2,1)} %bitcast.67), calls=%async_computation.1 | async-start | bytes 2097152 | tf_op jit(solution)/shard_map/all_to_all | solution.py:464
  239.1 1.6 copy-start
  240.7 1.6 copy-start.1
Sparse Core Ops, SparseCore 0:
  63.2 70.9 all-gather.4

commit v13 on v9

--- a/solution.py
+++ b/solution.py
@@ -412,7 +412,8 @@
     rows = lax.all_gather(shard, "z", axis=0)
     qkv = rows[:, :, : 3 * WIDTH].reshape(2, 32, 3 * WIDTH)
     out = rows[:, :, 3 * WIDTH :].reshape(4, 2, 8, WIDTH).transpose(1, 0, 2, 3).reshape(2, 32, WIDTH)
-    return stack(forwards(first_hops(jnp.concatenate([qkv, out], -1), "x"), "x"))
+    hops = first_hops(jnp.concatenate([qkv, out], -1), "x")
+    return hops, stack(forwards(hops, "x"))
 
 
 def column_line(inputs, output):
@@ -447,10 +448,9 @@
 
     hidden = normed_slots(core_scalar, residual, gain_first.reshape(1, D))
 
-    line = column_line(inputs_second, output_second)
-    inputs_first, output_first, line = lax.optimization_barrier((inputs_first, output_first, line))
+    inner_hops, own_stack = row_stack(inputs_first, output_first)
+    line, _ = lax.optimization_barrier((column_line(inputs_second, output_second), inner_hops))
     plane = column_plane(line)
-    own_stack = row_stack(inputs_first, output_first)
     pieces = forwards(first_hops(own_stack, "y"), "y")
     own_stack, hidden, row_tables, column_tables = lax.optimization_barrier(
         (own_stack, hidden, row_tables, column_tables)

time: 263 us -> 243 us (0.924)
  waiting for transfers between devices: 87.1 us -> 68.6 us
    ppermute x4, waiting for transfers between devices: 26.9 us -> 4.26 us  [shift(): return lax.ppermute(value, axis, [(i, (i + by) % 4) for i in range(4)])]
    ppermute x4, waiting for transfers between devices: 44.5 us -> 48.3 us  [shift(): lax.ppermute(value, ('ylo', 'yhi'), [(where(y), where((y + by) % 4)) for...]
  transfers between devices with their start and end apart: 16 -> 16, of which waited for: 9 -> 7; matrix products, arithmetic and copies ran while one was open for 6% -> 7% of each run, Pallas kernels for 10% -> 11%
where the time goes in v13:
time: 243 us; the launch traced here: 242 us
  waiting for transfers between devices  68.6 us (28%)
  blocking collectives  65.6 us (27%)
  Pallas kernels  51.9 us (21%)
  starting transfers between devices  19.8 us (8%)
  between operations  14.9 us (6%)
  local copies, waits for them, and re-layouts  14.5 us (6%)
  other arithmetic  6.94 us (3%)
    ppermute x4, waiting for transfers between devices, shift(): lax.ppermute(value, ('ylo', 'yhi'), [(where(y), where((y + by) % 4)) for...  48.3 us
    all_to_all x1, blocking collectives, shards(): lax.all_to_all(hidden, SEQ, split_axis=0, concat_axis=0, tiled=True)  35 us
    pallas_call x1, Pallas kernels, row_layer(): pl.pallas_call(row_kernel, out_shape=[shape, shape], in_specs=[pl.BlockSp...  24.6 us
    pallas_call x1, Pallas kernels, column_layer(): pl.pallas_call(column_kernel, out_shape=jax.ShapeDtypeStruct((C, WIDTH),...  21.4 us
    all_gather x1, blocking collectives, column_line(): return lax.all_gather(shard, ('ylo', 'yhi'), axis=0)  16.5 us
    all_gather x1, blocking collectives, row_stack(): rows = lax.all_gather(shard, 'z', axis=0)  14.1 us
    all_to_all x1, waiting for transfers between devices, shards(): lax.all_to_all(attended, SEQ, split_axis=0, concat_axis=0, tiled=True)  12.3 us
    ppermute x4, starting transfers between devices, shift(): return lax.ppermute(value, axis, [(i, (i + by) % 4) for i in range(4)])  6.68 us
  transfers between devices with their start and end apart: 16, of which 7 were waited for; matrix products, arithmetic and copies ran while one was open for 7% of the time, Pallas kernels for 11%

profile of v13, /device:TPU:0, one launch (start us, length us, event | category | flops | bytes accessed | tf_op | source)
XLA Modules:
  0.0 242.3 jit_solution(2768916300807211569)
XLA Ops:
  6.5 0.7 fusion.7
  7.3 1.0 reshape.95
  8.3 0.1 copy.23
  8.3 0.1 reshape.96
  8.5 14.1 %all-gather.1 = bf16[64,4096]{1,0:T(8,128)(2,1)S(1)} all-gather(bf16[16,4096]{1,0:T(8,128)(2,1)S(1)} %maximum_maximum_fusion.1), channel_id=3, replica_groups=mesh['ylo'=2,'core'=2,'x'=4,'yhi'=2,'z'=4] {'z'}, dimensions={0}, use_global_device_ids=true | all-gather | bytes 655360 | tf_op jit(solution)/shard_map/all_gather | solution.py:412
  22.6 0.1 fusion.6
  22.6 1.6 collective-permute-start
  24.2 1.7 collective-permute-start.1
  26.0 0.1 copy.24
  26.1 0.1 reshape.94
  26.2 16.5 %all-gather = bf16[64,4096]{1,0:T(8,128)(2,1)} all-gather(bf16[16,4096]{1,0:T(8,128)(2,1)S(1)} %maximum_maximum_fusion), channel_id=2, replica_groups=mesh['ylo'=2,'core'=2,'x'=4,'yhi'=2,'z'=4] {'ylo','yhi'}, dimensions={0}, use_global_device_ids=true | all-gather | bytes 655360 | tf_op jit(solution)/shard_map/all_gather | solution.py:421
  42.7 0.0 collective-permute-done
  42.7 0.0 collective-permute-done.1
  42.7 0.0 copy-start.6
  42.8 0.0 all-gather.5.cloned.1.call-update
  42.8 0.3 collective-permute-start.2
  43.2 3.0 %collective-permute-start.3 = (bf16[2,32,2048]{2,1,0:T(8,128)(2,1)S(1)}, bf16[2,32,2048]{2,1,0:T(8,128)(2,1)S(1)}, u32[]{:S(2)}, u32[]{:S(2)}) collective-permute-start(bf16[2,32,2048]{2,1,0:T(8,128)(2,1)S(1)} %slice.59), channel_id=1, source_target_pairs={{0,24},{8,0},{16,8},{24,16},{1,25},{9,1},{17,9},{25,17},{2,26},{10... | collective-permute-start | bytes 786440 | tf_op jit(solution)/shard_map/ppermute | solution.py:380
  46.2 4.3 %collective-permute-done.2 = bf16[2,32,2048]{2,1,0:T(8,128)(2,1)S(1)} collective-permute-done((bf16[2,32,2048]{2,1,0:T(8,128)(2,1)S(1)}, bf16[2,32,2048]{2,1,0:T(8,128)(2,1)S(1)}, u32[]{:S(2)}, u32[]{:S(2)}) %collective-permute-start.2) | collective-permute-done | bytes 262176 | tf_op jit(solution)/shard_map/ppermute | solution.py:380
  50.5 0.0 collective-permute-done.3
  50.5 0.0 copy-start.10
  50.5 0.0 copy-start.9
  50.5 0.0 copy-start.2
  50.6 0.0 copy-start.4
  50.6 2.9 %pad_maximum_fusion.refs_0_ = bf16[4,2,32,4096]{3,2,1,0:T(8,128)(2,1)} fusion(bf16[1,2,32,4096]{3,2,1,0:T(8,128)(2,1)S(1)} %maximum_bitcast_fusion, bf16[1,2,32,4096]{3,2,1,0:T(8,128)(2,1)} %bitcast.66, bf16[1,2,32,4096]{3,2,1,0:T(8,128)(2,1)S(1)} %bitcast.65, bf16[1,2,32,4096]{3,2,1,0:T(8,128)(2,1)S(1)} %get-tuple-element.27), kind=kLoop, calls=%fused_computation.1 | loop fusion | flops 3145728 | bytes 4194304 | tf_op jit(solution)/shard_map/stack | solution.py:395
  53.4 0.8 collective-permute-start.4
  54.2 2.4 collective-permute-start.5
  56.7 0.6 constant_dynamic-slice_fusion
  57.3 0.1 add_convert_fusion
  57.4 0.1 convert_element_type.35
  57.4 0.6 fusion.9
  59.3 2.1 shard_map.91.hid_ref
  61.4 0.0 copy-start.3
  61.5 0.7 add_convert_fusion.1
  62.1 1.9 fusion.4
  64.1 0.2 pad_maximum_fusion.2
  64.3 1.0 pad_maximum_fusion.4
  65.3 0.0 collective-permute-start.8
  65.3 32.8 %collective-permute-done.4.refs_1_ = bf16[4,2,32,4096]{3,2,1,0:T(8,128)(2,1)} collective-permute-done((bf16[4,2,32,4096]{3,2,1,0:T(8,128)(2,1)}, bf16[4,2,32,4096]{3,2,1,0:T(8,128)(2,1)}, u32[]{:S(2)}, u32[]{:S(2)}) %collective-permute-start.4) | collective-permute-done | bytes 2097184 | tf_op jit(solution)/shard_map/ppermute | solution.py:379
  98.0 1.3 slice.60
  99.3 0.1 collective-permute-start.6
  99.4 1.3 slice.61
  100.8 3.3 %collective-permute-start.7 = (bf16[4,2,32,2048]{3,2,1,0:T(8,128)(2,1)S(1)}, bf16[4,2,32,2048]{3,2,1,0:T(8,128)(2,1)S(1)}, u32[]{:S(2)}, u32[]{:S(2)}) collective-permute-start(bf16[4,2,32,2048]{3,2,1,0:T(8,128)(2,1)S(1)} %slice.61), channel_id=1, source_target_pairs={{0,68},{64,0},{4,64},{68,4},{1,69},{65,1},{5,65},{69,5},{2,70},{66... | collective-permute-start | bytes 3145736 | tf_op jit(solution)/shard_map/ppermute | solution.py:379
  104.1 0.5 collective-permute-start.9
  104.6 15.4 %collective-permute-done.6.refs_3_ = bf16[4,2,32,2048]{3,2,1,0:T(8,128)(2,1)S(1)} collective-permute-done((bf16[4,2,32,2048]{3,2,1,0:T(8,128)(2,1)S(1)}, bf16[4,2,32,2048]{3,2,1,0:T(8,128)(2,1)S(1)}, u32[]{:S(2)}, u32[]{:S(2)}) %collective-permute-start.6) | collective-permute-done | bytes 1048608 | tf_op jit(solution)/shard_map/ppermute | solution.py:379
  120.0 0.1 collective-permute-done.7.refs_4_
  120.1 0.4 collective-permute-start.12
  120.5 0.1 pad_add_fusion.place_ref
  120.5 0.0 collective-permute-done.8.refs_5_
  120.5 2.2 collective-permute-done.11.refs_8_
  122.7 1.5 collective-permute-done.12.refs_9_
  124.3 24.6 %shard_map.92 = (bf16[512,2048]{1,0:T(8,128)(2,1)}, bf16[512,2048]{1,0:T(8,128)(2,1)}) custom-call(s32[3]{0:T(128)S(1)} %pad_add_fusion.place_ref, bf16[512,2048]{1,0:T(8,128)(2,1)} %bitcast.55, bf16[512,2048]{1,0:T(8,128)(2,1)} %copy-done.3, f32[1,2048]{1,0:T(1,128)S(1)} %bitcast.58, f32[512,128]{1,0:T(8,128)S(1)} %get-tuple-element.18.cos_ref, ...), custom_call_target="tpu_custom_call" | custom-call | flops 9663676416 | bytes 25165824 | tf_op jit(solution)/shard_map/pallas_call | solution.py:224
  148.9 0.0 all-gather.5.cloned.1.call-done
  148.9 0.2 collective-permute-start.13
  149.1 35.0 %all_to_all.22 = bf16[32,16,2048]{2,1,0:T(8,128)(2,1)} all-to-all(bf16[32,16,2048]{2,1,0:T(8,128)(2,1)} %bitcast.62), channel_id=1, replica_groups=mesh['ylo'=2,'core'=2,'x'=4,'yhi'=2,'z'=4] {'x','yhi','z'}, dimensions={0} | all-to-all | bytes 4194304 | tf_op jit(solution)/shard_map/all_to_all | solution.py:463
  184.1 21.4 %shard_map.93 = bf16[512,1024]{1,0:T(8,128)(2,1)} custom-call(s32[1]{0:T(128)} %bitcast.core_ref, bf16[512,2048]{1,0:T(8,128)(2,1)} %bitcast.63, f32[512,128]{1,0:T(8,128)} %get-tuple-element.23.cos_ref, f32[512,128]{1,0:T(8,128)} %get-tuple-element.24.sin_ref, bf16[4,4,2,2,16,4096]{5,4,3,2,1,0:T(8,128)(2,1)} %bitcast.71, ...), custom_call_target="tpu_custom_call" | custom-call | flops 7516192768 | bytes 15728640 | tf_op jit(solution)/shard_map/pallas_call | solution.py:314
  205.5 5.4 %all-to-all-start.1 = ((bf16[32,16,1024]{2,1,0:T(8,128)(2,1)}), bf16[32,16,1024]{2,1,0:T(8,128)(2,1)S(1)}, u32[]{:S(2)}, u32[]{:S(2)}) async-start(bf16[32,16,1024]{2,1,0:T(8,128)(2,1)} %bitcast.67), calls=%async_computation.1 | async-start | bytes 2097152 | tf_op jit(solution)/shard_map/all_to_all | solution.py:465
  210.9 1.8 slice_bitcast_fusion.1
  212.7 0.2 copy.18
  212.9 1.8 slice_bitcast_fusion
  214.6 1.5 copy.19
  216.1 12.3 %all-to-all-done.1 = bf16[32,16,1024]{2,1,0:T(8,128)(2,1)S(1)} async-done(((bf16[32,16,1024]{2,1,0:T(8,128)(2,1)}), bf16[32,16,1024]{2,1,0:T(8,128)(2,1)S(1)}, u32[]{:S(2)}, u32[]{:S(2)}) %all-to-all-start.1) | async-done | bytes 1048608 | tf_op jit(solution)/shard_map/all_to_all | solution.py:465
  228.5 1.6 copy-done
  230.1 1.6 copy-done.1
  231.6 3.8 %shard_map.94 = bf16[512,2048]{1,0:T(8,128)(2,1)} custom-call(s32[1]{0:T(128)} %bitcast.core_ref, bf16[512,1024]{1,0:T(8,128)(2,1)S(1)} %bitcast.54, bf16[512,2048]{1,0:T(8,128)(2,1)S(1)} %bitcast.52, bf16[512,2048]{1,0:T(8,128)(2,1)S(1)} %bitcast.53, bf16[512,2048]{1,0:T(8,128)(2,1)S(1)} %copy-done.1), custom_call_target="tpu_custom_call" | custom-call | flops 2147483648 | bytes 9437184 | tf_op jit(solution)/shard_map/pallas_call | solution.py:353
  (32 shorter events, 0.2 us)
Async XLA Ops:
  6.5 142.4 %all-gather.5.cloned.1.call-start = ((), (), s32[]{:S(2)}) async-start(), calls=%async_computation.2 | async-start | bytes 8912896 | tf_op jit(solution)/shard_map/all_gather | solution.py:425
  7.3 18.7 %copy-start.8 = (bf16[8,2048]{1,0:T(8,128)(2,1)S(1)}, bf16[8,2048]{1,0:T(8,128)(2,1)}, u32[]{:S(2)}) copy-start(bf16[8,2048]{1,0:T(8,128)(2,1)} %param.15) | copy-start | bytes 98308
  7.3 18.7 %copy-start.7 = (bf16[16,3072]{1,0:T(8,128)(2,1)S(1)}, bf16[16,3072]{1,0:T(8,128)(2,1)}, u32[]{:S(2)}) copy-start(bf16[16,3072]{1,0:T(8,128)(2,1)} %param.14) | copy-start | bytes 294916
  22.6 20.1 %collective-permute-start = (bf16[2,32,4096]{2,1,0:T(8,128)(2,1)S(1)}, bf16[2,32,4096]{2,1,0:T(8,128)(2,1)S(1)}, u32[]{:S(2)}, u32[]{:S(2)}) collective-permute-start(bf16[2,32,4096]{2,1,0:T(8,128)(2,1)S(1)} %get-tuple-element.28), channel_id=1, source_target_pairs={{0,8},{8,16},{16,24},{24,0},{1,9},{9,17},{17,25},{25,1},{2,10},{10... | collective-permute-start | bytes 1572872 | tf_op jit(solution)/shard_map/ppermute | solution.py:380
  24.2 18.5 %collective-permute-start.1 = (bf16[2,32,4096]{2,1,0:T(8,128)(2,1)S(1)}, bf16[2,32,4096]{2,1,0:T(8,128)(2,1)S(1)}, u32[]{:S(2)}, u32[]{:S(2)}) collective-permute-start(bf16[2,32,4096]{2,1,0:T(8,128)(2,1)S(1)} %get-tuple-element.28), channel_id=1, source_target_pairs={{0,24},{8,0},{16,8},{24,16},{1,25},{9,1},{17,9},{25,17},{2,26},{10... | collective-permute-start | bytes 1572872 | tf_op jit(solution)/shard_map/ppermute | solution.py:380
  42.7 7.8 %copy-start.6 = (bf16[2,32,4096]{2,1,0:T(8,128)(2,1)}, bf16[2,32,4096]{2,1,0:T(8,128)(2,1)S(1)}, u32[]{:S(2)}) copy-start(bf16[2,32,4096]{2,1,0:T(8,128)(2,1)S(1)} %collective-permute-done.1) | copy-start | bytes 1572868
  42.8 7.7 %collective-permute-start.2 = (bf16[2,32,2048]{2,1,0:T(8,128)(2,1)S(1)}, bf16[2,32,2048]{2,1,0:T(8,128)(2,1)S(1)}, u32[]{:S(2)}, u32[]{:S(2)}) collective-permute-start(bf16[2,32,2048]{2,1,0:T(8,128)(2,1)S(1)} %slice.58), channel_id=1, source_target_pairs={{0,8},{8,16},{16,24},{24,0},{1,9},{9,17},{17,25},{25,1},{2,10},{10... | collective-permute-start | bytes 786440 | tf_op jit(solution)/shard_map/ppermute | solution.py:380
  43.2 7.3 %collective-permute-start.3 = (bf16[2,32,2048]{2,1,0:T(8,128)(2,1)S(1)}, bf16[2,32,2048]{2,1,0:T(8,128)(2,1)S(1)}, u32[]{:S(2)}, u32[]{:S(2)}) collective-permute-start(bf16[2,32,2048]{2,1,0:T(8,128)(2,1)S(1)} %slice.59), channel_id=1, source_target_pairs={{0,24},{8,0},{16,8},{24,16},{1,25},{9,1},{17,9},{25,17},{2,26},{10... | collective-permute-start | bytes 786440 | tf_op jit(solution)/shard_map/ppermute | solution.py:380
  50.5 6.1 %copy-start.10 = (s32[1,32]{1,0:T(1,128)S(1)}, s32[1,32]{1,0:T(1,128)}, u32[]{:S(2)}) copy-start(s32[1,32]{1,0:T(1,128)} %param.16) | copy-start | bytes 388
  50.5 6.9 %copy-start.9 = (s32[2]{0:T(128)S(1)}, s32[2]{0:T(128)}, u32[]{:S(2)}) copy-start(s32[2]{0:T(128)} %param.17) | copy-start | bytes 28
  50.5 8.8 %copy-start.2 = (bf16[1,512,2048]{2,1,0:T(8,128)(2,1)S(1)}, bf16[1,512,2048]{2,1,0:T(8,128)(2,1)}, u32[]{:S(2)}) copy-start(bf16[1,512,2048]{2,1,0:T(8,128)(2,1)} %param.9) | copy-start | bytes 6291460
  50.6 8.8 %copy-start.4 = (f32[2048]{0:T(1024)S(1)}, f32[2048]{0:T(1024)}, u32[]{:S(2)}) copy-start(f32[2048]{0:T(1024)} %param.10) | copy-start | bytes 24580
  53.4 44.6 %collective-permute-start.4 = (bf16[4,2,32,4096]{3,2,1,0:T(8,128)(2,1)}, bf16[4,2,32,4096]{3,2,1,0:T(8,128)(2,1)}, u32[]{:S(2)}, u32[]{:S(2)}) collective-permute-start(bf16[4,2,32,4096]{3,2,1,0:T(8,128)(2,1)} %pad_maximum_fusion.refs_0_), channel_id=1, source_target_pairs={{0,64},{64,4},{4,68},{68,0},{1,65},{65,5},{5,69},{69,1},{2,66},{66... | collective-permute-start | bytes 6291464 | tf_op jit(solution)/shard_map/ppermute | solution.py:379
  54.2 45.2 %collective-permute-start.5 = (bf16[4,2,32,4096]{3,2,1,0:T(8,128)(2,1)}, bf16[4,2,32,4096]{3,2,1,0:T(8,128)(2,1)}, u32[]{:S(2)}, u32[]{:S(2)}) collective-permute-start(bf16[4,2,32,4096]{3,2,1,0:T(8,128)(2,1)} %pad_maximum_fusion.refs_0_), channel_id=1, source_target_pairs={{0,68},{64,0},{4,64},{68,4},{1,69},{65,1},{5,65},{69,5},{2,70},{66... | collective-permute-start | bytes 6291464 | tf_op jit(solution)/shard_map/ppermute | solution.py:379
  61.4 3.8 %copy-start.3 = (bf16[512,2048]{1,0:T(8,128)(2,1)}, bf16[512,2048]{1,0:T(8,128)(2,1)S(1)}, u32[]{:S(2)}) copy-start(bf16[512,2048]{1,0:T(8,128)(2,1)S(1)} %shard_map.91.hid_ref) | copy-start | bytes 6291460
  65.3 59.0 %copy-start.5 = (f32[2048]{0:T(1024)S(1)}, f32[2048]{0:T(1024)}, u32[]{:S(2)}) copy-start(f32[2048]{0:T(1024)} %param.13) | copy-start | bytes 24580
  65.3 55.3 %collective-permute-start.8 = (bf16[4,2,32,4096]{3,2,1,0:T(8,128)(2,1)}, bf16[4,2,32,4096]{3,2,1,0:T(8,128)(2,1)}, u32[]{:S(2)}, u32[]{:S(2)}) collective-permute-start(bf16[4,2,32,4096]{3,2,1,0:T(8,128)(2,1)} %pad_maximum_fusion.refs_0_), channel_id=1, source_target_pairs={{0,32},{32,0},{1,33},{33,1},{2,34},{34,2},{3,35},{35,3},{4,36},{36... | collective-permute-start | bytes 6291464 | tf_op jit(solution)/shard_map/ppermute | solution.py:399
  99.3 20.6 %collective-permute-start.6 = (bf16[4,2,32,2048]{3,2,1,0:T(8,128)(2,1)S(1)}, bf16[4,2,32,2048]{3,2,1,0:T(8,128)(2,1)S(1)}, u32[]{:S(2)}, u32[]{:S(2)}) collective-permute-start(bf16[4,2,32,2048]{3,2,1,0:T(8,128)(2,1)S(1)} %slice.60), channel_id=1, source_target_pairs={{0,64},{64,4},{4,68},{68,0},{1,65},{65,5},{5,69},{69,1},{2,66},{66... | collective-permute-start | bytes 3145736 | tf_op jit(solution)/shard_map/ppermute | solution.py:379
  100.8 19.3 %collective-permute-start.7 = (bf16[4,2,32,2048]{3,2,1,0:T(8,128)(2,1)S(1)}, bf16[4,2,32,2048]{3,2,1,0:T(8,128)(2,1)S(1)}, u32[]{:S(2)}, u32[]{:S(2)}) collective-permute-start(bf16[4,2,32,2048]{3,2,1,0:T(8,128)(2,1)S(1)} %slice.61), channel_id=1, source_target_pairs={{0,68},{64,0},{4,64},{68,4},{1,69},{65,1},{5,65},{69,5},{2,70},{66... | collective-permute-start | bytes 3145736 | tf_op jit(solution)/shard_map/ppermute | solution.py:379
  104.1 20.2 %collective-permute-start.10 = (bf16[4,2,32,4096]{3,2,1,0:T(8,128)(2,1)}, bf16[4,2,32,4096]{3,2,1,0:T(8,128)(2,1)}, u32[]{:S(2)}, u32[]{:S(2)}) collective-permute-start(bf16[4,2,32,4096]{3,2,1,0:T(8,128)(2,1)} %collective-permute-done.5.refs_2_), channel_id=1, source_target_pairs={{0,32},{32,0},{1,33},{33,1},{2,34},{34,2},{3,35},{35,3},{4,36},{36... | collective-permute-start | bytes 6291464 | tf_op jit(solution)/shard_map/ppermute | solution.py:399
  104.1 20.2 %collective-permute-start.9 = (bf16[4,2,32,4096]{3,2,1,0:T(8,128)(2,1)}, bf16[4,2,32,4096]{3,2,1,0:T(8,128)(2,1)}, u32[]{:S(2)}, u32[]{:S(2)}) collective-permute-start(bf16[4,2,32,4096]{3,2,1,0:T(8,128)(2,1)} %collective-permute-done.4.refs_1_), channel_id=1, source_target_pairs={{0,32},{32,0},{1,33},{33,1},{2,34},{34,2},{3,35},{35,3},{4,36},{36... | collective-permute-start | bytes 6291464 | tf_op jit(solution)/shard_map/ppermute | solution.py:399
  119.9 2.8 %collective-permute-start.11 = (bf16[4,2,32,2048]{3,2,1,0:T(8,128)(2,1)S(1)}, bf16[4,2,32,2048]{3,2,1,0:T(8,128)(2,1)}, u32[]{:S(2)}, u32[]{:S(2)}) collective-permute-start(bf16[4,2,32,2048]{3,2,1,0:T(8,128)(2,1)S(1)} %collective-permute-done.6.refs_3_), channel_id=1, source_target_pairs={{0,32},{32,0},{1,33},{33,1},{2,34},{34,2},{3,35},{35,3},{4,36},{36... | collective-permute-start | bytes 3145736 | tf_op jit(solution)/shard_map/ppermute | solution.py:399
  120.1 4.1 %collective-permute-start.12 = (bf16[4,2,32,2048]{3,2,1,0:T(8,128)(2,1)S(1)}, bf16[4,2,32,2048]{3,2,1,0:T(8,128)(2,1)}, u32[]{:S(2)}, u32[]{:S(2)}) collective-permute-start(bf16[4,2,32,2048]{3,2,1,0:T(8,128)(2,1)S(1)} %collective-permute-done.7.refs_4_), channel_id=1, source_target_pairs={{0,32},{32,0},{1,33},{33,1},{2,34},{34,2},{3,35},{35,3},{4,36},{36... | collective-permute-start | bytes 3145736 | tf_op jit(solution)/shard_map/ppermute | solution.py:399
  148.9 35.2 %collective-permute-start.13 = (bf16[4,4,2,2,16,4096]{5,4,3,2,1,0:T(8,128)(2,1)}, bf16[4,4,2,2,16,4096]{5,4,3,2,1,0:T(8,128)(2,1)}, u32[]{:S(2)}, u32[]{:S(2)}) collective-permute-start(bf16[4,4,2,2,16,4096]{5,4,3,2,1,0:T(8,128)(2,1)} %bitcast.70), channel_id=1, source_target_pairs={{0,32},{32,0},{1,33},{33,1},{2,34},{34,2},{3,35},{35,3},{4,36},{36... | collective-permute-start | bytes 25165832 | tf_op jit(solution)/shard_map/ppermute | solution.py:399
  205.5 23.0 %all-to-all-start.1 = ((bf16[32,16,1024]{2,1,0:T(8,128)(2,1)}), bf16[32,16,1024]{2,1,0:T(8,128)(2,1)S(1)}, u32[]{:S(2)}, u32[]{:S(2)}) async-start(bf16[32,16,1024]{2,1,0:T(8,128)(2,1)} %bitcast.67), calls=%async_computation.1 | async-start | bytes 2097152 | tf_op jit(solution)/shard_map/all_to_all | solution.py:465
  228.5 1.6 copy-start
  230.1 1.6 copy-start.1
Sparse Core Ops, SparseCore 0:
  42.9 70.2 all-gather.4

commit v14 on v13

--- a/solution.py
+++ b/solution.py
@@ -20,7 +20,7 @@
 SEQ = ("x", "yhi", "z")
 QKV_HALF = 3 * WIDTH // 2
 PART = 4 * WIDTH
-RELATIVE = ((0, 0, PART), (3, 0, PART), (1, 0, PART), (2, 0, PART // 2), (2, PART // 2, PART))
+RELATIVE = tuple((ring, half * PART // 2, (half + 1) * PART // 2) for half in range(2) for ring in (0, 3, 1, 2))
 RINGS = (0, 3, 1, 2)
 LOG2E = 1.4426950408889634
 MIB = 1 << 20
@@ -395,6 +395,17 @@
     return jnp.stack([own, left, right, jnp.concatenate([low, high], -1)])
 
 
+def outer_ring(value):
+    half = value.shape[-1] // 2
+    low, high = value[..., :half], value[..., half:]
+    pieces = []
+    hops = [(part, shift(part, "y", 1), shift(part, "y", -1)) for part in (low, high)]
+    for index, (own, left, right) in enumerate(hops):
+        far = shift(right, "y", -1) if index else shift(left, "y", 1)
+        pieces += [own, left, right, far]
+    return pieces
+
+
 def swap(value):
     return lax.ppermute(value, "core", [(0, 1), (1, 0)])
 
@@ -451,11 +462,11 @@
     inner_hops, own_stack = row_stack(inputs_first, output_first)
     line, _ = lax.optimization_barrier((column_line(inputs_second, output_second), inner_hops))
     plane = column_plane(line)
-    pieces = forwards(first_hops(own_stack, "y"), "y")
-    own_stack, hidden, row_tables, column_tables = lax.optimization_barrier(
-        (own_stack, hidden, row_tables, column_tables)
+    pieces = outer_ring(own_stack)
+    early, hidden, row_tables, column_tables = lax.optimization_barrier(
+        (pieces[0], hidden, row_tables, column_tables)
     )
-    pieces = pieces + [swap(own_stack)] + [swap(piece) for piece in pieces[1:]]
+    pieces = pieces + [swap(early)] + [swap(piece) for piece in pieces[1:]]
 
     middle, hidden = row_layer(place, residual, hidden, gain_second.reshape(1, D), row_tables, pieces)
     plane, hidden = lax.optimization_barrier((plane, hidden))

time: 243 us -> 264 us (1.086)
  waiting for transfers between devices: 68.6 us -> 79.1 us
  local copies, waits for them, and re-layouts: 14.5 us -> 18.9 us
    ppermute x4 -> x6, waiting for transfers between devices: 48.3 us -> 61.5 us  [shift(): lax.ppermute(value, ('ylo', 'yhi'), [(where(y), where((y + by) % 4)) for...]
    unnamed x22 -> x40, local copies, waits for them, and re-layouts: 3.23 us -> 7.77 us
    ppermute x4, waiting for transfers between devices: 4.26 us -> 0.81 us  [shift(): return lax.ppermute(value, axis, [(i, (i + by) % 4) for i in range(4)])]
    ppermute x4 -> x6, starting transfers between devices: 6.59 us -> 8.71 us  [shift(): lax.ppermute(value, ('ylo', 'yhi'), [(where(y), where((y + by) % 4)) for...]
  transfers between devices with their start and end apart: 16 -> 21, of which waited for: 7 -> 8; matrix products, arithmetic and copies ran while one was open for 7% -> 6% of each run, Pallas kernels for 11% -> 10%
where the time goes in v14:
time: 264 us; the launch traced here: 263 us
  waiting for transfers between devices  79.1 us (30%)
  blocking collectives  67.8 us (26%)
  Pallas kernels  51.8 us (20%)
  starting transfers between devices  22 us (8%)
  local copies, waits for them, and re-layouts  18.9 us (7%)
  between operations  15 us (6%)
  other arithmetic  8.44 us (3%)
    ppermute x6, waiting for transfers between devices, shift(): lax.ppermute(value, ('ylo', 'yhi'), [(where(y), where((y + by) % 4)) for...  61.5 us
    all_to_all x1, blocking collectives, shards(): lax.all_to_all(hidden, SEQ, split_axis=0, concat_axis=0, tiled=True)  37.1 us
    pallas_call x1, Pallas kernels, row_layer(): pl.pallas_call(row_kernel, out_shape=[shape, shape], in_specs=[pl.BlockSp...  24.6 us
    pallas_call x1, Pallas kernels, column_layer(): pl.pallas_call(column_kernel, out_shape=jax.ShapeDtypeStruct((C, WIDTH),...  21.3 us
    all_gather x1, blocking collectives, column_line(): return lax.all_gather(shard, ('ylo', 'yhi'), axis=0)  16.7 us
    all_gather x1, blocking collectives, row_stack(): rows = lax.all_gather(shard, 'z', axis=0)  14.1 us
    all_to_all x1, waiting for transfers between devices, shards(): lax.all_to_all(attended, SEQ, split_axis=0, concat_axis=0, tiled=True)  12.3 us
    ppermute x6, starting transfers between devices, shift(): lax.ppermute(value, ('ylo', 'yhi'), [(where(y), where((y + by) % 4)) for...  8.71 us
  transfers between devices with their start and end apart: 21, of which 8 were waited for; matrix products, arithmetic and copies ran while one was open for 6% of the time, Pallas kernels for 10%

profile of v14, /device:TPU:0, one launch (start us, length us, event | category | flops | bytes accessed | tf_op | source)
XLA Modules:
  0.0 263.0 jit_solution(16270264919448438371)
XLA Ops:
  6.5 0.7 fusion.8
  7.3 1.0 reshape.95
  8.3 0.1 copy.23
  8.3 0.1 reshape.96
  8.5 14.1 %all-gather.1 = bf16[64,4096]{1,0:T(8,128)(2,1)S(1)} all-gather(bf16[16,4096]{1,0:T(8,128)(2,1)S(1)} %maximum_maximum_fusion.1), channel_id=3, replica_groups=mesh['ylo'=2,'core'=2,'x'=4,'yhi'=2,'z'=4] {'z'}, dimensions={0}, use_global_device_ids=true | all-gather | bytes 655360 | tf_op jit(solution)/shard_map/all_gather | solution.py:423
  22.6 0.9 fusion.6
  23.5 1.5 collective-permute-start
  25.0 1.7 collective-permute-start.1
  26.8 0.1 copy.24
  26.9 0.1 reshape.94
  27.0 16.7 %all-gather = bf16[64,4096]{1,0:T(8,128)(2,1)} all-gather(bf16[16,4096]{1,0:T(8,128)(2,1)S(1)} %maximum_maximum_fusion), channel_id=2, replica_groups=mesh['ylo'=2,'core'=2,'x'=4,'yhi'=2,'z'=4] {'ylo','yhi'}, dimensions={0}, use_global_device_ids=true | all-gather | bytes 655360 | tf_op jit(solution)/shard_map/all_gather | solution.py:432
  43.7 0.0 all-gather.5.cloned.1.call-update
  43.7 0.7 constant_dynamic-slice_fusion
  44.4 0.1 add_convert_fusion
  44.5 0.1 convert_element_type.35
  44.5 0.6 fusion.10
  46.4 0.6 add_convert_fusion.1
  47.1 0.7 slice.58
  47.8 0.3 collective-permute-start.2
  48.1 1.7 slice.59
  49.7 3.0 %collective-permute-start.3 = (bf16[2,32,2048]{2,1,0:T(8,128)(2,1)}, bf16[2,32,2048]{2,1,0:T(8,128)(2,1)}, u32[]{:S(2)}, u32[]{:S(2)}) collective-permute-start(bf16[2,32,2048]{2,1,0:T(8,128)(2,1)} %slice.59), channel_id=1, source_target_pairs={{0,24},{8,0},{16,8},{24,16},{1,25},{9,1},{17,9},{25,17},{2,26},{10... | collective-permute-start | bytes 786440 | tf_op jit(solution)/shard_map/ppermute | solution.py:380
  52.7 3.1 %fusion.4 = (f32[512,64]{1,0:T(8,128)S(1)}, f32[512,64]{1,0:T(8,128)}, f32[512,64]{1,0:T(8,128)}, f32[512,64]{1,0:T(8,128)}, f32[512,64]{1,0:T(8,128)}, /*index=5*/f32[512,64]{1,0:T(8,128)}) fusion(f32[64]{0:T(128)S(1)} %multiply_add_fusion, f32[512]{0:T(512)S(1)} %convert_element_type.35, f32[512]{0:T(512)S(1)} %add_convert_fusion.1), kind=kLoop, calls=%fused_computation.23 | loop fusion | flops 262144 | bytes 790784 | tf_op jit(solution)/shard_map/neg | solution.py:43
  55.9 2.1 shard_map.91.hid_ref
  58.0 1.3 copy-done.3
  59.3 0.2 pad_maximum_fusion.2
  59.6 1.0 pad_maximum_fusion.4
  60.6 0.8 collective-permute-done.3
  61.4 1.1 maximum_bitcast_fusion
  62.4 1.3 pad_maximum_fusion
  63.8 0.1 fusion.7
  63.9 0.1 collective-permute-start.10
  64.0 0.2 collective-permute-start.4
  64.2 3.1 %collective-permute-start.8 = (bf16[4,2,32,2048]{3,2,1,0:T(8,128)(2,1)S(1)}, bf16[4,2,32,2048]{3,2,1,0:T(8,128)(2,1)}, u32[]{:S(2)}, u32[]{:S(2)}) collective-permute-start(bf16[4,2,32,2048]{3,2,1,0:T(8,128)(2,1)S(1)} %get-tuple-element.27.refs_4_), channel_id=1, source_target_pairs={{0,68},{64,0},{4,64},{68,4},{1,69},{65,1},{5,65},{69,5},{2,70},{66... | collective-permute-start | bytes 3145736 | tf_op jit(solution)/shard_map/ppermute | solution.py:379
  67.3 1.0 collective-permute-start.5
  68.3 1.0 collective-permute-start.7
  69.3 21.9 %collective-permute-done.4.refs_1_ = bf16[4,2,32,2048]{3,2,1,0:T(8,128)(2,1)S(1)} collective-permute-done((bf16[4,2,32,2048]{3,2,1,0:T(8,128)(2,1)S(1)}, bf16[4,2,32,2048]{3,2,1,0:T(8,128)(2,1)S(1)}, u32[]{:S(2)}, u32[]{:S(2)}) %collective-permute-start.4) | collective-permute-done | bytes 1048608 | tf_op jit(solution)/shard_map/ppermute | solution.py:379
  91.3 3.4 %collective-permute-start.9 = (bf16[4,2,32,2048]{3,2,1,0:T(8,128)(2,1)}, bf16[4,2,32,2048]{3,2,1,0:T(8,128)(2,1)}, u32[]{:S(2)}, u32[]{:S(2)}) collective-permute-start(bf16[4,2,32,2048]{3,2,1,0:T(8,128)(2,1)} %collective-permute-done.8.refs_6_), channel_id=1, source_target_pairs={{0,68},{64,0},{4,64},{68,4},{1,69},{65,1},{5,65},{69,5},{2,70},{66... | collective-permute-start | bytes 3145736 | tf_op jit(solution)/shard_map/ppermute | solution.py:379
  94.6 18.7 %collective-permute-done.5.refs_2_ = bf16[4,2,32,2048]{3,2,1,0:T(8,128)(2,1)} collective-permute-done((bf16[4,2,32,2048]{3,2,1,0:T(8,128)(2,1)S(1)}, bf16[4,2,32,2048]{3,2,1,0:T(8,128)(2,1)}, u32[]{:S(2)}, u32[]{:S(2)}) %collective-permute-start.5) | collective-permute-done | bytes 1048608 | tf_op jit(solution)/shard_map/ppermute | solution.py:379
  113.3 1.0 copy-done.5
  114.3 0.5 collective-permute-start.16
  114.8 0.1 collective-permute-start.12
  114.9 20.9 %collective-permute-done.6.refs_3_ = bf16[4,2,32,2048]{3,2,1,0:T(8,128)(2,1)} collective-permute-done((bf16[4,2,32,2048]{3,2,1,0:T(8,128)(2,1)S(1)}, bf16[4,2,32,2048]{3,2,1,0:T(8,128)(2,1)}, u32[]{:S(2)}, u32[]{:S(2)}) %collective-permute-start.6) | collective-permute-done | bytes 1048608 | tf_op jit(solution)/shard_map/ppermute | solution.py:379
  135.8 0.5 collective-permute-start.13
  136.4 1.0 copy-done.19
  137.3 0.0 collective-permute-start.17
  137.4 0.1 pad_add_fusion.place_ref
  137.4 1.4 collective-permute-done.15.refs_13_
  138.8 1.5 collective-permute-done.13.refs_11_
  140.3 1.5 collective-permute-done.17.refs_15_
  141.8 1.2 copy-done.6
  143.1 24.6 %shard_map.92 = (bf16[512,2048]{1,0:T(8,128)(2,1)}, bf16[512,2048]{1,0:T(8,128)(2,1)}) custom-call(s32[3]{0:T(128)S(1)} %pad_add_fusion.place_ref, bf16[512,2048]{1,0:T(8,128)(2,1)} %bitcast.55, bf16[512,2048]{1,0:T(8,128)(2,1)} %copy-done.3, f32[1,2048]{1,0:T(1,128)S(1)} %bitcast.58, f32[512,128]{1,0:T(8,128)S(1)} %get-tuple-element.18.cos_ref, ...), custom_call_target="tpu_custom_call" | custom-call | flops 9663676416 | bytes 25165824 | tf_op jit(solution)/shard_map/pallas_call | solution.py:224
  167.7 0.0 all-gather.5.cloned.1.call-done
  167.7 0.1 collective-permute-start.18
  167.8 37.1 %all_to_all.22 = bf16[32,16,2048]{2,1,0:T(8,128)(2,1)} all-to-all(bf16[32,16,2048]{2,1,0:T(8,128)(2,1)} %bitcast.62), channel_id=1, replica_groups=mesh['ylo'=2,'core'=2,'x'=4,'yhi'=2,'z'=4] {'x','yhi','z'}, dimensions={0} | all-to-all | bytes 4194304 | tf_op jit(solution)/shard_map/all_to_all | solution.py:474
  204.9 21.3 %shard_map.93 = bf16[512,1024]{1,0:T(8,128)(2,1)} custom-call(s32[1]{0:T(128)} %bitcast.core_ref, bf16[512,2048]{1,0:T(8,128)(2,1)} %bitcast.63, f32[512,128]{1,0:T(8,128)} %get-tuple-element.23.cos_ref, f32[512,128]{1,0:T(8,128)} %get-tuple-element.24.sin_ref, bf16[4,4,2,2,16,4096]{5,4,3,2,1,0:T(8,128)(2,1)} %bitcast.70, ...), custom_call_target="tpu_custom_call" | custom-call | flops 7516192768 | bytes 15728640 | tf_op jit(solution)/shard_map/pallas_call | solution.py:314
  226.3 5.4 %all-to-all-start.1 = ((bf16[32,16,1024]{2,1,0:T(8,128)(2,1)}), bf16[32,16,1024]{2,1,0:T(8,128)(2,1)S(1)}, u32[]{:S(2)}, u32[]{:S(2)}) async-start(bf16[32,16,1024]{2,1,0:T(8,128)(2,1)} %bitcast.66), calls=%async_computation.1 | async-start | bytes 2097152 | tf_op jit(solution)/shard_map/all_to_all | solution.py:476
  231.7 1.8 slice_bitcast_fusion.1
  233.5 0.2 copy.18
  233.6 1.8 slice_bitcast_fusion
  235.4 1.5 copy.19
  236.9 12.3 %all-to-all-done.1 = bf16[32,16,1024]{2,1,0:T(8,128)(2,1)S(1)} async-done(((bf16[32,16,1024]{2,1,0:T(8,128)(2,1)}), bf16[32,16,1024]{2,1,0:T(8,128)(2,1)S(1)}, u32[]{:S(2)}, u32[]{:S(2)}) %all-to-all-start.1) | async-done | bytes 1048608 | tf_op jit(solution)/shard_map/all_to_all | solution.py:476
  249.2 1.6 copy-done
  250.8 1.6 copy-done.1
  252.4 3.8 %shard_map.94 = bf16[512,2048]{1,0:T(8,128)(2,1)} custom-call(s32[1]{0:T(128)} %bitcast.core_ref, bf16[512,1024]{1,0:T(8,128)(2,1)S(1)} %bitcast.54, bf16[512,2048]{1,0:T(8,128)(2,1)S(1)} %bitcast.52, bf16[512,2048]{1,0:T(8,128)(2,1)S(1)} %bitcast.53, bf16[512,2048]{1,0:T(8,128)(2,1)S(1)} %copy-done.1), custom_call_target="tpu_custom_call" | custom-call | flops 2147483648 | bytes 9437184 | tf_op jit(solution)/shard_map/pallas_call | solution.py:353
  (59 shorter events, 0.3 us)
Async XLA Ops:
  6.5 161.2 %all-gather.5.cloned.1.call-start = ((), (), s32[]{:S(2)}) async-start(), calls=%async_computation.2 | async-start | bytes 8912896 | tf_op jit(solution)/shard_map/all_gather | solution.py:436
  7.3 19.5 %copy-start.14 = (bf16[8,2048]{1,0:T(8,128)(2,1)S(1)}, bf16[8,2048]{1,0:T(8,128)(2,1)}, u32[]{:S(2)}) copy-start(bf16[8,2048]{1,0:T(8,128)(2,1)} %param.15) | copy-start | bytes 98308
  7.3 19.5 %copy-start.13 = (bf16[16,3072]{1,0:T(8,128)(2,1)S(1)}, bf16[16,3072]{1,0:T(8,128)(2,1)}, u32[]{:S(2)}) copy-start(bf16[16,3072]{1,0:T(8,128)(2,1)} %param.14) | copy-start | bytes 294916
  22.6 21.2 %copy-start.16 = (s32[1,32]{1,0:T(1,128)S(1)}, s32[1,32]{1,0:T(1,128)}, u32[]{:S(2)}) copy-start(s32[1,32]{1,0:T(1,128)} %param.16) | copy-start | bytes 388
  22.6 22.0 %copy-start.15 = (s32[2]{0:T(128)S(1)}, s32[2]{0:T(128)}, u32[]{:S(2)}) copy-start(s32[2]{0:T(128)} %param.17) | copy-start | bytes 28
  23.5 20.2 %collective-permute-start = (bf16[2,32,4096]{2,1,0:T(8,128)(2,1)}, bf16[2,32,4096]{2,1,0:T(8,128)(2,1)S(1)}, u32[]{:S(2)}, u32[]{:S(2)}) collective-permute-start(bf16[2,32,4096]{2,1,0:T(8,128)(2,1)} %get-tuple-element.30), channel_id=1, source_target_pairs={{0,8},{8,16},{16,24},{24,0},{1,9},{9,17},{17,25},{25,1},{2,10},{10... | collective-permute-start | bytes 1572872 | tf_op jit(solution)/shard_map/ppermute | solution.py:380
  25.0 18.7 %collective-permute-start.1 = (bf16[2,32,4096]{2,1,0:T(8,128)(2,1)}, bf16[2,32,4096]{2,1,0:T(8,128)(2,1)}, u32[]{:S(2)}, u32[]{:S(2)}) collective-permute-start(bf16[2,32,4096]{2,1,0:T(8,128)(2,1)} %get-tuple-element.30), channel_id=1, source_target_pairs={{0,24},{8,0},{16,8},{24,16},{1,25},{9,1},{17,9},{25,17},{2,26},{10... | collective-permute-start | bytes 1572872 | tf_op jit(solution)/shard_map/ppermute | solution.py:380
  27.0 28.9 %copy-start.2 = (bf16[1,512,2048]{2,1,0:T(8,128)(2,1)S(1)}, bf16[1,512,2048]{2,1,0:T(8,128)(2,1)}, u32[]{:S(2)}) copy-start(bf16[1,512,2048]{2,1,0:T(8,128)(2,1)} %param.9) | copy-start | bytes 6291460
  27.0 28.8 %copy-start.4 = (f32[2048]{0:T(1024)S(1)}, f32[2048]{0:T(1024)}, u32[]{:S(2)}) copy-start(f32[2048]{0:T(1024)} %param.10) | copy-start | bytes 24580
  47.8 12.8 %collective-permute-start.2 = (bf16[2,32,2048]{2,1,0:T(8,128)(2,1)}, bf16[2,32,2048]{2,1,0:T(8,128)(2,1)}, u32[]{:S(2)}, u32[]{:S(2)}) collective-permute-start(bf16[2,32,2048]{2,1,0:T(8,128)(2,1)} %slice.58), channel_id=1, source_target_pairs={{0,8},{8,16},{16,24},{24,0},{1,9},{9,17},{17,25},{25,1},{2,10},{10... | collective-permute-start | bytes 786440 | tf_op jit(solution)/shard_map/ppermute | solution.py:380
  49.7 11.6 %collective-permute-start.3 = (bf16[2,32,2048]{2,1,0:T(8,128)(2,1)}, bf16[2,32,2048]{2,1,0:T(8,128)(2,1)}, u32[]{:S(2)}, u32[]{:S(2)}) collective-permute-start(bf16[2,32,2048]{2,1,0:T(8,128)(2,1)} %slice.59), channel_id=1, source_target_pairs={{0,24},{8,0},{16,8},{24,16},{1,25},{9,1},{17,9},{25,17},{2,26},{10... | collective-permute-start | bytes 786440 | tf_op jit(solution)/shard_map/ppermute | solution.py:380
  55.8 3.5 %copy-start.10 = (f32[512,64]{1,0:T(8,128)S(1)}, f32[512,64]{1,0:T(8,128)}, u32[]{:S(2)}) copy-start(f32[512,64]{1,0:T(8,128)} %get-tuple-element.41) | copy-start | bytes 393220
  55.8 3.5 %copy-start.11 = (f32[512,64]{1,0:T(8,128)S(1)}, f32[512,64]{1,0:T(8,128)}, u32[]{:S(2)}) copy-start(f32[512,64]{1,0:T(8,128)} %get-tuple-element.42) | copy-start | bytes 393220
  55.9 3.5 %copy-start.12 = (f32[512,64]{1,0:T(8,128)S(1)}, f32[512,64]{1,0:T(8,128)}, u32[]{:S(2)}) copy-start(f32[512,64]{1,0:T(8,128)} %get-tuple-element.43) | copy-start | bytes 393220
  55.9 3.7 %copy-start.8 = (f32[512,64]{1,0:T(8,128)S(1)}, f32[512,64]{1,0:T(8,128)}, u32[]{:S(2)}) copy-start(f32[512,64]{1,0:T(8,128)} %get-tuple-element.36) | copy-start | bytes 393220
  55.9 3.7 %copy-start.9 = (f32[512,64]{1,0:T(8,128)S(1)}, f32[512,64]{1,0:T(8,128)}, u32[]{:S(2)}) copy-start(f32[512,64]{1,0:T(8,128)} %get-tuple-element.37) | copy-start | bytes 393220
  58.0 1.3 copy-start.3
  63.7 78.1 %copy-start.7 = (f32[2048]{0:T(1024)S(1)}, f32[2048]{0:T(1024)}, u32[]{:S(2)}) copy-start(f32[2048]{0:T(1024)} %param.13) | copy-start | bytes 24580
  63.9 5.4 %collective-permute-start.10 = (bf16[4,2,32,2048]{3,2,1,0:T(8,128)(2,1)S(1)}, bf16[4,2,32,2048]{3,2,1,0:T(8,128)(2,1)S(1)}, u32[]{:S(2)}, u32[]{:S(2)}) collective-permute-start(bf16[4,2,32,2048]{3,2,1,0:T(8,128)(2,1)S(1)} %get-tuple-element.20.refs_0_), channel_id=1, source_target_pairs={{0,32},{32,0},{1,33},{33,1},{2,34},{34,2},{3,35},{35,3},{4,36},{36... | collective-permute-start | bytes 3145736 | tf_op jit(solution)/shard_map/ppermute | solution.py:410
  64.0 27.2 %collective-permute-start.4 = (bf16[4,2,32,2048]{3,2,1,0:T(8,128)(2,1)S(1)}, bf16[4,2,32,2048]{3,2,1,0:T(8,128)(2,1)S(1)}, u32[]{:S(2)}, u32[]{:S(2)}) collective-permute-start(bf16[4,2,32,2048]{3,2,1,0:T(8,128)(2,1)S(1)} %get-tuple-element.20.refs_0_), channel_id=1, source_target_pairs={{0,64},{64,4},{4,68},{68,0},{1,65},{65,5},{5,69},{69,1},{2,66},{66... | collective-permute-start | bytes 3145736 | tf_op jit(solution)/shard_map/ppermute | solution.py:379
  64.2 27.1 %collective-permute-start.8 = (bf16[4,2,32,2048]{3,2,1,0:T(8,128)(2,1)S(1)}, bf16[4,2,32,2048]{3,2,1,0:T(8,128)(2,1)}, u32[]{:S(2)}, u32[]{:S(2)}) collective-permute-start(bf16[4,2,32,2048]{3,2,1,0:T(8,128)(2,1)S(1)} %get-tuple-element.27.refs_4_), channel_id=1, source_target_pairs={{0,68},{64,0},{4,64},{68,4},{1,69},{65,1},{5,65},{69,5},{2,70},{66... | collective-permute-start | bytes 3145736 | tf_op jit(solution)/shard_map/ppermute | solution.py:379
  67.3 46.0 %collective-permute-start.5 = (bf16[4,2,32,2048]{3,2,1,0:T(8,128)(2,1)S(1)}, bf16[4,2,32,2048]{3,2,1,0:T(8,128)(2,1)}, u32[]{:S(2)}, u32[]{:S(2)}) collective-permute-start(bf16[4,2,32,2048]{3,2,1,0:T(8,128)(2,1)S(1)} %get-tuple-element.20.refs_0_), channel_id=1, source_target_pairs={{0,68},{64,0},{4,64},{68,4},{1,69},{65,1},{5,65},{69,5},{2,70},{66... | collective-permute-start | bytes 3145736 | tf_op jit(solution)/shard_map/ppermute | solution.py:379
  68.3 46.0 %collective-permute-start.7 = (bf16[4,2,32,2048]{3,2,1,0:T(8,128)(2,1)S(1)}, bf16[4,2,32,2048]{3,2,1,0:T(8,128)(2,1)}, u32[]{:S(2)}, u32[]{:S(2)}) collective-permute-start(bf16[4,2,32,2048]{3,2,1,0:T(8,128)(2,1)S(1)} %get-tuple-element.27.refs_4_), channel_id=1, source_target_pairs={{0,64},{64,4},{4,68},{68,0},{1,65},{65,5},{5,69},{69,1},{2,66},{66... | collective-permute-start | bytes 3145736 | tf_op jit(solution)/shard_map/ppermute | solution.py:379
  69.3 67.0 %copy-start.17 = (bf16[4,2,32,2048]{3,2,1,0:T(8,128)(2,1)}, bf16[4,2,32,2048]{3,2,1,0:T(8,128)(2,1)S(1)}, u32[]{:S(2)}) copy-start(bf16[4,2,32,2048]{3,2,1,0:T(8,128)(2,1)S(1)} %collective-permute-done.10.refs_8_) | copy-start | bytes 3145732
  69.3 45.5 %collective-permute-start.14 = (bf16[4,2,32,2048]{3,2,1,0:T(8,128)(2,1)S(1)}, bf16[4,2,32,2048]{3,2,1,0:T(8,128)(2,1)S(1)}, u32[]{:S(2)}, u32[]{:S(2)}) collective-permute-start(bf16[4,2,32,2048]{3,2,1,0:T(8,128)(2,1)S(1)} %get-tuple-element.27.refs_4_), channel_id=1, source_target_pairs={{0,32},{32,0},{1,33},{33,1},{2,34},{34,2},{3,35},{35,3},{4,36},{36... | collective-permute-start | bytes 3145736 | tf_op jit(solution)/shard_map/ppermute | solution.py:410
  91.2 44.6 %collective-permute-start.6 = (bf16[4,2,32,2048]{3,2,1,0:T(8,128)(2,1)S(1)}, bf16[4,2,32,2048]{3,2,1,0:T(8,128)(2,1)}, u32[]{:S(2)}, u32[]{:S(2)}) collective-permute-start(bf16[4,2,32,2048]{3,2,1,0:T(8,128)(2,1)S(1)} %collective-permute-done.4.refs_1_), channel_id=1, source_target_pairs={{0,64},{64,4},{4,68},{68,0},{1,65},{65,5},{5,69},{69,1},{2,66},{66... | collective-permute-start | bytes 3145736 | tf_op jit(solution)/shard_map/ppermute | solution.py:379
  91.3 44.6 %collective-permute-start.9 = (bf16[4,2,32,2048]{3,2,1,0:T(8,128)(2,1)}, bf16[4,2,32,2048]{3,2,1,0:T(8,128)(2,1)}, u32[]{:S(2)}, u32[]{:S(2)}) collective-permute-start(bf16[4,2,32,2048]{3,2,1,0:T(8,128)(2,1)} %collective-permute-done.8.refs_6_), channel_id=1, source_target_pairs={{0,68},{64,0},{4,64},{68,4},{1,69},{65,1},{5,65},{69,5},{2,70},{66... | collective-permute-start | bytes 3145736 | tf_op jit(solution)/shard_map/ppermute | solution.py:379
  113.3 23.0 %collective-permute-start.11 = (bf16[4,2,32,2048]{3,2,1,0:T(8,128)(2,1)S(1)}, bf16[4,2,32,2048]{3,2,1,0:T(8,128)(2,1)S(1)}, u32[]{:S(2)}, u32[]{:S(2)}) collective-permute-start(bf16[4,2,32,2048]{3,2,1,0:T(8,128)(2,1)S(1)} %collective-permute-done.4.refs_1_), channel_id=1, source_target_pairs={{0,32},{32,0},{1,33},{33,1},{2,34},{34,2},{3,35},{35,3},{4,36},{36... | collective-permute-start | bytes 3145736 | tf_op jit(solution)/shard_map/ppermute | solution.py:410
  113.3 1.0 copy-start.5
  114.3 23.1 %collective-permute-start.16 = (bf16[4,2,32,2048]{3,2,1,0:T(8,128)(2,1)}, bf16[4,2,32,2048]{3,2,1,0:T(8,128)(2,1)}, u32[]{:S(2)}, u32[]{:S(2)}) collective-permute-start(bf16[4,2,32,2048]{3,2,1,0:T(8,128)(2,1)} %collective-permute-done.8.refs_6_), channel_id=1, source_target_pairs={{0,32},{32,0},{1,33},{33,1},{2,34},{34,2},{3,35},{35,3},{4,36},{36... | collective-permute-start | bytes 3145736 | tf_op jit(solution)/shard_map/ppermute | solution.py:410
  114.8 21.5 %copy-start.18 = (bf16[4,2,32,2048]{3,2,1,0:T(8,128)(2,1)}, bf16[4,2,32,2048]{3,2,1,0:T(8,128)(2,1)S(1)}, u32[]{:S(2)}) copy-start(bf16[4,2,32,2048]{3,2,1,0:T(8,128)(2,1)S(1)} %collective-permute-done.14.refs_12_) | copy-start | bytes 3145732
  114.8 22.6 %collective-permute-start.12 = (bf16[4,2,32,2048]{3,2,1,0:T(8,128)(2,1)}, bf16[4,2,32,2048]{3,2,1,0:T(8,128)(2,1)}, u32[]{:S(2)}, u32[]{:S(2)}) collective-permute-start(bf16[4,2,32,2048]{3,2,1,0:T(8,128)(2,1)} %collective-permute-done.5.refs_2_), channel_id=1, source_target_pairs={{0,32},{32,0},{1,33},{33,1},{2,34},{34,2},{3,35},{35,3},{4,36},{36... | collective-permute-start | bytes 3145736 | tf_op jit(solution)/shard_map/ppermute | solution.py:410
  135.8 3.0 %collective-permute-start.15 = (bf16[4,2,32,2048]{3,2,1,0:T(8,128)(2,1)}, bf16[4,2,32,2048]{3,2,1,0:T(8,128)(2,1)}, u32[]{:S(2)}, u32[]{:S(2)}) collective-permute-start(bf16[4,2,32,2048]{3,2,1,0:T(8,128)(2,1)} %collective-permute-done.7.refs_5_), channel_id=1, source_target_pairs={{0,32},{32,0},{1,33},{33,1},{2,34},{34,2},{3,35},{35,3},{4,36},{36... | collective-permute-start | bytes 3145736 | tf_op jit(solution)/shard_map/ppermute | solution.py:410
  135.8 4.5 %collective-permute-start.13 = (bf16[4,2,32,2048]{3,2,1,0:T(8,128)(2,1)}, bf16[4,2,32,2048]{3,2,1,0:T(8,128)(2,1)}, u32[]{:S(2)}, u32[]{:S(2)}) collective-permute-start(bf16[4,2,32,2048]{3,2,1,0:T(8,128)(2,1)} %collective-permute-done.6.refs_3_), channel_id=1, source_target_pairs={{0,32},{32,0},{1,33},{33,1},{2,34},{34,2},{3,35},{35,3},{4,36},{36... | collective-permute-start | bytes 3145736 | tf_op jit(solution)/shard_map/ppermute | solution.py:410
  136.4 1.0 copy-start.19
  137.3 4.5 %collective-permute-start.17 = (bf16[4,2,32,2048]{3,2,1,0:T(8,128)(2,1)}, bf16[4,2,32,2048]{3,2,1,0:T(8,128)(2,1)}, u32[]{:S(2)}, u32[]{:S(2)}) collective-permute-start(bf16[4,2,32,2048]{3,2,1,0:T(8,128)(2,1)} %collective-permute-done.9.refs_7_), channel_id=1, source_target_pairs={{0,32},{32,0},{1,33},{33,1},{2,34},{34,2},{3,35},{35,3},{4,36},{36... | collective-permute-start | bytes 3145736 | tf_op jit(solution)/shard_map/ppermute | solution.py:410
  141.8 1.2 copy-start.6
  167.7 37.2 %collective-permute-start.18 = (bf16[4,4,2,2,16,4096]{5,4,3,2,1,0:T(8,128)(2,1)}, bf16[4,4,2,2,16,4096]{5,4,3,2,1,0:T(8,128)(2,1)}, u32[]{:S(2)}, u32[]{:S(2)}) collective-permute-start(bf16[4,4,2,2,16,4096]{5,4,3,2,1,0:T(8,128)(2,1)} %bitcast.69), channel_id=1, source_target_pairs={{0,32},{32,0},{1,33},{33,1},{2,34},{34,2},{3,35},{35,3},{4,36},{36... | collective-permute-start | bytes 25165832 | tf_op jit(solution)/shard_map/ppermute | solution.py:410
  226.3 22.9 %all-to-all-start.1 = ((bf16[32,16,1024]{2,1,0:T(8,128)(2,1)}), bf16[32,16,1024]{2,1,0:T(8,128)(2,1)S(1)}, u32[]{:S(2)}, u32[]{:S(2)}) async-start(bf16[32,16,1024]{2,1,0:T(8,128)(2,1)} %bitcast.66), calls=%async_computation.1 | async-start | bytes 2097152 | tf_op jit(solution)/shard_map/all_to_all | solution.py:476
  249.2 1.6 copy-start
  250.8 1.6 copy-start.1
Sparse Core Ops, SparseCore 0:
  43.8 70.3 all-gather.4

commit v15 on v13

--- a/solution.py
+++ b/solution.py
@@ -182,7 +182,7 @@
             q = rotate(q2[:, lanes], cos_ref[...], sin_ref[...]).astype(jnp.bfloat16)
             k = rotate(k2[:, lanes], cos_ref[...], sin_ref[...]).astype(jnp.bfloat16)
             v = v2[:, lanes]
-            size = 256
+            size = 128
             for b in range(C // size):
                 end = (b + 1) * size
                 scores = dot_t(q[b * size : end], k[:end])

time: 243 us -> 247 us (1.016)
  Pallas kernels: 51.9 us -> 55.1 us
    pallas_call x1, Pallas kernels: 24.6 us -> 27.9 us  [row_layer(): pl.pallas_call(row_kernel, out_shape=[shape, shape], in_specs=[pl.BlockSp...]
  transfers between devices with their start and end apart: 16 -> 16, of which waited for: 7 -> 7; matrix products, arithmetic and copies ran while one was open for 7% -> 7% of each run, Pallas kernels for 11% -> 12%
where the time goes in v15:
time: 247 us; the launch traced here: 246 us
  waiting for transfers between devices  68.7 us (28%)
  blocking collectives  65.7 us (27%)
  Pallas kernels  55.1 us (22%)
  starting transfers between devices  19.8 us (8%)
  between operations  14.9 us (6%)
  local copies, waits for them, and re-layouts  14.5 us (6%)
  other arithmetic  6.94 us (3%)
    ppermute x4, waiting for transfers between devices, shift(): lax.ppermute(value, ('ylo', 'yhi'), [(where(y), where((y + by) % 4)) for...  48.3 us
    all_to_all x1, blocking collectives, shards(): lax.all_to_all(hidden, SEQ, split_axis=0, concat_axis=0, tiled=True)  35.1 us
    pallas_call x1, Pallas kernels, row_layer(): pl.pallas_call(row_kernel, out_shape=[shape, shape], in_specs=[pl.BlockSp...  27.9 us
    pallas_call x1, Pallas kernels, column_layer(): pl.pallas_call(column_kernel, out_shape=jax.ShapeDtypeStruct((C, WIDTH),...  21.4 us
    all_gather x1, blocking collectives, column_line(): return lax.all_gather(shard, ('ylo', 'yhi'), axis=0)  16.5 us
    all_gather x1, blocking collectives, row_stack(): rows = lax.all_gather(shard, 'z', axis=0)  14.1 us
    all_to_all x1, waiting for transfers between devices, shards(): lax.all_to_all(attended, SEQ, split_axis=0, concat_axis=0, tiled=True)  12.4 us
    ppermute x4, starting transfers between devices, shift(): return lax.ppermute(value, axis, [(i, (i + by) % 4) for i in range(4)])  6.68 us
  transfers between devices with their start and end apart: 16, of which 7 were waited for; matrix products, arithmetic and copies ran while one was open for 7% of the time, Pallas kernels for 12%

profile of v15, /device:TPU:0, one launch (start us, length us, event | category | flops | bytes accessed | tf_op | source)
XLA Modules:
  0.0 245.6 jit_solution(2164184744972020240)
XLA Ops:
  6.5 0.7 fusion.7
  7.3 1.0 reshape.95
  8.3 0.1 copy.23
  8.3 0.1 reshape.96
  8.5 14.1 %all-gather.1 = bf16[64,4096]{1,0:T(8,128)(2,1)S(1)} all-gather(bf16[16,4096]{1,0:T(8,128)(2,1)S(1)} %maximum_maximum_fusion.1), channel_id=3, replica_groups=mesh['ylo'=2,'core'=2,'x'=4,'yhi'=2,'z'=4] {'z'}, dimensions={0}, use_global_device_ids=true | all-gather | bytes 655360 | tf_op jit(solution)/shard_map/all_gather | solution.py:412
  22.6 0.1 fusion.6
  22.6 1.6 collective-permute-start
  24.2 1.7 collective-permute-start.1
  26.0 0.1 copy.24
  26.1 0.1 reshape.94
  26.2 16.5 %all-gather = bf16[64,4096]{1,0:T(8,128)(2,1)} all-gather(bf16[16,4096]{1,0:T(8,128)(2,1)S(1)} %maximum_maximum_fusion), channel_id=2, replica_groups=mesh['ylo'=2,'core'=2,'x'=4,'yhi'=2,'z'=4] {'ylo','yhi'}, dimensions={0}, use_global_device_ids=true | all-gather | bytes 655360 | tf_op jit(solution)/shard_map/all_gather | solution.py:421
  42.7 0.0 collective-permute-done.1
  42.7 0.0 copy-start.6
  42.8 0.0 all-gather.5.cloned.1.call-update
  42.8 0.3 collective-permute-start.2
  43.2 3.0 %collective-permute-start.3 = (bf16[2,32,2048]{2,1,0:T(8,128)(2,1)S(1)}, bf16[2,32,2048]{2,1,0:T(8,128)(2,1)S(1)}, u32[]{:S(2)}, u32[]{:S(2)}) collective-permute-start(bf16[2,32,2048]{2,1,0:T(8,128)(2,1)S(1)} %slice.59), channel_id=1, source_target_pairs={{0,24},{8,0},{16,8},{24,16},{1,25},{9,1},{17,9},{25,17},{2,26},{10... | collective-permute-start | bytes 786440 | tf_op jit(solution)/shard_map/ppermute | solution.py:380
  46.2 4.3 %collective-permute-done.2 = bf16[2,32,2048]{2,1,0:T(8,128)(2,1)S(1)} collective-permute-done((bf16[2,32,2048]{2,1,0:T(8,128)(2,1)S(1)}, bf16[2,32,2048]{2,1,0:T(8,128)(2,1)S(1)}, u32[]{:S(2)}, u32[]{:S(2)}) %collective-permute-start.2) | collective-permute-done | bytes 262176 | tf_op jit(solution)/shard_map/ppermute | solution.py:380
  50.5 0.0 collective-permute-done.3
  50.5 0.0 copy-start.10
  50.5 0.0 copy-start.9
  50.5 0.0 copy-start.2
  50.6 0.0 copy-start.4
  50.6 2.9 %pad_maximum_fusion.refs_0_ = bf16[4,2,32,4096]{3,2,1,0:T(8,128)(2,1)} fusion(bf16[1,2,32,4096]{3,2,1,0:T(8,128)(2,1)S(1)} %maximum_bitcast_fusion, bf16[1,2,32,4096]{3,2,1,0:T(8,128)(2,1)} %bitcast.66, bf16[1,2,32,4096]{3,2,1,0:T(8,128)(2,1)S(1)} %bitcast.65, bf16[1,2,32,4096]{3,2,1,0:T(8,128)(2,1)S(1)} %get-tuple-element.27), kind=kLoop, calls=%fused_computation.1 | loop fusion | flops 3145728 | bytes 4194304 | tf_op jit(solution)/shard_map/stack | solution.py:395
  53.4 0.8 collective-permute-start.4
  54.2 2.4 collective-permute-start.5
  56.7 0.6 constant_dynamic-slice_fusion
  57.3 0.1 add_convert_fusion
  57.4 0.1 convert_element_type.35
  57.4 0.6 fusion.9
  59.3 2.1 shard_map.91.hid_ref
  61.4 0.0 copy-start.3
  61.5 0.7 add_convert_fusion.1
  62.1 1.9 fusion.4
  64.1 0.2 pad_maximum_fusion.2
  64.3 1.0 pad_maximum_fusion.4
  65.3 32.8 %collective-permute-done.4.refs_1_ = bf16[4,2,32,4096]{3,2,1,0:T(8,128)(2,1)} collective-permute-done((bf16[4,2,32,4096]{3,2,1,0:T(8,128)(2,1)}, bf16[4,2,32,4096]{3,2,1,0:T(8,128)(2,1)}, u32[]{:S(2)}, u32[]{:S(2)}) %collective-permute-start.4) | collective-permute-done | bytes 2097184 | tf_op jit(solution)/shard_map/ppermute | solution.py:379
  98.0 1.3 slice.60
  99.3 0.1 collective-permute-start.6
  99.4 0.0 collective-permute-done.5.refs_2_
  99.4 1.3 slice.61
  100.8 3.3 %collective-permute-start.7 = (bf16[4,2,32,2048]{3,2,1,0:T(8,128)(2,1)S(1)}, bf16[4,2,32,2048]{3,2,1,0:T(8,128)(2,1)S(1)}, u32[]{:S(2)}, u32[]{:S(2)}) collective-permute-start(bf16[4,2,32,2048]{3,2,1,0:T(8,128)(2,1)S(1)} %slice.61), channel_id=1, source_target_pairs={{0,68},{64,0},{4,64},{68,4},{1,69},{65,1},{5,65},{69,5},{2,70},{66... | collective-permute-start | bytes 3145736 | tf_op jit(solution)/shard_map/ppermute | solution.py:379
  104.1 0.0 collective-permute-start.10
  104.1 0.5 collective-permute-start.9
  104.6 15.4 %collective-permute-done.6.refs_3_ = bf16[4,2,32,2048]{3,2,1,0:T(8,128)(2,1)S(1)} collective-permute-done((bf16[4,2,32,2048]{3,2,1,0:T(8,128)(2,1)S(1)}, bf16[4,2,32,2048]{3,2,1,0:T(8,128)(2,1)S(1)}, u32[]{:S(2)}, u32[]{:S(2)}) %collective-permute-start.6) | collective-permute-done | bytes 1048608 | tf_op jit(solution)/shard_map/ppermute | solution.py:379
  119.9 0.0 collective-permute-start.11
  120.0 0.1 collective-permute-done.7.refs_4_
  120.1 0.4 collective-permute-start.12
  120.5 0.1 pad_add_fusion.place_ref
  120.5 2.2 collective-permute-done.11.refs_8_
  122.7 1.5 collective-permute-done.12.refs_9_
  124.3 27.9 %shard_map.92 = (bf16[512,2048]{1,0:T(8,128)(2,1)}, bf16[512,2048]{1,0:T(8,128)(2,1)}) custom-call(s32[3]{0:T(128)S(1)} %pad_add_fusion.place_ref, bf16[512,2048]{1,0:T(8,128)(2,1)} %bitcast.55, bf16[512,2048]{1,0:T(8,128)(2,1)} %copy-done.3, f32[1,2048]{1,0:T(1,128)S(1)} %bitcast.58, f32[512,128]{1,0:T(8,128)S(1)} %get-tuple-element.18.cos_ref, ...), custom_call_target="tpu_custom_call" | custom-call | flops 9663676416 | bytes 25165824 | tf_op jit(solution)/shard_map/pallas_call | solution.py:224
  152.1 0.0 all-gather.5.cloned.1.call-done
  152.2 0.2 collective-permute-start.13
  152.3 35.1 %all_to_all.22 = bf16[32,16,2048]{2,1,0:T(8,128)(2,1)} all-to-all(bf16[32,16,2048]{2,1,0:T(8,128)(2,1)} %bitcast.62), channel_id=1, replica_groups=mesh['ylo'=2,'core'=2,'x'=4,'yhi'=2,'z'=4] {'x','yhi','z'}, dimensions={0} | all-to-all | bytes 4194304 | tf_op jit(solution)/shard_map/all_to_all | solution.py:463
  187.4 21.4 %shard_map.93 = bf16[512,1024]{1,0:T(8,128)(2,1)} custom-call(s32[1]{0:T(128)} %bitcast.core_ref, bf16[512,2048]{1,0:T(8,128)(2,1)} %bitcast.63, f32[512,128]{1,0:T(8,128)} %get-tuple-element.23.cos_ref, f32[512,128]{1,0:T(8,128)} %get-tuple-element.24.sin_ref, bf16[4,4,2,2,16,4096]{5,4,3,2,1,0:T(8,128)(2,1)} %bitcast.71, ...), custom_call_target="tpu_custom_call" | custom-call | flops 7516192768 | bytes 15728640 | tf_op jit(solution)/shard_map/pallas_call | solution.py:314
  208.8 5.4 %all-to-all-start.1 = ((bf16[32,16,1024]{2,1,0:T(8,128)(2,1)}), bf16[32,16,1024]{2,1,0:T(8,128)(2,1)S(1)}, u32[]{:S(2)}, u32[]{:S(2)}) async-start(bf16[32,16,1024]{2,1,0:T(8,128)(2,1)} %bitcast.67), calls=%async_computation.1 | async-start | bytes 2097152 | tf_op jit(solution)/shard_map/all_to_all | solution.py:465
  214.3 1.8 slice_bitcast_fusion.1
  216.0 0.2 copy.18
  216.2 1.8 slice_bitcast_fusion
  218.0 1.5 copy.19
  219.5 12.4 %all-to-all-done.1 = bf16[32,16,1024]{2,1,0:T(8,128)(2,1)S(1)} async-done(((bf16[32,16,1024]{2,1,0:T(8,128)(2,1)}), bf16[32,16,1024]{2,1,0:T(8,128)(2,1)S(1)}, u32[]{:S(2)}, u32[]{:S(2)}) %all-to-all-start.1) | async-done | bytes 1048608 | tf_op jit(solution)/shard_map/all_to_all | solution.py:465
  231.8 1.6 copy-done
  233.4 1.6 copy-done.1
  235.0 3.8 %shard_map.94 = bf16[512,2048]{1,0:T(8,128)(2,1)} custom-call(s32[1]{0:T(128)} %bitcast.core_ref, bf16[512,1024]{1,0:T(8,128)(2,1)S(1)} %bitcast.54, bf16[512,2048]{1,0:T(8,128)(2,1)S(1)} %bitcast.52, bf16[512,2048]{1,0:T(8,128)(2,1)S(1)} %bitcast.53, bf16[512,2048]{1,0:T(8,128)(2,1)S(1)} %copy-done.1), custom_call_target="tpu_custom_call" | custom-call | flops 2147483648 | bytes 9437184 | tf_op jit(solution)/shard_map/pallas_call | solution.py:353
  (32 shorter events, 0.2 us)
Async XLA Ops:
  6.5 145.6 %all-gather.5.cloned.1.call-start = ((), (), s32[]{:S(2)}) async-start(), calls=%async_computation.2 | async-start | bytes 8912896 | tf_op jit(solution)/shard_map/all_gather | solution.py:425
  7.3 18.7 %copy-start.8 = (bf16[8,2048]{1,0:T(8,128)(2,1)S(1)}, bf16[8,2048]{1,0:T(8,128)(2,1)}, u32[]{:S(2)}) copy-start(bf16[8,2048]{1,0:T(8,128)(2,1)} %param.15) | copy-start | bytes 98308
  7.3 18.7 %copy-start.7 = (bf16[16,3072]{1,0:T(8,128)(2,1)S(1)}, bf16[16,3072]{1,0:T(8,128)(2,1)}, u32[]{:S(2)}) copy-start(bf16[16,3072]{1,0:T(8,128)(2,1)} %param.14) | copy-start | bytes 294916
  22.6 20.1 %collective-permute-start = (bf16[2,32,4096]{2,1,0:T(8,128)(2,1)S(1)}, bf16[2,32,4096]{2,1,0:T(8,128)(2,1)S(1)}, u32[]{:S(2)}, u32[]{:S(2)}) collective-permute-start(bf16[2,32,4096]{2,1,0:T(8,128)(2,1)S(1)} %get-tuple-element.28), channel_id=1, source_target_pairs={{0,8},{8,16},{16,24},{24,0},{1,9},{9,17},{17,25},{25,1},{2,10},{10... | collective-permute-start | bytes 1572872 | tf_op jit(solution)/shard_map/ppermute | solution.py:380
  24.2 18.5 %collective-permute-start.1 = (bf16[2,32,4096]{2,1,0:T(8,128)(2,1)S(1)}, bf16[2,32,4096]{2,1,0:T(8,128)(2,1)S(1)}, u32[]{:S(2)}, u32[]{:S(2)}) collective-permute-start(bf16[2,32,4096]{2,1,0:T(8,128)(2,1)S(1)} %get-tuple-element.28), channel_id=1, source_target_pairs={{0,24},{8,0},{16,8},{24,16},{1,25},{9,1},{17,9},{25,17},{2,26},{10... | collective-permute-start | bytes 1572872 | tf_op jit(solution)/shard_map/ppermute | solution.py:380
  42.7 7.8 %copy-start.6 = (bf16[2,32,4096]{2,1,0:T(8,128)(2,1)}, bf16[2,32,4096]{2,1,0:T(8,128)(2,1)S(1)}, u32[]{:S(2)}) copy-start(bf16[2,32,4096]{2,1,0:T(8,128)(2,1)S(1)} %collective-permute-done.1) | copy-start | bytes 1572868
  42.8 7.7 %collective-permute-start.2 = (bf16[2,32,2048]{2,1,0:T(8,128)(2,1)S(1)}, bf16[2,32,2048]{2,1,0:T(8,128)(2,1)S(1)}, u32[]{:S(2)}, u32[]{:S(2)}) collective-permute-start(bf16[2,32,2048]{2,1,0:T(8,128)(2,1)S(1)} %slice.58), channel_id=1, source_target_pairs={{0,8},{8,16},{16,24},{24,0},{1,9},{9,17},{17,25},{25,1},{2,10},{10... | collective-permute-start | bytes 786440 | tf_op jit(solution)/shard_map/ppermute | solution.py:380
  43.2 7.3 %collective-permute-start.3 = (bf16[2,32,2048]{2,1,0:T(8,128)(2,1)S(1)}, bf16[2,32,2048]{2,1,0:T(8,128)(2,1)S(1)}, u32[]{:S(2)}, u32[]{:S(2)}) collective-permute-start(bf16[2,32,2048]{2,1,0:T(8,128)(2,1)S(1)} %slice.59), channel_id=1, source_target_pairs={{0,24},{8,0},{16,8},{24,16},{1,25},{9,1},{17,9},{25,17},{2,26},{10... | collective-permute-start | bytes 786440 | tf_op jit(solution)/shard_map/ppermute | solution.py:380
  50.5 6.1 %copy-start.10 = (s32[1,32]{1,0:T(1,128)S(1)}, s32[1,32]{1,0:T(1,128)}, u32[]{:S(2)}) copy-start(s32[1,32]{1,0:T(1,128)} %param.16) | copy-start | bytes 388
  50.5 6.9 %copy-start.9 = (s32[2]{0:T(128)S(1)}, s32[2]{0:T(128)}, u32[]{:S(2)}) copy-start(s32[2]{0:T(128)} %param.17) | copy-start | bytes 28
  50.5 8.8 %copy-start.2 = (bf16[1,512,2048]{2,1,0:T(8,128)(2,1)S(1)}, bf16[1,512,2048]{2,1,0:T(8,128)(2,1)}, u32[]{:S(2)}) copy-start(bf16[1,512,2048]{2,1,0:T(8,128)(2,1)} %param.9) | copy-start | bytes 6291460
  50.6 8.8 %copy-start.4 = (f32[2048]{0:T(1024)S(1)}, f32[2048]{0:T(1024)}, u32[]{:S(2)}) copy-start(f32[2048]{0:T(1024)} %param.10) | copy-start | bytes 24580
  53.4 44.6 %collective-permute-start.4 = (bf16[4,2,32,4096]{3,2,1,0:T(8,128)(2,1)}, bf16[4,2,32,4096]{3,2,1,0:T(8,128)(2,1)}, u32[]{:S(2)}, u32[]{:S(2)}) collective-permute-start(bf16[4,2,32,4096]{3,2,1,0:T(8,128)(2,1)} %pad_maximum_fusion.refs_0_), channel_id=1, source_target_pairs={{0,64},{64,4},{4,68},{68,0},{1,65},{65,5},{5,69},{69,1},{2,66},{66... | collective-permute-start | bytes 6291464 | tf_op jit(solution)/shard_map/ppermute | solution.py:379
  54.2 45.2 %collective-permute-start.5 = (bf16[4,2,32,4096]{3,2,1,0:T(8,128)(2,1)}, bf16[4,2,32,4096]{3,2,1,0:T(8,128)(2,1)}, u32[]{:S(2)}, u32[]{:S(2)}) collective-permute-start(bf16[4,2,32,4096]{3,2,1,0:T(8,128)(2,1)} %pad_maximum_fusion.refs_0_), channel_id=1, source_target_pairs={{0,68},{64,0},{4,64},{68,4},{1,69},{65,1},{5,65},{69,5},{2,70},{66... | collective-permute-start | bytes 6291464 | tf_op jit(solution)/shard_map/ppermute | solution.py:379
  61.4 3.8 %copy-start.3 = (bf16[512,2048]{1,0:T(8,128)(2,1)}, bf16[512,2048]{1,0:T(8,128)(2,1)S(1)}, u32[]{:S(2)}) copy-start(bf16[512,2048]{1,0:T(8,128)(2,1)S(1)} %shard_map.91.hid_ref) | copy-start | bytes 6291460
  65.3 59.0 %copy-start.5 = (f32[2048]{0:T(1024)S(1)}, f32[2048]{0:T(1024)}, u32[]{:S(2)}) copy-start(f32[2048]{0:T(1024)} %param.13) | copy-start | bytes 24580
  65.3 55.3 %collective-permute-start.8 = (bf16[4,2,32,4096]{3,2,1,0:T(8,128)(2,1)}, bf16[4,2,32,4096]{3,2,1,0:T(8,128)(2,1)}, u32[]{:S(2)}, u32[]{:S(2)}) collective-permute-start(bf16[4,2,32,4096]{3,2,1,0:T(8,128)(2,1)} %pad_maximum_fusion.refs_0_), channel_id=1, source_target_pairs={{0,32},{32,0},{1,33},{33,1},{2,34},{34,2},{3,35},{35,3},{4,36},{36... | collective-permute-start | bytes 6291464 | tf_op jit(solution)/shard_map/ppermute | solution.py:399
  99.3 20.6 %collective-permute-start.6 = (bf16[4,2,32,2048]{3,2,1,0:T(8,128)(2,1)S(1)}, bf16[4,2,32,2048]{3,2,1,0:T(8,128)(2,1)S(1)}, u32[]{:S(2)}, u32[]{:S(2)}) collective-permute-start(bf16[4,2,32,2048]{3,2,1,0:T(8,128)(2,1)S(1)} %slice.60), channel_id=1, source_target_pairs={{0,64},{64,4},{4,68},{68,0},{1,65},{65,5},{5,69},{69,1},{2,66},{66... | collective-permute-start | bytes 3145736 | tf_op jit(solution)/shard_map/ppermute | solution.py:379
  100.8 19.3 %collective-permute-start.7 = (bf16[4,2,32,2048]{3,2,1,0:T(8,128)(2,1)S(1)}, bf16[4,2,32,2048]{3,2,1,0:T(8,128)(2,1)S(1)}, u32[]{:S(2)}, u32[]{:S(2)}) collective-permute-start(bf16[4,2,32,2048]{3,2,1,0:T(8,128)(2,1)S(1)} %slice.61), channel_id=1, source_target_pairs={{0,68},{64,0},{4,64},{68,4},{1,69},{65,1},{5,65},{69,5},{2,70},{66... | collective-permute-start | bytes 3145736 | tf_op jit(solution)/shard_map/ppermute | solution.py:379
  104.1 20.2 %collective-permute-start.10 = (bf16[4,2,32,4096]{3,2,1,0:T(8,128)(2,1)}, bf16[4,2,32,4096]{3,2,1,0:T(8,128)(2,1)}, u32[]{:S(2)}, u32[]{:S(2)}) collective-permute-start(bf16[4,2,32,4096]{3,2,1,0:T(8,128)(2,1)} %collective-permute-done.5.refs_2_), channel_id=1, source_target_pairs={{0,32},{32,0},{1,33},{33,1},{2,34},{34,2},{3,35},{35,3},{4,36},{36... | collective-permute-start | bytes 6291464 | tf_op jit(solution)/shard_map/ppermute | solution.py:399
  104.1 20.2 %collective-permute-start.9 = (bf16[4,2,32,4096]{3,2,1,0:T(8,128)(2,1)}, bf16[4,2,32,4096]{3,2,1,0:T(8,128)(2,1)}, u32[]{:S(2)}, u32[]{:S(2)}) collective-permute-start(bf16[4,2,32,4096]{3,2,1,0:T(8,128)(2,1)} %collective-permute-done.4.refs_1_), channel_id=1, source_target_pairs={{0,32},{32,0},{1,33},{33,1},{2,34},{34,2},{3,35},{35,3},{4,36},{36... | collective-permute-start | bytes 6291464 | tf_op jit(solution)/shard_map/ppermute | solution.py:399
  119.9 2.8 %collective-permute-start.11 = (bf16[4,2,32,2048]{3,2,1,0:T(8,128)(2,1)S(1)}, bf16[4,2,32,2048]{3,2,1,0:T(8,128)(2,1)}, u32[]{:S(2)}, u32[]{:S(2)}) collective-permute-start(bf16[4,2,32,2048]{3,2,1,0:T(8,128)(2,1)S(1)} %collective-permute-done.6.refs_3_), channel_id=1, source_target_pairs={{0,32},{32,0},{1,33},{33,1},{2,34},{34,2},{3,35},{35,3},{4,36},{36... | collective-permute-start | bytes 3145736 | tf_op jit(solution)/shard_map/ppermute | solution.py:399
  120.1 4.1 %collective-permute-start.12 = (bf16[4,2,32,2048]{3,2,1,0:T(8,128)(2,1)S(1)}, bf16[4,2,32,2048]{3,2,1,0:T(8,128)(2,1)}, u32[]{:S(2)}, u32[]{:S(2)}) collective-permute-start(bf16[4,2,32,2048]{3,2,1,0:T(8,128)(2,1)S(1)} %collective-permute-done.7.refs_4_), channel_id=1, source_target_pairs={{0,32},{32,0},{1,33},{33,1},{2,34},{34,2},{3,35},{35,3},{4,36},{36... | collective-permute-start | bytes 3145736 | tf_op jit(solution)/shard_map/ppermute | solution.py:399
  152.2 35.2 %collective-permute-start.13 = (bf16[4,4,2,2,16,4096]{5,4,3,2,1,0:T(8,128)(2,1)}, bf16[4,4,2,2,16,4096]{5,4,3,2,1,0:T(8,128)(2,1)}, u32[]{:S(2)}, u32[]{:S(2)}) collective-permute-start(bf16[4,4,2,2,16,4096]{5,4,3,2,1,0:T(8,128)(2,1)} %bitcast.70), channel_id=1, source_target_pairs={{0,32},{32,0},{1,33},{33,1},{2,34},{34,2},{3,35},{35,3},{4,36},{36... | collective-permute-start | bytes 25165832 | tf_op jit(solution)/shard_map/ppermute | solution.py:399
  208.8 23.0 %all-to-all-start.1 = ((bf16[32,16,1024]{2,1,0:T(8,128)(2,1)}), bf16[32,16,1024]{2,1,0:T(8,128)(2,1)S(1)}, u32[]{:S(2)}, u32[]{:S(2)}) async-start(bf16[32,16,1024]{2,1,0:T(8,128)(2,1)} %bitcast.67), calls=%async_computation.1 | async-start | bytes 2097152 | tf_op jit(solution)/shard_map/all_to_all | solution.py:465
  231.8 1.6 copy-start
  233.4 1.6 copy-start.1
Sparse Core Ops, SparseCore 0:
  42.9 70.2 all-gather.4
